TPU v7x, 128 devices: a whole 4x4x4 slice. The times are simulated.
128 devices in a mesh: grid: 32 (over x, y, core), sub: 4 (over z).
Axes of the slice: x: 4, y: 4, z: 4, core: 2. Of those that a mesh axis runs over, the one named last changes fastest.
Arguments:
- grid_x: bfloat16 [262144, 512], P(('grid', 'sub')), may hold values from -6 to 6
- mesh_h: bfloat16 [8192, 512], P(('grid', 'sub')), may hold values from -6 to 6
- gain_grid: float32 [512], replicated, may hold values from 0.1 to 1.9
- gain_mesh: float32 [512], replicated, may hold values from 0.1 to 1.9
- w_query: bfloat16 [512, 512], replicated, may hold values from -0.25 to 0.25
- w_key: bfloat16 [512, 512], replicated, may hold values from -0.25 to 0.25
- w_value: bfloat16 [512, 512], replicated, may hold values from -0.25 to 0.25
- w_out: bfloat16 [512, 512], replicated, may hold values from -0.25 to 0.25
- edge_bias: float32 [8192, 384], P(('grid', 'sub')), may hold values from -9 to 300
- neighbours: int32 [8192, 96], P(('grid', 'sub')), may hold values from 0 to 767, as said below
- valid: int32 [8192, 96], P(('grid', 'sub')), may hold values from 0 to 1, as said below
- send_rows: int32 [128, 3, 4, 64], P(('grid', 'sub')), may hold values from 0 to 2047, as said below
- out_grad: bfloat16 [8192, 512], P(('grid', 'sub')), may hold values from -24 to 24
Outputs:
- mesh_out: bfloat16 [8192, 512], P(('grid', 'sub'))
- mesh_grad: bfloat16 [8192, 512], P(('grid', 'sub'))
- grid_grad: bfloat16 [262144, 512], P(('grid', 'sub'))
- weight_grads: float32 [4, 512, 512], replicated
Inputs may be any that keep to these rules, and one draw needn't show every extreme that they name: `send_rows`: for each source device, slab offset and destination sub index the 64 local rows are distinct; rows sent to the slab below (o = 0) lie in the lower half of the device's 2048 rows, rows sent to the slab above (o = 2) in the upper half. `neighbours`: a slot (o * 4 + s) * 64 + t names row t of what device s of slab g - o + 1 sends to the node's device; slots of slabs outside the grid are never named; the 96 entries of a node are distinct; some slots are named by no node. The first two edges of every node are valid.
All inputs are finite; a program needn't handle non-finite values.
Results may differ from a plain program's by a relative error of at most 0.009.
Values may be sent and summed in bfloat16 or wider, within the bound.
No kernel may reach another device: no remote copies, remote signals or barrier semaphores. Data moves between devices by JAX's collectives and lax.ppermute only.
A program may use at most 128 MiB of HBM per device.

v0:
```python
import jax
import jax.numpy as jnp
from jax import lax
from jax.sharding import Mesh
from jax.sharding import PartitionSpec as P

GRID = ("grid_0", "grid_1", "grid_2")
GRID_SUB = ("grid_0", "grid_1", "grid_2", "sub")


EPSILON = 1e-06
NEG_FILL = -1e30


def from_behind(block, axis, distance):
    devices = range(lax.axis_size(axis))
    route = [(i - distance, i) for i in devices if i - distance in devices]
    return lax.ppermute(block, axis, route)


def in_blocks(array, dim, count):
    lengths = array.shape
    blocks = array.reshape(*lengths[:dim], count, lengths[dim] // count, *lengths[dim + 1 :])
    return jnp.moveaxis(blocks, dim, 0)


def summed_on_arrival(array, axis, dim):
    count = lax.axis_size(axis)
    blocks = lax.all_to_all(in_blocks(array, dim, count), axis, 0, 0, tiled=True)
    return jnp.sum(blocks.astype(jnp.float32), axis=0)


def sum_in_two_steps(array, axes, dim):
    far, near = axes
    blocks = in_blocks(array, dim, lax.axis_size(far))
    nearer = summed_on_arrival(blocks, near, dim + 1)
    arrived = lax.all_to_all(
        nearer.astype(jnp.bfloat16), far, split_axis=0, concat_axis=0, tiled=True
    )
    return arrived.astype(jnp.float32).sum(axis=0)


def rows_for(lines, count):
    spare = -lines.shape[0] % count
    if not spare:
        return lines
    return jnp.concatenate([lines, jnp.zeros((spare, *lines.shape[1:]), lines.dtype)])


def sent_to_all(array, axis):
    count = lax.axis_size(axis)
    return lax.all_to_all(
        jnp.broadcast_to(array[None], (count, *array.shape)), axis, 0, 0, tiled=True
    )


def laid_out(blocks, dim):
    blocks = jnp.moveaxis(blocks, 0, dim)
    lengths = blocks.shape
    return blocks.reshape(*lengths[:dim], lengths[dim] * lengths[dim + 1], *lengths[dim + 2 :])


def gather_axes(array, axes, dim):
    far, near = axes
    leading = sent_to_all(array, far)
    blocks = jnp.swapaxes(sent_to_all(leading, near), 0, 1)
    return laid_out(blocks.reshape(-1, *array.shape), dim)


def total_of(array, axes):
    lines = array.reshape(-1, array.shape[-1])
    own = sum_in_two_steps(
        rows_for(lines, lax.axis_size(axes[0]) * lax.axis_size(axes[1])), axes, 0
    )
    whole = gather_axes(own.astype(jnp.bfloat16), axes, 0)
    return whole[: len(lines)].reshape(array.shape).astype(jnp.float32)


def normalize(values_in, gain_row):
    widened = values_in.astype(jnp.float32)
    factor = lax.rsqrt(jnp.mean(widened * widened, axis=-1, keepdims=True) + EPSILON)
    return (widened, factor, (widened * factor * gain_row).astype(jnp.bfloat16))


def normalize_back(widened, factor, gain_row, upstream):
    scaled = gain_row * upstream
    inner_mean = jnp.mean(widened * scaled, axis=-1, keepdims=True)
    return factor * scaled - widened * factor**3 * inner_mean


def shards(
    grid_x,
    mesh_h,
    gain_grid,
    gain_mesh,
    w_query,
    w_key,
    w_value,
    w_out,
    edge_bias,
    neighbours,
    valid,
    send_rows,
    out_grad,
):
    point_count, model_width = grid_x.shape
    node_count = mesh_h.shape[0]
    sub_count = send_rows.shape[2]
    slots_per = send_rows.shape[3]
    block = sub_count * slots_per
    slot_count = 3 * block
    fanout = neighbours.shape[1]
    head_count = edge_bias.shape[1] // fanout
    head_width = model_width // head_count
    logit_scale = head_width ** (-0.5)
    w_pair = jnp.concatenate([w_key, w_value], axis=1)
    grid_wide, grid_factor, grid_normed = normalize(grid_x, gain_grid)
    flat_rows = send_rows[0].reshape(slot_count)
    send_match = flat_rows[:, None] == jnp.arange(point_count, dtype=jnp.int32)[None, :]
    send_onehot = send_match.astype(jnp.bfloat16)
    sent_normed = jnp.dot(send_onehot, grid_normed, preferred_element_type=jnp.float32).astype(
        jnp.bfloat16
    )
    packet = sent_normed.reshape(3, sub_count, slots_per, model_width)
    packet_width = packet.shape[3]
    mixed = lax.all_to_all(packet, "sub", split_axis=1, concat_axis=1, tiled=True).reshape(
        3, block, packet_width
    )
    pieces = []
    for offset in (0, 1, 2):
        piece = mixed[offset]
        if offset != 1:
            piece = from_behind(piece, GRID, offset - 1)
        pieces.append(piece)
    arrived = jnp.concatenate(pieces, axis=0)
    recv_pair = jnp.dot(arrived, w_pair, preferred_element_type=jnp.float32).astype(jnp.bfloat16)
    slot_onehot = (
        neighbours[:, :, None] == jnp.arange(slot_count, dtype=jnp.int32)[None, None, :]
    ).astype(jnp.bfloat16)
    edge_pair = jnp.einsum(
        "gjc,ce->gje", slot_onehot, recv_pair, preferred_element_type=jnp.float32
    ).astype(jnp.bfloat16)
    edge_keys = edge_pair[:, :, :model_width].reshape(node_count, fanout, head_count, head_width)
    edge_values = edge_pair[:, :, model_width:].reshape(node_count, fanout, head_count, head_width)
    mesh_wide, mesh_factor, mesh_normed = normalize(mesh_h, gain_mesh)
    queries = (
        jnp.dot(mesh_normed, w_query, preferred_element_type=jnp.float32) * logit_scale
    ).astype(jnp.bfloat16)
    query_head_rows = queries.reshape(node_count, head_count, head_width)
    score_matrix = jnp.einsum(
        "gip,gjip->gij", query_head_rows, edge_keys, preferred_element_type=jnp.float32
    ) + edge_bias.reshape(node_count, head_count, fanout)
    live_mask = (valid == 1)[:, None, :]
    row_peak = jnp.max(jnp.where(live_mask, score_matrix, NEG_FILL), axis=2, keepdims=True)
    exp_terms = jnp.exp(jnp.where(live_mask, score_matrix - row_peak, NEG_FILL))
    attn_probs = exp_terms / jnp.sum(exp_terms, axis=2, keepdims=True)
    probabilities_batch = attn_probs.astype(jnp.bfloat16)
    attended_rows = (
        jnp.einsum(
            "gij,gjik->gik", probabilities_batch, edge_values, preferred_element_type=jnp.float32
        )
        .reshape(node_count, model_width)
        .astype(jnp.bfloat16)
    )
    mesh_out = (
        mesh_wide + jnp.dot(attended_rows, w_out, preferred_element_type=jnp.float32)
    ).astype(jnp.bfloat16)
    grad_wo = jnp.einsum("md,me->de", attended_rows, out_grad, preferred_element_type=jnp.float32)
    att_grad = jnp.einsum("me,de->md", out_grad, w_out, preferred_element_type=jnp.float32).astype(
        jnp.bfloat16
    )
    head_gradient = att_grad.reshape(node_count, head_count, head_width)
    probability_gradient = jnp.einsum(
        "gip,gjip->gij", head_gradient, edge_values, preferred_element_type=jnp.float32
    )
    score_gradient = (
        attn_probs
        * (probability_gradient - jnp.sum(attn_probs * probability_gradient, axis=2, keepdims=True))
    ).astype(jnp.bfloat16)
    query_gradient = (
        (
            jnp.einsum(
                "gij,gjik->gik", score_gradient, edge_keys, preferred_element_type=jnp.float32
            )
            * logit_scale
        )
        .reshape(node_count, model_width)
        .astype(jnp.bfloat16)
    )
    dense_score_gradient = jnp.einsum(
        "gij,gjc->gic", score_gradient, slot_onehot, preferred_element_type=jnp.float32
    ).astype(jnp.bfloat16)
    dense_probabilities = jnp.einsum(
        "gij,gjc->gic", probabilities_batch, slot_onehot, preferred_element_type=jnp.float32
    ).astype(jnp.bfloat16)
    key_part = jnp.einsum(
        "uza,uzt->azt", dense_score_gradient, query_head_rows, preferred_element_type=jnp.float32
    ).reshape(slot_count, model_width)
    value_part = jnp.einsum(
        "uza,uzt->azt", dense_probabilities, head_gradient, preferred_element_type=jnp.float32
    ).reshape(slot_count, model_width)
    back_packet = (
        jnp.concatenate([key_part, value_part], axis=1)
        .astype(jnp.bfloat16)
        .reshape(3, block, 2 * model_width)
    )
    home_pieces = []
    for offset in (0, 1, 2):
        piece = back_packet[offset]
        if offset != 1:
            piece = from_behind(piece, GRID, 1 - offset)
        home_pieces.append(piece)
    home = jnp.stack(home_pieces)
    home = home.reshape(3, sub_count, slots_per, 2 * model_width)
    returned = lax.all_to_all(home, "sub", split_axis=1, concat_axis=1, tiled=True).reshape(
        slot_count, 2 * model_width
    )
    pair_grads = jnp.einsum("sd,se->de", sent_normed, returned, preferred_element_type=jnp.float32)
    slot_back = jnp.einsum("se,de->sd", returned, w_pair, preferred_element_type=jnp.float32)
    normed_grad = jnp.einsum(
        "sp,sd->pd",
        send_match.astype(jnp.float32),
        slot_back,
        precision=lax.Precision.HIGHEST,
        preferred_element_type=jnp.float32,
    )
    grid_grad = normalize_back(grid_wide, grid_factor, gain_grid, normed_grad).astype(jnp.bfloat16)
    grad_wq = jnp.einsum(
        "md,me->de", mesh_normed, query_gradient, preferred_element_type=jnp.float32
    )
    mesh_normed_grad = jnp.einsum(
        "me,de->md", query_gradient, w_query, preferred_element_type=jnp.float32
    )
    mesh_grad = (
        out_grad.astype(jnp.float32)
        + normalize_back(mesh_wide, mesh_factor, gain_mesh, mesh_normed_grad)
    ).astype(jnp.bfloat16)
    local_grads = jnp.stack(
        [grad_wq, pair_grads[:, :model_width], pair_grads[:, model_width:], grad_wo]
    )
    weight_grads = total_of(
        local_grads.astype(jnp.bfloat16), (("grid_0", "grid_1"), ("grid_2", "sub"))
    )
    return (mesh_out, mesh_grad, grid_grad, weight_grads)


def solution(mesh):
    split = Mesh(
        mesh.devices.reshape(4, 4, 2, mesh.shape["sub"]), ("grid_0", "grid_1", "grid_2", "sub")
    )
    return jax.shard_map(
        shards,
        mesh=split,
        in_specs=(
            P(GRID_SUB, None),
            P(GRID_SUB, None),
            P(),
            P(),
            P(),
            P(),
            P(),
            P(),
            P(GRID_SUB, None),
            P(GRID_SUB, None),
            P(GRID_SUB, None),
            P(GRID_SUB, None, None, None),
            P(GRID_SUB, None),
        ),
        out_specs=(P(GRID_SUB, None), P(GRID_SUB, None), P(GRID_SUB, None), P()),
        check_vma=False,
    )
```

profile of v0, /device:TPU:1, one launch (start us, length us, event | category | flops | bytes accessed | tf_op | source)
XLA Modules:
  0.0 209.8 jit_solution(1306217201877086940)
XLA Ops:
  8.3 5.9 %all-to-all-start = ((bf16[3,4,64,512]{3,2,0,1:T(8,128)(2,1)}), bf16[3,4,64,512]{3,2,0,1:T(8,128)(2,1)S(1)}, u32[]{:S(2)}, u32[]{:S(2)}) async-start(bf16[3,4,64,512]{3,2,0,1:T(8,128)(2,1)} %copy.53), calls=%async_computation | async-start | bytes 1572864 | tf_op jit(solution)/shard_map/all_to_all | solution.py:126
  16.3 9.3 %all-to-all-done = bf16[3,4,64,512]{3,2,0,1:T(8,128)(2,1)S(1)} async-done(((bf16[3,4,64,512]{3,2,0,1:T(8,128)(2,1)}), bf16[3,4,64,512]{3,2,0,1:T(8,128)(2,1)S(1)}, u32[]{:S(2)}, u32[]{:S(2)}) %all-to-all-start) | async-done | bytes 786464 | tf_op jit(solution)/shard_map/all_to_all | solution.py:126
  25.6 3.8 %collective-permute-start = (bf16[256,512]{1,0:T(8,128)(2,1)S(1)}, bf16[256,512]{1,0:T(8,128)(2,1)S(1)}, u32[]{:S(2)}, u32[]{:S(2)}) collective-permute-start(bf16[256,512]{1,0:T(8,128)(2,1)S(1)} %bitcast.130), channel_id=1, source_target_pairs={{4,0},{8,4},{12,8},{16,12},{20,16},{24,20},{28,24},{32,28},{36,32}... | collective-permute-start | bytes 786440 | tf_op jit(solution)/shard_map/ppermute | solution.py:18
  38.0 10.7 %fusion.7 = bf16[64,96,1024]{2,1,0:T(8,128)(2,1)S(1)} fusion(s32[64,96]{1,0:T(8,128)S(1)} %copy-done.29, bf16[768,1024,1]{1,0,2:T(8,128)(2,1)S(1)} %fusion.124), kind=kOutput, calls=%fused_computation.12 | convolution fusion | flops 9674686464 | bytes 14180352 | tf_op jit(solution)/shard_map/gjc,ce->gje/dot_general | solution.py:140
  48.7 3.7 %slice_bitcast_fusion.1 = (bf16[64,12,4,8,128]{4,3,2,1,0:T(8,128)(2,1)S(1)}, bf16[64,12,4,8,128]{4,3,2,1,0:T(8,128)(2,1)S(1)}) fusion(bf16[64,96,1024]{2,1,0:T(8,128)(2,1)S(1)} %fusion.7), kind=kLoop, calls=%fused_computation.22 | loop fusion | bytes 25165824
  52.5 3.3 %fusion.14 = f32[64,4,1,96]{3,2,1,0:T(1,128)S(1)} fusion(bf16[64,4,128,1]{2,3,1,0:T(2,128)(2,1)S(1)} %reshape.131, bf16[64,12,4,8,128]{4,3,2,1,0:T(8,128)(2,1)S(1)} %get-tuple-element.24), kind=kOutput, calls=%fused_computation.19 | convolution fusion | flops 6291456 | bytes 6455296 | tf_op jit(solution)/shard_map/gip,gjip->gij/dot_general | solution.py:150
  55.8 3.3 %fusion.8 = f32[64,4,1,96]{3,2,1,0:T(1,128)S(1)} fusion(bf16[64,4,128,1]{2,3,1,0:T(2,128)(2,1)S(1)} %reshape.133, bf16[64,12,4,8,128]{4,3,2,1,0:T(8,128)(2,1)S(1)} %get-tuple-element.25), kind=kOutput, calls=%fused_computation.13 | convolution fusion | flops 6291456 | bytes 6455296 | tf_op jit(solution)/shard_map/gip,gjip->gij/dot_general | solution.py:173
  59.5 3.6 %fusion.39 = bf16[64,4,768]{2,1,0:T(4,128)(2,1)S(1)} fusion(s32[64,96]{1,0:T(8,128)S(1)} %copy-done.29, f32[64,4,96]{2,1,0:T(4,128)S(1)} %get-tuple-element.41, f32[64,4]{1,0:T(8,128)S(1)} %get-tuple-element.40), kind=kOutput, calls=%fused_computation.58 | convolution fusion | flops 42713088 | bytes 517120 | tf_op jit(solution)/shard_map/gij,gjc->gic/dot_general | solution.py:193
  64.1 3.5 %fusion.38 = bf16[64,4,768]{2,1,0:T(4,128)(2,1)S(1)} fusion(bf16[64,4,96]{2,1,0:T(4,128)(2,1)S(1)} %get-tuple-element.34, s32[64,96]{1,0:T(8,128)S(1)} %copy-done.29), kind=kOutput, calls=%fused_computation.57 | convolution fusion | flops 42663936 | bytes 466944 | tf_op jit(solution)/shard_map/gij,gjc->gic/dot_general | solution.py:190
  69.2 4.4 %collective-permute-start.2 = (bf16[256,1024]{1,0:T(8,128)(2,1)S(1)}, bf16[256,1024]{1,0:T(8,128)(2,1)S(1)}, u32[]{:S(2)}, u32[]{:S(2)}) collective-permute-start(bf16[256,1024]{1,0:T(8,128)(2,1)S(1)} %get-tuple-element.26), channel_id=1, source_target_pairs={{0,4},{4,8},{8,12},{12,16},{16,20},{20,24},{24,28},{28,32},{32,36}... | collective-permute-start | bytes 1572872 | tf_op jit(solution)/shard_map/ppermute | solution.py:18
  75.8 4.0 %collective-permute-done.2 = bf16[256,1024]{1,0:T(8,128)(2,1)S(1)} collective-permute-done((bf16[256,1024]{1,0:T(8,128)(2,1)S(1)}, bf16[256,1024]{1,0:T(8,128)(2,1)S(1)}, u32[]{:S(2)}, u32[]{:S(2)}) %collective-permute-start.2) | collective-permute-done | bytes 524320 | tf_op jit(solution)/shard_map/ppermute | solution.py:18
  79.7 4.4 %collective-permute-done.3 = bf16[256,1024]{1,0:T(8,128)(2,1)S(1)} collective-permute-done((bf16[256,1024]{1,0:T(8,128)(2,1)S(1)}, bf16[256,1024]{1,0:T(8,128)(2,1)S(1)}, u32[]{:S(2)}, u32[]{:S(2)}) %collective-permute-start.3) | collective-permute-done | bytes 524320 | tf_op jit(solution)/shard_map/ppermute | solution.py:18
  85.6 4.5 %all-to-all-start.1 = ((bf16[3,4,64,1024]{3,2,0,1:T(8,128)(2,1)}), bf16[3,4,64,1024]{3,2,0,1:T(8,128)(2,1)}, u32[]{:S(2)}, u32[]{:S(2)}) async-start(bf16[3,4,64,1024]{3,2,0,1:T(8,128)(2,1)} %copy.60), calls=%async_computation.1 | async-start | bytes 3145728 | tf_op jit(solution)/shard_map/all_to_all | solution.py:215
  90.1 4.7 %fusion.10 = f32[64,4,1,128]{3,2,1,0:T(1,128)S(1)} fusion(bf16[64,12,4,8,128]{4,3,2,1,0:T(8,128)(2,1)} %copy-done.2, bf16[64,4,96,1]{2,1,0,3:T(4,128)(2,1)S(1)} %copy-done.16), kind=kOutput, calls=%fused_computation.15 | convolution fusion | flops 6291456 | bytes 6471680 | tf_op jit(solution)/shard_map/gij,gjik->gik/dot_general | solution.py:159
  98.2 6.7 %all-to-all-done.1 = bf16[3,4,64,1024]{3,2,0,1:T(8,128)(2,1)} async-done(((bf16[3,4,64,1024]{3,2,0,1:T(8,128)(2,1)}), bf16[3,4,64,1024]{3,2,0,1:T(8,128)(2,1)}, u32[]{:S(2)}, u32[]{:S(2)}) %all-to-all-start.1) | async-done | bytes 1572896 | tf_op jit(solution)/shard_map/all_to_all | solution.py:215
  111.4 28.6 %all_to_all.30 = bf16[8,16,16,512]{3,2,1,0:T(8,128)(2,1)S(1)} all-to-all(bf16[8,16,16,512]{3,2,1,0:T(8,128)(2,1)S(1)} %bitcast.112), channel_id=1, replica_groups=mesh['grid_0'=4,'grid_1'=4,'grid_2'=2,'sub'=4] {'grid_2','sub'}, dimensions={0} | all-to-all | bytes 4194304 | tf_op jit(solution)/shard_map/all_to_all | solution.py:29
  141.0 12.3 %all-to-all-start.3 = ((bf16[16,16,512]{2,1,0:T(8,128)(2,1)}), bf16[16,16,512]{2,1,0:T(8,128)(2,1)S(1)}, u32[]{:S(2)}, u32[]{:S(2)}) async-start(bf16[16,16,512]{2,1,0:T(8,128)(2,1)} %reduce_sum.84), calls=%async_computation.3 | async-start | bytes 524288 | tf_op jit(solution)/shard_map/all_to_all | solution.py:37
  154.4 6.5 %all-to-all-done.3 = bf16[16,16,512]{2,1,0:T(8,128)(2,1)S(1)} async-done(((bf16[16,16,512]{2,1,0:T(8,128)(2,1)}), bf16[16,16,512]{2,1,0:T(8,128)(2,1)S(1)}, u32[]{:S(2)}, u32[]{:S(2)}) %all-to-all-start.3) | async-done | bytes 262176 | tf_op jit(solution)/shard_map/all_to_all | solution.py:37
  161.7 3.7 %all-to-all-start.4 = ((bf16[16,16,512]{2,1,0:T(8,128)(2,1)}), bf16[16,16,512]{2,1,0:T(8,128)(2,1)S(1)}, u32[]{:S(2)}, u32[]{:S(2)}) async-start(bf16[16,16,512]{2,1,0:T(8,128)(2,1)} %broadcast_in_dim.22), calls=%async_computation.4 | async-start | bytes 524288 | tf_op jit(solution)/shard_map/all_to_all | solution.py:52
  166.3 6.5 %all-to-all-done.4 = bf16[16,16,512]{2,1,0:T(8,128)(2,1)S(1)} async-done(((bf16[16,16,512]{2,1,0:T(8,128)(2,1)}), bf16[16,16,512]{2,1,0:T(8,128)(2,1)S(1)}, u32[]{:S(2)}, u32[]{:S(2)}) %all-to-all-start.4) | async-done | bytes 262176 | tf_op jit(solution)/shard_map/all_to_all | solution.py:52
  174.4 6.6 %all-to-all-start.5 = ((bf16[8,16,16,512]{3,2,1,0:T(8,128)(2,1)}), bf16[8,16,16,512]{3,2,1,0:T(8,128)(2,1)S(1)}, u32[]{:S(2)}, u32[]{:S(2)}) async-start(bf16[8,16,16,512]{3,2,1,0:T(8,128)(2,1)} %broadcast_in_dim.23), calls=%async_computation.5 | async-start | bytes 4194304 | tf_op jit(solution)/shard_map/all_to_all | solution.py:52
  184.6 6.1 %fusion.28 = (f32[2048]{0:T(1024)S(1)}, f32[2048,512]{0,1:T(8,128)S(1)}) fusion(bf16[2048,512]{0,1:T(8,128)(2,1)S(1)} %copy-done.4, f32[512]{0:T(512)S(1)} %copy-done.27, f32[768,512]{1,0:T(8,128)S(1)} %fusion.95, s32[768]{0:T(1024)S(1)} %copy-done.25), kind=kOutput, calls=%fused_computation.36 | convolution fusion | flops 9669441536 | bytes 7877632 | tf_op jit(solution)/shard_map/sp,sd->pd/dot_general | solution.py:220
  193.3 3.9 %copy.64 = bf16[2048,512]{1,0:T(8,128)(2,1)} copy(bf16[2048,512]{0,1:T(8,128)(2,1)} %fusion.27) | data formatting | bytes 4194304
  197.2 10.0 %all-to-all-done.5 = bf16[8,16,16,512]{3,2,1,0:T(8,128)(2,1)S(1)} async-done(((bf16[8,16,16,512]{3,2,1,0:T(8,128)(2,1)}), bf16[8,16,16,512]{3,2,1,0:T(8,128)(2,1)S(1)}, u32[]{:S(2)}, u32[]{:S(2)}) %all-to-all-start.5) | async-done | bytes 2097184 | tf_op jit(solution)/shard_map/all_to_all | solution.py:52
  (119 shorter events, 48.7 us)
Async XLA Ops:
  0.6 15.3 %copy-start = (bf16[512,512]{1,0:T(8,128)(2,1)S(1)}, bf16[512,512]{1,0:T(8,128)(2,1)}, u32[]{:S(2)}) copy-start(bf16[512,512]{1,0:T(8,128)(2,1)} %param.17) | copy-start | bytes 1572868
  6.4 7.7 %copy-start.5 = (bf16[64,512]{1,0:T(8,128)(2,1)S(1)}, bf16[64,512]{1,0:T(8,128)(2,1)}, u32[]{:S(2)}) copy-start(bf16[64,512]{1,0:T(8,128)(2,1)} %param.14) | copy-start | bytes 196612
  7.3 7.5 %copy-start.11 = (bf16[512,512]{1,0:T(8,128)(2,1)S(1)}, bf16[512,512]{1,0:T(8,128)(2,1)}, u32[]{:S(2)}) copy-start(bf16[512,512]{1,0:T(8,128)(2,1)} %param.18) | copy-start | bytes 1572868
  7.3 8.3 %copy-start.6 = (bf16[512,512]{1,0:T(8,128)(2,1)S(1)}, bf16[512,512]{1,0:T(8,128)(2,1)}, u32[]{:S(2)}) copy-start(bf16[512,512]{1,0:T(8,128)(2,1)} %param.20) | copy-start | bytes 1572868
  7.4 8.3 %copy-start.10 = (bf16[64,512]{1,0:T(8,128)(2,1)S(1)}, bf16[64,512]{1,0:T(8,128)(2,1)}, u32[]{:S(2)}) copy-start(bf16[64,512]{1,0:T(8,128)(2,1)} %param.25) | copy-start | bytes 196612
  7.4 8.6 %copy-start.18 = (f32[512]{0:T(512)S(1)}, f32[512]{0:T(512)}, u32[]{:S(2)}) copy-start(f32[512]{0:T(512)} %param.16) | copy-start | bytes 6148
  8.3 17.2 %all-to-all-start = ((bf16[3,4,64,512]{3,2,0,1:T(8,128)(2,1)}), bf16[3,4,64,512]{3,2,0,1:T(8,128)(2,1)S(1)}, u32[]{:S(2)}, u32[]{:S(2)}) async-start(bf16[3,4,64,512]{3,2,0,1:T(8,128)(2,1)} %copy.53), calls=%async_computation | async-start | bytes 1572864 | tf_op jit(solution)/shard_map/all_to_all | solution.py:126
  14.2 18.5 %copy-start.12 = (bf16[512,512]{1,0:T(8,128)(2,1)S(1)}, bf16[512,512]{1,0:T(8,128)(2,1)}, u32[]{:S(2)}) copy-start(bf16[512,512]{1,0:T(8,128)(2,1)} %param.19) | copy-start | bytes 1572868
  15.7 17.9 %copy-start.13 = (f32[64,384]{1,0:T(8,128)S(1)}, f32[64,384]{1,0:T(8,128)}, u32[]{:S(2)}) copy-start(f32[64,384]{1,0:T(8,128)} %param.21) | copy-start | bytes 294916
  16.0 17.8 %copy-start.17 = (s32[64,96]{1,0:T(8,128)S(1)}, s32[64,96]{1,0:T(8,128)}, u32[]{:S(2)}) copy-start(s32[64,96]{1,0:T(8,128)} %param.23) | copy-start | bytes 73732
  25.6 9.0 %collective-permute-start = (bf16[256,512]{1,0:T(8,128)(2,1)S(1)}, bf16[256,512]{1,0:T(8,128)(2,1)S(1)}, u32[]{:S(2)}, u32[]{:S(2)}) collective-permute-start(bf16[256,512]{1,0:T(8,128)(2,1)S(1)} %bitcast.130), channel_id=1, source_target_pairs={{4,0},{8,4},{12,8},{16,12},{20,16},{24,20},{28,24},{32,28},{36,32}... | collective-permute-start | bytes 786440 | tf_op jit(solution)/shard_map/ppermute | solution.py:18
  29.4 6.4 %collective-permute-start.1 = (bf16[256,512]{1,0:T(8,128)(2,1)S(1)}, bf16[256,512]{1,0:T(8,128)(2,1)S(1)}, u32[]{:S(2)}, u32[]{:S(2)}) collective-permute-start(bf16[256,512]{1,0:T(8,128)(2,1)S(1)} %bitcast.129), channel_id=1, source_target_pairs={{0,4},{4,8},{8,12},{12,16},{16,20},{20,24},{24,28},{28,32},{32,36}... | collective-permute-start | bytes 786440 | tf_op jit(solution)/shard_map/ppermute | solution.py:18
  52.5 6.7 %copy-start.2 = (bf16[64,12,4,8,128]{4,3,2,1,0:T(8,128)(2,1)}, bf16[64,12,4,8,128]{4,3,2,1,0:T(8,128)(2,1)S(1)}, u32[]{:S(2)}) copy-start(bf16[64,12,4,8,128]{4,3,2,1,0:T(8,128)(2,1)S(1)} %get-tuple-element.25) | copy-start | bytes 18874372
  69.2 10.5 %collective-permute-start.2 = (bf16[256,1024]{1,0:T(8,128)(2,1)S(1)}, bf16[256,1024]{1,0:T(8,128)(2,1)S(1)}, u32[]{:S(2)}, u32[]{:S(2)}) collective-permute-start(bf16[256,1024]{1,0:T(8,128)(2,1)S(1)} %get-tuple-element.26), channel_id=1, source_target_pairs={{0,4},{4,8},{8,12},{12,16},{16,20},{20,24},{24,28},{28,32},{32,36}... | collective-permute-start | bytes 1572872 | tf_op jit(solution)/shard_map/ppermute | solution.py:18
  73.6 10.5 %collective-permute-start.3 = (bf16[256,1024]{1,0:T(8,128)(2,1)S(1)}, bf16[256,1024]{1,0:T(8,128)(2,1)S(1)}, u32[]{:S(2)}, u32[]{:S(2)}) collective-permute-start(bf16[256,1024]{1,0:T(8,128)(2,1)S(1)} %get-tuple-element.27), channel_id=1, source_target_pairs={{4,0},{8,4},{12,8},{16,12},{20,16},{24,20},{28,24},{32,28},{36,32}... | collective-permute-start | bytes 1572872 | tf_op jit(solution)/shard_map/ppermute | solution.py:18
  84.3 11.7 %slice-start = ((s8[6291456]{0:T(1024)(128)(4,1)}), s8[2097152]{0:T(1024)(128)(4,1)S(1)}, s32[]{:S(2)}) async-start(s8[6291456]{0:T(1024)(128)(4,1)} %bitcast.109), calls=%async_computation.6 | async-start | bytes 4194304
  85.6 19.3 %all-to-all-start.1 = ((bf16[3,4,64,1024]{3,2,0,1:T(8,128)(2,1)}), bf16[3,4,64,1024]{3,2,0,1:T(8,128)(2,1)}, u32[]{:S(2)}, u32[]{:S(2)}) async-start(bf16[3,4,64,1024]{3,2,0,1:T(8,128)(2,1)} %copy.60), calls=%async_computation.1 | async-start | bytes 3145728 | tf_op jit(solution)/shard_map/all_to_all | solution.py:215
  90.1 5.9 %slice-start.1 = ((s8[6291456]{0:T(1024)(128)(4,1)}), s8[4194304]{0:T(1024)(128)(4,1)S(1)}, s32[]{:S(2)}) async-start(s8[6291456]{0:T(1024)(128)(4,1)} %bitcast.109), calls=%async_computation.7 | async-start | bytes 8388608
  90.1 5.9 %copy-start.15 = (bf16[64,4,96]{2,1,0:T(4,128)(2,1)S(1)}, bf16[64,4,96]{2,1,0:T(4,128)(2,1)}, u32[]{:S(2)}) copy-start(bf16[64,4,96]{2,1,0:T(4,128)(2,1)} %copy-done.14) | copy-start | bytes 147460
  141.0 19.9 %all-to-all-start.3 = ((bf16[16,16,512]{2,1,0:T(8,128)(2,1)}), bf16[16,16,512]{2,1,0:T(8,128)(2,1)S(1)}, u32[]{:S(2)}, u32[]{:S(2)}) async-start(bf16[16,16,512]{2,1,0:T(8,128)(2,1)} %reduce_sum.84), calls=%async_computation.3 | async-start | bytes 524288 | tf_op jit(solution)/shard_map/all_to_all | solution.py:37
  161.7 11.1 %all-to-all-start.4 = ((bf16[16,16,512]{2,1,0:T(8,128)(2,1)}), bf16[16,16,512]{2,1,0:T(8,128)(2,1)S(1)}, u32[]{:S(2)}, u32[]{:S(2)}) async-start(bf16[16,16,512]{2,1,0:T(8,128)(2,1)} %broadcast_in_dim.22), calls=%async_computation.4 | async-start | bytes 524288 | tf_op jit(solution)/shard_map/all_to_all | solution.py:52
  174.4 6.6 %copy-start.23 = (f32[64]{0:T(128)S(1)}, f32[64]{0:T(128)}, u32[]{:S(2)}) copy-start(f32[64]{0:T(128)} %copy-done.21) | copy-start | bytes 772
  174.4 6.6 %copy-start.28 = (f32[64]{0:T(128)S(1)}, f32[64]{0:T(128)}, u32[]{:S(2)}) copy-start(f32[64]{0:T(128)} %get-tuple-element.38) | copy-start | bytes 772
  174.4 32.8 %all-to-all-start.5 = ((bf16[8,16,16,512]{3,2,1,0:T(8,128)(2,1)}), bf16[8,16,16,512]{3,2,1,0:T(8,128)(2,1)S(1)}, u32[]{:S(2)}, u32[]{:S(2)}) async-start(bf16[8,16,16,512]{3,2,1,0:T(8,128)(2,1)} %broadcast_in_dim.23), calls=%async_computation.5 | async-start | bytes 4194304 | tf_op jit(solution)/shard_map/all_to_all | solution.py:52
  (17 other events, 36.7 us)
where the time goes:
time: 211 us; the launch traced here: 210 us
  matrix products  50.9 us (24%)
  waiting for transfers between devices  49.3 us (23%)
  starting transfers between devices  46.6 us (22%)
  blocking collectives  28.6 us (14%)
  local copies, waits for them, and re-layouts  23.1 us (11%)
  other arithmetic  10.2 us (5%)
    all_to_all x1, blocking collectives, summed_on_arrival(): lax.all_to_all(in_blocks(array, dim, count), axis, 0, 0, tiled=True)  28.6 us
    all_to_all x2, waiting for transfers between devices, sent_to_all(): lax.all_to_all(jnp.broadcast_to(array[None], (count, *array.shape)), axis...  16.5 us
    unnamed x68, local copies, waits for them, and re-layouts  14.9 us
    ppermute x4, starting transfers between devices, from_behind(): return lax.ppermute(block, axis, route)  13.6 us
    all_to_all x1, starting transfers between devices, sum_in_two_steps(): lax.all_to_all(nearer.astype(jnp.bfloat16), far, split_axis=0, concat_axi...  12.3 us
    dot_general x1, matrix products, shards(): jnp.einsum('gjc,ce->gje', slot_onehot, recv_pair, preferred_element_type=...  10.7 us
    ppermute x4, waiting for transfers between devices, from_behind(): return lax.ppermute(block, axis, route)  10.3 us
    all_to_all x2, starting transfers between devices, sent_to_all(): lax.all_to_all(jnp.broadcast_to(array[None], (count, *array.shape)), axis...  10.3 us
  transfers between devices with their start and end apart: 9, of which 9 were waited for; matrix products, arithmetic and copies ran while one was open for 14% of the time, Pallas kernels for 0%

commit v1 on v0

v1 whole, which is shorter than its diff:
```python
import functools

import jax
import jax.numpy as jnp
from jax import lax
from jax.experimental import pallas as pl
from jax.experimental.pallas import tpu as pltpu
from jax.sharding import Mesh
from jax.sharding import PartitionSpec as P

SLAB = ("gx", "gy", "gc")
CHIPS = ("gx", "gy", "z")
ALL = ("gx", "gy", "gc", "z")

EPSILON = 1e-06
ABSENT = -1e30
F32 = jnp.float32
BF16 = jnp.bfloat16

VM = pl.BlockSpec(memory_space=pltpu.VMEM)
SM = pl.BlockSpec(memory_space=pltpu.SMEM)
ANY = pl.BlockSpec(memory_space=pl.ANY)


def nn(a, b):
    return lax.dot_general(a, b, (((1,), (0,)), ((), ())), preferred_element_type=F32)


def nt(a, b):
    return lax.dot_general(a, b, (((1,), (1,)), ((), ())), preferred_element_type=F32)


def tn(a, b):
    return lax.dot_general(a, b, (((0,), (0,)), ((), ())), preferred_element_type=F32)


def inv_rms(wide):
    return lax.rsqrt(jnp.mean(wide * wide, axis=-1, keepdims=True) + EPSILON)


def norm_back(wide, factor, gain_row, upstream):
    scaled = gain_row * upstream
    inner = jnp.mean(wide * scaled, axis=-1, keepdims=True)
    return factor * scaled - wide * (factor * factor * factor * inner)


def call(body, outs, in_specs, args, flops, nbytes, name, scratch=(), vmem=None):
    return pl.pallas_call(
        body,
        out_shape=outs,
        in_specs=in_specs,
        out_specs=[VM] * len(outs),
        scratch_shapes=list(scratch),
        compiler_params=pltpu.CompilerParams(vmem_limit_bytes=vmem or (40 << 20)),
        cost_estimate=pl.CostEstimate(flops=flops, bytes_accessed=nbytes, transcendentals=0),
        name=name,
    )(*args)


def gather_body(sub_ref, rows_ref, x_hbm, gain_ref, o0, o1, o2, o3, x_ref, sems):
    half = x_ref.shape[0] // 2
    cap = rows_ref.shape[3]
    outs = (o0, o1, o2, o3)
    copies = []
    for i in range(2):
        part = pl.ds(i * half, half)
        cp = pltpu.make_async_copy(x_hbm.at[part], x_ref.at[part], sems.at[i])
        cp.start()
        copies.append(cp)
    me = sub_ref[0]
    eye = lax.broadcasted_iota(jnp.int32, (cap, cap), 0) == lax.broadcasted_iota(
        jnp.int32, (cap, cap), 1
    )
    gain = gain_ref[...]
    for step, (o, first, count) in enumerate(((0, 0, half), (2, half, half), (1, 0, 2 * half))):
        cols = []
        for k in range(4):
            s = lax.rem(me + k, 4)
            row = rows_ref[0, o, pl.ds(s, 1), :].astype(F32)
            cols.append(jnp.sum(jnp.where(eye, row, 0.0), axis=1, keepdims=True))
        col = jnp.concatenate(cols, axis=0).astype(jnp.int32) - first
        lanes = lax.broadcasted_iota(jnp.int32, (4 * cap, count), 1)
        onehot = jnp.where(lanes == col, 1.0, 0.0).astype(BF16)
        if step < 2:
            copies[step].wait()
        wide = nn(onehot, x_ref[first : first + count, :])
        normed = (wide * inv_rms(wide) * gain).astype(BF16)
        for k in range(4):
            outs[k][o] = normed[k * cap : (k + 1) * cap]


def prep_body(mesh_ref, gain_ref, wq_ref, wo_ref, og_ref, nbr_ref, bias_ref,
              normed_ref, q_ref, ag_ref, dense_ref, inv_ref):
    heads, nodes, slots = dense_ref.shape
    wide = mesh_ref[...].astype(F32)
    normed = (wide * inv_rms(wide) * gain_ref[...]).astype(BF16)
    normed_ref[...] = normed
    q_ref[...] = (nn(normed, wq_ref[...]) * (128 ** -0.5)).astype(BF16)
    ag_ref[...] = nt(og_ref[...], wo_ref[...]).astype(BF16)
    groups, fan, per = nbr_ref.shape
    lanes = lax.broadcasted_iota(jnp.int32, (fan, slots), 1)
    edge = lax.broadcasted_iota(jnp.int32, (fan, slots), 0) + 1

    def group(g, carry):
        block = nbr_ref[g]
        found = []
        for i in range(per):
            hit = jnp.where(block[:, i : i + 1] == lanes, edge, 0)
            found.append(jnp.sum(hit, axis=0, keepdims=True))
        inv_ref[pl.ds(pl.multiple_of(g * per, per), per), :] = jnp.concatenate(found, axis=0)
        return carry

    lax.fori_loop(0, groups, group, 0)
    for b in range(slots // 128):
        at = inv_ref[:, b * 128 : (b + 1) * 128] - 1
        here = at >= 0
        at = jnp.maximum(at, 0)
        for h in range(heads):
            got = jnp.take_along_axis(bias_ref[h], at, axis=1, mode="promise_in_bounds")
            dense_ref[h, :, b * 128 : (b + 1) * 128] = jnp.where(here, got, ABSENT)


def middle_body(core_ref, a0, a2, b0, b1, b2, b3, wk_ref, wv_ref, q_ref, ag_ref, mn_ref, og_ref,
                bias_ref, keep_ref, send_ref, kp_ref, vp_ref, att_ref, qg_ref, rows, keys, vals):
    heads = bias_ref.shape[0]
    block = a0.shape[0]
    cap = b0.shape[1]
    rows[0:block] = a0[...]
    for k, piece in enumerate((b0, b1, b2, b3)):
        rows[block + k * cap : block + (k + 1) * cap] = piece[1]
    rows[2 * block : 3 * block] = a2[...]
    keys[...] = nn(rows[...], wk_ref[...]).astype(BF16)
    vals[...] = nn(rows[...], wv_ref[...]).astype(BF16)
    for h in range(heads):
        at = slice(h * 128, (h + 1) * 128)
        q, ag = q_ref[:, at], ag_ref[:, at]
        kh, vh = keys[:, at], vals[:, at]
        scores = nt(q, kh) + bias_ref[h]
        peak = jnp.max(scores, axis=1, keepdims=True)
        terms = jnp.exp(scores - peak)
        probs = terms / jnp.sum(terms, axis=1, keepdims=True)
        probs_b = probs.astype(BF16)
        att_ref[:, at] = nn(probs_b, vh).astype(BF16)
        pg = nt(ag, vh)
        sg = (probs * (pg - jnp.sum(probs * pg, axis=1, keepdims=True))).astype(BF16)
        qg_ref[:, at] = (nn(sg, kh) * (128 ** -0.5)).astype(BF16)
        kp_ref[:, at] = tn(sg, q).astype(BF16)
        vp_ref[:, at] = tn(probs_b, ag).astype(BF16)
    core = core_ref[0]
    width = wk_ref.shape[0]

    def place(half, row, value):
        @pl.when(core == half)
        def _():
            keep_ref[row : row + width, :] = value

        @pl.when(core != half)
        def _():
            send_ref[row : row + width, :] = value

    place(0, 0, tn(mn_ref[...], qg_ref[...]).astype(BF16))
    place(0, width, tn(rows[...], kp_ref[...]).astype(BF16))
    place(1, 0, tn(rows[...], vp_ref[...]).astype(BF16))
    place(1, width, tn(att_ref[...], og_ref[...]).astype(BF16))


def tail_body(kp_ref, vp_ref, wk_ref, wv_ref, att_ref, wo_ref, mesh_ref, qg_ref, wq_ref, gain_ref,
              og_ref, out_ref, grad_ref, s0, s1, s2, s3):
    cap = s0.shape[1]
    back = (nt(kp_ref[...], wk_ref[...]) + nt(vp_ref[...], wv_ref[...])).astype(BF16)
    for o in range(3):
        for k, piece in enumerate((s0, s1, s2, s3)):
            first = (o * 4 + k) * cap
            piece[o] = back[first : first + cap]
    wide = mesh_ref[...].astype(F32)
    out_ref[...] = (wide + nn(att_ref[...], wo_ref[...])).astype(BF16)
    upstream = nt(qg_ref[...], wq_ref[...])
    back = norm_back(wide, inv_rms(wide), gain_ref[...], upstream)
    grad_ref[...] = (og_ref[...].astype(F32) + back).astype(BF16)


def grid_body(sub_ref, rows_ref, x_ref, gain_ref, r0, r2, s0, s1, s2, s3, out_ref, got):
    points = x_ref.shape[0]
    half = points // 2
    cap = rows_ref.shape[3]
    block = 4 * cap
    me = sub_ref[0]
    gain = gain_ref[...]
    got[0:block] = r0[...]
    for k, piece in enumerate((s0, s1, s2, s3)):
        got[block + k * cap : block + (k + 1) * cap] = piece[1]
    got[2 * block : 3 * block] = r2[...]
    idx = []
    for o in range(3):
        for k in range(4):
            idx.append(rows_ref[0, o, pl.ds(lax.rem(me + k, 4), 1), :])
    idx = jnp.concatenate(idx, axis=1)
    tile = 256
    for t in range(points // tile):
        first = t * tile
        low = 0 if first < half else block
        ids = lax.broadcasted_iota(jnp.int32, (tile, 2 * block), 0) + first
        onehot = jnp.where(ids == idx[:, low : low + 2 * block], 1.0, 0.0).astype(BF16)
        upstream = nn(onehot, got[low : low + 2 * block, :])
        wide = x_ref[first : first + tile, :].astype(F32)
        out_ref[first : first + tile, :] = norm_back(
            wide, inv_rms(wide), gain, upstream
        ).astype(BF16)


def shifted(block, axis, k):
    n = lax.axis_size(axis)
    return lax.ppermute(block, axis, [(i, (i + k) % n) for i in range(n)])


def to_slab(block, d):
    n = lax.axis_size(SLAB)
    return lax.ppermute(block, SLAB, [(i, i + d) for i in range(n) if 0 <= i + d < n])


def sds(shape, dtype=BF16):
    return jax.ShapeDtypeStruct(shape, dtype)


def shards(grid_x, mesh_h, gain_grid, gain_mesh, w_query, w_key, w_value, w_out, edge_bias,
           neighbours, valid, send_rows, out_grad):
    points, width = grid_x.shape
    nodes, fan = neighbours.shape
    cap = send_rows.shape[3]
    block = 4 * cap
    slots = 3 * block
    heads = edge_bias.shape[1] // fan
    sub = lax.axis_index("z").astype(jnp.int32)
    core = lax.axis_index("gc").astype(jnp.int32)
    sub1, core1 = sub.reshape(1), core.reshape(1)
    gain_g, gain_m = gain_grid.reshape(1, width), gain_mesh.reshape(1, width)
    piece = sds((3, cap, width))

    b0, b1, b2, b3 = call(
        gather_body, [piece] * 4, [SM, VM, ANY, VM], (sub1, send_rows, grid_x, gain_g),
        1 << 30, 4 << 20, "gather_rows",
        [pltpu.VMEM((points, width), BF16), pltpu.SemaphoreType.DMA((2,))],
    )
    c1 = shifted(b1, "z", 1)
    c2 = shifted(b2, "z", 2)
    c3 = shifted(b3, "z", 3)

    source = (neighbours >> 6) & 3
    slot = (neighbours & ~192) | (((sub - source) & 3) << 6)
    nbr = slot.reshape(nodes // 8, 8, fan).transpose(0, 2, 1)
    bias = jnp.where((valid == 1)[:, None, :], edge_bias.reshape(nodes, heads, fan), ABSENT)
    bias = jnp.pad(bias.transpose(1, 0, 2), ((0, 0), (0, 0), (0, 128 - fan)))
    mesh_normed, queries, att_grad, dense = call(
        prep_body,
        [sds((nodes, width))] * 3 + [sds((heads, nodes, slots), F32)],
        [VM] * 7, (mesh_h, gain_m, w_query, w_out, out_grad, nbr, bias),
        1 << 26, 4 << 20, "prep", [pltpu.VMEM((nodes, slots), jnp.int32)],
    )

    def of(o):
        return jnp.concatenate([b0[o], c1[o], c2[o], c3[o]], axis=0)

    a0 = to_slab(of(0), -1)
    a2 = to_slab(of(2), 1)
    keep, send, key_part, value_part, attended, query_grad = call(
        middle_body,
        [sds((2 * width, width))] * 2 + [sds((slots, width))] * 2 + [sds((nodes, width))] * 2,
        [SM] + [VM] * 13,
        (core1, a0, a2, b0, c1, c2, c3, w_key, w_value, queries, att_grad, mesh_normed, out_grad,
         dense),
        3 << 30, 8 << 20, "middle", [pltpu.VMEM((slots, width), BF16)] * 3,
    )
    other = shifted(send, "gc", 1)
    mesh_out, mesh_grad, s0, s1, s2, s3 = call(
        tail_body, [sds((nodes, width))] * 2 + [piece] * 4, [VM] * 11,
        (key_part, value_part, w_key, w_value, attended, w_out, mesh_h, query_grad, w_query, gain_m,
         out_grad),
        1 << 30, 5 << 20, "tail",
    )
    chips = lax.axis_size(CHIPS)
    own = (keep.astype(F32) + other.astype(F32)).astype(BF16)
    own = own.reshape(chips, 2 * width // chips, width)
    parts = lax.all_to_all(own, CHIPS, 0, 0, tiled=True)

    t1 = shifted(s1, "z", -1)
    t2 = shifted(s2, "z", -2)
    t3 = shifted(s3, "z", -3)

    def back_of(o):
        return jnp.concatenate([s0[o], t1[o], t2[o], t3[o]], axis=0)

    r0 = to_slab(back_of(0), 1)
    r2 = to_slab(back_of(2), -1)
    (grid_grad,) = call(
        grid_body, [sds((points, width))], [SM] + [VM] * 9,
        (sub1, send_rows, grid_x, gain_g, r0, r2, s0, t1, t2, t3),
        1 << 30, 5 << 20, "grid_grad", [pltpu.VMEM((slots, width), BF16)],
    )

    total = jnp.sum(parts.astype(F32), axis=0).astype(BF16)
    mine = lax.all_to_all(
        jnp.broadcast_to(total[None], (chips, *total.shape)), CHIPS, 0, 0, tiled=True
    ).reshape(2 * width, width)
    theirs = shifted(mine, "gc", 1)
    first = jnp.where(core == 0, mine, theirs)
    second = jnp.where(core == 0, theirs, mine)
    weight_grads = jnp.concatenate([first, second], axis=0).astype(F32).reshape(4, width, width)
    return mesh_out, mesh_grad, grid_grad, weight_grads


def solution(mesh):
    split = Mesh(mesh.devices.reshape(4, 4, 2, mesh.shape["sub"]), ALL)
    rows = P(ALL, None)
    return jax.shard_map(
        shards,
        mesh=split,
        in_specs=(rows, rows, P(), P(), P(), P(), P(), P(), rows, rows, rows,
                  P(ALL, None, None, None), rows),
        out_specs=(rows, rows, rows, P()),
        check_vma=False,
    )
```

time: 211 us -> 128 us (0.61)
  the two profiles are of different devices: /device:TPU:1 before, /device:TPU:2 now
where the time goes in v1:
time: 128 us; the launch traced here: 127 us
  starting transfers between devices  30.8 us (24%)
  waiting for transfers between devices  29.2 us (23%)
  blocking collectives  27.4 us (21%)
  Pallas kernels  18.8 us (15%)
  local copies, waits for them, and re-layouts  11.8 us (9%)
  other arithmetic  7.81 us (6%)
    all_to_all x1, blocking collectives, shards(): parts = lax.all_to_all(own, CHIPS, 0, 0, tiled=True)  27.4 us
    ppermute x8, waiting for transfers between devices, shifted(): return lax.ppermute(block, axis, [(i, (i + k) % n) for i in range(n)])  21.1 us
    pallas_call x5, Pallas kernels, call(): pl.pallas_call(body, out_shape=outs, in_specs=in_specs, out_specs=[VM] *...  18.8 us
    ppermute x4, starting transfers between devices, to_slab(): lax.ppermute(block, SLAB, [(i, i + d) for i in range(n) if 0 <= i + d < n])  12.9 us
    ppermute x8, starting transfers between devices, shifted(): return lax.ppermute(block, axis, [(i, (i + k) % n) for i in range(n)])  11.3 us
    unnamed x48, local copies, waits for them, and re-layouts  10.3 us
    ppermute x4, waiting for transfers between devices, to_slab(): lax.ppermute(block, SLAB, [(i, i + d) for i in range(n) if 0 <= i + d < n])  8.08 us
    all_to_all x1, starting transfers between devices, shards(): lax.all_to_all(jnp.broadcast_to(total[None], (chips, *total.shape)), CHIP...  6.59 us
  transfers between devices with their start and end apart: 13, of which 7 were waited for; matrix products, arithmetic and copies ran while one was open for 2% of the time, Pallas kernels for 8%

profile of v1, /device:TPU:2, one launch (start us, length us, event | category | flops | bytes accessed | tf_op | source)
XLA Modules:
  0.0 126.7 jit_solution(7317418005312414769)
XLA Ops:
  0.6 1.6 %copy-done = bf16[2048,512]{1,0:T(8,128)(2,1)S(1)} copy-done((bf16[2048,512]{1,0:T(8,128)(2,1)S(1)}, bf16[2048,512]{1,0:T(8,128)(2,1)}, u32[]{:S(2)}) %copy-start) | copy-done | bytes 2097176
  3.6 2.1 %gather_rows.1 = (bf16[3,64,512]{2,1,0:T(8,128)(2,1)S(1)}, bf16[3,64,512]{2,1,0:T(8,128)(2,1)S(1)}, bf16[3,64,512]{2,1,0:T(8,128)(2,1)S(1)}, bf16[3,64,512]{2,1,0:T(8,128)(2,1)S(1)}) custom-call(s32[1]{0:T(128)} %bitcast.1.sub_ref, s32[1,3,4,64]{3,2,1,0:T(4,128)S(1)} %copy-done.6, bf16[2048,512]{1,0:T(8,128)(2,1)S(1)} %copy-done, f32[1,512]{1,0:T(1,128)S(1)} %bitcast.50), custom_call_target="tpu_custom_call" | custom-call | flops 1073741824 | bytes 4194304 | tf_op jit(solution)/shard_map/gather_rows/pallas_call | solution.py:48
  5.8 2.0 %collective-permute-start = (bf16[3,64,512]{2,1,0:T(8,128)(2,1)S(1)}, bf16[3,64,512]{2,1,0:T(8,128)(2,1)S(1)}, u32[]{:S(2)}, u32[]{:S(2)}) collective-permute-start(bf16[3,64,512]{2,1,0:T(8,128)(2,1)S(1)} %get-tuple-element.25), channel_id=1, source_target_pairs={{0,1},{1,2},{2,3},{3,0},{4,5},{5,6},{6,7},{7,4},{8,9},{9,10},{10,1... | collective-permute-start | bytes 589832 | tf_op jit(solution)/shard_map/ppermute | solution.py:213
  7.8 3.6 %collective-permute-start.1 = (bf16[3,64,512]{2,1,0:T(8,128)(2,1)S(1)}, bf16[3,64,512]{2,1,0:T(8,128)(2,1)S(1)}, u32[]{:S(2)}, u32[]{:S(2)}) collective-permute-start(bf16[3,64,512]{2,1,0:T(8,128)(2,1)S(1)} %get-tuple-element.26), channel_id=1, source_target_pairs={{0,2},{1,3},{2,0},{3,1},{4,6},{5,7},{6,4},{7,5},{8,10},{9,11},{10,... | collective-permute-start | bytes 589832 | tf_op jit(solution)/shard_map/ppermute | solution.py:213
  12.4 2.4 %collective-permute-done.b1 = bf16[3,64,512]{2,1,0:T(8,128)(2,1)S(1)} collective-permute-done((bf16[3,64,512]{2,1,0:T(8,128)(2,1)S(1)}, bf16[3,64,512]{2,1,0:T(8,128)(2,1)S(1)}, u32[]{:S(2)}, u32[]{:S(2)}) %collective-permute-start) | collective-permute-done | bytes 196640 | tf_op jit(solution)/shard_map/ppermute | solution.py:213
  14.8 5.4 %collective-permute-done.1.b2 = bf16[3,64,512]{2,1,0:T(8,128)(2,1)S(1)} collective-permute-done((bf16[3,64,512]{2,1,0:T(8,128)(2,1)S(1)}, bf16[3,64,512]{2,1,0:T(8,128)(2,1)S(1)}, u32[]{:S(2)}, u32[]{:S(2)}) %collective-permute-start.1) | collective-permute-done | bytes 196640 | tf_op jit(solution)/shard_map/ppermute | solution.py:213
  20.9 1.9 %collective-permute-start.4 = (bf16[256,512]{1,0:T(8,128)(2,1)}, bf16[256,512]{1,0:T(8,128)(2,1)S(1)}, u32[]{:S(2)}, u32[]{:S(2)}) collective-permute-start(bf16[256,512]{1,0:T(8,128)(2,1)} %pad_maximum_fusion.2), channel_id=1, source_target_pairs={{0,4},{4,8},{8,12},{12,16},{16,20},{20,24},{24,28},{28,32},{32,36}... | collective-permute-start | bytes 786440 | tf_op jit(solution)/shard_map/ppermute | solution.py:218
  23.6 5.7 %collective-permute-start.3 = (bf16[256,512]{1,0:T(8,128)(2,1)}, bf16[256,512]{1,0:T(8,128)(2,1)}, u32[]{:S(2)}, u32[]{:S(2)}) collective-permute-start(bf16[256,512]{1,0:T(8,128)(2,1)} %pad_maximum_fusion.1), channel_id=1, source_target_pairs={{4,0},{8,4},{12,8},{16,12},{20,16},{24,20},{28,24},{32,28},{36,32}... | collective-permute-start | bytes 786440 | tf_op jit(solution)/shard_map/ppermute | solution.py:218
  29.8 4.3 %prep.1 = (bf16[64,512]{1,0:T(8,128)(2,1)S(1)}, bf16[64,512]{1,0:T(8,128)(2,1)S(1)}, bf16[64,512]{1,0:T(8,128)(2,1)S(1)}, f32[4,64,768]{2,1,0:T(8,128)S(1)}) custom-call(bf16[64,512]{1,0:T(8,128)(2,1)S(1)} %copy-done.4, f32[1,512]{1,0:T(1,128)S(1)} %bitcast.48, bf16[512,512]{1,0:T(8,128)(2,1)S(1)} %copy-done.2, bf16[512,512]{1,0:T(8,128)(2,1)S(1)} %copy-done.3, ...), custom_call_target="tpu_custom_call" | custom-call | flops 67108864 | bytes 4194304 | tf_op jit(solution)/shard_map/prep/pallas_call | solution.py:48
  36.2 7.1 %middle.1 = (bf16[1024,512]{1,0:T(8,128)(2,1)S(1)}, bf16[1024,512]{1,0:T(8,128)(2,1)S(1)}, bf16[768,512]{1,0:T(8,128)(2,1)S(1)}, bf16[768,512]{1,0:T(8,128)(2,1)...) custom-call(s32[1]{0:T(128)} %bitcast.core_ref, bf16[256,512]{1,0:T(8,128)(2,1)} %collective-permute-done.3.a0, ...), custom_call_target="tpu_custom_call" | custom-call | flops 3221225472 | bytes 8388608 | tf_op jit(solution)/shard_map/middle/pallas_call | solution.py:48
  43.4 2.6 %collective-permute-done.10 = bf16[1024,512]{1,0:T(8,128)(2,1)S(1)} collective-permute-done((bf16[1024,512]{1,0:T(8,128)(2,1)S(1)}, bf16[1024,512]{1,0:T(8,128)(2,1)S(1)}, u32[]{:S(2)}, u32[]{:S(2)}) %collective-permute-start.10) | collective-permute-done | bytes 1048608 | tf_op jit(solution)/shard_map/ppermute | solution.py:213
  46.4 27.4 %all_to_all.10 = bf16[64,16,512]{2,1,0:T(8,128)(2,1)S(1)} all-to-all(bf16[64,16,512]{2,1,0:T(8,128)(2,1)S(1)} %bitcast.53), channel_id=1, replica_groups=mesh['gx'=4,'gy'=4,'gc'=2,'z'=4] {'gx','gy','z'}, dimensions={0} | all-to-all | bytes 2097152 | tf_op jit(solution)/shard_map/all_to_all | solution.py:283
  75.0 6.6 %all-to-all-start.1 = ((bf16[64,16,512]{2,1,0:T(8,128)(2,1)}), bf16[64,16,512]{2,1,0:T(8,128)(2,1)}, u32[]{:S(2)}, u32[]{:S(2)}) async-start(bf16[64,16,512]{2,1,0:T(8,128)(2,1)} %broadcast_in_dim.21), calls=%async_computation.1 | async-start | bytes 2097152 | tf_op jit(solution)/shard_map/all_to_all | solution.py:301
  86.8 2.0 %tail.1 = (bf16[64,512]{1,0:T(8,128)(2,1)}, bf16[64,512]{1,0:T(8,128)(2,1)}, bf16[3,64,512]{2,1,0:T(8,128)(2,1)S(1)}, bf16[3,64,512]{2,1,0:T(8,128)(2,1)S(1)}, b...) custom-call(bf16[768,512]{1,0:T(8,128)(2,1)S(1)} %copy-done.16, bf16[768,512]{1,0:T(8,128)(2,1)S(1)} %copy-done.18, ...), custom_call_target="tpu_custom_call" | custom-call | flops 1073741824 | bytes 5242880 | tf_op jit(solution)/shard_map/tail/pallas_call | solution.py:48
  88.8 2.7 %collective-permute-start.5 = (bf16[3,64,512]{2,1,0:T(8,128)(2,1)S(1)}, bf16[3,64,512]{2,1,0:T(8,128)(2,1)S(1)}, u32[]{:S(2)}, u32[]{:S(2)}) collective-permute-start(bf16[3,64,512]{2,1,0:T(8,128)(2,1)S(1)} %get-tuple-element.39), channel_id=1, source_target_pairs={{0,3},{1,0},{2,1},{3,2},{4,7},{5,4},{6,5},{7,6},{8,11},{9,8},{10,9... | collective-permute-start | bytes 589832 | tf_op jit(solution)/shard_map/ppermute | solution.py:213
  93.3 9.0 %collective-permute-done.5.s1 = bf16[3,64,512]{2,1,0:T(8,128)(2,1)S(1)} collective-permute-done((bf16[3,64,512]{2,1,0:T(8,128)(2,1)S(1)}, bf16[3,64,512]{2,1,0:T(8,128)(2,1)S(1)}, u32[]{:S(2)}, u32[]{:S(2)}) %collective-permute-start.5) | collective-permute-done | bytes 196640 | tf_op jit(solution)/shard_map/ppermute | solution.py:213
  102.5 1.7 %collective-permute-done.7.s3 = bf16[3,64,512]{2,1,0:T(8,128)(2,1)S(1)} collective-permute-done((bf16[3,64,512]{2,1,0:T(8,128)(2,1)}, bf16[3,64,512]{2,1,0:T(8,128)(2,1)S(1)}, u32[]{:S(2)}, u32[]{:S(2)}) %collective-permute-start.7) | collective-permute-done | bytes 196640 | tf_op jit(solution)/shard_map/ppermute | solution.py:213
  104.9 3.4 %collective-permute-start.9 = (bf16[256,512]{1,0:T(8,128)(2,1)}, bf16[256,512]{1,0:T(8,128)(2,1)S(1)}, u32[]{:S(2)}, u32[]{:S(2)}) collective-permute-start(bf16[256,512]{1,0:T(8,128)(2,1)} %pad_maximum_fusion.4), channel_id=1, source_target_pairs={{4,0},{8,4},{12,8},{16,12},{20,16},{24,20},{28,24},{32,28},{36,32}... | collective-permute-start | bytes 786440 | tf_op jit(solution)/shard_map/ppermute | solution.py:218
  109.0 1.9 %collective-permute-start.8 = (bf16[256,512]{1,0:T(8,128)(2,1)}, bf16[256,512]{1,0:T(8,128)(2,1)S(1)}, u32[]{:S(2)}, u32[]{:S(2)}) collective-permute-start(bf16[256,512]{1,0:T(8,128)(2,1)} %pad_maximum_fusion.3), channel_id=1, source_target_pairs={{0,4},{4,8},{8,12},{12,16},{16,20},{20,24},{24,28},{28,32},{32,36}... | collective-permute-start | bytes 786440 | tf_op jit(solution)/shard_map/ppermute | solution.py:218
  110.9 1.5 %collective-permute-done.9.r2 = bf16[256,512]{1,0:T(8,128)(2,1)S(1)} collective-permute-done((bf16[256,512]{1,0:T(8,128)(2,1)}, bf16[256,512]{1,0:T(8,128)(2,1)S(1)}, u32[]{:S(2)}, u32[]{:S(2)}) %collective-permute-start.9) | collective-permute-done | bytes 262176 | tf_op jit(solution)/shard_map/ppermute | solution.py:218
  112.5 6.5 %collective-permute-done.8.r0 = bf16[256,512]{1,0:T(8,128)(2,1)S(1)} collective-permute-done((bf16[256,512]{1,0:T(8,128)(2,1)}, bf16[256,512]{1,0:T(8,128)(2,1)S(1)}, u32[]{:S(2)}, u32[]{:S(2)}) %collective-permute-start.8) | collective-permute-done | bytes 262176 | tf_op jit(solution)/shard_map/ppermute | solution.py:218
  119.0 3.3 %grid_grad.1 = bf16[2048,512]{1,0:T(8,128)(2,1)} custom-call(s32[1]{0:T(128)} %bitcast.1.sub_ref, s32[1,3,4,64]{3,2,1,0:T(4,128)S(1)} %copy-done.7, bf16[2048,512]{1,0:T(8,128)(2,1)S(1)} %copy-done.1, f32[1,512]{1,0:T(1,128)S(1)} %bitcast.51, bf16[256,512]{1,0:T(8,128)(2,1)S(1)} %collective-permute-done.8.r0, ...), custom_call_target="tpu_custom_call" | custom-call | flops 1073741824 | bytes 5242880 | tf_op jit(solution)/shard_map/grid_grad/pallas_call | solution.py:48
  122.3 1.7 %broadcast_select_fusion.1 = (bf16[1024,512]{1,0:T(8,128)(2,1)S(1)}, bf16[1024,512]{1,0:T(8,128)(2,1)S(1)}) fusion(bf16[1024,512]{1,0:T(8,128)(2,1)} %collective-permute-done.11, pred[]{:T(512)S(6)} %eq.12, bf16[64,16,512]{2,1,0:T(8,128)(2,1)} %all-to-all-done.1), kind=kLoop, calls=%fused_computation.3 | loop fusion | flops 1048576 | bytes 4194305 | tf_op jit(solution)/shard_map/jit(_where)/select_n | solution.py:305
  124.1 2.6 %convert.2 = f32[4,512,512]{2,1,0:T(8,128)} convert(bf16[4,512,512]{2,1,0:T(8,128)(2,1)S(1)} %bitcast.52) | non-fusion elementwise | flops 1048576 | bytes 6291456 | tf_op jit(solution)/shard_map/convert_element_type | solution.py:307
  (80 shorter events, 16.7 us)
Async XLA Ops:
  3.6 8.8 %copy-start.23 = (s32[64,96]{1,0:T(8,128)S(1)}, s32[64,96]{1,0:T(8,128)}, u32[]{:S(2)}) copy-start(s32[64,96]{1,0:T(8,128)} %param.22) | copy-start | bytes 73732
  3.6 25.7 %copy-start.22 = (s32[64,96]{1,0:T(8,128)S(1)}, s32[64,96]{1,0:T(8,128)}, u32[]{:S(2)}) copy-start(s32[64,96]{1,0:T(8,128)} %param.23) | copy-start | bytes 73732
  5.7 23.8 %copy-start.21 = (f32[64,384]{1,0:T(8,128)S(1)}, f32[64,384]{1,0:T(8,128)}, u32[]{:S(2)}) copy-start(f32[64,384]{1,0:T(8,128)} %param.21) | copy-start | bytes 294916
  5.7 24.0 %copy-start.2 = (bf16[512,512]{1,0:T(8,128)(2,1)S(1)}, bf16[512,512]{1,0:T(8,128)(2,1)}, u32[]{:S(2)}) copy-start(bf16[512,512]{1,0:T(8,128)(2,1)} %wq_ref.3) | copy-start | bytes 1572868
  5.7 24.0 %copy-start.3 = (bf16[512,512]{1,0:T(8,128)(2,1)S(1)}, bf16[512,512]{1,0:T(8,128)(2,1)}, u32[]{:S(2)}) copy-start(bf16[512,512]{1,0:T(8,128)(2,1)} %wo_ref.3) | copy-start | bytes 1572868
  5.7 24.0 %copy-start.4 = (bf16[64,512]{1,0:T(8,128)(2,1)S(1)}, bf16[64,512]{1,0:T(8,128)(2,1)}, u32[]{:S(2)}) copy-start(bf16[64,512]{1,0:T(8,128)(2,1)} %mesh_ref.3) | copy-start | bytes 196612
  5.8 24.0 %copy-start.5 = (bf16[64,512]{1,0:T(8,128)(2,1)S(1)}, bf16[64,512]{1,0:T(8,128)(2,1)}, u32[]{:S(2)}) copy-start(bf16[64,512]{1,0:T(8,128)(2,1)} %og_ref.5) | copy-start | bytes 196612
  5.8 24.0 %copy-start.8 = (f32[512]{0:T(512)S(1)}, f32[512]{0:T(512)}, u32[]{:S(2)}) copy-start(f32[512]{0:T(512)} %param.16) | copy-start | bytes 6148
  5.8 9.0 %collective-permute-start = (bf16[3,64,512]{2,1,0:T(8,128)(2,1)S(1)}, bf16[3,64,512]{2,1,0:T(8,128)(2,1)S(1)}, u32[]{:S(2)}, u32[]{:S(2)}) collective-permute-start(bf16[3,64,512]{2,1,0:T(8,128)(2,1)S(1)} %get-tuple-element.25), channel_id=1, source_target_pairs={{0,1},{1,2},{2,3},{3,0},{4,5},{5,6},{6,7},{7,4},{8,9},{9,10},{10,1... | collective-permute-start | bytes 589832 | tf_op jit(solution)/shard_map/ppermute | solution.py:213
  7.8 12.4 %collective-permute-start.1 = (bf16[3,64,512]{2,1,0:T(8,128)(2,1)S(1)}, bf16[3,64,512]{2,1,0:T(8,128)(2,1)S(1)}, u32[]{:S(2)}, u32[]{:S(2)}) collective-permute-start(bf16[3,64,512]{2,1,0:T(8,128)(2,1)S(1)} %get-tuple-element.26), channel_id=1, source_target_pairs={{0,2},{1,3},{2,0},{3,1},{4,6},{5,7},{6,4},{7,5},{8,10},{9,11},{10,... | collective-permute-start | bytes 589832 | tf_op jit(solution)/shard_map/ppermute | solution.py:213
  11.3 8.8 %collective-permute-start.2 = (bf16[3,64,512]{2,1,0:T(8,128)(2,1)S(1)}, bf16[3,64,512]{2,1,0:T(8,128)(2,1)S(1)}, u32[]{:S(2)}, u32[]{:S(2)}) collective-permute-start(bf16[3,64,512]{2,1,0:T(8,128)(2,1)S(1)} %get-tuple-element.27), channel_id=1, source_target_pairs={{0,3},{1,0},{2,1},{3,2},{4,7},{5,4},{6,5},{7,6},{8,11},{9,8},{10,9... | collective-permute-start | bytes 589832 | tf_op jit(solution)/shard_map/ppermute | solution.py:213
  20.9 13.1 %collective-permute-start.4 = (bf16[256,512]{1,0:T(8,128)(2,1)}, bf16[256,512]{1,0:T(8,128)(2,1)S(1)}, u32[]{:S(2)}, u32[]{:S(2)}) collective-permute-start(bf16[256,512]{1,0:T(8,128)(2,1)} %pad_maximum_fusion.2), channel_id=1, source_target_pairs={{0,4},{4,8},{8,12},{12,16},{16,20},{20,24},{24,28},{28,32},{32,36}... | collective-permute-start | bytes 786440 | tf_op jit(solution)/shard_map/ppermute | solution.py:218
  23.6 10.5 %collective-permute-start.3 = (bf16[256,512]{1,0:T(8,128)(2,1)}, bf16[256,512]{1,0:T(8,128)(2,1)}, u32[]{:S(2)}, u32[]{:S(2)}) collective-permute-start(bf16[256,512]{1,0:T(8,128)(2,1)} %pad_maximum_fusion.1), channel_id=1, source_target_pairs={{4,0},{8,4},{12,8},{16,12},{20,16},{24,20},{28,24},{32,28},{36,32}... | collective-permute-start | bytes 786440 | tf_op jit(solution)/shard_map/ppermute | solution.py:218
  43.3 2.7 %collective-permute-start.10 = (bf16[1024,512]{1,0:T(8,128)(2,1)S(1)}, bf16[1024,512]{1,0:T(8,128)(2,1)S(1)}, u32[]{:S(2)}, u32[]{:S(2)}) collective-permute-start(bf16[1024,512]{1,0:T(8,128)(2,1)S(1)} %get-tuple-element.43), channel_id=1, source_target_pairs={{0,4},{4,0},{1,5},{5,1},{2,6},{6,2},{3,7},{7,3},{8,12},{12,8},{9,1... | collective-permute-start | bytes 3145736 | tf_op jit(solution)/shard_map/ppermute | solution.py:213
  75.0 27.3 %all-to-all-start.1 = ((bf16[64,16,512]{2,1,0:T(8,128)(2,1)}), bf16[64,16,512]{2,1,0:T(8,128)(2,1)}, u32[]{:S(2)}, u32[]{:S(2)}) async-start(bf16[64,16,512]{2,1,0:T(8,128)(2,1)} %broadcast_in_dim.21), calls=%async_computation.1 | async-start | bytes 2097152 | tf_op jit(solution)/shard_map/all_to_all | solution.py:301
  86.8 32.2 %copy-start.1 = (bf16[2048,512]{1,0:T(8,128)(2,1)S(1)}, bf16[2048,512]{1,0:T(8,128)(2,1)}, u32[]{:S(2)}) copy-start(bf16[2048,512]{1,0:T(8,128)(2,1)} %x_ref.1) | copy-start | bytes 6291460
  86.8 32.2 %copy-start.7 = (s32[1,3,4,64]{3,2,1,0:T(4,128)S(1)}, s32[1,3,4,64]{3,2,1,0:T(4,128)}, u32[]{:S(2)}) copy-start(s32[1,3,4,64]{3,2,1,0:T(4,128)} %rows_ref.3) | copy-start | bytes 9220
  86.8 32.2 %copy-start.10 = (f32[512]{0:T(512)S(1)}, f32[512]{0:T(512)}, u32[]{:S(2)}) copy-start(f32[512]{0:T(512)} %param.15) | copy-start | bytes 6148
  88.8 13.4 %collective-permute-start.5 = (bf16[3,64,512]{2,1,0:T(8,128)(2,1)S(1)}, bf16[3,64,512]{2,1,0:T(8,128)(2,1)S(1)}, u32[]{:S(2)}, u32[]{:S(2)}) collective-permute-start(bf16[3,64,512]{2,1,0:T(8,128)(2,1)S(1)} %get-tuple-element.39), channel_id=1, source_target_pairs={{0,3},{1,0},{2,1},{3,2},{4,7},{5,4},{6,5},{7,6},{8,11},{9,8},{10,9... | collective-permute-start | bytes 589832 | tf_op jit(solution)/shard_map/ppermute | solution.py:213
  91.5 11.0 %collective-permute-start.6 = (bf16[3,64,512]{2,1,0:T(8,128)(2,1)}, bf16[3,64,512]{2,1,0:T(8,128)(2,1)S(1)}, u32[]{:S(2)}, u32[]{:S(2)}) collective-permute-start(bf16[3,64,512]{2,1,0:T(8,128)(2,1)} %get-tuple-element.40), channel_id=1, source_target_pairs={{0,2},{1,3},{2,0},{3,1},{4,6},{5,7},{6,4},{7,5},{8,10},{9,11},{10,... | collective-permute-start | bytes 589832 | tf_op jit(solution)/shard_map/ppermute | solution.py:213
  92.4 11.8 %collective-permute-start.7 = (bf16[3,64,512]{2,1,0:T(8,128)(2,1)}, bf16[3,64,512]{2,1,0:T(8,128)(2,1)S(1)}, u32[]{:S(2)}, u32[]{:S(2)}) collective-permute-start(bf16[3,64,512]{2,1,0:T(8,128)(2,1)} %get-tuple-element.41), channel_id=1, source_target_pairs={{0,1},{1,2},{2,3},{3,0},{4,5},{5,6},{6,7},{7,4},{8,9},{9,10},{10,1... | collective-permute-start | bytes 589832 | tf_op jit(solution)/shard_map/ppermute | solution.py:213
  102.3 20.0 %collective-permute-start.11 = (bf16[1024,512]{1,0:T(8,128)(2,1)}, bf16[1024,512]{1,0:T(8,128)(2,1)}, u32[]{:S(2)}, u32[]{:S(2)}) collective-permute-start(bf16[1024,512]{1,0:T(8,128)(2,1)} %bitcast.24), channel_id=1, source_target_pairs={{0,4},{4,0},{1,5},{5,1},{2,6},{6,2},{3,7},{7,3},{8,12},{12,8},{9,1... | collective-permute-start | bytes 3145736 | tf_op jit(solution)/shard_map/ppermute | solution.py:213
  104.9 7.6 %collective-permute-start.9 = (bf16[256,512]{1,0:T(8,128)(2,1)}, bf16[256,512]{1,0:T(8,128)(2,1)S(1)}, u32[]{:S(2)}, u32[]{:S(2)}) collective-permute-start(bf16[256,512]{1,0:T(8,128)(2,1)} %pad_maximum_fusion.4), channel_id=1, source_target_pairs={{4,0},{8,4},{12,8},{16,12},{20,16},{24,20},{28,24},{32,28},{36,32}... | collective-permute-start | bytes 786440 | tf_op jit(solution)/shard_map/ppermute | solution.py:218
  109.0 10.0 %collective-permute-start.8 = (bf16[256,512]{1,0:T(8,128)(2,1)}, bf16[256,512]{1,0:T(8,128)(2,1)S(1)}, u32[]{:S(2)}, u32[]{:S(2)}) collective-permute-start(bf16[256,512]{1,0:T(8,128)(2,1)} %pad_maximum_fusion.3), channel_id=1, source_target_pairs={{0,4},{4,8},{8,12},{12,16},{16,20},{20,24},{24,28},{28,32},{32,36}... | collective-permute-start | bytes 786440 | tf_op jit(solution)/shard_map/ppermute | solution.py:218
  (13 other events, 19.5 us)

commit v2 on v1

--- a/solution.py
+++ b/solution.py
@@ -19,7 +19,7 @@
 
 VM = pl.BlockSpec(memory_space=pltpu.VMEM)
 SM = pl.BlockSpec(memory_space=pltpu.SMEM)
-ANY = pl.BlockSpec(memory_space=pl.ANY)
+HB = pl.BlockSpec(memory_space=pltpu.HBM)
 
 
 def nn(a, b):
@@ -44,29 +44,44 @@
     return factor * scaled - wide * (factor * factor * factor * inner)
 
 
-def call(body, outs, in_specs, args, flops, nbytes, name, scratch=(), vmem=None):
+def call(body, outs, in_specs, args, flops, nbytes, name, scratch=(), out_specs=None, aliases=None):
     return pl.pallas_call(
         body,
         out_shape=outs,
         in_specs=in_specs,
-        out_specs=[VM] * len(outs),
+        out_specs=out_specs or [VM] * len(outs),
         scratch_shapes=list(scratch),
-        compiler_params=pltpu.CompilerParams(vmem_limit_bytes=vmem or (40 << 20)),
+        input_output_aliases=aliases or {},
+        compiler_params=pltpu.CompilerParams(vmem_limit_bytes=24 << 20),
         cost_estimate=pl.CostEstimate(flops=flops, bytes_accessed=nbytes, transcendentals=0),
         name=name,
     )(*args)
 
 
-def gather_body(sub_ref, rows_ref, x_hbm, gain_ref, o0, o1, o2, o3, x_ref, sems):
+def fetch(sources, targets, sems):
+    copies = []
+    for i, (source, target) in enumerate(zip(sources, targets)):
+        copies.append(pltpu.make_async_copy(source, target, sems.at[i]))
+        copies[-1].start()
+    return copies
+
+
+def held(*args):
+    return [pltpu.VMEM(a.shape, a.dtype) for a in args] + [pltpu.SemaphoreType.DMA((len(args),))]
+
+
+def gather_body(sub_ref, rows_hbm, gain_hbm, x_hbm, o0, o1, o2, o3, rows_ref, gain_ref, x_ref, sems):
     half = x_ref.shape[0] // 2
     cap = rows_ref.shape[3]
     outs = (o0, o1, o2, o3)
-    copies = []
-    for i in range(2):
-        part = pl.ds(i * half, half)
-        cp = pltpu.make_async_copy(x_hbm.at[part], x_ref.at[part], sems.at[i])
-        cp.start()
-        copies.append(cp)
+    parts = [pl.ds(i * half, half) for i in range(2)]
+    copies = fetch(
+        [rows_hbm, gain_hbm] + [x_hbm.at[p] for p in parts],
+        [rows_ref, gain_ref] + [x_ref.at[p] for p in parts],
+        sems,
+    )
+    copies[0].wait()
+    copies[1].wait()
     me = sub_ref[0]
     eye = lax.broadcasted_iota(jnp.int32, (cap, cap), 0) == lax.broadcasted_iota(
         jnp.int32, (cap, cap), 1
@@ -82,21 +97,20 @@
         lanes = lax.broadcasted_iota(jnp.int32, (4 * cap, count), 1)
         onehot = jnp.where(lanes == col, 1.0, 0.0).astype(BF16)
         if step < 2:
-            copies[step].wait()
+            copies[2 + step].wait()
         wide = nn(onehot, x_ref[first : first + count, :])
         normed = (wide * inv_rms(wide) * gain).astype(BF16)
         for k in range(4):
             outs[k][o] = normed[k * cap : (k + 1) * cap]
 
 
-def prep_body(mesh_ref, gain_ref, wq_ref, wo_ref, og_ref, nbr_ref, bias_ref,
-              normed_ref, q_ref, ag_ref, dense_ref, inv_ref):
+def prep_body(nbr_ref, bias_ref, mesh_hbm, gain_hbm, wq_hbm, wo_hbm, og_hbm,
+              normed_ref, q_ref, ag_ref, dense_ref, inv_ref,
+              mesh_ref, gain_ref, wq_ref, wo_ref, og_ref, sems):
+    copies = fetch(
+        (mesh_hbm, gain_hbm, wq_hbm, wo_hbm, og_hbm), (mesh_ref, gain_ref, wq_ref, wo_ref, og_ref), sems
+    )
     heads, nodes, slots = dense_ref.shape
-    wide = mesh_ref[...].astype(F32)
-    normed = (wide * inv_rms(wide) * gain_ref[...]).astype(BF16)
-    normed_ref[...] = normed
-    q_ref[...] = (nn(normed, wq_ref[...]) * (128 ** -0.5)).astype(BF16)
-    ag_ref[...] = nt(og_ref[...], wo_ref[...]).astype(BF16)
     groups, fan, per = nbr_ref.shape
     lanes = lax.broadcasted_iota(jnp.int32, (fan, slots), 1)
     edge = lax.broadcasted_iota(jnp.int32, (fan, slots), 0) + 1
@@ -118,10 +132,19 @@
         for h in range(heads):
             got = jnp.take_along_axis(bias_ref[h], at, axis=1, mode="promise_in_bounds")
             dense_ref[h, :, b * 128 : (b + 1) * 128] = jnp.where(here, got, ABSENT)
-
-
-def middle_body(core_ref, a0, a2, b0, b1, b2, b3, wk_ref, wv_ref, q_ref, ag_ref, mn_ref, og_ref,
-                bias_ref, keep_ref, send_ref, kp_ref, vp_ref, att_ref, qg_ref, rows, keys, vals):
+    for copy in copies:
+        copy.wait()
+    wide = mesh_ref[...].astype(F32)
+    normed = (wide * inv_rms(wide) * gain_ref[...]).astype(BF16)
+    normed_ref[...] = normed
+    q_ref[...] = (nn(normed, wq_ref[...]) * (128 ** -0.5)).astype(BF16)
+    ag_ref[...] = nt(og_ref[...], wo_ref[...]).astype(BF16)
+
+
+def middle_body(core_ref, a0, a2, b0, b1, b2, b3, q_ref, ag_ref, mn_ref, bias_ref,
+                wk_hbm, wv_hbm, og_hbm, keep_ref, send_ref, kp_ref, vp_ref, att_ref, qg_ref,
+                rows, keys, vals, wk_ref, wv_ref, og_ref, sems):
+    copies = fetch((wk_hbm, wv_hbm, og_hbm), (wk_ref, wv_ref, og_ref), sems)
     heads = bias_ref.shape[0]
     block = a0.shape[0]
     cap = b0.shape[1]
@@ -129,7 +152,10 @@
     for k, piece in enumerate((b0, b1, b2, b3)):
         rows[block + k * cap : block + (k + 1) * cap] = piece[1]
     rows[2 * block : 3 * block] = a2[...]
+    copies[0].wait()
     keys[...] = nn(rows[...], wk_ref[...]).astype(BF16)
+    copies[1].wait()
+    copies[2].wait()
     vals[...] = nn(rows[...], wv_ref[...]).astype(BF16)
     for h in range(heads):
         at = slice(h * 128, (h + 1) * 128)
@@ -164,14 +190,24 @@
     place(1, width, tn(att_ref[...], og_ref[...]).astype(BF16))
 
 
-def tail_body(kp_ref, vp_ref, wk_ref, wv_ref, att_ref, wo_ref, mesh_ref, qg_ref, wq_ref, gain_ref,
-              og_ref, out_ref, grad_ref, s0, s1, s2, s3):
+def tail_body(kp_ref, vp_ref, att_ref, qg_ref, wk_hbm, wv_hbm, wo_hbm, wq_hbm, mesh_hbm, gain_hbm,
+              og_hbm, out_ref, grad_ref, s0, s1, s2, s3,
+              wk_ref, wv_ref, wo_ref, wq_ref, mesh_ref, gain_ref, og_ref, sems):
+    copies = fetch(
+        (wk_hbm, wv_hbm, wo_hbm, wq_hbm, mesh_hbm, gain_hbm, og_hbm),
+        (wk_ref, wv_ref, wo_ref, wq_ref, mesh_ref, gain_ref, og_ref),
+        sems,
+    )
     cap = s0.shape[1]
+    copies[0].wait()
+    copies[1].wait()
     back = (nt(kp_ref[...], wk_ref[...]) + nt(vp_ref[...], wv_ref[...])).astype(BF16)
     for o in range(3):
         for k, piece in enumerate((s0, s1, s2, s3)):
             first = (o * 4 + k) * cap
             piece[o] = back[first : first + cap]
+    for copy in copies[2:]:
+        copy.wait()
     wide = mesh_ref[...].astype(F32)
     out_ref[...] = (wide + nn(att_ref[...], wo_ref[...])).astype(BF16)
     upstream = nt(qg_ref[...], wq_ref[...])
@@ -179,23 +215,35 @@
     grad_ref[...] = (og_ref[...].astype(F32) + back).astype(BF16)
 
 
-def grid_body(sub_ref, rows_ref, x_ref, gain_ref, r0, r2, s0, s1, s2, s3, out_ref, got):
+def pack_body(p0, p1, p2, p3, low_ref, high_ref):
+    cap = p0.shape[1]
+    for k, piece in enumerate((p0, p1, p2, p3)):
+        low_ref[k * cap : (k + 1) * cap, :] = piece[0]
+        high_ref[k * cap : (k + 1) * cap, :] = piece[2]
+
+
+def grid_body(sub_ref, r0, r2, s0, s1, s2, s3, rows_hbm, gain_hbm, x_hbm, out_hbm,
+              got, done_ref, done_sems, rows_ref, gain_ref, x_ref, sems):
+    copies = fetch((rows_hbm, gain_hbm, x_hbm), (rows_ref, gain_ref, x_ref), sems)
     points = x_ref.shape[0]
     half = points // 2
     cap = rows_ref.shape[3]
     block = 4 * cap
     me = sub_ref[0]
-    gain = gain_ref[...]
     got[0:block] = r0[...]
     for k, piece in enumerate((s0, s1, s2, s3)):
         got[block + k * cap : block + (k + 1) * cap] = piece[1]
     got[2 * block : 3 * block] = r2[...]
+    for copy in copies:
+        copy.wait()
+    gain = gain_ref[...]
     idx = []
     for o in range(3):
         for k in range(4):
             idx.append(rows_ref[0, o, pl.ds(lax.rem(me + k, 4), 1), :])
     idx = jnp.concatenate(idx, axis=1)
     tile = 256
+    stores = []
     for t in range(points // tile):
         first = t * tile
         low = 0 if first < half else block
@@ -203,9 +251,31 @@
         onehot = jnp.where(ids == idx[:, low : low + 2 * block], 1.0, 0.0).astype(BF16)
         upstream = nn(onehot, got[low : low + 2 * block, :])
         wide = x_ref[first : first + tile, :].astype(F32)
-        out_ref[first : first + tile, :] = norm_back(
-            wide, inv_rms(wide), gain, upstream
-        ).astype(BF16)
+        part = slice(first, first + tile)
+        done_ref[part, :] = norm_back(wide, inv_rms(wide), gain, upstream).astype(BF16)
+        stores.append(
+            pltpu.make_async_copy(done_ref.at[part], out_hbm.at[part], done_sems.at[t])
+        )
+        stores[-1].start()
+    for store in stores:
+        store.wait()
+
+
+def widen_body(turn, core_ref, half_ref, *refs):
+    out_hbm, wide, sems = refs[-3:]
+    count, width, _ = wide.shape
+    first = (core_ref[0] ^ turn) * count
+    part = width // 2
+    copies = []
+    for i in range(2 * count):
+        m, rows = i // 2, pl.ds((i % 2) * part, part)
+        wide[m, rows, :] = half_ref[i * part : (i + 1) * part, :].astype(F32)
+        copies.append(
+            pltpu.make_async_copy(wide.at[m, rows], out_hbm.at[first + m, rows], sems.at[i])
+        )
+        copies[-1].start()
+    for copy in copies:
+        copy.wait()
 
 
 def shifted(block, axis, k):
@@ -235,16 +305,21 @@
     sub1, core1 = sub.reshape(1), core.reshape(1)
     gain_g, gain_m = gain_grid.reshape(1, width), gain_mesh.reshape(1, width)
     piece = sds((3, cap, width))
+    grid_x, mesh_h, out_grad, send_rows, w_key, w_value, w_query, w_out, gain_g, gain_m = (
+        pltpu.with_memory_space_constraint(a, pltpu.HBM)
+        for a in (grid_x, mesh_h, out_grad, send_rows, w_key, w_value, w_query, w_out, gain_g, gain_m)
+    )
 
     b0, b1, b2, b3 = call(
-        gather_body, [piece] * 4, [SM, VM, ANY, VM], (sub1, send_rows, grid_x, gain_g),
+        gather_body, [piece] * 4, [SM, HB, HB, HB], (sub1, send_rows, gain_g, grid_x),
         1 << 30, 4 << 20, "gather_rows",
-        [pltpu.VMEM((points, width), BF16), pltpu.SemaphoreType.DMA((2,))],
+        held(send_rows, gain_g, grid_x)[:-1] + [pltpu.SemaphoreType.DMA((4,))],
     )
     c1 = shifted(b1, "z", 1)
     c2 = shifted(b2, "z", 2)
     c3 = shifted(b3, "z", 3)
 
+    neighbours, b0 = lax.optimization_barrier((neighbours, b0))
     source = (neighbours >> 6) & 3
     slot = (neighbours & ~192) | (((sub - source) & 3) << 6)
     nbr = slot.reshape(nodes // 8, 8, fan).transpose(0, 2, 1)
@@ -253,30 +328,35 @@
     mesh_normed, queries, att_grad, dense = call(
         prep_body,
         [sds((nodes, width))] * 3 + [sds((heads, nodes, slots), F32)],
-        [VM] * 7, (mesh_h, gain_m, w_query, w_out, out_grad, nbr, bias),
-        1 << 26, 4 << 20, "prep", [pltpu.VMEM((nodes, slots), jnp.int32)],
-    )
-
-    def of(o):
-        return jnp.concatenate([b0[o], c1[o], c2[o], c3[o]], axis=0)
-
-    a0 = to_slab(of(0), -1)
-    a2 = to_slab(of(2), 1)
+        [VM] * 2 + [HB] * 5, (nbr, bias, mesh_h, gain_m, w_query, w_out, out_grad),
+        1 << 30, 8 << 20, "prep",
+        [pltpu.VMEM((nodes, slots), jnp.int32)] + held(mesh_h, gain_m, w_query, w_out, out_grad),
+    )
+    c1, c2, c3, dense = lax.optimization_barrier((c1, c2, c3, dense))
+
+    def packed(*pieces):
+        return call(pack_body, [sds((block, width))] * 2, [VM] * 4, pieces, 0, 1 << 20, "pack")
+
+    low, high = packed(b0, c1, c2, c3)
+    a0 = to_slab(low, -1)
+    a2 = to_slab(high, 1)
     keep, send, key_part, value_part, attended, query_grad = call(
         middle_body,
         [sds((2 * width, width))] * 2 + [sds((slots, width))] * 2 + [sds((nodes, width))] * 2,
-        [SM] + [VM] * 13,
-        (core1, a0, a2, b0, c1, c2, c3, w_key, w_value, queries, att_grad, mesh_normed, out_grad,
-         dense),
-        3 << 30, 8 << 20, "middle", [pltpu.VMEM((slots, width), BF16)] * 3,
+        [SM] + [VM] * 10 + [HB] * 3,
+        (core1, a0, a2, b0, c1, c2, c3, queries, att_grad, mesh_normed, dense, w_key, w_value,
+         out_grad),
+        3 << 30, 8 << 20, "middle",
+        [pltpu.VMEM((slots, width), BF16)] * 3 + held(w_key, w_value, out_grad),
     )
     other = shifted(send, "gc", 1)
     mesh_out, mesh_grad, s0, s1, s2, s3 = call(
-        tail_body, [sds((nodes, width))] * 2 + [piece] * 4, [VM] * 11,
-        (key_part, value_part, w_key, w_value, attended, w_out, mesh_h, query_grad, w_query, gain_m,
+        tail_body, [sds((nodes, width))] * 2 + [piece] * 4, [VM] * 4 + [HB] * 7,
+        (key_part, value_part, attended, query_grad, w_key, w_value, w_out, w_query, mesh_h, gain_m,
          out_grad),
-        1 << 30, 5 << 20, "tail",
-    )
+        1 << 30, 5 << 20, "tail", held(w_key, w_value, w_out, w_query, mesh_h, gain_m, out_grad),
+    )
+    other, s1 = lax.optimization_barrier((other, s1))
     chips = lax.axis_size(CHIPS)
     own = (keep.astype(F32) + other.astype(F32)).astype(BF16)
     own = own.reshape(chips, 2 * width // chips, width)
@@ -285,26 +365,36 @@
     t1 = shifted(s1, "z", -1)
     t2 = shifted(s2, "z", -2)
     t3 = shifted(s3, "z", -3)
-
-    def back_of(o):
-        return jnp.concatenate([s0[o], t1[o], t2[o], t3[o]], axis=0)
-
-    r0 = to_slab(back_of(0), 1)
-    r2 = to_slab(back_of(2), -1)
+    parts, t1, t2, t3 = lax.optimization_barrier((parts, t1, t2, t3))
+
+    low, high = packed(s0, t1, t2, t3)
+    r0 = to_slab(low, 1)
+    r2 = to_slab(high, -1)
     (grid_grad,) = call(
-        grid_body, [sds((points, width))], [SM] + [VM] * 9,
-        (sub1, send_rows, grid_x, gain_g, r0, r2, s0, t1, t2, t3),
-        1 << 30, 5 << 20, "grid_grad", [pltpu.VMEM((slots, width), BF16)],
+        grid_body, [sds((points, width))], [SM] + [VM] * 6 + [HB] * 3,
+        (sub1, r0, r2, s0, t1, t2, t3, send_rows, gain_g, grid_x),
+        1 << 30, 5 << 20, "grid_grad",
+        [pltpu.VMEM((slots, width), BF16), pltpu.VMEM((points, width), BF16),
+         pltpu.SemaphoreType.DMA((points // 256,))] + held(send_rows, gain_g, grid_x),
+        [HB],
     )
 
     total = jnp.sum(parts.astype(F32), axis=0).astype(BF16)
     mine = lax.all_to_all(
         jnp.broadcast_to(total[None], (chips, *total.shape)), CHIPS, 0, 0, tiled=True
     ).reshape(2 * width, width)
+    mine, grid_grad = lax.optimization_barrier((mine, grid_grad))
     theirs = shifted(mine, "gc", 1)
-    first = jnp.where(core == 0, mine, theirs)
-    second = jnp.where(core == 0, theirs, mine)
-    weight_grads = jnp.concatenate([first, second], axis=0).astype(F32).reshape(4, width, width)
+    whole = sds((4, width, width), F32)
+    wide = [pltpu.VMEM((2, width, width), F32), pltpu.SemaphoreType.DMA((4,))]
+    (weight_grads,) = call(
+        functools.partial(widen_body, 0), [whole], [SM, VM], (core1, mine), 1 << 20, 3 << 20, "widen_own",
+        wide, [HB],
+    )
+    (weight_grads,) = call(
+        functools.partial(widen_body, 1), [whole], [SM, VM, HB], (core1, theirs, weight_grads),
+        1 << 20, 3 << 20, "widen_other", wide, [HB], {2: 0},
+    )
     return mesh_out, mesh_grad, grid_grad, weight_grads
 
 

time: 128 us -> 112 us (0.88)
  the two profiles are of different devices: /device:TPU:2 before, /device:TPU:1 now
where the time goes in v2:
time: 112 us
  starting transfers between devices  45.3 us (40%)
  waiting for transfers between devices  37.1 us (33%)
  Pallas kernels  25.3 us (23%)
  other arithmetic  1.48 us (1%)
  local copies, waits for them, and re-layouts  1.42 us (1%)
    pallas_call x9, Pallas kernels, call(): pl.pallas_call(body, out_shape=outs, in_specs=in_specs, out_specs=out_spe...  25.3 us
    ppermute x8, waiting for transfers between devices, shifted(): return lax.ppermute(block, axis, [(i, (i + k) % n) for i in range(n)])  22.3 us
    ppermute x4, waiting for transfers between devices, to_slab(): lax.ppermute(block, SLAB, [(i, i + d) for i in range(n) if 0 <= i + d < n])  14.8 us
    all_to_all x1, starting transfers between devices, shards(): parts = lax.all_to_all(own, CHIPS, 0, 0, tiled=True)  12.6 us
    ppermute x4, starting transfers between devices, to_slab(): lax.ppermute(block, SLAB, [(i, i + d) for i in range(n) if 0 <= i + d < n])  12.2 us
    ppermute x8, starting transfers between devices, shifted(): return lax.ppermute(block, axis, [(i, (i + k) % n) for i in range(n)])  12 us
    all_to_all x1, starting transfers between devices, shards(): lax.all_to_all(jnp.broadcast_to(total[None], (chips, *total.shape)), CHIP...  8.41 us
  transfers between devices with their start and end apart: 14, of which 8 were waited for; matrix products, arithmetic and copies ran while one was open for 0% of the time, Pallas kernels for 12%

profile of v2, /device:TPU:1, one launch (start us, length us, event | category | flops | bytes accessed | tf_op | source)
XLA Modules:
  0.0 111.7 jit_solution(8910007173051790879)
XLA Ops:
  0.7 3.0 %gather_rows.1 = (bf16[3,64,512]{2,1,0:T(8,128)(2,1)S(1)}, bf16[3,64,512]{2,1,0:T(8,128)(2,1)S(1)}, bf16[3,64,512]{2,1,0:T(8,128)(2,1)S(1)}, bf16[3,64,512]{2,1,0:T(8,128)(2,1)S(1)}) custom-call(s32[1]{0:T(128)} %bitcast.1.sub_ref, s32[1,3,4,64]{3,2,1,0:T(4,128)} %rows_hbm.3, f32[1,512]{1,0:T(1,128)} %bitcast.14, bf16[2048,512]{1,0:T(8,128)(2,1)} %x_hbm.3), custom_call_target="tpu_custom_call" | custom-call | flops 1073741824 | bytes 4194304 | tf_op jit(solution)/shard_map/gather_rows/pallas_call | solution.py:48
  3.7 2.5 %collective-permute-start = (bf16[3,64,512]{2,1,0:T(8,128)(2,1)S(1)}, bf16[3,64,512]{2,1,0:T(8,128)(2,1)S(1)}, u32[]{:S(2)}, u32[]{:S(2)}) collective-permute-start(bf16[3,64,512]{2,1,0:T(8,128)(2,1)S(1)} %get-tuple-element.44), channel_id=1, source_target_pairs={{0,1},{1,2},{2,3},{3,0},{4,5},{5,6},{6,7},{7,4},{8,9},{9,10},{10,1... | collective-permute-start | bytes 589832 | tf_op jit(solution)/shard_map/ppermute | solution.py:283
  6.2 3.3 %collective-permute-start.1 = (bf16[3,64,512]{2,1,0:T(8,128)(2,1)S(1)}, bf16[3,64,512]{2,1,0:T(8,128)(2,1)S(1)}, u32[]{:S(2)}, u32[]{:S(2)}) collective-permute-start(bf16[3,64,512]{2,1,0:T(8,128)(2,1)S(1)} %get-tuple-element.45), channel_id=1, source_target_pairs={{0,2},{1,3},{2,0},{3,1},{4,6},{5,7},{6,4},{7,5},{8,10},{9,11},{10,... | collective-permute-start | bytes 589832 | tf_op jit(solution)/shard_map/ppermute | solution.py:283
  10.6 4.4 %prep.1 = (bf16[64,512]{1,0:T(8,128)(2,1)S(1)}, bf16[64,512]{1,0:T(8,128)(2,1)S(1)}, bf16[64,512]{1,0:T(8,128)(2,1)S(1)}, f32[4,64,768]{2,1,0:T(8,128)S(1)}) custom-call(s32[8,96,8]{2,1,0:T(8,128)S(1)} %bitcast.13, f32[4,64,128]{2,1,0:T(8,128)S(1)} %pad.4.bias_ref, bf16[64,512]{1,0:T(8,128)(2,1)} %mesh_hbm.3, f32[1,512]{1,0:T(1,128)} %bitcast.16, ...), custom_call_target="tpu_custom_call" | custom-call | flops 1073741824 | bytes 8388608 | tf_op jit(solution)/shard_map/prep/pallas_call | solution.py:48
  15.0 3.0 %collective-permute-done.1.p2.b2 = bf16[3,64,512]{2,1,0:T(8,128)(2,1)S(1)} collective-permute-done((bf16[3,64,512]{2,1,0:T(8,128)(2,1)S(1)}, bf16[3,64,512]{2,1,0:T(8,128)(2,1)S(1)}, u32[]{:S(2)}, u32[]{:S(2)}) %collective-permute-start.1) | collective-permute-done | bytes 196640 | tf_op jit(solution)/shard_map/ppermute | solution.py:283
  18.1 3.5 %collective-permute-start.3 = (bf16[256,512]{1,0:T(8,128)(2,1)S(1)}, bf16[256,512]{1,0:T(8,128)(2,1)S(1)}, u32[]{:S(2)}, u32[]{:S(2)}) collective-permute-start(bf16[256,512]{1,0:T(8,128)(2,1)S(1)} %get-tuple-element.52), channel_id=1, source_target_pairs={{4,0},{8,4},{12,8},{16,12},{20,16},{24,20},{28,24},{32,28},{36,32}... | collective-permute-start | bytes 786440 | tf_op jit(solution)/shard_map/ppermute | solution.py:288
  21.5 3.1 %collective-permute-start.4 = (bf16[256,512]{1,0:T(8,128)(2,1)S(1)}, bf16[256,512]{1,0:T(8,128)(2,1)S(1)}, u32[]{:S(2)}, u32[]{:S(2)}) collective-permute-start(bf16[256,512]{1,0:T(8,128)(2,1)S(1)} %get-tuple-element.53), channel_id=1, source_target_pairs={{0,4},{4,8},{8,12},{12,16},{16,20},{20,24},{24,28},{28,32},{32,36}... | collective-permute-start | bytes 786440 | tf_op jit(solution)/shard_map/ppermute | solution.py:288
  24.6 2.1 %collective-permute-done.3.a0 = bf16[256,512]{1,0:T(8,128)(2,1)S(1)} collective-permute-done((bf16[256,512]{1,0:T(8,128)(2,1)S(1)}, bf16[256,512]{1,0:T(8,128)(2,1)S(1)}, u32[]{:S(2)}, u32[]{:S(2)}) %collective-permute-start.3) | collective-permute-done | bytes 262176 | tf_op jit(solution)/shard_map/ppermute | solution.py:288
  27.9 7.4 %middle.1 = (bf16[1024,512]{1,0:T(8,128)(2,1)S(1)}, bf16[1024,512]{1,0:T(8,128)(2,1)S(1)}, bf16[768,512]{1,0:T(8,128)(2,1)S(1)}, bf16[768,512]{1,0:T(8,128)(2,1)...) custom-call(s32[1]{0:T(128)} %bitcast.core_ref, bf16[256,512]{1,0:T(8,128)(2,1)S(1)} %collective-permute-done.3.a0, ...), custom_call_target="tpu_custom_call" | custom-call | flops 3221225472 | bytes 8388608 | tf_op jit(solution)/shard_map/middle/pallas_call | solution.py:48
  35.4 3.4 %tail.1 = (bf16[64,512]{1,0:T(8,128)(2,1)}, bf16[64,512]{1,0:T(8,128)(2,1)}, bf16[3,64,512]{2,1,0:T(8,128)(2,1)S(1)}, bf16[3,64,512]{2,1,0:T(8,128)(2,1)S(1)}, b...) custom-call(bf16[768,512]{1,0:T(8,128)(2,1)S(1)} %get-tuple-element.58.kp_ref, ...), custom_call_target="tpu_custom_call" | custom-call | flops 1073741824 | bytes 5242880 | tf_op jit(solution)/shard_map/tail/pallas_call | solution.py:48
  38.8 1.3 %add_convert_fusion = bf16[1024,512]{1,0:T(8,128)(2,1)} fusion(bf16[1024,512]{1,0:T(8,128)(2,1)S(1)} %collective-permute-done.5, bf16[1024,512]{1,0:T(8,128)(2,1)S(1)} %get-tuple-element.64), kind=kLoop, calls=%fused_computation | loop fusion | flops 2097152 | bytes 3145728 | tf_op jit(solution)/shard_map/convert_element_type | solution.py:361
  40.1 12.6 %all-to-all-start = ((bf16[64,16,512]{2,1,0:T(8,128)(2,1)}), bf16[64,16,512]{2,1,0:T(8,128)(2,1)S(1)}, u32[]{:S(2)}, u32[]{:S(2)}) async-start(bf16[64,16,512]{2,1,0:T(8,128)(2,1)} %bitcast.7), calls=%async_computation | async-start | bytes 2097152 | tf_op jit(solution)/shard_map/all_to_all | solution.py:363
  52.7 2.6 %collective-permute-start.7 = (bf16[3,64,512]{2,1,0:T(8,128)(2,1)S(1)}, bf16[3,64,512]{2,1,0:T(8,128)(2,1)S(1)}, u32[]{:S(2)}, u32[]{:S(2)}) collective-permute-start(bf16[3,64,512]{2,1,0:T(8,128)(2,1)S(1)} %get-tuple-element.69), channel_id=1, source_target_pairs={{0,2},{1,3},{2,0},{3,1},{4,6},{5,7},{6,4},{7,5},{8,10},{9,11},{10,... | collective-permute-start | bytes 589832 | tf_op jit(solution)/shard_map/ppermute | solution.py:283
  55.6 2.4 %collective-permute-start.6 = (bf16[3,64,512]{2,1,0:T(8,128)(2,1)S(1)}, bf16[3,64,512]{2,1,0:T(8,128)(2,1)S(1)}, u32[]{:S(2)}, u32[]{:S(2)}) collective-permute-start(bf16[3,64,512]{2,1,0:T(8,128)(2,1)S(1)} %get-tuple-element.68), channel_id=1, source_target_pairs={{0,3},{1,0},{2,1},{3,2},{4,7},{5,4},{6,5},{7,6},{8,11},{9,8},{10,9... | collective-permute-start | bytes 589832 | tf_op jit(solution)/shard_map/ppermute | solution.py:283
  58.0 13.7 %collective-permute-done.7.p2.s2 = bf16[3,64,512]{2,1,0:T(8,128)(2,1)S(1)} collective-permute-done((bf16[3,64,512]{2,1,0:T(8,128)(2,1)S(1)}, bf16[3,64,512]{2,1,0:T(8,128)(2,1)S(1)}, u32[]{:S(2)}, u32[]{:S(2)}) %collective-permute-start.7) | collective-permute-done | bytes 196640 | tf_op jit(solution)/shard_map/ppermute | solution.py:283
  71.7 4.3 %collective-permute-done.8.p3.s3 = bf16[3,64,512]{2,1,0:T(8,128)(2,1)S(1)} collective-permute-done((bf16[3,64,512]{2,1,0:T(8,128)(2,1)S(1)}, bf16[3,64,512]{2,1,0:T(8,128)(2,1)S(1)}, u32[]{:S(2)}, u32[]{:S(2)}) %collective-permute-start.8) | collective-permute-done | bytes 196640 | tf_op jit(solution)/shard_map/ppermute | solution.py:283
  77.3 8.4 %all-to-all-start.1 = ((bf16[64,16,512]{2,1,0:T(8,128)(2,1)}), bf16[64,16,512]{2,1,0:T(8,128)(2,1)S(1)}, u32[]{:S(2)}, u32[]{:S(2)}) async-start(bf16[64,16,512]{2,1,0:T(8,128)(2,1)} %broadcast_in_dim.21), calls=%async_computation.1 | async-start | bytes 2097152 | tf_op jit(solution)/shard_map/all_to_all | solution.py:383
  85.8 3.8 %collective-permute-start.9 = (bf16[256,512]{1,0:T(8,128)(2,1)S(1)}, bf16[256,512]{1,0:T(8,128)(2,1)S(1)}, u32[]{:S(2)}, u32[]{:S(2)}) collective-permute-start(bf16[256,512]{1,0:T(8,128)(2,1)S(1)} %get-tuple-element.76), channel_id=1, source_target_pairs={{0,4},{4,8},{8,12},{12,16},{16,20},{20,24},{24,28},{28,32},{32,36}... | collective-permute-start | bytes 786440 | tf_op jit(solution)/shard_map/ppermute | solution.py:288
  89.6 1.9 %collective-permute-start.10 = (bf16[256,512]{1,0:T(8,128)(2,1)S(1)}, bf16[256,512]{1,0:T(8,128)(2,1)S(1)}, u32[]{:S(2)}, u32[]{:S(2)}) collective-permute-start(bf16[256,512]{1,0:T(8,128)(2,1)S(1)} %get-tuple-element.77), channel_id=1, source_target_pairs={{4,0},{8,4},{12,8},{16,12},{20,16},{24,20},{28,24},{32,28},{36,32}... | collective-permute-start | bytes 786440 | tf_op jit(solution)/shard_map/ppermute | solution.py:288
  91.5 8.5 %collective-permute-done.9.r0 = bf16[256,512]{1,0:T(8,128)(2,1)S(1)} collective-permute-done((bf16[256,512]{1,0:T(8,128)(2,1)S(1)}, bf16[256,512]{1,0:T(8,128)(2,1)S(1)}, u32[]{:S(2)}, u32[]{:S(2)}) %collective-permute-start.9) | collective-permute-done | bytes 262176 | tf_op jit(solution)/shard_map/ppermute | solution.py:288
  100.0 3.0 %collective-permute-done.10.r2 = bf16[256,512]{1,0:T(8,128)(2,1)S(1)} collective-permute-done((bf16[256,512]{1,0:T(8,128)(2,1)S(1)}, bf16[256,512]{1,0:T(8,128)(2,1)S(1)}, u32[]{:S(2)}, u32[]{:S(2)}) %collective-permute-start.10) | collective-permute-done | bytes 262176 | tf_op jit(solution)/shard_map/ppermute | solution.py:288
  103.0 4.4 %grid_grad.1 = bf16[2048,512]{1,0:T(8,128)(2,1)} custom-call(s32[1]{0:T(128)} %bitcast.1.sub_ref, bf16[256,512]{1,0:T(8,128)(2,1)S(1)} %collective-permute-done.9.r0, bf16[256,512]{1,0:T(8,128)(2,1)S(1)} %collective-permute-done.10.r2, bf16[3,64,512]{2,1,0:T(8,128)(2,1)S(1)} %get-tuple-element.72.p0.s0, ...), custom_call_target="tpu_custom_call" | custom-call | flops 1073741824 | bytes 5242880 | tf_op jit(solution)/shard_map/grid_grad/pallas_call | solution.py:48
  107.5 1.4 %widen_own.1.refs_0_ = f32[4,512,512]{2,1,0:T(8,128)} custom-call(s32[1]{0:T(128)} %bitcast.core_ref, bf16[1024,512]{1,0:T(8,128)(2,1)S(1)} %bitcast.12), custom_call_target="tpu_custom_call" | custom-call | flops 1048576 | bytes 3145728 | tf_op jit(solution)/shard_map/widen_own/pallas_call | solution.py:48
  110.1 1.4 %widen_other.1 = f32[4,512,512]{2,1,0:T(8,128)} custom-call(s32[1]{0:T(128)} %bitcast.core_ref, bf16[1024,512]{1,0:T(8,128)(2,1)S(1)} %collective-permute-done.11.half_ref, f32[4,512,512]{2,1,0:T(8,128)} %widen_own.1.refs_0_), custom_call_target="tpu_custom_call", output_to_operand_aliasing={{}: (2, {})} | custom-call | flops 1048576 | bytes 3145728 | tf_op jit(solution)/shard_map/widen_other/pallas_call | solution.py:48
  (28 shorter events, 5.3 us)
Async XLA Ops:
  0.6 9.6 %copy-start.1 = (s32[64,96]{1,0:T(8,128)S(1)}, s32[64,96]{1,0:T(8,128)}, u32[]{:S(2)}) copy-start(s32[64,96]{1,0:T(8,128)} %param.23) | copy-start | bytes 73732
  0.6 9.6 %copy-start = (f32[64,384]{1,0:T(8,128)S(1)}, f32[64,384]{1,0:T(8,128)}, u32[]{:S(2)}) copy-start(f32[64,384]{1,0:T(8,128)} %param.21) | copy-start | bytes 294916
  0.7 9.8 %copy-start.2 = (s32[64,96]{1,0:T(8,128)S(1)}, s32[64,96]{1,0:T(8,128)}, u32[]{:S(2)}) copy-start(s32[64,96]{1,0:T(8,128)} %param.22) | copy-start | bytes 73732
  3.7 11.3 %collective-permute-start = (bf16[3,64,512]{2,1,0:T(8,128)(2,1)S(1)}, bf16[3,64,512]{2,1,0:T(8,128)(2,1)S(1)}, u32[]{:S(2)}, u32[]{:S(2)}) collective-permute-start(bf16[3,64,512]{2,1,0:T(8,128)(2,1)S(1)} %get-tuple-element.44), channel_id=1, source_target_pairs={{0,1},{1,2},{2,3},{3,0},{4,5},{5,6},{6,7},{7,4},{8,9},{9,10},{10,1... | collective-permute-start | bytes 589832 | tf_op jit(solution)/shard_map/ppermute | solution.py:283
  6.2 11.8 %collective-permute-start.1 = (bf16[3,64,512]{2,1,0:T(8,128)(2,1)S(1)}, bf16[3,64,512]{2,1,0:T(8,128)(2,1)S(1)}, u32[]{:S(2)}, u32[]{:S(2)}) collective-permute-start(bf16[3,64,512]{2,1,0:T(8,128)(2,1)S(1)} %get-tuple-element.45), channel_id=1, source_target_pairs={{0,2},{1,3},{2,0},{3,1},{4,6},{5,7},{6,4},{7,5},{8,10},{9,11},{10,... | collective-permute-start | bytes 589832 | tf_op jit(solution)/shard_map/ppermute | solution.py:283
  9.5 8.5 %collective-permute-start.2 = (bf16[3,64,512]{2,1,0:T(8,128)(2,1)S(1)}, bf16[3,64,512]{2,1,0:T(8,128)(2,1)S(1)}, u32[]{:S(2)}, u32[]{:S(2)}) collective-permute-start(bf16[3,64,512]{2,1,0:T(8,128)(2,1)S(1)} %get-tuple-element.46), channel_id=1, source_target_pairs={{0,3},{1,0},{2,1},{3,2},{4,7},{5,4},{6,5},{7,6},{8,11},{9,8},{10,9... | collective-permute-start | bytes 589832 | tf_op jit(solution)/shard_map/ppermute | solution.py:283
  18.1 8.7 %collective-permute-start.3 = (bf16[256,512]{1,0:T(8,128)(2,1)S(1)}, bf16[256,512]{1,0:T(8,128)(2,1)S(1)}, u32[]{:S(2)}, u32[]{:S(2)}) collective-permute-start(bf16[256,512]{1,0:T(8,128)(2,1)S(1)} %get-tuple-element.52), channel_id=1, source_target_pairs={{4,0},{8,4},{12,8},{16,12},{20,16},{24,20},{28,24},{32,28},{36,32}... | collective-permute-start | bytes 786440 | tf_op jit(solution)/shard_map/ppermute | solution.py:288
  21.5 6.4 %collective-permute-start.4 = (bf16[256,512]{1,0:T(8,128)(2,1)S(1)}, bf16[256,512]{1,0:T(8,128)(2,1)S(1)}, u32[]{:S(2)}, u32[]{:S(2)}) collective-permute-start(bf16[256,512]{1,0:T(8,128)(2,1)S(1)} %get-tuple-element.53), channel_id=1, source_target_pairs={{0,4},{4,8},{8,12},{12,16},{16,20},{20,24},{24,28},{28,32},{32,36}... | collective-permute-start | bytes 786440 | tf_op jit(solution)/shard_map/ppermute | solution.py:288
  35.3 3.5 %collective-permute-start.5 = (bf16[1024,512]{1,0:T(8,128)(2,1)S(1)}, bf16[1024,512]{1,0:T(8,128)(2,1)S(1)}, u32[]{:S(2)}, u32[]{:S(2)}) collective-permute-start(bf16[1024,512]{1,0:T(8,128)(2,1)S(1)} %get-tuple-element.65), channel_id=1, source_target_pairs={{0,4},{4,0},{1,5},{5,1},{2,6},{6,2},{3,7},{7,3},{8,12},{12,8},{9,1... | collective-permute-start | bytes 3145736 | tf_op jit(solution)/shard_map/ppermute | solution.py:283
  40.1 36.0 %all-to-all-start = ((bf16[64,16,512]{2,1,0:T(8,128)(2,1)}), bf16[64,16,512]{2,1,0:T(8,128)(2,1)S(1)}, u32[]{:S(2)}, u32[]{:S(2)}) async-start(bf16[64,16,512]{2,1,0:T(8,128)(2,1)} %bitcast.7), calls=%async_computation | async-start | bytes 2097152 | tf_op jit(solution)/shard_map/all_to_all | solution.py:363
  52.7 19.0 %collective-permute-start.7 = (bf16[3,64,512]{2,1,0:T(8,128)(2,1)S(1)}, bf16[3,64,512]{2,1,0:T(8,128)(2,1)S(1)}, u32[]{:S(2)}, u32[]{:S(2)}) collective-permute-start(bf16[3,64,512]{2,1,0:T(8,128)(2,1)S(1)} %get-tuple-element.69), channel_id=1, source_target_pairs={{0,2},{1,3},{2,0},{3,1},{4,6},{5,7},{6,4},{7,5},{8,10},{9,11},{10,... | collective-permute-start | bytes 589832 | tf_op jit(solution)/shard_map/ppermute | solution.py:283
  55.3 20.7 %collective-permute-start.8 = (bf16[3,64,512]{2,1,0:T(8,128)(2,1)S(1)}, bf16[3,64,512]{2,1,0:T(8,128)(2,1)S(1)}, u32[]{:S(2)}, u32[]{:S(2)}) collective-permute-start(bf16[3,64,512]{2,1,0:T(8,128)(2,1)S(1)} %get-tuple-element.70), channel_id=1, source_target_pairs={{0,1},{1,2},{2,3},{3,0},{4,5},{5,6},{6,7},{7,4},{8,9},{9,10},{10,1... | collective-permute-start | bytes 589832 | tf_op jit(solution)/shard_map/ppermute | solution.py:283
  55.6 20.5 %collective-permute-start.6 = (bf16[3,64,512]{2,1,0:T(8,128)(2,1)S(1)}, bf16[3,64,512]{2,1,0:T(8,128)(2,1)S(1)}, u32[]{:S(2)}, u32[]{:S(2)}) collective-permute-start(bf16[3,64,512]{2,1,0:T(8,128)(2,1)S(1)} %get-tuple-element.68), channel_id=1, source_target_pairs={{0,3},{1,0},{2,1},{3,2},{4,7},{5,4},{6,5},{7,6},{8,11},{9,8},{10,9... | collective-permute-start | bytes 589832 | tf_op jit(solution)/shard_map/ppermute | solution.py:283
  77.3 30.1 %all-to-all-start.1 = ((bf16[64,16,512]{2,1,0:T(8,128)(2,1)}), bf16[64,16,512]{2,1,0:T(8,128)(2,1)S(1)}, u32[]{:S(2)}, u32[]{:S(2)}) async-start(bf16[64,16,512]{2,1,0:T(8,128)(2,1)} %broadcast_in_dim.21), calls=%async_computation.1 | async-start | bytes 2097152 | tf_op jit(solution)/shard_map/all_to_all | solution.py:383
  85.8 14.2 %collective-permute-start.9 = (bf16[256,512]{1,0:T(8,128)(2,1)S(1)}, bf16[256,512]{1,0:T(8,128)(2,1)S(1)}, u32[]{:S(2)}, u32[]{:S(2)}) collective-permute-start(bf16[256,512]{1,0:T(8,128)(2,1)S(1)} %get-tuple-element.76), channel_id=1, source_target_pairs={{0,4},{4,8},{8,12},{12,16},{16,20},{20,24},{24,28},{28,32},{32,36}... | collective-permute-start | bytes 786440 | tf_op jit(solution)/shard_map/ppermute | solution.py:288
  89.6 13.4 %collective-permute-start.10 = (bf16[256,512]{1,0:T(8,128)(2,1)S(1)}, bf16[256,512]{1,0:T(8,128)(2,1)S(1)}, u32[]{:S(2)}, u32[]{:S(2)}) collective-permute-start(bf16[256,512]{1,0:T(8,128)(2,1)S(1)} %get-tuple-element.77), channel_id=1, source_target_pairs={{4,0},{8,4},{12,8},{16,12},{20,16},{24,20},{28,24},{32,28},{36,32}... | collective-permute-start | bytes 786440 | tf_op jit(solution)/shard_map/ppermute | solution.py:288
  107.4 2.7 %collective-permute-start.11 = (bf16[1024,512]{1,0:T(8,128)(2,1)S(1)}, bf16[1024,512]{1,0:T(8,128)(2,1)S(1)}, u32[]{:S(2)}, u32[]{:S(2)}) collective-permute-start(bf16[1024,512]{1,0:T(8,128)(2,1)S(1)} %bitcast.11), channel_id=1, source_target_pairs={{0,4},{4,0},{1,5},{5,1},{2,6},{6,2},{3,7},{7,3},{8,12},{12,8},{9,1... | collective-permute-start | bytes 3145736 | tf_op jit(solution)/shard_map/ppermute | solution.py:283

commit v3 on v2

--- a/solution.py
+++ b/solution.py
@@ -9,7 +9,7 @@
 from jax.sharding import PartitionSpec as P
 
 SLAB = ("gx", "gy", "gc")
-CHIPS = ("gx", "gy", "z")
+PLANE = ("gx", "gy")
 ALL = ("gx", "gy", "gc", "z")
 
 EPSILON = 1e-06
@@ -70,10 +70,10 @@
     return [pltpu.VMEM(a.shape, a.dtype) for a in args] + [pltpu.SemaphoreType.DMA((len(args),))]
 
 
-def gather_body(sub_ref, rows_hbm, gain_hbm, x_hbm, o0, o1, o2, o3, rows_ref, gain_ref, x_ref, sems):
+def gather_body(sub_ref, rows_hbm, gain_hbm, x_hbm, n0, n1, n2, n3, w0, w1, w2, w3,
+                rows_ref, gain_ref, x_ref, sems):
     half = x_ref.shape[0] // 2
     cap = rows_ref.shape[3]
-    outs = (o0, o1, o2, o3)
     parts = [pl.ds(i * half, half) for i in range(2)]
     copies = fetch(
         [rows_hbm, gain_hbm] + [x_hbm.at[p] for p in parts],
@@ -101,38 +101,46 @@
         wide = nn(onehot, x_ref[first : first + count, :])
         normed = (wide * inv_rms(wide) * gain).astype(BF16)
         for k in range(4):
-            outs[k][o] = normed[k * cap : (k + 1) * cap]
-
-
-def prep_body(nbr_ref, bias_ref, mesh_hbm, gain_hbm, wq_hbm, wo_hbm, og_hbm,
-              normed_ref, q_ref, ag_ref, dense_ref, inv_ref,
-              mesh_ref, gain_ref, wq_ref, wo_ref, og_ref, sems):
+            piece = normed[k * cap : (k + 1) * cap]
+            if step < 2:
+                (n0, n1, n2, n3)[k][step] = piece
+            else:
+                (w0, w1, w2, w3)[k][...] = piece
+
+
+def prep_body(sub_ref, mesh_hbm, gain_hbm, wq_hbm, wo_hbm, og_hbm, nbr_hbm, valid_hbm, bias_hbm,
+              normed_ref, q_ref, ag_ref, dense_ref, inv_ref, edge_ref,
+              nbr_ref, valid_ref, bias_ref, mesh_ref, gain_ref, wq_ref, wo_ref, og_ref, sems):
     copies = fetch(
-        (mesh_hbm, gain_hbm, wq_hbm, wo_hbm, og_hbm), (mesh_ref, gain_ref, wq_ref, wo_ref, og_ref), sems
+        (nbr_hbm, valid_hbm, bias_hbm, mesh_hbm, gain_hbm, wq_hbm, wo_hbm, og_hbm),
+        (nbr_ref, valid_ref, bias_ref, mesh_ref, gain_ref, wq_ref, wo_ref, og_ref),
+        sems,
     )
     heads, nodes, slots = dense_ref.shape
-    groups, fan, per = nbr_ref.shape
-    lanes = lax.broadcasted_iota(jnp.int32, (fan, slots), 1)
-    edge = lax.broadcasted_iota(jnp.int32, (fan, slots), 0) + 1
-
-    def group(g, carry):
-        block = nbr_ref[g]
-        found = []
-        for i in range(per):
-            hit = jnp.where(block[:, i : i + 1] == lanes, edge, 0)
-            found.append(jnp.sum(hit, axis=0, keepdims=True))
-        inv_ref[pl.ds(pl.multiple_of(g * per, per), per), :] = jnp.concatenate(found, axis=0)
-        return carry
-
-    lax.fori_loop(0, groups, group, 0)
+    fan = nbr_ref.shape[1]
+    for copy in copies[:3]:
+        copy.wait()
+    slot = nbr_ref[...]
+    slot = (slot & ~192) | (((sub_ref[0] - (slot >> 6)) & 3) << 6)
+    high, low = slot >> 7, slot & 127
+    blocks = lax.broadcasted_iota(jnp.int32, (8, fan), 0)
+    lanes = lax.broadcasted_iota(jnp.int32, (128, fan), 0)
+    edge = lax.broadcasted_iota(jnp.int32, (8, fan), 1).astype(F32) + 1.0
+    for m in range(nodes):
+        named = jnp.where(high[m : m + 1, :] == blocks, edge, 0.0).astype(BF16)
+        places = jnp.where(low[m : m + 1, :] == lanes, 1.0, 0.0).astype(BF16)
+        inv_ref[m * 8 : (m + 1) * 8, :] = nt(named, places)
+    live = valid_ref[...] == 1
+    for h in range(heads):
+        edge_ref[h, :, 0:fan] = jnp.where(live, bias_ref[:, h * fan : (h + 1) * fan], ABSENT)
     for b in range(slots // 128):
-        at = inv_ref[:, b * 128 : (b + 1) * 128] - 1
+        at = inv_ref[pl.ds(b, nodes, stride=8), :].astype(jnp.int32) - 1
         here = at >= 0
         at = jnp.maximum(at, 0)
         for h in range(heads):
-            got = jnp.take_along_axis(bias_ref[h], at, axis=1, mode="promise_in_bounds")
+            got = jnp.take_along_axis(edge_ref[h], at, axis=1, mode="promise_in_bounds")
             dense_ref[h, :, b * 128 : (b + 1) * 128] = jnp.where(here, got, ABSENT)
-    for copy in copies:
+    for copy in copies[3:]:
         copy.wait()
     wide = mesh_ref[...].astype(F32)
     normed = (wide * inv_rms(wide) * gain_ref[...]).astype(BF16)
@@ -143,14 +151,14 @@
 
 def middle_body(core_ref, a0, a2, b0, b1, b2, b3, q_ref, ag_ref, mn_ref, bias_ref,
                 wk_hbm, wv_hbm, og_hbm, keep_ref, send_ref, kp_ref, vp_ref, att_ref, qg_ref,
-                rows, keys, vals, wk_ref, wv_ref, og_ref, sems):
+                wk_ref, wv_ref, og_ref, rows, keys, vals, sems):
     copies = fetch((wk_hbm, wv_hbm, og_hbm), (wk_ref, wv_ref, og_ref), sems)
     heads = bias_ref.shape[0]
     block = a0.shape[0]
-    cap = b0.shape[1]
+    cap = b0.shape[0]
     rows[0:block] = a0[...]
     for k, piece in enumerate((b0, b1, b2, b3)):
-        rows[block + k * cap : block + (k + 1) * cap] = piece[1]
+        rows[block + k * cap : block + (k + 1) * cap] = piece[...]
     rows[2 * block : 3 * block] = a2[...]
     copies[0].wait()
     keys[...] = nn(rows[...], wk_ref[...]).astype(BF16)
@@ -190,23 +198,19 @@
     place(1, width, tn(att_ref[...], og_ref[...]).astype(BF16))
 
 
-def tail_body(kp_ref, vp_ref, att_ref, qg_ref, wk_hbm, wv_hbm, wo_hbm, wq_hbm, mesh_hbm, gain_hbm,
-              og_hbm, out_ref, grad_ref, s0, s1, s2, s3,
-              wk_ref, wv_ref, wo_ref, wq_ref, mesh_ref, gain_ref, og_ref, sems):
+def tail_body(kp_ref, vp_ref, att_ref, qg_ref, wk_ref, wv_ref, og_ref, wo_hbm, wq_hbm, mesh_hbm,
+              gain_hbm, out_ref, grad_ref, s0, s1, s2, s3,
+              wo_ref, wq_ref, mesh_ref, gain_ref, sems):
     copies = fetch(
-        (wk_hbm, wv_hbm, wo_hbm, wq_hbm, mesh_hbm, gain_hbm, og_hbm),
-        (wk_ref, wv_ref, wo_ref, wq_ref, mesh_ref, gain_ref, og_ref),
-        sems,
+        (wo_hbm, wq_hbm, mesh_hbm, gain_hbm), (wo_ref, wq_ref, mesh_ref, gain_ref), sems
     )
     cap = s0.shape[1]
-    copies[0].wait()
-    copies[1].wait()
     back = (nt(kp_ref[...], wk_ref[...]) + nt(vp_ref[...], wv_ref[...])).astype(BF16)
     for o in range(3):
         for k, piece in enumerate((s0, s1, s2, s3)):
             first = (o * 4 + k) * cap
             piece[o] = back[first : first + cap]
-    for copy in copies[2:]:
+    for copy in copies:
         copy.wait()
     wide = mesh_ref[...].astype(F32)
     out_ref[...] = (wide + nn(att_ref[...], wo_ref[...])).astype(BF16)
@@ -219,7 +223,7 @@
     cap = p0.shape[1]
     for k, piece in enumerate((p0, p1, p2, p3)):
         low_ref[k * cap : (k + 1) * cap, :] = piece[0]
-        high_ref[k * cap : (k + 1) * cap, :] = piece[2]
+        high_ref[k * cap : (k + 1) * cap, :] = piece[piece.shape[0] - 1]
 
 
 def grid_body(sub_ref, r0, r2, s0, s1, s2, s3, rows_hbm, gain_hbm, x_hbm, out_hbm,
@@ -278,6 +282,30 @@
         copy.wait()
 
 
+def pair_body(keep_ref, other_ref, out_hbm, sums, sems):
+    part = sums.shape[0] // 4
+    copies = []
+    for i in range(4):
+        at = slice(i * part, (i + 1) * part)
+        sums[at, :] = (keep_ref[at, :].astype(F32) + other_ref[at, :].astype(F32)).astype(BF16)
+        copies.append(pltpu.make_async_copy(sums.at[at], out_hbm.at[at], sems.at[i]))
+        copies[-1].start()
+    for copy in copies:
+        copy.wait()
+
+
+def spread_body(p0, p1, p2, p3, out_hbm, total, sems):
+    even = p0[...].astype(F32) + p2[...].astype(F32)
+    odd = p1[...].astype(F32) + p3[...].astype(F32)
+    total[...] = (even + odd).astype(BF16)
+    copies = []
+    for i in range(out_hbm.shape[0]):
+        copies.append(pltpu.make_async_copy(total, out_hbm.at[i], sems.at[i]))
+        copies[-1].start()
+    for copy in copies:
+        copy.wait()
+
+
 def shifted(block, axis, k):
     n = lax.axis_size(axis)
     return lax.ppermute(block, axis, [(i, (i + k) % n) for i in range(n)])
@@ -300,76 +328,79 @@
     block = 4 * cap
     slots = 3 * block
     heads = edge_bias.shape[1] // fan
-    sub = lax.axis_index("z").astype(jnp.int32)
-    core = lax.axis_index("gc").astype(jnp.int32)
-    sub1, core1 = sub.reshape(1), core.reshape(1)
+    sub1 = lax.axis_index("z").astype(jnp.int32).reshape(1)
+    core1 = lax.axis_index("gc").astype(jnp.int32).reshape(1)
     gain_g, gain_m = gain_grid.reshape(1, width), gain_mesh.reshape(1, width)
-    piece = sds((3, cap, width))
-    grid_x, mesh_h, out_grad, send_rows, w_key, w_value, w_query, w_out, gain_g, gain_m = (
+    (grid_x, mesh_h, out_grad, send_rows, w_key, w_value, w_query, w_out, gain_g, gain_m, edge_bias,
+     neighbours, valid) = (
         pltpu.with_memory_space_constraint(a, pltpu.HBM)
-        for a in (grid_x, mesh_h, out_grad, send_rows, w_key, w_value, w_query, w_out, gain_g, gain_m)
-    )
-
-    b0, b1, b2, b3 = call(
-        gather_body, [piece] * 4, [SM, HB, HB, HB], (sub1, send_rows, gain_g, grid_x),
-        1 << 30, 4 << 20, "gather_rows",
+        for a in (grid_x, mesh_h, out_grad, send_rows, w_key, w_value, w_query, w_out, gain_g, gain_m,
+                  edge_bias, neighbours, valid)
+    )
+
+    n0, n1, n2, n3, w0, w1, w2, w3 = call(
+        gather_body, [sds((2, cap, width))] * 4 + [sds((cap, width))] * 4, [SM, HB, HB, HB],
+        (sub1, send_rows, gain_g, grid_x), 1 << 30, 4 << 20, "gather_rows",
         held(send_rows, gain_g, grid_x)[:-1] + [pltpu.SemaphoreType.DMA((4,))],
     )
-    c1 = shifted(b1, "z", 1)
-    c2 = shifted(b2, "z", 2)
-    c3 = shifted(b3, "z", 3)
-
-    neighbours, b0 = lax.optimization_barrier((neighbours, b0))
-    source = (neighbours >> 6) & 3
-    slot = (neighbours & ~192) | (((sub - source) & 3) << 6)
-    nbr = slot.reshape(nodes // 8, 8, fan).transpose(0, 2, 1)
-    bias = jnp.where((valid == 1)[:, None, :], edge_bias.reshape(nodes, heads, fan), ABSENT)
-    bias = jnp.pad(bias.transpose(1, 0, 2), ((0, 0), (0, 0), (0, 128 - fan)))
+    n1, n2, n3 = (shifted(n, "z", k) for k, n in ((1, n1), (2, n2), (3, n3)))
+    w1, w2, w3 = (shifted(w, "z", k) for k, w in ((1, w1), (2, w2), (3, w3)))
+
+    def packed(*pieces):
+        return call(pack_body, [sds((block, width))] * 2, [VM] * 4, pieces, 0, 1 << 20, "pack")
+
+    low, high = packed(n0, n1, n2, n3)
+    sub2, low = lax.optimization_barrier((sub1, low))
+    a0 = to_slab(low, -1)
+    a2 = to_slab(high, 1)
+    prep_args = (mesh_h, gain_m, w_query, w_out, out_grad, neighbours, valid, edge_bias)
     mesh_normed, queries, att_grad, dense = call(
         prep_body,
         [sds((nodes, width))] * 3 + [sds((heads, nodes, slots), F32)],
-        [VM] * 2 + [HB] * 5, (nbr, bias, mesh_h, gain_m, w_query, w_out, out_grad),
-        1 << 30, 8 << 20, "prep",
-        [pltpu.VMEM((nodes, slots), jnp.int32)] + held(mesh_h, gain_m, w_query, w_out, out_grad),
-    )
-    c1, c2, c3, dense = lax.optimization_barrier((c1, c2, c3, dense))
-
-    def packed(*pieces):
-        return call(pack_body, [sds((block, width))] * 2, [VM] * 4, pieces, 0, 1 << 20, "pack")
-
-    low, high = packed(b0, c1, c2, c3)
-    a0 = to_slab(low, -1)
-    a2 = to_slab(high, 1)
-    keep, send, key_part, value_part, attended, query_grad = call(
+        [SM] + [HB] * 8, (sub2, *prep_args), 1 << 30, 8 << 20, "prep",
+        [pltpu.VMEM((nodes * 8, 128), F32), pltpu.VMEM((heads, nodes, 128), F32)]
+        + held(neighbours, valid, edge_bias, mesh_h, gain_m, w_query, w_out, out_grad),
+    )
+    keep, send, key_part, value_part, attended, query_grad, wk_near, wv_near, og_near = call(
         middle_body,
-        [sds((2 * width, width))] * 2 + [sds((slots, width))] * 2 + [sds((nodes, width))] * 2,
+        [sds((2 * width, width))] * 2 + [sds((slots, width))] * 2 + [sds((nodes, width))] * 2
+        + [sds((width, width))] * 2 + [sds((nodes, width))],
         [SM] + [VM] * 10 + [HB] * 3,
-        (core1, a0, a2, b0, c1, c2, c3, queries, att_grad, mesh_normed, dense, w_key, w_value,
+        (core1, a0, a2, w0, w1, w2, w3, queries, att_grad, mesh_normed, dense, w_key, w_value,
          out_grad),
         3 << 30, 8 << 20, "middle",
-        [pltpu.VMEM((slots, width), BF16)] * 3 + held(w_key, w_value, out_grad),
-    )
+        [pltpu.VMEM((slots, width), BF16)] * 3 + [pltpu.SemaphoreType.DMA((3,))],
+    )
+
     other = shifted(send, "gc", 1)
+    piece = sds((3, cap, width))
     mesh_out, mesh_grad, s0, s1, s2, s3 = call(
-        tail_body, [sds((nodes, width))] * 2 + [piece] * 4, [VM] * 4 + [HB] * 7,
-        (key_part, value_part, attended, query_grad, w_key, w_value, w_out, w_query, mesh_h, gain_m,
-         out_grad),
-        1 << 30, 5 << 20, "tail", held(w_key, w_value, w_out, w_query, mesh_h, gain_m, out_grad),
+        tail_body, [sds((nodes, width))] * 2 + [piece] * 4, [VM] * 7 + [HB] * 4,
+        (key_part, value_part, attended, query_grad, wk_near, wv_near, og_near, w_out, w_query, mesh_h,
+         gain_m),
+        1 << 30, 5 << 20, "tail", held(w_out, w_query, mesh_h, gain_m),
     )
     other, s1 = lax.optimization_barrier((other, s1))
-    chips = lax.axis_size(CHIPS)
-    own = (keep.astype(F32) + other.astype(F32)).astype(BF16)
-    own = own.reshape(chips, 2 * width // chips, width)
-    parts = lax.all_to_all(own, CHIPS, 0, 0, tiled=True)
-
-    t1 = shifted(s1, "z", -1)
-    t2 = shifted(s2, "z", -2)
-    t3 = shifted(s3, "z", -3)
-    parts, t1, t2, t3 = lax.optimization_barrier((parts, t1, t2, t3))
-
+    (own,) = call(
+        pair_body, [sds((2 * width, width))], [VM] * 2, (keep, other), 1 << 20, 3 << 20, "pair",
+        [pltpu.VMEM((2 * width, width), BF16), pltpu.SemaphoreType.DMA((4,))], [HB],
+    )
+    plane = lax.axis_size(PLANE)
+    share = 2 * width // plane
+    parts = lax.all_to_all(own.reshape(plane, share, width), PLANE, 0, 0, tiled=True)
+
+    t1, t2, t3 = (shifted(s, "z", -k) for k, s in ((1, s1), (2, s2), (3, s3)))
     low, high = packed(s0, t1, t2, t3)
+    parts, low, high = lax.optimization_barrier((parts, low, high))
     r0 = to_slab(low, 1)
     r2 = to_slab(high, -1)
+    part = jnp.sum(parts.astype(F32), axis=0).astype(BF16)
+    p1, p2, p3 = (shifted(part, "z", k) for k in (1, 2, 3))
+    (spread,) = call(
+        spread_body, [sds((plane, share, width))], [VM] * 4, (part, p1, p2, p3), 1 << 18, 1 << 20,
+        "spread", [pltpu.VMEM((share, width), BF16), pltpu.SemaphoreType.DMA((plane,))], [HB],
+    )
+    mine = lax.all_to_all(spread, PLANE, 0, 0, tiled=True).reshape(2 * width, width)
     (grid_grad,) = call(
         grid_body, [sds((points, width))], [SM] + [VM] * 6 + [HB] * 3,
         (sub1, r0, r2, s0, t1, t2, t3, send_rows, gain_g, grid_x),
@@ -378,11 +409,6 @@
          pltpu.SemaphoreType.DMA((points // 256,))] + held(send_rows, gain_g, grid_x),
         [HB],
     )
-
-    total = jnp.sum(parts.astype(F32), axis=0).astype(BF16)
-    mine = lax.all_to_all(
-        jnp.broadcast_to(total[None], (chips, *total.shape)), CHIPS, 0, 0, tiled=True
-    ).reshape(2 * width, width)
     mine, grid_grad = lax.optimization_barrier((mine, grid_grad))
     theirs = shifted(mine, "gc", 1)
     whole = sds((4, width, width), F32)

time: 112 us -> 104 us (0.929)
  waiting for transfers between devices: 37.1 us -> 31.2 us
  local copies, waits for them, and re-layouts: 1.42 us -> 0 us
  other arithmetic: 1.48 us -> 0.15 us
  starting transfers between devices: 45.3 us -> 46.5 us
    all_to_all x2, starting transfers between devices: 21 us -> 11.9 us  [the longest x1 7.08 us: shards(): lax.all_to_all(own.reshape(plane, share, width), PLANE, 0, 0, tiled=True)]
    ppermute x8 -> x14, starting transfers between devices: 12 us -> 19.4 us  [shifted(): return lax.ppermute(block, axis, [(i, (i + k) % n) for i in range(n)])]
    ppermute x4, waiting for transfers between devices: 14.8 us -> 9.57 us  [to_slab(): lax.ppermute(block, SLAB, [(i, i + d) for i in range(n) if 0 <= i + d < n])]
    ppermute x4, starting transfers between devices: 12.2 us -> 15.3 us  [to_slab(): lax.ppermute(block, SLAB, [(i, i + d) for i in range(n) if 0 <= i + d < n])]
    ppermute x8 -> x14, waiting for transfers between devices: 22.3 us -> 19.3 us  [shifted(): return lax.ppermute(block, axis, [(i, (i + k) % n) for i in range(n)])]
    all_to_all x2, waiting for transfers between devices: 0.01 us -> 2.33 us  [the longest x1 2.33 us: shards(): lax.all_to_all(own.reshape(plane, share, width), PLANE, 0, 0, tiled=True)]
    convert_element_type x1 -> x0, other arithmetic: 1.27 us -> none  [shards(): own = (keep.astype(F32) + other.astype(F32)).astype(BF16)]
    pallas_call x9 -> x11, Pallas kernels: 25.3 us -> 25 us  [call(): pl.pallas_call(body, out_shape=outs, in_specs=in_specs, out_specs=out_spe...]
  transfers between devices with their start and end apart: 14 -> 20, of which waited for: 8 -> 12; matrix products, arithmetic and copies ran while one was open for 0% -> 0% of each run, Pallas kernels for 12% -> 11%
where the time goes in v3:
time: 104 us
  starting transfers between devices  46.5 us (45%)
  waiting for transfers between devices  31.2 us (30%)
  Pallas kernels  25 us (24%)
    pallas_call x11, Pallas kernels, call(): pl.pallas_call(body, out_shape=outs, in_specs=in_specs, out_specs=out_spe...  25 us
    ppermute x14, starting transfers between devices, shifted(): return lax.ppermute(block, axis, [(i, (i + k) % n) for i in range(n)])  19.4 us
    ppermute x14, waiting for transfers between devices, shifted(): return lax.ppermute(block, axis, [(i, (i + k) % n) for i in range(n)])  19.3 us
    ppermute x4, starting transfers between devices, to_slab(): lax.ppermute(block, SLAB, [(i, i + d) for i in range(n) if 0 <= i + d < n])  15.3 us
    ppermute x4, waiting for transfers between devices, to_slab(): lax.ppermute(block, SLAB, [(i, i + d) for i in range(n) if 0 <= i + d < n])  9.57 us
    all_to_all x1, starting transfers between devices, shards(): lax.all_to_all(own.reshape(plane, share, width), PLANE, 0, 0, tiled=True)  7.08 us
    all_to_all x1, starting transfers between devices, shards(): lax.all_to_all(spread, PLANE, 0, 0, tiled=True).reshape(2 * width, width)  4.8 us
    all_to_all x1, waiting for transfers between devices, shards(): lax.all_to_all(own.reshape(plane, share, width), PLANE, 0, 0, tiled=True)  2.33 us
  transfers between devices with their start and end apart: 20, of which 12 were waited for; matrix products, arithmetic and copies ran while one was open for 0% of the time, Pallas kernels for 11%

profile of v3, /device:TPU:1, one launch (start us, length us, event | category | flops | bytes accessed | tf_op | source)
XLA Modules:
  0.0 103.9 jit_solution(13965696702575338695)
XLA Ops:
  0.6 3.0 %gather_rows.1 = (bf16[2,64,512]{2,1,0:T(8,128)(2,1)S(1)}, bf16[2,64,512]{2,1,0:T(8,128)(2,1)S(1)}, bf16[2,64,512]{2,1,0:T(8,128)(2,1)S(1)}, bf16[2,64,512]{2,1,...) custom-call(s32[1]{0:T(128)} %bitcast.1.sub_ref, ...), custom_call_target="tpu_custom_call" | custom-call | flops 1073741824 | bytes 4194304 | tf_op jit(solution)/shard_map/gather_rows/pallas_call | solution.py:48
  3.6 2.5 %collective-permute-start = (bf16[2,64,512]{2,1,0:T(8,128)(2,1)S(1)}, bf16[2,64,512]{2,1,0:T(8,128)(2,1)S(1)}, u32[]{:S(2)}, u32[]{:S(2)}) collective-permute-start(bf16[2,64,512]{2,1,0:T(8,128)(2,1)S(1)} %get-tuple-element.45), channel_id=1, source_target_pairs={{0,1},{1,2},{2,3},{3,0},{4,5},{5,6},{6,7},{7,4},{8,9},{9,10},{10,1... | collective-permute-start | bytes 393224 | tf_op jit(solution)/shard_map/ppermute | solution.py:311
  6.1 3.3 %collective-permute-start.1 = (bf16[2,64,512]{2,1,0:T(8,128)(2,1)S(1)}, bf16[2,64,512]{2,1,0:T(8,128)(2,1)S(1)}, u32[]{:S(2)}, u32[]{:S(2)}) collective-permute-start(bf16[2,64,512]{2,1,0:T(8,128)(2,1)S(1)} %get-tuple-element.46), channel_id=1, source_target_pairs={{0,2},{1,3},{2,0},{3,1},{4,6},{5,7},{6,4},{7,5},{8,10},{9,11},{10,... | collective-permute-start | bytes 393224 | tf_op jit(solution)/shard_map/ppermute | solution.py:311
  11.5 3.7 %collective-permute-done.1.p2 = bf16[2,64,512]{2,1,0:T(8,128)(2,1)S(1)} collective-permute-done((bf16[2,64,512]{2,1,0:T(8,128)(2,1)S(1)}, bf16[2,64,512]{2,1,0:T(8,128)(2,1)S(1)}, u32[]{:S(2)}, u32[]{:S(2)}) %collective-permute-start.1) | collective-permute-done | bytes 131104 | tf_op jit(solution)/shard_map/ppermute | solution.py:311
  15.2 3.5 %collective-permute-start.3 = (bf16[256,512]{1,0:T(8,128)(2,1)S(1)}, bf16[256,512]{1,0:T(8,128)(2,1)S(1)}, u32[]{:S(2)}, u32[]{:S(2)}) collective-permute-start(bf16[256,512]{1,0:T(8,128)(2,1)S(1)} %get-tuple-element.49), channel_id=1, source_target_pairs={{4,0},{8,4},{12,8},{16,12},{20,16},{24,20},{28,24},{32,28},{36,32}... | collective-permute-start | bytes 786440 | tf_op jit(solution)/shard_map/ppermute | solution.py:316
  18.6 3.1 %collective-permute-start.4 = (bf16[256,512]{1,0:T(8,128)(2,1)S(1)}, bf16[256,512]{1,0:T(8,128)(2,1)S(1)}, u32[]{:S(2)}, u32[]{:S(2)}) collective-permute-start(bf16[256,512]{1,0:T(8,128)(2,1)S(1)} %get-tuple-element.50), channel_id=1, source_target_pairs={{0,4},{4,8},{8,12},{12,16},{16,20},{20,24},{24,28},{28,32},{32,36}... | collective-permute-start | bytes 786440 | tf_op jit(solution)/shard_map/ppermute | solution.py:316
  22.8 2.1 %collective-permute-start.6 = (bf16[64,512]{1,0:T(8,128)(2,1)S(1)}, bf16[64,512]{1,0:T(8,128)(2,1)S(1)}, u32[]{:S(2)}, u32[]{:S(2)}) collective-permute-start(bf16[64,512]{1,0:T(8,128)(2,1)S(1)} %get-tuple-element.53), channel_id=1, source_target_pairs={{0,2},{1,3},{2,0},{3,1},{4,6},{5,7},{6,4},{7,5},{8,10},{9,11},{10,... | collective-permute-start | bytes 196616 | tf_op jit(solution)/shard_map/ppermute | solution.py:311
  25.9 2.8 %prep.1 = (bf16[64,512]{1,0:T(8,128)(2,1)S(1)}, bf16[64,512]{1,0:T(8,128)(2,1)S(1)}, bf16[64,512]{1,0:T(8,128)(2,1)S(1)}, f32[4,64,768]{2,1,0:T(8,128)S(1)}) custom-call(s32[1]{0:T(128)} %bitcast.1.sub_ref, bf16[64,512]{1,0:T(8,128)(2,1)} %mesh_hbm.3, f32[1,512]{1,0:T(1,128)} %bitcast.10, bf16[512,512]{1,0:T(8,128)(2,1)} %wq_hbm.3, bf16[512,512]{1,0:T(8,128)(2,1)} %wo_hbm.3, ...), custom_call_target="tpu_custom_call" | custom-call | flops 1073741824 | bytes 8388608 | tf_op jit(solution)/shard_map/prep/pallas_call | solution.py:48
  28.9 7.4 %middle.1 = (bf16[1024,512]{1,0:T(8,128)(2,1)S(1)}, bf16[1024,512]{1,0:T(8,128)(2,1)S(1)}, bf16[768,512]{1,0:T(8,128)(2,1)S(1)}, bf16[768,512]{1,0:T(8,128)(2,1)...) custom-call(s32[1]{0:T(128)} %bitcast.core_ref, ...), custom_call_target="tpu_custom_call" | custom-call | flops 3221225472 | bytes 8388608 | tf_op jit(solution)/shard_map/middle/pallas_call | solution.py:48
  37.0 2.5 %tail.1 = (bf16[64,512]{1,0:T(8,128)(2,1)}, bf16[64,512]{1,0:T(8,128)(2,1)}, bf16[3,64,512]{2,1,0:T(8,128)(2,1)S(1)}, bf16[3,64,512]{2,1,0:T(8,128)(2,1)S(1)}, b...) custom-call(bf16[768,512]{1,0:T(8,128)(2,1)S(1)} %get-tuple-element.60.kp_ref, ...), custom_call_target="tpu_custom_call" | custom-call | flops 1073741824 | bytes 5242880 | tf_op jit(solution)/shard_map/tail/pallas_call | solution.py:48
  40.6 7.1 %all-to-all-start = ((bf16[16,64,512]{2,1,0:T(8,128)(2,1)}), bf16[16,64,512]{2,1,0:T(8,128)(2,1)S(1)}, u32[]{:S(2)}, u32[]{:S(2)}) async-start(bf16[16,64,512]{2,1,0:T(8,128)(2,1)} %bitcast.4), calls=%async_computation | async-start | bytes 2097152 | tf_op jit(solution)/shard_map/all_to_all | solution.py:390
  47.7 1.4 %collective-permute-start.10 = (bf16[3,64,512]{2,1,0:T(8,128)(2,1)S(1)}, bf16[3,64,512]{2,1,0:T(8,128)(2,1)S(1)}, u32[]{:S(2)}, u32[]{:S(2)}) collective-permute-start(bf16[3,64,512]{2,1,0:T(8,128)(2,1)S(1)} %get-tuple-element.75), channel_id=1, source_target_pairs={{0,2},{1,3},{2,0},{3,1},{4,6},{5,7},{6,4},{7,5},{8,10},{9,11},{10,... | collective-permute-start | bytes 589832 | tf_op jit(solution)/shard_map/ppermute | solution.py:311
  50.3 1.5 %collective-permute-start.9 = (bf16[3,64,512]{2,1,0:T(8,128)(2,1)S(1)}, bf16[3,64,512]{2,1,0:T(8,128)(2,1)S(1)}, u32[]{:S(2)}, u32[]{:S(2)}) collective-permute-start(bf16[3,64,512]{2,1,0:T(8,128)(2,1)S(1)} %get-tuple-element.74), channel_id=1, source_target_pairs={{0,3},{1,0},{2,1},{3,2},{4,7},{5,4},{6,5},{7,6},{8,11},{9,8},{10,9... | collective-permute-start | bytes 589832 | tf_op jit(solution)/shard_map/ppermute | solution.py:311
  51.8 3.3 %collective-permute-done.10.p2.s2 = bf16[3,64,512]{2,1,0:T(8,128)(2,1)S(1)} collective-permute-done((bf16[3,64,512]{2,1,0:T(8,128)(2,1)S(1)}, bf16[3,64,512]{2,1,0:T(8,128)(2,1)S(1)}, u32[]{:S(2)}, u32[]{:S(2)}) %collective-permute-start.10) | collective-permute-done | bytes 196640 | tf_op jit(solution)/shard_map/ppermute | solution.py:311
  55.1 5.2 %collective-permute-done.11.p3.s3 = bf16[3,64,512]{2,1,0:T(8,128)(2,1)S(1)} collective-permute-done((bf16[3,64,512]{2,1,0:T(8,128)(2,1)S(1)}, bf16[3,64,512]{2,1,0:T(8,128)(2,1)S(1)}, u32[]{:S(2)}, u32[]{:S(2)}) %collective-permute-start.11) | collective-permute-done | bytes 196640 | tf_op jit(solution)/shard_map/ppermute | solution.py:311
  60.3 2.3 %all-to-all-done = bf16[16,64,512]{2,1,0:T(8,128)(2,1)S(1)} async-done(((bf16[16,64,512]{2,1,0:T(8,128)(2,1)}), bf16[16,64,512]{2,1,0:T(8,128)(2,1)S(1)}, u32[]{:S(2)}, u32[]{:S(2)}) %all-to-all-start) | async-done | bytes 1048608 | tf_op jit(solution)/shard_map/all_to_all | solution.py:390
  62.8 3.1 %collective-permute-start.14 = (bf16[64,512]{1,0:T(8,128)(2,1)S(1)}, bf16[64,512]{1,0:T(8,128)(2,1)S(1)}, u32[]{:S(2)}, u32[]{:S(2)}) collective-permute-start(bf16[64,512]{1,0:T(8,128)(2,1)S(1)} %reduce_sum.12.p0), channel_id=1, source_target_pairs={{0,3},{1,0},{2,1},{3,2},{4,7},{5,4},{6,5},{7,6},{8,11},{9,8},{10,9... | collective-permute-start | bytes 196616 | tf_op jit(solution)/shard_map/ppermute | solution.py:311
  67.8 2.8 %collective-permute-done.13.p2 = bf16[64,512]{1,0:T(8,128)(2,1)S(1)} collective-permute-done((bf16[64,512]{1,0:T(8,128)(2,1)S(1)}, bf16[64,512]{1,0:T(8,128)(2,1)S(1)}, u32[]{:S(2)}, u32[]{:S(2)}) %collective-permute-start.13) | collective-permute-done | bytes 65568 | tf_op jit(solution)/shard_map/ppermute | solution.py:311
  72.1 4.8 %all-to-all-start.1 = ((bf16[16,64,512]{2,1,0:T(8,128)(2,1)}), bf16[16,64,512]{2,1,0:T(8,128)(2,1)S(1)}, u32[]{:S(2)}, u32[]{:S(2)}) async-start(bf16[16,64,512]{2,1,0:T(8,128)(2,1)} %spread.1), calls=%async_computation.1 | async-start | bytes 2097152 | tf_op jit(solution)/shard_map/all_to_all | solution.py:403
  76.9 6.8 %collective-permute-start.15 = (bf16[256,512]{1,0:T(8,128)(2,1)S(1)}, bf16[256,512]{1,0:T(8,128)(2,1)S(1)}, u32[]{:S(2)}, u32[]{:S(2)}) collective-permute-start(bf16[256,512]{1,0:T(8,128)(2,1)S(1)} %get-tuple-element.80), channel_id=1, source_target_pairs={{0,4},{4,8},{8,12},{12,16},{16,20},{20,24},{24,28},{28,32},{32,36}... | collective-permute-start | bytes 786440 | tf_op jit(solution)/shard_map/ppermute | solution.py:316
  83.7 1.9 %collective-permute-start.16 = (bf16[256,512]{1,0:T(8,128)(2,1)S(1)}, bf16[256,512]{1,0:T(8,128)(2,1)S(1)}, u32[]{:S(2)}, u32[]{:S(2)}) collective-permute-start(bf16[256,512]{1,0:T(8,128)(2,1)S(1)} %get-tuple-element.81), channel_id=1, source_target_pairs={{4,0},{8,4},{12,8},{16,12},{20,16},{24,20},{28,24},{32,28},{36,32}... | collective-permute-start | bytes 786440 | tf_op jit(solution)/shard_map/ppermute | solution.py:316
  85.6 7.6 %collective-permute-done.15.r0 = bf16[256,512]{1,0:T(8,128)(2,1)S(1)} collective-permute-done((bf16[256,512]{1,0:T(8,128)(2,1)S(1)}, bf16[256,512]{1,0:T(8,128)(2,1)S(1)}, u32[]{:S(2)}, u32[]{:S(2)}) %collective-permute-start.15) | collective-permute-done | bytes 262176 | tf_op jit(solution)/shard_map/ppermute | solution.py:316
  93.2 2.0 %collective-permute-done.16.r2 = bf16[256,512]{1,0:T(8,128)(2,1)S(1)} collective-permute-done((bf16[256,512]{1,0:T(8,128)(2,1)S(1)}, bf16[256,512]{1,0:T(8,128)(2,1)S(1)}, u32[]{:S(2)}, u32[]{:S(2)}) %collective-permute-start.16) | collective-permute-done | bytes 262176 | tf_op jit(solution)/shard_map/ppermute | solution.py:316
  95.2 4.4 %grid_grad.1 = bf16[2048,512]{1,0:T(8,128)(2,1)} custom-call(s32[1]{0:T(128)} %bitcast.1.sub_ref, bf16[256,512]{1,0:T(8,128)(2,1)S(1)} %collective-permute-done.15.r0, bf16[256,512]{1,0:T(8,128)(2,1)S(1)} %collective-permute-done.16.r2, bf16[3,64,512]{2,1,0:T(8,128)(2,1)S(1)} %get-tuple-element.73.p0.s0, ...), custom_call_target="tpu_custom_call" | custom-call | flops 1073741824 | bytes 5242880 | tf_op jit(solution)/shard_map/grid_grad/pallas_call | solution.py:48
  (28 shorter events, 14.9 us)
Async XLA Ops:
  3.6 7.9 %collective-permute-start = (bf16[2,64,512]{2,1,0:T(8,128)(2,1)S(1)}, bf16[2,64,512]{2,1,0:T(8,128)(2,1)S(1)}, u32[]{:S(2)}, u32[]{:S(2)}) collective-permute-start(bf16[2,64,512]{2,1,0:T(8,128)(2,1)S(1)} %get-tuple-element.45), channel_id=1, source_target_pairs={{0,1},{1,2},{2,3},{3,0},{4,5},{5,6},{6,7},{7,4},{8,9},{9,10},{10,1... | collective-permute-start | bytes 393224 | tf_op jit(solution)/shard_map/ppermute | solution.py:311
  6.1 9.0 %collective-permute-start.1 = (bf16[2,64,512]{2,1,0:T(8,128)(2,1)S(1)}, bf16[2,64,512]{2,1,0:T(8,128)(2,1)S(1)}, u32[]{:S(2)}, u32[]{:S(2)}) collective-permute-start(bf16[2,64,512]{2,1,0:T(8,128)(2,1)S(1)} %get-tuple-element.46), channel_id=1, source_target_pairs={{0,2},{1,3},{2,0},{3,1},{4,6},{5,7},{6,4},{7,5},{8,10},{9,11},{10,... | collective-permute-start | bytes 393224 | tf_op jit(solution)/shard_map/ppermute | solution.py:311
  9.4 5.7 %collective-permute-start.2 = (bf16[2,64,512]{2,1,0:T(8,128)(2,1)S(1)}, bf16[2,64,512]{2,1,0:T(8,128)(2,1)S(1)}, u32[]{:S(2)}, u32[]{:S(2)}) collective-permute-start(bf16[2,64,512]{2,1,0:T(8,128)(2,1)S(1)} %get-tuple-element.47), channel_id=1, source_target_pairs={{0,3},{1,0},{2,1},{3,2},{4,7},{5,4},{6,5},{7,6},{8,11},{9,8},{10,9... | collective-permute-start | bytes 393224 | tf_op jit(solution)/shard_map/ppermute | solution.py:311
  15.2 13.7 %collective-permute-start.3 = (bf16[256,512]{1,0:T(8,128)(2,1)S(1)}, bf16[256,512]{1,0:T(8,128)(2,1)S(1)}, u32[]{:S(2)}, u32[]{:S(2)}) collective-permute-start(bf16[256,512]{1,0:T(8,128)(2,1)S(1)} %get-tuple-element.49), channel_id=1, source_target_pairs={{4,0},{8,4},{12,8},{16,12},{20,16},{24,20},{28,24},{32,28},{36,32}... | collective-permute-start | bytes 786440 | tf_op jit(solution)/shard_map/ppermute | solution.py:316
  18.6 10.2 %collective-permute-start.4 = (bf16[256,512]{1,0:T(8,128)(2,1)S(1)}, bf16[256,512]{1,0:T(8,128)(2,1)S(1)}, u32[]{:S(2)}, u32[]{:S(2)}) collective-permute-start(bf16[256,512]{1,0:T(8,128)(2,1)S(1)} %get-tuple-element.50), channel_id=1, source_target_pairs={{0,4},{4,8},{8,12},{12,16},{16,20},{20,24},{24,28},{28,32},{32,36}... | collective-permute-start | bytes 786440 | tf_op jit(solution)/shard_map/ppermute | solution.py:316
  21.8 6.9 %collective-permute-start.5 = (bf16[64,512]{1,0:T(8,128)(2,1)S(1)}, bf16[64,512]{1,0:T(8,128)(2,1)S(1)}, u32[]{:S(2)}, u32[]{:S(2)}) collective-permute-start(bf16[64,512]{1,0:T(8,128)(2,1)S(1)} %get-tuple-element.52), channel_id=1, source_target_pairs={{0,1},{1,2},{2,3},{3,0},{4,5},{5,6},{6,7},{7,4},{8,9},{9,10},{10,1... | collective-permute-start | bytes 196616 | tf_op jit(solution)/shard_map/ppermute | solution.py:311
  22.8 5.9 %collective-permute-start.6 = (bf16[64,512]{1,0:T(8,128)(2,1)S(1)}, bf16[64,512]{1,0:T(8,128)(2,1)S(1)}, u32[]{:S(2)}, u32[]{:S(2)}) collective-permute-start(bf16[64,512]{1,0:T(8,128)(2,1)S(1)} %get-tuple-element.53), channel_id=1, source_target_pairs={{0,2},{1,3},{2,0},{3,1},{4,6},{5,7},{6,4},{7,5},{8,10},{9,11},{10,... | collective-permute-start | bytes 196616 | tf_op jit(solution)/shard_map/ppermute | solution.py:311
  24.9 4.0 %collective-permute-start.7 = (bf16[64,512]{1,0:T(8,128)(2,1)S(1)}, bf16[64,512]{1,0:T(8,128)(2,1)S(1)}, u32[]{:S(2)}, u32[]{:S(2)}) collective-permute-start(bf16[64,512]{1,0:T(8,128)(2,1)S(1)} %get-tuple-element.54), channel_id=1, source_target_pairs={{0,3},{1,0},{2,1},{3,2},{4,7},{5,4},{6,5},{7,6},{8,11},{9,8},{10,9... | collective-permute-start | bytes 196616 | tf_op jit(solution)/shard_map/ppermute | solution.py:311
  36.2 3.3 %collective-permute-start.8 = (bf16[1024,512]{1,0:T(8,128)(2,1)S(1)}, bf16[1024,512]{1,0:T(8,128)(2,1)S(1)}, u32[]{:S(2)}, u32[]{:S(2)}) collective-permute-start(bf16[1024,512]{1,0:T(8,128)(2,1)S(1)} %get-tuple-element.70), channel_id=1, source_target_pairs={{0,4},{4,0},{1,5},{5,1},{2,6},{6,2},{3,7},{7,3},{8,12},{12,8},{9,1... | collective-permute-start | bytes 3145736 | tf_op jit(solution)/shard_map/ppermute | solution.py:311
  40.6 22.1 %all-to-all-start = ((bf16[16,64,512]{2,1,0:T(8,128)(2,1)}), bf16[16,64,512]{2,1,0:T(8,128)(2,1)S(1)}, u32[]{:S(2)}, u32[]{:S(2)}) async-start(bf16[16,64,512]{2,1,0:T(8,128)(2,1)} %bitcast.4), calls=%async_computation | async-start | bytes 2097152 | tf_op jit(solution)/shard_map/all_to_all | solution.py:390
  47.7 7.4 %collective-permute-start.10 = (bf16[3,64,512]{2,1,0:T(8,128)(2,1)S(1)}, bf16[3,64,512]{2,1,0:T(8,128)(2,1)S(1)}, u32[]{:S(2)}, u32[]{:S(2)}) collective-permute-start(bf16[3,64,512]{2,1,0:T(8,128)(2,1)S(1)} %get-tuple-element.75), channel_id=1, source_target_pairs={{0,2},{1,3},{2,0},{3,1},{4,6},{5,7},{6,4},{7,5},{8,10},{9,11},{10,... | collective-permute-start | bytes 589832 | tf_op jit(solution)/shard_map/ppermute | solution.py:311
  49.1 11.2 %collective-permute-start.11 = (bf16[3,64,512]{2,1,0:T(8,128)(2,1)S(1)}, bf16[3,64,512]{2,1,0:T(8,128)(2,1)S(1)}, u32[]{:S(2)}, u32[]{:S(2)}) collective-permute-start(bf16[3,64,512]{2,1,0:T(8,128)(2,1)S(1)} %get-tuple-element.76), channel_id=1, source_target_pairs={{0,1},{1,2},{2,3},{3,0},{4,5},{5,6},{6,7},{7,4},{8,9},{9,10},{10,1... | collective-permute-start | bytes 589832 | tf_op jit(solution)/shard_map/ppermute | solution.py:311
  50.3 10.0 %collective-permute-start.9 = (bf16[3,64,512]{2,1,0:T(8,128)(2,1)S(1)}, bf16[3,64,512]{2,1,0:T(8,128)(2,1)S(1)}, u32[]{:S(2)}, u32[]{:S(2)}) collective-permute-start(bf16[3,64,512]{2,1,0:T(8,128)(2,1)S(1)} %get-tuple-element.74), channel_id=1, source_target_pairs={{0,3},{1,0},{2,1},{3,2},{4,7},{5,4},{6,5},{7,6},{8,11},{9,8},{10,9... | collective-permute-start | bytes 589832 | tf_op jit(solution)/shard_map/ppermute | solution.py:311
  62.8 5.0 %collective-permute-start.14 = (bf16[64,512]{1,0:T(8,128)(2,1)S(1)}, bf16[64,512]{1,0:T(8,128)(2,1)S(1)}, u32[]{:S(2)}, u32[]{:S(2)}) collective-permute-start(bf16[64,512]{1,0:T(8,128)(2,1)S(1)} %reduce_sum.12.p0), channel_id=1, source_target_pairs={{0,3},{1,0},{2,1},{3,2},{4,7},{5,4},{6,5},{7,6},{8,11},{9,8},{10,9... | collective-permute-start | bytes 196616 | tf_op jit(solution)/shard_map/ppermute | solution.py:311
  65.9 4.7 %collective-permute-start.13 = (bf16[64,512]{1,0:T(8,128)(2,1)S(1)}, bf16[64,512]{1,0:T(8,128)(2,1)S(1)}, u32[]{:S(2)}, u32[]{:S(2)}) collective-permute-start(bf16[64,512]{1,0:T(8,128)(2,1)S(1)} %reduce_sum.12.p0), channel_id=1, source_target_pairs={{0,2},{1,3},{2,0},{3,1},{4,6},{5,7},{6,4},{7,5},{8,10},{9,11},{10,... | collective-permute-start | bytes 196616 | tf_op jit(solution)/shard_map/ppermute | solution.py:311
  65.9 5.0 %collective-permute-start.12 = (bf16[64,512]{1,0:T(8,128)(2,1)S(1)}, bf16[64,512]{1,0:T(8,128)(2,1)S(1)}, u32[]{:S(2)}, u32[]{:S(2)}) collective-permute-start(bf16[64,512]{1,0:T(8,128)(2,1)S(1)} %reduce_sum.12.p0), channel_id=1, source_target_pairs={{0,1},{1,2},{2,3},{3,0},{4,5},{5,6},{6,7},{7,4},{8,9},{9,10},{10,1... | collective-permute-start | bytes 196616 | tf_op jit(solution)/shard_map/ppermute | solution.py:311
  72.1 27.5 %all-to-all-start.1 = ((bf16[16,64,512]{2,1,0:T(8,128)(2,1)}), bf16[16,64,512]{2,1,0:T(8,128)(2,1)S(1)}, u32[]{:S(2)}, u32[]{:S(2)}) async-start(bf16[16,64,512]{2,1,0:T(8,128)(2,1)} %spread.1), calls=%async_computation.1 | async-start | bytes 2097152 | tf_op jit(solution)/shard_map/all_to_all | solution.py:403
  76.9 16.4 %collective-permute-start.15 = (bf16[256,512]{1,0:T(8,128)(2,1)S(1)}, bf16[256,512]{1,0:T(8,128)(2,1)S(1)}, u32[]{:S(2)}, u32[]{:S(2)}) collective-permute-start(bf16[256,512]{1,0:T(8,128)(2,1)S(1)} %get-tuple-element.80), channel_id=1, source_target_pairs={{0,4},{4,8},{8,12},{12,16},{16,20},{20,24},{24,28},{28,32},{32,36}... | collective-permute-start | bytes 786440 | tf_op jit(solution)/shard_map/ppermute | solution.py:316
  83.7 11.5 %collective-permute-start.16 = (bf16[256,512]{1,0:T(8,128)(2,1)S(1)}, bf16[256,512]{1,0:T(8,128)(2,1)S(1)}, u32[]{:S(2)}, u32[]{:S(2)}) collective-permute-start(bf16[256,512]{1,0:T(8,128)(2,1)S(1)} %get-tuple-element.81), channel_id=1, source_target_pairs={{4,0},{8,4},{12,8},{16,12},{20,16},{24,20},{28,24},{32,28},{36,32}... | collective-permute-start | bytes 786440 | tf_op jit(solution)/shard_map/ppermute | solution.py:316
  99.6 2.7 %collective-permute-start.17 = (bf16[1024,512]{1,0:T(8,128)(2,1)S(1)}, bf16[1024,512]{1,0:T(8,128)(2,1)S(1)}, u32[]{:S(2)}, u32[]{:S(2)}) collective-permute-start(bf16[1024,512]{1,0:T(8,128)(2,1)S(1)} %bitcast.6), channel_id=1, source_target_pairs={{0,4},{4,0},{1,5},{5,1},{2,6},{6,2},{3,7},{7,3},{8,12},{12,8},{9,1... | collective-permute-start | bytes 3145736 | tf_op jit(solution)/shard_map/ppermute | solution.py:311

commit v4 on v3

--- a/solution.py
+++ b/solution.py
@@ -70,7 +70,7 @@
     return [pltpu.VMEM(a.shape, a.dtype) for a in args] + [pltpu.SemaphoreType.DMA((len(args),))]
 
 
-def gather_body(sub_ref, rows_hbm, gain_hbm, x_hbm, n0, n1, n2, n3, w0, w1, w2, w3,
+def gather_body(sub_ref, rows_hbm, gain_hbm, x_hbm, p0, p1, p2, p3,
                 rows_ref, gain_ref, x_ref, sems):
     half = x_ref.shape[0] // 2
     cap = rows_ref.shape[3]
@@ -101,11 +101,7 @@
         wide = nn(onehot, x_ref[first : first + count, :])
         normed = (wide * inv_rms(wide) * gain).astype(BF16)
         for k in range(4):
-            piece = normed[k * cap : (k + 1) * cap]
-            if step < 2:
-                (n0, n1, n2, n3)[k][step] = piece
-            else:
-                (w0, w1, w2, w3)[k][...] = piece
+            (p0, p1, p2, p3)[k][o] = normed[k * cap : (k + 1) * cap]
 
 
 def prep_body(sub_ref, mesh_hbm, gain_hbm, wq_hbm, wo_hbm, og_hbm, nbr_hbm, valid_hbm, bias_hbm,
@@ -149,22 +145,28 @@
     ag_ref[...] = nt(og_ref[...], wo_ref[...]).astype(BF16)
 
 
-def middle_body(core_ref, a0, a2, b0, b1, b2, b3, q_ref, ag_ref, mn_ref, bias_ref,
-                wk_hbm, wv_hbm, og_hbm, keep_ref, send_ref, kp_ref, vp_ref, att_ref, qg_ref,
-                wk_ref, wv_ref, og_ref, rows, keys, vals, sems):
-    copies = fetch((wk_hbm, wv_hbm, og_hbm), (wk_ref, wv_ref, og_ref), sems)
+def middle_body(core_ref, near, far, b0, b1, b2, b3, q_ref, ag_ref, mn_ref, bias_ref,
+                wk_hbm, wv_hbm, og_hbm, keep_ref, send_ref, part_ref, att_ref, qg_ref,
+                wkv_ref, og_ref, rows, keys, vals, sems):
+    width = q_ref.shape[1]
+    copies = fetch(
+        (wk_hbm, wv_hbm, og_hbm),
+        (wkv_ref.at[:, pl.ds(0, width)], wkv_ref.at[:, pl.ds(width, width)], og_ref),
+        sems,
+    )
     heads = bias_ref.shape[0]
-    block = a0.shape[0]
-    cap = b0.shape[0]
-    rows[0:block] = a0[...]
+    block = near.shape[0]
+    cap = b0.shape[1]
+    core = core_ref[0]
+    rows[pl.ds(pl.multiple_of(core * (2 * block), block), block), :] = near[...]
+    rows[pl.ds(pl.multiple_of((1 - core) * (2 * block), block), block), :] = far[...]
     for k, piece in enumerate((b0, b1, b2, b3)):
-        rows[block + k * cap : block + (k + 1) * cap] = piece[...]
-    rows[2 * block : 3 * block] = a2[...]
+        rows[block + k * cap : block + (k + 1) * cap] = piece[1]
     copies[0].wait()
-    keys[...] = nn(rows[...], wk_ref[...]).astype(BF16)
+    keys[...] = nn(rows[...], wkv_ref[:, :width]).astype(BF16)
     copies[1].wait()
     copies[2].wait()
-    vals[...] = nn(rows[...], wv_ref[...]).astype(BF16)
+    vals[...] = nn(rows[...], wkv_ref[:, width:]).astype(BF16)
     for h in range(heads):
         at = slice(h * 128, (h + 1) * 128)
         q, ag = q_ref[:, at], ag_ref[:, at]
@@ -178,10 +180,8 @@
         pg = nt(ag, vh)
         sg = (probs * (pg - jnp.sum(probs * pg, axis=1, keepdims=True))).astype(BF16)
         qg_ref[:, at] = (nn(sg, kh) * (128 ** -0.5)).astype(BF16)
-        kp_ref[:, at] = tn(sg, q).astype(BF16)
-        vp_ref[:, at] = tn(probs_b, ag).astype(BF16)
-    core = core_ref[0]
-    width = wk_ref.shape[0]
+        part_ref[:, at] = tn(sg, q).astype(BF16)
+        part_ref[:, width + h * 128 : width + (h + 1) * 128] = tn(probs_b, ag).astype(BF16)
 
     def place(half, row, value):
         @pl.when(core == half)
@@ -192,20 +192,21 @@
         def _():
             send_ref[row : row + width, :] = value
 
+    both = tn(rows[...], part_ref[...]).astype(BF16)
     place(0, 0, tn(mn_ref[...], qg_ref[...]).astype(BF16))
-    place(0, width, tn(rows[...], kp_ref[...]).astype(BF16))
-    place(1, 0, tn(rows[...], vp_ref[...]).astype(BF16))
+    place(0, width, both[:, :width])
+    place(1, 0, both[:, width:])
     place(1, width, tn(att_ref[...], og_ref[...]).astype(BF16))
 
 
-def tail_body(kp_ref, vp_ref, att_ref, qg_ref, wk_ref, wv_ref, og_ref, wo_hbm, wq_hbm, mesh_hbm,
+def tail_body(part_ref, att_ref, qg_ref, wkv_ref, og_ref, wo_hbm, wq_hbm, mesh_hbm,
               gain_hbm, out_ref, grad_ref, s0, s1, s2, s3,
               wo_ref, wq_ref, mesh_ref, gain_ref, sems):
     copies = fetch(
         (wo_hbm, wq_hbm, mesh_hbm, gain_hbm), (wo_ref, wq_ref, mesh_ref, gain_ref), sems
     )
     cap = s0.shape[1]
-    back = (nt(kp_ref[...], wk_ref[...]) + nt(vp_ref[...], wv_ref[...])).astype(BF16)
+    back = nt(part_ref[...], wkv_ref[...]).astype(BF16)
     for o in range(3):
         for k, piece in enumerate((s0, s1, s2, s3)):
             first = (o * 4 + k) * cap
@@ -219,14 +220,15 @@
     grad_ref[...] = (og_ref[...].astype(F32) + back).astype(BF16)
 
 
-def pack_body(p0, p1, p2, p3, low_ref, high_ref):
+def pack_body(near_if_first, core_ref, p0, p1, p2, p3, near_ref, far_ref):
     cap = p0.shape[1]
+    near = lax.select(core_ref[0] == 0, near_if_first, 2 - near_if_first)
     for k, piece in enumerate((p0, p1, p2, p3)):
-        low_ref[k * cap : (k + 1) * cap, :] = piece[0]
-        high_ref[k * cap : (k + 1) * cap, :] = piece[piece.shape[0] - 1]
-
-
-def grid_body(sub_ref, r0, r2, s0, s1, s2, s3, rows_hbm, gain_hbm, x_hbm, out_hbm,
+        near_ref[k * cap : (k + 1) * cap, :] = piece[near]
+        far_ref[k * cap : (k + 1) * cap, :] = piece[2 - near]
+
+
+def grid_body(sub_ref, core_ref, near, far, s0, s1, s2, s3, rows_hbm, gain_hbm, x_hbm, out_hbm,
               got, done_ref, done_sems, rows_ref, gain_ref, x_ref, sems):
     copies = fetch((rows_hbm, gain_hbm, x_hbm), (rows_ref, gain_ref, x_ref), sems)
     points = x_ref.shape[0]
@@ -234,10 +236,11 @@
     cap = rows_ref.shape[3]
     block = 4 * cap
     me = sub_ref[0]
-    got[0:block] = r0[...]
+    core = core_ref[0]
+    got[pl.ds(pl.multiple_of((1 - core) * (2 * block), block), block), :] = near[...]
+    got[pl.ds(pl.multiple_of(core * (2 * block), block), block), :] = far[...]
     for k, piece in enumerate((s0, s1, s2, s3)):
         got[block + k * cap : block + (k + 1) * cap] = piece[1]
-    got[2 * block : 3 * block] = r2[...]
     for copy in copies:
         copy.wait()
     gain = gain_ref[...]
@@ -311,9 +314,10 @@
     return lax.ppermute(block, axis, [(i, (i + k) % n) for i in range(n)])
 
 
-def to_slab(block, d):
+def swapped_far(block):
     n = lax.axis_size(SLAB)
-    return lax.ppermute(block, SLAB, [(i, i + d) for i in range(n) if 0 <= i + d < n])
+    pairs = [(i, i + 1) for i in range(1, n - 1, 2)]
+    return lax.ppermute(block, SLAB, pairs + [(j, i) for i, j in pairs])
 
 
 def sds(shape, dtype=BF16):
@@ -338,21 +342,14 @@
                   edge_bias, neighbours, valid)
     )
 
-    n0, n1, n2, n3, w0, w1, w2, w3 = call(
-        gather_body, [sds((2, cap, width))] * 4 + [sds((cap, width))] * 4, [SM, HB, HB, HB],
+    piece = sds((3, cap, width))
+    b0, b1, b2, b3 = call(
+        gather_body, [piece] * 4, [SM, HB, HB, HB],
         (sub1, send_rows, gain_g, grid_x), 1 << 30, 4 << 20, "gather_rows",
         held(send_rows, gain_g, grid_x)[:-1] + [pltpu.SemaphoreType.DMA((4,))],
     )
-    n1, n2, n3 = (shifted(n, "z", k) for k, n in ((1, n1), (2, n2), (3, n3)))
-    w1, w2, w3 = (shifted(w, "z", k) for k, w in ((1, w1), (2, w2), (3, w3)))
-
-    def packed(*pieces):
-        return call(pack_body, [sds((block, width))] * 2, [VM] * 4, pieces, 0, 1 << 20, "pack")
-
-    low, high = packed(n0, n1, n2, n3)
-    sub2, low = lax.optimization_barrier((sub1, low))
-    a0 = to_slab(low, -1)
-    a2 = to_slab(high, 1)
+    b1, b2, b3 = (shifted(b, "z", k) for k, b in ((1, b1), (2, b2), (3, b3)))
+    sub2, b0 = lax.optimization_barrier((sub1, b0))
     prep_args = (mesh_h, gain_m, w_query, w_out, out_grad, neighbours, valid, edge_bias)
     mesh_normed, queries, att_grad, dense = call(
         prep_body,
@@ -361,23 +358,30 @@
         [pltpu.VMEM((nodes * 8, 128), F32), pltpu.VMEM((heads, nodes, 128), F32)]
         + held(neighbours, valid, edge_bias, mesh_h, gain_m, w_query, w_out, out_grad),
     )
-    keep, send, key_part, value_part, attended, query_grad, wk_near, wv_near, og_near = call(
+    b1, b2, b3, dense = lax.optimization_barrier((b1, b2, b3, dense))
+
+    def packed(near_if_first, *pieces):
+        body = functools.partial(pack_body, near_if_first)
+        return call(body, [sds((block, width))] * 2, [SM] + [VM] * 4, (core1, *pieces), 0, 1 << 20, "pack")
+
+    near, far = packed(2, b0, b1, b2, b3)
+    far = swapped_far(far)
+    near = shifted(near, "gc", 1)
+    keep, send, part_grads, attended, query_grad, weights_near, og_near = call(
         middle_body,
-        [sds((2 * width, width))] * 2 + [sds((slots, width))] * 2 + [sds((nodes, width))] * 2
-        + [sds((width, width))] * 2 + [sds((nodes, width))],
+        [sds((2 * width, width))] * 2 + [sds((slots, 2 * width))] + [sds((nodes, width))] * 2
+        + [sds((width, 2 * width)), sds((nodes, width))],
         [SM] + [VM] * 10 + [HB] * 3,
-        (core1, a0, a2, w0, w1, w2, w3, queries, att_grad, mesh_normed, dense, w_key, w_value,
+        (core1, near, far, b0, b1, b2, b3, queries, att_grad, mesh_normed, dense, w_key, w_value,
          out_grad),
         3 << 30, 8 << 20, "middle",
         [pltpu.VMEM((slots, width), BF16)] * 3 + [pltpu.SemaphoreType.DMA((3,))],
     )
 
     other = shifted(send, "gc", 1)
-    piece = sds((3, cap, width))
     mesh_out, mesh_grad, s0, s1, s2, s3 = call(
-        tail_body, [sds((nodes, width))] * 2 + [piece] * 4, [VM] * 7 + [HB] * 4,
-        (key_part, value_part, attended, query_grad, wk_near, wv_near, og_near, w_out, w_query, mesh_h,
-         gain_m),
+        tail_body, [sds((nodes, width))] * 2 + [piece] * 4, [VM] * 5 + [HB] * 4,
+        (part_grads, attended, query_grad, weights_near, og_near, w_out, w_query, mesh_h, gain_m),
         1 << 30, 5 << 20, "tail", held(w_out, w_query, mesh_h, gain_m),
     )
     other, s1 = lax.optimization_barrier((other, s1))
@@ -390,20 +394,21 @@
     parts = lax.all_to_all(own.reshape(plane, share, width), PLANE, 0, 0, tiled=True)
 
     t1, t2, t3 = (shifted(s, "z", -k) for k, s in ((1, s1), (2, s2), (3, s3)))
-    low, high = packed(s0, t1, t2, t3)
-    parts, low, high = lax.optimization_barrier((parts, low, high))
-    r0 = to_slab(low, 1)
-    r2 = to_slab(high, -1)
+    near, far = packed(0, s0, t1, t2, t3)
+    parts, near, far = lax.optimization_barrier((parts, near, far))
+    far = swapped_far(far)
+    near = shifted(near, "gc", 1)
     part = jnp.sum(parts.astype(F32), axis=0).astype(BF16)
     p1, p2, p3 = (shifted(part, "z", k) for k in (1, 2, 3))
+    p1, near, far = lax.optimization_barrier((p1, near, far))
     (spread,) = call(
         spread_body, [sds((plane, share, width))], [VM] * 4, (part, p1, p2, p3), 1 << 18, 1 << 20,
         "spread", [pltpu.VMEM((share, width), BF16), pltpu.SemaphoreType.DMA((plane,))], [HB],
     )
     mine = lax.all_to_all(spread, PLANE, 0, 0, tiled=True).reshape(2 * width, width)
     (grid_grad,) = call(
-        grid_body, [sds((points, width))], [SM] + [VM] * 6 + [HB] * 3,
-        (sub1, r0, r2, s0, t1, t2, t3, send_rows, gain_g, grid_x),
+        grid_body, [sds((points, width))], [SM] * 2 + [VM] * 6 + [HB] * 3,
+        (sub1, core1, near, far, s0, t1, t2, t3, send_rows, gain_g, grid_x),
         1 << 30, 5 << 20, "grid_grad",
         [pltpu.VMEM((slots, width), BF16), pltpu.VMEM((points, width), BF16),
          pltpu.SemaphoreType.DMA((points // 256,))] + held(send_rows, gain_g, grid_x),

time: 104 us -> 105 us (level)
  waiting for transfers between devices: 31.2 us -> 35.7 us
  starting transfers between devices: 46.5 us -> 43 us
    all_to_all x1, waiting for transfers between devices: 0.01 us -> 10.6 us  [shards(): lax.all_to_all(spread, PLANE, 0, 0, tiled=True).reshape(2 * width, width)]
    ppermute x4 -> x2, starting transfers between devices: 15.3 us -> 5.18 us  [swapped_far(): return lax.ppermute(block, SLAB, pairs + [(j, i) for i, j in pairs])]
    ppermute x14 -> x13, starting transfers between devices: 19.4 us -> 24 us  [shifted(): return lax.ppermute(block, axis, [(i, (i + k) % n) for i in range(n)])]
    ppermute x4 -> x2, waiting for transfers between devices: 9.57 us -> 5.42 us  [swapped_far(): return lax.ppermute(block, SLAB, pairs + [(j, i) for i, j in pairs])]
    ppermute x14 -> x13, waiting for transfers between devices: 19.3 us -> 17.1 us  [shifted(): return lax.ppermute(block, axis, [(i, (i + k) % n) for i in range(n)])]
    all_to_all x1, starting transfers between devices: 7.08 us -> 8.69 us  [shards(): lax.all_to_all(own.reshape(plane, share, width), PLANE, 0, 0, tiled=True)]
  transfers between devices with their start and end apart: 20 -> 17, of which waited for: 12 -> 10; matrix products, arithmetic and copies ran while one was open for 0% -> 0% of each run, Pallas kernels for 11% -> 11%
where the time goes in v4:
time: 105 us
  starting transfers between devices  43 us (41%)
  waiting for transfers between devices  35.7 us (34%)
  Pallas kernels  25.2 us (24%)
    pallas_call x11, Pallas kernels, call(): pl.pallas_call(body, out_shape=outs, in_specs=in_specs, out_specs=out_spe...  25.2 us
    ppermute x13, starting transfers between devices, shifted(): return lax.ppermute(block, axis, [(i, (i + k) % n) for i in range(n)])  24 us
    ppermute x13, waiting for transfers between devices, shifted(): return lax.ppermute(block, axis, [(i, (i + k) % n) for i in range(n)])  17.1 us
    all_to_all x1, waiting for transfers between devices, shards(): lax.all_to_all(spread, PLANE, 0, 0, tiled=True).reshape(2 * width, width)  10.6 us
    all_to_all x1, starting transfers between devices, shards(): lax.all_to_all(own.reshape(plane, share, width), PLANE, 0, 0, tiled=True)  8.69 us
    ppermute x2, waiting for transfers between devices, swapped_far(): return lax.ppermute(block, SLAB, pairs + [(j, i) for i, j in pairs])  5.42 us
    ppermute x2, starting transfers between devices, swapped_far(): return lax.ppermute(block, SLAB, pairs + [(j, i) for i, j in pairs])  5.18 us
    all_to_all x1, starting transfers between devices, shards(): lax.all_to_all(spread, PLANE, 0, 0, tiled=True).reshape(2 * width, width)  5.14 us
  transfers between devices with their start and end apart: 17, of which 10 were waited for; matrix products, arithmetic and copies ran while one was open for 0% of the time, Pallas kernels for 11%

profile of v4, /device:TPU:1, one launch (start us, length us, event | category | flops | bytes accessed | tf_op | source)
XLA Modules:
  0.0 104.9 jit_solution(15783191233746390697)
XLA Ops:
  0.6 3.0 %gather_rows.1 = (bf16[3,64,512]{2,1,0:T(8,128)(2,1)S(1)}, bf16[3,64,512]{2,1,0:T(8,128)(2,1)S(1)}, bf16[3,64,512]{2,1,0:T(8,128)(2,1)S(1)}, bf16[3,64,512]{2,1,0:T(8,128)(2,1)S(1)}) custom-call(s32[1]{0:T(128)} %bitcast.1.sub_ref, s32[1,3,4,64]{3,2,1,0:T(4,128)} %rows_hbm.3, f32[1,512]{1,0:T(1,128)} %bitcast.8, bf16[2048,512]{1,0:T(8,128)(2,1)} %x_hbm.3), custom_call_target="tpu_custom_call" | custom-call | flops 1073741824 | bytes 4194304 | tf_op jit(solution)/shard_map/gather_rows/pallas_call | solution.py:48
  3.6 2.5 %collective-permute-start = (bf16[3,64,512]{2,1,0:T(8,128)(2,1)S(1)}, bf16[3,64,512]{2,1,0:T(8,128)(2,1)S(1)}, u32[]{:S(2)}, u32[]{:S(2)}) collective-permute-start(bf16[3,64,512]{2,1,0:T(8,128)(2,1)S(1)} %get-tuple-element.47), channel_id=1, source_target_pairs={{0,1},{1,2},{2,3},{3,0},{4,5},{5,6},{6,7},{7,4},{8,9},{9,10},{10,1... | collective-permute-start | bytes 589832 | tf_op jit(solution)/shard_map/ppermute | solution.py:314
  6.1 3.3 %collective-permute-start.1 = (bf16[3,64,512]{2,1,0:T(8,128)(2,1)S(1)}, bf16[3,64,512]{2,1,0:T(8,128)(2,1)S(1)}, u32[]{:S(2)}, u32[]{:S(2)}) collective-permute-start(bf16[3,64,512]{2,1,0:T(8,128)(2,1)S(1)} %get-tuple-element.48), channel_id=1, source_target_pairs={{0,2},{1,3},{2,0},{3,1},{4,6},{5,7},{6,4},{7,5},{8,10},{9,11},{10,... | collective-permute-start | bytes 589832 | tf_op jit(solution)/shard_map/ppermute | solution.py:314
  10.2 2.8 %prep.1 = (bf16[64,512]{1,0:T(8,128)(2,1)S(1)}, bf16[64,512]{1,0:T(8,128)(2,1)S(1)}, bf16[64,512]{1,0:T(8,128)(2,1)S(1)}, f32[4,64,768]{2,1,0:T(8,128)S(1)}) custom-call(s32[1]{0:T(128)} %bitcast.1.sub_ref, bf16[64,512]{1,0:T(8,128)(2,1)} %mesh_hbm.3, f32[1,512]{1,0:T(1,128)} %bitcast.10, bf16[512,512]{1,0:T(8,128)(2,1)} %wq_hbm.3, bf16[512,512]{1,0:T(8,128)(2,1)} %wo_hbm.3, ...), custom_call_target="tpu_custom_call" | custom-call | flops 1073741824 | bytes 8388608 | tf_op jit(solution)/shard_map/prep/pallas_call | solution.py:48
  13.0 5.0 %collective-permute-done.1.p2.b2 = bf16[3,64,512]{2,1,0:T(8,128)(2,1)S(1)} collective-permute-done((bf16[3,64,512]{2,1,0:T(8,128)(2,1)S(1)}, bf16[3,64,512]{2,1,0:T(8,128)(2,1)S(1)}, u32[]{:S(2)}, u32[]{:S(2)}) %collective-permute-start.1) | collective-permute-done | bytes 196640 | tf_op jit(solution)/shard_map/ppermute | solution.py:314
  18.0 1.6 %collective-permute-start.3 = (bf16[256,512]{1,0:T(8,128)(2,1)S(1)}, bf16[256,512]{1,0:T(8,128)(2,1)S(1)}, u32[]{:S(2)}, u32[]{:S(2)}) collective-permute-start(bf16[256,512]{1,0:T(8,128)(2,1)S(1)} %get-tuple-element.55), channel_id=1, source_target_pairs={{0,4},{4,0},{1,5},{5,1},{2,6},{6,2},{3,7},{7,3},{8,12},{12,8},{9,1... | collective-permute-start | bytes 786440 | tf_op jit(solution)/shard_map/ppermute | solution.py:314
  19.6 3.1 %collective-permute-start.4 = (bf16[256,512]{1,0:T(8,128)(2,1)S(1)}, bf16[256,512]{1,0:T(8,128)(2,1)S(1)}, u32[]{:S(2)}, u32[]{:S(2)}) collective-permute-start(bf16[256,512]{1,0:T(8,128)(2,1)S(1)} %get-tuple-element.56), channel_id=1, source_target_pairs={{4,8},{12,16},{20,24},{28,32},{36,40},{44,48},{52,56},{60,64},{68,... | collective-permute-start | bytes 786440 | tf_op jit(solution)/shard_map/ppermute | solution.py:320
  22.7 4.6 %collective-permute-done.4.far = bf16[256,512]{1,0:T(8,128)(2,1)S(1)} collective-permute-done((bf16[256,512]{1,0:T(8,128)(2,1)S(1)}, bf16[256,512]{1,0:T(8,128)(2,1)S(1)}, u32[]{:S(2)}, u32[]{:S(2)}) %collective-permute-start.4) | collective-permute-done | bytes 262176 | tf_op jit(solution)/shard_map/ppermute | solution.py:320
  27.3 7.1 %middle.1 = (bf16[1024,512]{1,0:T(8,128)(2,1)S(1)}, bf16[1024,512]{1,0:T(8,128)(2,1)S(1)}, bf16[768,1024]{1,0:T(8,128)(2,1)S(1)}, bf16[64,512]{1,0:T(8,128)(2,1)...) custom-call(s32[1]{0:T(128)} %bitcast.core_ref, ...), custom_call_target="tpu_custom_call" | custom-call | flops 3221225472 | bytes 8388608 | tf_op jit(solution)/shard_map/middle/pallas_call | solution.py:48
  34.5 2.9 %tail.1 = (bf16[64,512]{1,0:T(8,128)(2,1)}, bf16[64,512]{1,0:T(8,128)(2,1)}, bf16[3,64,512]{2,1,0:T(8,128)(2,1)S(1)}, bf16[3,64,512]{2,1,0:T(8,128)(2,1)S(1)}, b...) custom-call(bf16[768,1024]{1,0:T(8,128)(2,1)S(1)} %get-tuple-element.61.part_ref, ...), custom_call_target="tpu_custom_call" | custom-call | flops 1073741824 | bytes 5242880 | tf_op jit(solution)/shard_map/tail/pallas_call | solution.py:48
  38.5 8.7 %all-to-all-start = ((bf16[16,64,512]{2,1,0:T(8,128)(2,1)}), bf16[16,64,512]{2,1,0:T(8,128)(2,1)S(1)}, u32[]{:S(2)}, u32[]{:S(2)}) async-start(bf16[16,64,512]{2,1,0:T(8,128)(2,1)} %bitcast.4), calls=%async_computation | async-start | bytes 2097152 | tf_op jit(solution)/shard_map/all_to_all | solution.py:394
  47.2 2.0 %collective-permute-start.7 = (bf16[3,64,512]{2,1,0:T(8,128)(2,1)S(1)}, bf16[3,64,512]{2,1,0:T(8,128)(2,1)S(1)}, u32[]{:S(2)}, u32[]{:S(2)}) collective-permute-start(bf16[3,64,512]{2,1,0:T(8,128)(2,1)S(1)} %get-tuple-element.74), channel_id=1, source_target_pairs={{0,2},{1,3},{2,0},{3,1},{4,6},{5,7},{6,4},{7,5},{8,10},{9,11},{10,... | collective-permute-start | bytes 589832 | tf_op jit(solution)/shard_map/ppermute | solution.py:314
  49.8 2.2 %collective-permute-start.6 = (bf16[3,64,512]{2,1,0:T(8,128)(2,1)S(1)}, bf16[3,64,512]{2,1,0:T(8,128)(2,1)S(1)}, u32[]{:S(2)}, u32[]{:S(2)}) collective-permute-start(bf16[3,64,512]{2,1,0:T(8,128)(2,1)S(1)} %get-tuple-element.73), channel_id=1, source_target_pairs={{0,3},{1,0},{2,1},{3,2},{4,7},{5,4},{6,5},{7,6},{8,11},{9,8},{10,9... | collective-permute-start | bytes 589832 | tf_op jit(solution)/shard_map/ppermute | solution.py:314
  51.9 2.5 %collective-permute-done.7.p2.s2 = bf16[3,64,512]{2,1,0:T(8,128)(2,1)S(1)} collective-permute-done((bf16[3,64,512]{2,1,0:T(8,128)(2,1)S(1)}, bf16[3,64,512]{2,1,0:T(8,128)(2,1)S(1)}, u32[]{:S(2)}, u32[]{:S(2)}) %collective-permute-start.7) | collective-permute-done | bytes 196640 | tf_op jit(solution)/shard_map/ppermute | solution.py:314
  54.5 5.4 %collective-permute-done.8.p3.s3 = bf16[3,64,512]{2,1,0:T(8,128)(2,1)S(1)} collective-permute-done((bf16[3,64,512]{2,1,0:T(8,128)(2,1)S(1)}, bf16[3,64,512]{2,1,0:T(8,128)(2,1)S(1)}, u32[]{:S(2)}, u32[]{:S(2)}) %collective-permute-start.8) | collective-permute-done | bytes 196640 | tf_op jit(solution)/shard_map/ppermute | solution.py:314
  59.9 2.6 %all-to-all-done = bf16[16,64,512]{2,1,0:T(8,128)(2,1)S(1)} async-done(((bf16[16,64,512]{2,1,0:T(8,128)(2,1)}), bf16[16,64,512]{2,1,0:T(8,128)(2,1)S(1)}, u32[]{:S(2)}, u32[]{:S(2)}) %all-to-all-start) | async-done | bytes 1048608 | tf_op jit(solution)/shard_map/all_to_all | solution.py:394
  62.4 3.6 %collective-permute-start.10 = (bf16[256,512]{1,0:T(8,128)(2,1)S(1)}, bf16[256,512]{1,0:T(8,128)(2,1)S(1)}, u32[]{:S(2)}, u32[]{:S(2)}) collective-permute-start(bf16[256,512]{1,0:T(8,128)(2,1)S(1)} %get-tuple-element.79), channel_id=1, source_target_pairs={{0,4},{4,0},{1,5},{5,1},{2,6},{6,2},{3,7},{7,3},{8,12},{12,8},{9,1... | collective-permute-start | bytes 786440 | tf_op jit(solution)/shard_map/ppermute | solution.py:314
  66.0 2.1 %collective-permute-start.11 = (bf16[256,512]{1,0:T(8,128)(2,1)S(1)}, bf16[256,512]{1,0:T(8,128)(2,1)S(1)}, u32[]{:S(2)}, u32[]{:S(2)}) collective-permute-start(bf16[256,512]{1,0:T(8,128)(2,1)S(1)} %get-tuple-element.80), channel_id=1, source_target_pairs={{4,8},{12,16},{20,24},{28,32},{36,40},{44,48},{52,56},{60,64},{68,... | collective-permute-start | bytes 786440 | tf_op jit(solution)/shard_map/ppermute | solution.py:320
  69.4 1.7 %collective-permute-start.13 = (bf16[64,512]{1,0:T(8,128)(2,1)S(1)}, bf16[64,512]{1,0:T(8,128)(2,1)S(1)}, u32[]{:S(2)}, u32[]{:S(2)}) collective-permute-start(bf16[64,512]{1,0:T(8,128)(2,1)S(1)} %reduce_sum.12.p0), channel_id=1, source_target_pairs={{0,3},{1,0},{2,1},{3,2},{4,7},{5,4},{6,5},{7,6},{8,11},{9,8},{10,9... | collective-permute-start | bytes 196616 | tf_op jit(solution)/shard_map/ppermute | solution.py:314
  73.7 2.4 %collective-permute-done.12.p2 = bf16[64,512]{1,0:T(8,128)(2,1)S(1)} collective-permute-done((bf16[64,512]{1,0:T(8,128)(2,1)S(1)}, bf16[64,512]{1,0:T(8,128)(2,1)S(1)}, u32[]{:S(2)}, u32[]{:S(2)}) %collective-permute-start.12) | collective-permute-done | bytes 65568 | tf_op jit(solution)/shard_map/ppermute | solution.py:314
  77.2 5.1 %all-to-all-start.1 = ((bf16[16,64,512]{2,1,0:T(8,128)(2,1)}), bf16[16,64,512]{2,1,0:T(8,128)(2,1)S(1)}, u32[]{:S(2)}, u32[]{:S(2)}) async-start(bf16[16,64,512]{2,1,0:T(8,128)(2,1)} %spread.1), calls=%async_computation.1 | async-start | bytes 2097152 | tf_op jit(solution)/shard_map/all_to_all | solution.py:408
  82.3 4.4 %grid_grad.1 = bf16[2048,512]{1,0:T(8,128)(2,1)} custom-call(s32[1]{0:T(128)} %bitcast.1.sub_ref, s32[1]{0:T(128)} %bitcast.core_ref, bf16[256,512]{1,0:T(8,128)(2,1)S(1)} %collective-permute-done.10.near, bf16[256,512]{1,0:T(8,128)(2,1)S(1)} %collective-permute-done.11.far, bf16[3,64,512]{2,1,0:T(8,128)(2,1)S(1)} %get-tuple-element.72.p0.s0, ...), custom_call_target="tpu_custom_call" | custom-call | flops 1073741824 | bytes 5242880 | tf_op jit(solution)/shard_map/grid_grad/pallas_call | solution.py:48
  86.7 10.6 %all-to-all-done.1 = bf16[16,64,512]{2,1,0:T(8,128)(2,1)S(1)} async-done(((bf16[16,64,512]{2,1,0:T(8,128)(2,1)}), bf16[16,64,512]{2,1,0:T(8,128)(2,1)S(1)}, u32[]{:S(2)}, u32[]{:S(2)}) %all-to-all-start.1) | async-done | bytes 1048608 | tf_op jit(solution)/shard_map/all_to_all | solution.py:408
  97.4 3.7 %collective-permute-start.14 = (bf16[1024,512]{1,0:T(8,128)(2,1)S(1)}, bf16[1024,512]{1,0:T(8,128)(2,1)S(1)}, u32[]{:S(2)}, u32[]{:S(2)}) collective-permute-start(bf16[1024,512]{1,0:T(8,128)(2,1)S(1)} %bitcast.6), channel_id=1, source_target_pairs={{0,4},{4,0},{1,5},{5,1},{2,6},{6,2},{3,7},{7,3},{8,12},{12,8},{9,1... | collective-permute-start | bytes 3145736 | tf_op jit(solution)/shard_map/ppermute | solution.py:314
  (22 shorter events, 11.1 us)
Async XLA Ops:
  3.6 9.4 %collective-permute-start = (bf16[3,64,512]{2,1,0:T(8,128)(2,1)S(1)}, bf16[3,64,512]{2,1,0:T(8,128)(2,1)S(1)}, u32[]{:S(2)}, u32[]{:S(2)}) collective-permute-start(bf16[3,64,512]{2,1,0:T(8,128)(2,1)S(1)} %get-tuple-element.47), channel_id=1, source_target_pairs={{0,1},{1,2},{2,3},{3,0},{4,5},{5,6},{6,7},{7,4},{8,9},{9,10},{10,1... | collective-permute-start | bytes 589832 | tf_op jit(solution)/shard_map/ppermute | solution.py:314
  6.1 11.8 %collective-permute-start.1 = (bf16[3,64,512]{2,1,0:T(8,128)(2,1)S(1)}, bf16[3,64,512]{2,1,0:T(8,128)(2,1)S(1)}, u32[]{:S(2)}, u32[]{:S(2)}) collective-permute-start(bf16[3,64,512]{2,1,0:T(8,128)(2,1)S(1)} %get-tuple-element.48), channel_id=1, source_target_pairs={{0,2},{1,3},{2,0},{3,1},{4,6},{5,7},{6,4},{7,5},{8,10},{9,11},{10,... | collective-permute-start | bytes 589832 | tf_op jit(solution)/shard_map/ppermute | solution.py:314
  9.4 8.5 %collective-permute-start.2 = (bf16[3,64,512]{2,1,0:T(8,128)(2,1)S(1)}, bf16[3,64,512]{2,1,0:T(8,128)(2,1)S(1)}, u32[]{:S(2)}, u32[]{:S(2)}) collective-permute-start(bf16[3,64,512]{2,1,0:T(8,128)(2,1)S(1)} %get-tuple-element.49), channel_id=1, source_target_pairs={{0,3},{1,0},{2,1},{3,2},{4,7},{5,4},{6,5},{7,6},{8,11},{9,8},{10,9... | collective-permute-start | bytes 589832 | tf_op jit(solution)/shard_map/ppermute | solution.py:314
  18.0 4.7 %collective-permute-start.3 = (bf16[256,512]{1,0:T(8,128)(2,1)S(1)}, bf16[256,512]{1,0:T(8,128)(2,1)S(1)}, u32[]{:S(2)}, u32[]{:S(2)}) collective-permute-start(bf16[256,512]{1,0:T(8,128)(2,1)S(1)} %get-tuple-element.55), channel_id=1, source_target_pairs={{0,4},{4,0},{1,5},{5,1},{2,6},{6,2},{3,7},{7,3},{8,12},{12,8},{9,1... | collective-permute-start | bytes 786440 | tf_op jit(solution)/shard_map/ppermute | solution.py:314
  19.6 7.7 %collective-permute-start.4 = (bf16[256,512]{1,0:T(8,128)(2,1)S(1)}, bf16[256,512]{1,0:T(8,128)(2,1)S(1)}, u32[]{:S(2)}, u32[]{:S(2)}) collective-permute-start(bf16[256,512]{1,0:T(8,128)(2,1)S(1)} %get-tuple-element.56), channel_id=1, source_target_pairs={{4,8},{12,16},{20,24},{28,32},{36,40},{44,48},{52,56},{60,64},{68,... | collective-permute-start | bytes 786440 | tf_op jit(solution)/shard_map/ppermute | solution.py:320
  34.4 3.0 %collective-permute-start.5 = (bf16[1024,512]{1,0:T(8,128)(2,1)S(1)}, bf16[1024,512]{1,0:T(8,128)(2,1)S(1)}, u32[]{:S(2)}, u32[]{:S(2)}) collective-permute-start(bf16[1024,512]{1,0:T(8,128)(2,1)S(1)} %get-tuple-element.69), channel_id=1, source_target_pairs={{0,4},{4,0},{1,5},{5,1},{2,6},{6,2},{3,7},{7,3},{8,12},{12,8},{9,1... | collective-permute-start | bytes 3145736 | tf_op jit(solution)/shard_map/ppermute | solution.py:314
  38.5 23.9 %all-to-all-start = ((bf16[16,64,512]{2,1,0:T(8,128)(2,1)}), bf16[16,64,512]{2,1,0:T(8,128)(2,1)S(1)}, u32[]{:S(2)}, u32[]{:S(2)}) async-start(bf16[16,64,512]{2,1,0:T(8,128)(2,1)} %bitcast.4), calls=%async_computation | async-start | bytes 2097152 | tf_op jit(solution)/shard_map/all_to_all | solution.py:394
  47.2 7.2 %collective-permute-start.7 = (bf16[3,64,512]{2,1,0:T(8,128)(2,1)S(1)}, bf16[3,64,512]{2,1,0:T(8,128)(2,1)S(1)}, u32[]{:S(2)}, u32[]{:S(2)}) collective-permute-start(bf16[3,64,512]{2,1,0:T(8,128)(2,1)S(1)} %get-tuple-element.74), channel_id=1, source_target_pairs={{0,2},{1,3},{2,0},{3,1},{4,6},{5,7},{6,4},{7,5},{8,10},{9,11},{10,... | collective-permute-start | bytes 589832 | tf_op jit(solution)/shard_map/ppermute | solution.py:314
  49.3 10.6 %collective-permute-start.8 = (bf16[3,64,512]{2,1,0:T(8,128)(2,1)S(1)}, bf16[3,64,512]{2,1,0:T(8,128)(2,1)S(1)}, u32[]{:S(2)}, u32[]{:S(2)}) collective-permute-start(bf16[3,64,512]{2,1,0:T(8,128)(2,1)S(1)} %get-tuple-element.75), channel_id=1, source_target_pairs={{0,1},{1,2},{2,3},{3,0},{4,5},{5,6},{6,7},{7,4},{8,9},{9,10},{10,1... | collective-permute-start | bytes 589832 | tf_op jit(solution)/shard_map/ppermute | solution.py:314
  49.8 10.1 %collective-permute-start.6 = (bf16[3,64,512]{2,1,0:T(8,128)(2,1)S(1)}, bf16[3,64,512]{2,1,0:T(8,128)(2,1)S(1)}, u32[]{:S(2)}, u32[]{:S(2)}) collective-permute-start(bf16[3,64,512]{2,1,0:T(8,128)(2,1)S(1)} %get-tuple-element.73), channel_id=1, source_target_pairs={{0,3},{1,0},{2,1},{3,2},{4,7},{5,4},{6,5},{7,6},{8,11},{9,8},{10,9... | collective-permute-start | bytes 589832 | tf_op jit(solution)/shard_map/ppermute | solution.py:314
  62.4 10.4 %collective-permute-start.10 = (bf16[256,512]{1,0:T(8,128)(2,1)S(1)}, bf16[256,512]{1,0:T(8,128)(2,1)S(1)}, u32[]{:S(2)}, u32[]{:S(2)}) collective-permute-start(bf16[256,512]{1,0:T(8,128)(2,1)S(1)} %get-tuple-element.79), channel_id=1, source_target_pairs={{0,4},{4,0},{1,5},{5,1},{2,6},{6,2},{3,7},{7,3},{8,12},{12,8},{9,1... | collective-permute-start | bytes 786440 | tf_op jit(solution)/shard_map/ppermute | solution.py:314
  66.0 7.7 %collective-permute-start.11 = (bf16[256,512]{1,0:T(8,128)(2,1)S(1)}, bf16[256,512]{1,0:T(8,128)(2,1)S(1)}, u32[]{:S(2)}, u32[]{:S(2)}) collective-permute-start(bf16[256,512]{1,0:T(8,128)(2,1)S(1)} %get-tuple-element.80), channel_id=1, source_target_pairs={{4,8},{12,16},{20,24},{28,32},{36,40},{44,48},{52,56},{60,64},{68,... | collective-permute-start | bytes 786440 | tf_op jit(solution)/shard_map/ppermute | solution.py:320
  68.2 4.6 %collective-permute-start.9 = (bf16[64,512]{1,0:T(8,128)(2,1)S(1)}, bf16[64,512]{1,0:T(8,128)(2,1)S(1)}, u32[]{:S(2)}, u32[]{:S(2)}) collective-permute-start(bf16[64,512]{1,0:T(8,128)(2,1)S(1)} %reduce_sum.12.p0), channel_id=1, source_target_pairs={{0,1},{1,2},{2,3},{3,0},{4,5},{5,6},{6,7},{7,4},{8,9},{9,10},{10,1... | collective-permute-start | bytes 196616 | tf_op jit(solution)/shard_map/ppermute | solution.py:314
  69.4 4.2 %collective-permute-start.13 = (bf16[64,512]{1,0:T(8,128)(2,1)S(1)}, bf16[64,512]{1,0:T(8,128)(2,1)S(1)}, u32[]{:S(2)}, u32[]{:S(2)}) collective-permute-start(bf16[64,512]{1,0:T(8,128)(2,1)S(1)} %reduce_sum.12.p0), channel_id=1, source_target_pairs={{0,3},{1,0},{2,1},{3,2},{4,7},{5,4},{6,5},{7,6},{8,11},{9,8},{10,9... | collective-permute-start | bytes 196616 | tf_op jit(solution)/shard_map/ppermute | solution.py:314
  71.1 4.9 %collective-permute-start.12 = (bf16[64,512]{1,0:T(8,128)(2,1)S(1)}, bf16[64,512]{1,0:T(8,128)(2,1)S(1)}, u32[]{:S(2)}, u32[]{:S(2)}) collective-permute-start(bf16[64,512]{1,0:T(8,128)(2,1)S(1)} %reduce_sum.12.p0), channel_id=1, source_target_pairs={{0,2},{1,3},{2,0},{3,1},{4,6},{5,7},{6,4},{7,5},{8,10},{9,11},{10,... | collective-permute-start | bytes 196616 | tf_op jit(solution)/shard_map/ppermute | solution.py:314
  77.2 20.2 %all-to-all-start.1 = ((bf16[16,64,512]{2,1,0:T(8,128)(2,1)}), bf16[16,64,512]{2,1,0:T(8,128)(2,1)S(1)}, u32[]{:S(2)}, u32[]{:S(2)}) async-start(bf16[16,64,512]{2,1,0:T(8,128)(2,1)} %spread.1), calls=%async_computation.1 | async-start | bytes 2097152 | tf_op jit(solution)/shard_map/all_to_all | solution.py:408
  97.4 6.0 %collective-permute-start.14 = (bf16[1024,512]{1,0:T(8,128)(2,1)S(1)}, bf16[1024,512]{1,0:T(8,128)(2,1)S(1)}, u32[]{:S(2)}, u32[]{:S(2)}) collective-permute-start(bf16[1024,512]{1,0:T(8,128)(2,1)S(1)} %bitcast.6), channel_id=1, source_target_pairs={{0,4},{4,0},{1,5},{5,1},{2,6},{6,2},{3,7},{7,3},{8,12},{12,8},{9,1... | collective-permute-start | bytes 3145736 | tf_op jit(solution)/shard_map/ppermute | solution.py:314

commit v5 on v4

--- a/solution.py
+++ b/solution.py
@@ -70,7 +70,21 @@
     return [pltpu.VMEM(a.shape, a.dtype) for a in args] + [pltpu.SemaphoreType.DMA((len(args),))]
 
 
-def gather_body(sub_ref, rows_hbm, gain_hbm, x_hbm, p0, p1, p2, p3,
+def assemble(rows, near_first, near, far, own, m1, m2, m3, f1, f2, f3):
+    block = near.shape[0]
+    cap = block // 4
+    near_at = pl.multiple_of((1 - near_first) * (2 * block), block)
+    far_at = pl.multiple_of(near_first * (2 * block), block)
+    rows[block : block + cap] = own[0:cap]
+    rows[pl.ds(near_at, cap), :] = near[0:cap]
+    rows[pl.ds(far_at, cap), :] = far[0:cap]
+    for k, (mixed, outer) in enumerate(((m1, f1), (m2, f2), (m3, f3)), 1):
+        rows[block + k * cap : block + (k + 1) * cap] = mixed[0:cap]
+        rows[pl.ds(near_at + k * cap, cap), :] = mixed[cap : 2 * cap]
+        rows[pl.ds(far_at + k * cap, cap), :] = outer[...]
+
+
+def gather_body(sub_ref, core_ref, rows_hbm, gain_hbm, x_hbm, near_ref, far_ref, own_ref,
                 rows_ref, gain_ref, x_ref, sems):
     half = x_ref.shape[0] // 2
     cap = rows_ref.shape[3]
@@ -100,8 +114,18 @@
             copies[2 + step].wait()
         wide = nn(onehot, x_ref[first : first + count, :])
         normed = (wide * inv_rms(wide) * gain).astype(BF16)
-        for k in range(4):
-            (p0, p1, p2, p3)[k][o] = normed[k * cap : (k + 1) * cap]
+        if o == 1:
+            own_ref[...] = normed
+            continue
+        to_near = core_ref[0] == (2 - o) // 2
+
+        @pl.when(to_near)
+        def _():
+            near_ref[...] = normed
+
+        @pl.when(jnp.logical_not(to_near))
+        def _():
+            far_ref[...] = normed
 
 
 def prep_body(sub_ref, mesh_hbm, gain_hbm, wq_hbm, wo_hbm, og_hbm, nbr_hbm, valid_hbm, bias_hbm,
@@ -145,7 +169,7 @@
     ag_ref[...] = nt(og_ref[...], wo_ref[...]).astype(BF16)
 
 
-def middle_body(core_ref, near, far, b0, b1, b2, b3, q_ref, ag_ref, mn_ref, bias_ref,
+def middle_body(core_ref, near, far, own, m1, m2, m3, f1, f2, f3, q_ref, ag_ref, mn_ref, bias_ref,
                 wk_hbm, wv_hbm, og_hbm, keep_ref, send_ref, part_ref, att_ref, qg_ref,
                 wkv_ref, og_ref, rows, keys, vals, sems):
     width = q_ref.shape[1]
@@ -155,13 +179,8 @@
         sems,
     )
     heads = bias_ref.shape[0]
-    block = near.shape[0]
-    cap = b0.shape[1]
     core = core_ref[0]
-    rows[pl.ds(pl.multiple_of(core * (2 * block), block), block), :] = near[...]
-    rows[pl.ds(pl.multiple_of((1 - core) * (2 * block), block), block), :] = far[...]
-    for k, piece in enumerate((b0, b1, b2, b3)):
-        rows[block + k * cap : block + (k + 1) * cap] = piece[1]
+    assemble(rows, 1 - core, near, far, own, m1, m2, m3, f1, f2, f3)
     copies[0].wait()
     keys[...] = nn(rows[...], wkv_ref[:, :width]).astype(BF16)
     copies[1].wait()
@@ -199,18 +218,18 @@
     place(1, width, tn(att_ref[...], og_ref[...]).astype(BF16))
 
 
-def tail_body(part_ref, att_ref, qg_ref, wkv_ref, og_ref, wo_hbm, wq_hbm, mesh_hbm,
-              gain_hbm, out_ref, grad_ref, s0, s1, s2, s3,
-              wo_ref, wq_ref, mesh_ref, gain_ref, sems):
+def tail_body(core_ref, part_ref, att_ref, qg_ref, wkv_ref, og_ref, wo_hbm, wq_hbm, mesh_hbm,
+              gain_hbm, out_ref, grad_ref, near_ref, far_ref, own_ref, back_ref, wo_ref, wq_ref, mesh_ref, gain_ref, sems):
     copies = fetch(
         (wo_hbm, wq_hbm, mesh_hbm, gain_hbm), (wo_ref, wq_ref, mesh_ref, gain_ref), sems
     )
-    cap = s0.shape[1]
-    back = nt(part_ref[...], wkv_ref[...]).astype(BF16)
-    for o in range(3):
-        for k, piece in enumerate((s0, s1, s2, s3)):
-            first = (o * 4 + k) * cap
-            piece[o] = back[first : first + cap]
+    block = own_ref.shape[0]
+    back_ref[...] = nt(part_ref[...], wkv_ref[...]).astype(BF16)
+    near_at = core_ref[0] * (2 * block)
+    far_at = (1 - core_ref[0]) * (2 * block)
+    near_ref[...] = back_ref[pl.ds(pl.multiple_of(near_at, block), block), :]
+    far_ref[...] = back_ref[pl.ds(pl.multiple_of(far_at, block), block), :]
+    own_ref[...] = back_ref[block : 2 * block, :]
     for copy in copies:
         copy.wait()
     wide = mesh_ref[...].astype(F32)
@@ -220,15 +239,20 @@
     grad_ref[...] = (og_ref[...].astype(F32) + back).astype(BF16)
 
 
-def pack_body(near_if_first, core_ref, p0, p1, p2, p3, near_ref, far_ref):
-    cap = p0.shape[1]
-    near = lax.select(core_ref[0] == 0, near_if_first, 2 - near_if_first)
-    for k, piece in enumerate((p0, p1, p2, p3)):
-        near_ref[k * cap : (k + 1) * cap, :] = piece[near]
-        far_ref[k * cap : (k + 1) * cap, :] = piece[2 - near]
-
-
-def grid_body(sub_ref, core_ref, near, far, s0, s1, s2, s3, rows_hbm, gain_hbm, x_hbm, out_hbm,
+def mix_body(own, near, m1, m2, m3):
+    cap = m1.shape[0] // 2
+    for k, mixed in enumerate((m1, m2, m3), 1):
+        mixed[0:cap] = own[k * cap : (k + 1) * cap]
+        mixed[cap : 2 * cap] = near[k * cap : (k + 1) * cap]
+
+
+def split_body(block, f1, f2, f3):
+    cap = f1.shape[0]
+    for k, piece in enumerate((f1, f2, f3), 1):
+        piece[...] = block[k * cap : (k + 1) * cap]
+
+
+def grid_body(sub_ref, core_ref, near, far, own, m1, m2, m3, f1, f2, f3, rows_hbm, gain_hbm, x_hbm, out_hbm,
               got, done_ref, done_sems, rows_ref, gain_ref, x_ref, sems):
     copies = fetch((rows_hbm, gain_hbm, x_hbm), (rows_ref, gain_ref, x_ref), sems)
     points = x_ref.shape[0]
@@ -236,11 +260,7 @@
     cap = rows_ref.shape[3]
     block = 4 * cap
     me = sub_ref[0]
-    core = core_ref[0]
-    got[pl.ds(pl.multiple_of((1 - core) * (2 * block), block), block), :] = near[...]
-    got[pl.ds(pl.multiple_of(core * (2 * block), block), block), :] = far[...]
-    for k, piece in enumerate((s0, s1, s2, s3)):
-        got[block + k * cap : block + (k + 1) * cap] = piece[1]
+    assemble(got, core_ref[0], near, far, own, m1, m2, m3, f1, f2, f3)
     for copy in copies:
         copy.wait()
     gain = gain_ref[...]
@@ -342,14 +362,25 @@
                   edge_bias, neighbours, valid)
     )
 
-    piece = sds((3, cap, width))
-    b0, b1, b2, b3 = call(
-        gather_body, [piece] * 4, [SM, HB, HB, HB],
-        (sub1, send_rows, gain_g, grid_x), 1 << 30, 4 << 20, "gather_rows",
+    one, two, four = sds((cap, width)), sds((2 * cap, width)), sds((block, width))
+    near, far, own = call(
+        gather_body, [four] * 3, [SM, SM, HB, HB, HB],
+        (sub1, core1, send_rows, gain_g, grid_x), 1 << 30, 4 << 20, "gather_rows",
         held(send_rows, gain_g, grid_x)[:-1] + [pltpu.SemaphoreType.DMA((4,))],
     )
-    b1, b2, b3 = (shifted(b, "z", k) for k, b in ((1, b1), (2, b2), (3, b3)))
-    sub2, b0 = lax.optimization_barrier((sub1, b0))
+
+    def exchange(near, far, own, sign):
+        far = swapped_far(far)
+        near = shifted(near, "gc", 1)
+        mixed = call(mix_body, [two] * 3, [VM] * 2, (own, near), 0, 1 << 20, "mix")
+        mixed = [shifted(m, "z", sign * k) for k, m in enumerate(mixed, 1)]
+        far, mixed[0] = lax.optimization_barrier((far, mixed[0]))
+        outer = call(split_body, [one] * 3, [VM], (far,), 0, 1 << 19, "split")
+        outer = [shifted(f, "z", sign * k) for k, f in enumerate(outer, 1)]
+        return near, far, own, *mixed, *outer
+
+    received = exchange(near, far, own, 1)
+    sub2, near = lax.optimization_barrier((sub1, received[1]))
     prep_args = (mesh_h, gain_m, w_query, w_out, out_grad, neighbours, valid, edge_bias)
     mesh_normed, queries, att_grad, dense = call(
         prep_body,
@@ -358,33 +389,25 @@
         [pltpu.VMEM((nodes * 8, 128), F32), pltpu.VMEM((heads, nodes, 128), F32)]
         + held(neighbours, valid, edge_bias, mesh_h, gain_m, w_query, w_out, out_grad),
     )
-    b1, b2, b3, dense = lax.optimization_barrier((b1, b2, b3, dense))
-
-    def packed(near_if_first, *pieces):
-        body = functools.partial(pack_body, near_if_first)
-        return call(body, [sds((block, width))] * 2, [SM] + [VM] * 4, (core1, *pieces), 0, 1 << 20, "pack")
-
-    near, far = packed(2, b0, b1, b2, b3)
-    far = swapped_far(far)
-    near = shifted(near, "gc", 1)
     keep, send, part_grads, attended, query_grad, weights_near, og_near = call(
         middle_body,
         [sds((2 * width, width))] * 2 + [sds((slots, 2 * width))] + [sds((nodes, width))] * 2
         + [sds((width, 2 * width)), sds((nodes, width))],
-        [SM] + [VM] * 10 + [HB] * 3,
-        (core1, near, far, b0, b1, b2, b3, queries, att_grad, mesh_normed, dense, w_key, w_value,
+        [SM] + [VM] * 13 + [HB] * 3,
+        (core1, *received, queries, att_grad, mesh_normed, dense, w_key, w_value,
          out_grad),
         3 << 30, 8 << 20, "middle",
         [pltpu.VMEM((slots, width), BF16)] * 3 + [pltpu.SemaphoreType.DMA((3,))],
     )
 
     other = shifted(send, "gc", 1)
-    mesh_out, mesh_grad, s0, s1, s2, s3 = call(
-        tail_body, [sds((nodes, width))] * 2 + [piece] * 4, [VM] * 5 + [HB] * 4,
-        (part_grads, attended, query_grad, weights_near, og_near, w_out, w_query, mesh_h, gain_m),
-        1 << 30, 5 << 20, "tail", held(w_out, w_query, mesh_h, gain_m),
-    )
-    other, s1 = lax.optimization_barrier((other, s1))
+    mesh_out, mesh_grad, near, far, back_own = call(
+        tail_body, [sds((nodes, width))] * 2 + [four] * 3, [SM] + [VM] * 5 + [HB] * 4,
+        (core1, part_grads, attended, query_grad, weights_near, og_near, w_out, w_query, mesh_h, gain_m),
+        1 << 30, 5 << 20, "tail",
+        [pltpu.VMEM((slots, width), BF16)] + held(w_out, w_query, mesh_h, gain_m),
+    )
+    other, near = lax.optimization_barrier((other, near))
     (own,) = call(
         pair_body, [sds((2 * width, width))], [VM] * 2, (keep, other), 1 << 20, 3 << 20, "pair",
         [pltpu.VMEM((2 * width, width), BF16), pltpu.SemaphoreType.DMA((4,))], [HB],
@@ -393,22 +416,18 @@
     share = 2 * width // plane
     parts = lax.all_to_all(own.reshape(plane, share, width), PLANE, 0, 0, tiled=True)
 
-    t1, t2, t3 = (shifted(s, "z", -k) for k, s in ((1, s1), (2, s2), (3, s3)))
-    near, far = packed(0, s0, t1, t2, t3)
-    parts, near, far = lax.optimization_barrier((parts, near, far))
-    far = swapped_far(far)
-    near = shifted(near, "gc", 1)
+    returned = exchange(near, far, back_own, -1)
+    parts, *returned = lax.optimization_barrier((parts, *returned))
     part = jnp.sum(parts.astype(F32), axis=0).astype(BF16)
     p1, p2, p3 = (shifted(part, "z", k) for k in (1, 2, 3))
-    p1, near, far = lax.optimization_barrier((p1, near, far))
     (spread,) = call(
         spread_body, [sds((plane, share, width))], [VM] * 4, (part, p1, p2, p3), 1 << 18, 1 << 20,
         "spread", [pltpu.VMEM((share, width), BF16), pltpu.SemaphoreType.DMA((plane,))], [HB],
     )
     mine = lax.all_to_all(spread, PLANE, 0, 0, tiled=True).reshape(2 * width, width)
     (grid_grad,) = call(
-        grid_body, [sds((points, width))], [SM] * 2 + [VM] * 6 + [HB] * 3,
-        (sub1, core1, near, far, s0, t1, t2, t3, send_rows, gain_g, grid_x),
+        grid_body, [sds((points, width))], [SM] * 2 + [VM] * 9 + [HB] * 3,
+        (sub1, core1, *returned, send_rows, gain_g, grid_x),
         1 << 30, 5 << 20, "grid_grad",
         [pltpu.VMEM((slots, width), BF16), pltpu.VMEM((points, width), BF16),
          pltpu.SemaphoreType.DMA((points // 256,))] + held(send_rows, gain_g, grid_x),

time: 105 us -> 107 us (1.019)
  starting transfers between devices: 43 us -> 47.6 us
  waiting for transfers between devices: 35.7 us -> 31.4 us
  Pallas kernels: 25.2 us -> 26.3 us
    ppermute x13 -> x19, waiting for transfers between devices: 17.1 us -> 10.3 us  [shifted(): return lax.ppermute(block, axis, [(i, (i + k) % n) for i in range(n)])]
    ppermute x2, waiting for transfers between devices: 5.42 us -> 10.3 us  [swapped_far(): return lax.ppermute(block, SLAB, pairs + [(j, i) for i, j in pairs])]
    all_to_all x1, starting transfers between devices: 5.14 us -> 9.39 us  [shards(): lax.all_to_all(spread, PLANE, 0, 0, tiled=True).reshape(2 * width, width)]
    all_to_all x1, waiting for transfers between devices: 2.55 us -> 0.01 us  [shards(): lax.all_to_all(own.reshape(plane, share, width), PLANE, 0, 0, tiled=True)]
    ppermute x13 -> x19, starting transfers between devices: 24 us -> 22.4 us  [shifted(): return lax.ppermute(block, axis, [(i, (i + k) % n) for i in range(n)])]
    ppermute x2, starting transfers between devices: 5.18 us -> 6.55 us  [swapped_far(): return lax.ppermute(block, SLAB, pairs + [(j, i) for i, j in pairs])]
    pallas_call x11 -> x13, Pallas kernels: 25.2 us -> 26.3 us  [call(): pl.pallas_call(body, out_shape=outs, in_specs=in_specs, out_specs=out_spe...]
  transfers between devices with their start and end apart: 17 -> 23, of which waited for: 10 -> 11; matrix products, arithmetic and copies ran while one was open for 0% -> 0% of each run, Pallas kernels for 11% -> 11%
where the time goes in v5:
time: 107 us; the launch traced here: 106 us
  starting transfers between devices  47.6 us (44%)
  waiting for transfers between devices  31.4 us (29%)
  Pallas kernels  26.3 us (25%)
    pallas_call x13, Pallas kernels, call(): pl.pallas_call(body, out_shape=outs, in_specs=in_specs, out_specs=out_spe...  26.3 us
    ppermute x19, starting transfers between devices, shifted(): return lax.ppermute(block, axis, [(i, (i + k) % n) for i in range(n)])  22.4 us
    all_to_all x1, waiting for transfers between devices, shards(): lax.all_to_all(spread, PLANE, 0, 0, tiled=True).reshape(2 * width, width)  10.9 us
    ppermute x2, waiting for transfers between devices, swapped_far(): return lax.ppermute(block, SLAB, pairs + [(j, i) for i, j in pairs])  10.3 us
    ppermute x19, waiting for transfers between devices, shifted(): return lax.ppermute(block, axis, [(i, (i + k) % n) for i in range(n)])  10.3 us
    all_to_all x1, starting transfers between devices, shards(): lax.all_to_all(spread, PLANE, 0, 0, tiled=True).reshape(2 * width, width)  9.39 us
    all_to_all x1, starting transfers between devices, shards(): lax.all_to_all(own.reshape(plane, share, width), PLANE, 0, 0, tiled=True)  9.3 us
    ppermute x2, starting transfers between devices, swapped_far(): return lax.ppermute(block, SLAB, pairs + [(j, i) for i, j in pairs])  6.55 us
  transfers between devices with their start and end apart: 23, of which 11 were waited for; matrix products, arithmetic and copies ran while one was open for 0% of the time, Pallas kernels for 11%

profile of v5, /device:TPU:1, one launch (start us, length us, event | category | flops | bytes accessed | tf_op | source)
XLA Modules:
  0.0 106.5 jit_solution(7886267877794288673)
XLA Ops:
  0.6 3.7 %gather_rows.1 = (bf16[256,512]{1,0:T(8,128)(2,1)S(1)}, bf16[256,512]{1,0:T(8,128)(2,1)S(1)}, bf16[256,512]{1,0:T(8,128)(2,1)S(1)}) custom-call(s32[1]{0:T(128)} %bitcast.1.sub_ref, s32[1]{0:T(128)} %bitcast.core_ref, s32[1,3,4,64]{3,2,1,0:T(4,128)} %rows_hbm.3, f32[1,512]{1,0:T(1,128)} %bitcast.8, bf16[2048,512]{1,0:T(8,128)(2,1)} %x_hbm.3), custom_call_target="tpu_custom_call" | custom-call | flops 1073741824 | bytes 4194304 | tf_op jit(solution)/shard_map/gather_rows/pallas_call | solution.py:48
  4.3 1.5 %collective-permute-start = (bf16[256,512]{1,0:T(8,128)(2,1)S(1)}, bf16[256,512]{1,0:T(8,128)(2,1)S(1)}, u32[]{:S(2)}, u32[]{:S(2)}) collective-permute-start(bf16[256,512]{1,0:T(8,128)(2,1)S(1)} %get-tuple-element.54), channel_id=1, source_target_pairs={{0,4},{4,0},{1,5},{5,1},{2,6},{6,2},{3,7},{7,3},{8,12},{12,8},{9,1... | collective-permute-start | bytes 786440 | tf_op jit(solution)/shard_map/ppermute | solution.py:334
  5.8 3.2 %collective-permute-start.1 = (bf16[256,512]{1,0:T(8,128)(2,1)S(1)}, bf16[256,512]{1,0:T(8,128)(2,1)S(1)}, u32[]{:S(2)}, u32[]{:S(2)}) collective-permute-start(bf16[256,512]{1,0:T(8,128)(2,1)S(1)} %get-tuple-element.55), channel_id=1, source_target_pairs={{4,8},{12,16},{20,24},{28,32},{36,40},{44,48},{52,56},{60,64},{68,... | collective-permute-start | bytes 786440 | tf_op jit(solution)/shard_map/ppermute | solution.py:340
  9.0 1.7 %collective-permute-start.2 = (bf16[128,512]{1,0:T(8,128)(2,1)S(1)}, bf16[128,512]{1,0:T(8,128)(2,1)S(1)}, u32[]{:S(2)}, u32[]{:S(2)}) collective-permute-start(bf16[128,512]{1,0:T(8,128)(2,1)S(1)} %get-tuple-element.57), channel_id=1, source_target_pairs={{0,1},{1,2},{2,3},{3,0},{4,5},{5,6},{6,7},{7,4},{8,9},{9,10},{10,1... | collective-permute-start | bytes 393224 | tf_op jit(solution)/shard_map/ppermute | solution.py:334
  10.8 3.3 %collective-permute-start.3 = (bf16[128,512]{1,0:T(8,128)(2,1)S(1)}, bf16[128,512]{1,0:T(8,128)(2,1)S(1)}, u32[]{:S(2)}, u32[]{:S(2)}) collective-permute-start(bf16[128,512]{1,0:T(8,128)(2,1)S(1)} %get-tuple-element.60), channel_id=1, source_target_pairs={{0,2},{1,3},{2,0},{3,1},{4,6},{5,7},{6,4},{7,5},{8,10},{9,11},{10,... | collective-permute-start | bytes 393224 | tf_op jit(solution)/shard_map/ppermute | solution.py:334
  15.6 4.1 %collective-permute-start.6 = (bf16[64,512]{1,0:T(8,128)(2,1)S(1)}, bf16[64,512]{1,0:T(8,128)(2,1)S(1)}, u32[]{:S(2)}, u32[]{:S(2)}) collective-permute-start(bf16[64,512]{1,0:T(8,128)(2,1)S(1)} %get-tuple-element.63), channel_id=1, source_target_pairs={{0,2},{1,3},{2,0},{3,1},{4,6},{5,7},{6,4},{7,5},{8,10},{9,11},{10,... | collective-permute-start | bytes 196616 | tf_op jit(solution)/shard_map/ppermute | solution.py:334
  19.7 2.8 %prep.1 = (bf16[64,512]{1,0:T(8,128)(2,1)S(1)}, bf16[64,512]{1,0:T(8,128)(2,1)S(1)}, bf16[64,512]{1,0:T(8,128)(2,1)S(1)}, f32[4,64,768]{2,1,0:T(8,128)S(1)}) custom-call(s32[1]{0:T(128)} %bitcast.1.sub_ref, bf16[64,512]{1,0:T(8,128)(2,1)} %mesh_hbm.3, f32[1,512]{1,0:T(1,128)} %bitcast.10, bf16[512,512]{1,0:T(8,128)(2,1)} %wq_hbm.3, bf16[512,512]{1,0:T(8,128)(2,1)} %wo_hbm.3, ...), custom_call_target="tpu_custom_call" | custom-call | flops 1073741824 | bytes 8388608 | tf_op jit(solution)/shard_map/prep/pallas_call | solution.py:48
  22.8 7.1 %middle.1 = (bf16[1024,512]{1,0:T(8,128)(2,1)S(1)}, bf16[1024,512]{1,0:T(8,128)(2,1)S(1)}, bf16[768,1024]{1,0:T(8,128)(2,1)S(1)}, bf16[64,512]{1,0:T(8,128)(2,1)...) custom-call(s32[1]{0:T(128)} %bitcast.core_ref, ...), custom_call_target="tpu_custom_call" | custom-call | flops 3221225472 | bytes 8388608 | tf_op jit(solution)/shard_map/middle/pallas_call | solution.py:48
  30.0 3.3 %tail.1 = (bf16[64,512]{1,0:T(8,128)(2,1)}, bf16[64,512]{1,0:T(8,128)(2,1)}, bf16[256,512]{1,0:T(8,128)(2,1)S(1)}, bf16[256,512]{1,0:T(8,128)(2,1)S(1)}, bf16[256,512]{1,0:T(8,128)(2,1)S(1)}) custom-call(s32[1]{0:T(128)} %bitcast.core_ref, bf16[768,1024]{1,0:T(8,128)(2,1)S(1)} %get-tuple-element.70.part_ref, bf16[64,512]{1,0:T(8,128)(2,1)S(1)} %get-tuple-element.71.att_ref, ...), custom_call_target="tpu_custom_call" | custom-call | flops 1073741824 | bytes 5242880 | tf_op jit(solution)/shard_map/tail/pallas_call | solution.py:48
  34.4 9.3 %all-to-all-start = ((bf16[16,64,512]{2,1,0:T(8,128)(2,1)}), bf16[16,64,512]{2,1,0:T(8,128)(2,1)S(1)}, u32[]{:S(2)}, u32[]{:S(2)}) async-start(bf16[16,64,512]{2,1,0:T(8,128)(2,1)} %bitcast.4), calls=%async_computation | async-start | bytes 2097152 | tf_op jit(solution)/shard_map/all_to_all | solution.py:417
  44.1 3.4 %collective-permute-start.10 = (bf16[256,512]{1,0:T(8,128)(2,1)S(1)}, bf16[256,512]{1,0:T(8,128)(2,1)S(1)}, u32[]{:S(2)}, u32[]{:S(2)}) collective-permute-start(bf16[256,512]{1,0:T(8,128)(2,1)S(1)} %get-tuple-element.82), channel_id=1, source_target_pairs={{4,8},{12,16},{20,24},{28,32},{36,40},{44,48},{52,56},{60,64},{68,... | collective-permute-start | bytes 786440 | tf_op jit(solution)/shard_map/ppermute | solution.py:340
  47.5 2.1 %collective-permute-start.11 = (bf16[128,512]{1,0:T(8,128)(2,1)S(1)}, bf16[128,512]{1,0:T(8,128)(2,1)S(1)}, u32[]{:S(2)}, u32[]{:S(2)}) collective-permute-start(bf16[128,512]{1,0:T(8,128)(2,1)S(1)} %get-tuple-element.84), channel_id=1, source_target_pairs={{0,3},{1,0},{2,1},{3,2},{4,7},{5,4},{6,5},{7,6},{8,11},{9,8},{10,9... | collective-permute-start | bytes 393224 | tf_op jit(solution)/shard_map/ppermute | solution.py:334
  50.3 10.3 %collective-permute-done.10.block.far = bf16[256,512]{1,0:T(8,128)(2,1)S(1)} collective-permute-done((bf16[256,512]{1,0:T(8,128)(2,1)S(1)}, bf16[256,512]{1,0:T(8,128)(2,1)S(1)}, u32[]{:S(2)}, u32[]{:S(2)}) %collective-permute-start.10) | collective-permute-done | bytes 262176 | tf_op jit(solution)/shard_map/ppermute | solution.py:340
  60.6 1.9 %collective-permute-start.14 = (bf16[64,512]{1,0:T(8,128)(2,1)S(1)}, bf16[64,512]{1,0:T(8,128)(2,1)S(1)}, u32[]{:S(2)}, u32[]{:S(2)}) collective-permute-start(bf16[64,512]{1,0:T(8,128)(2,1)S(1)} %get-tuple-element.89), channel_id=1, source_target_pairs={{0,3},{1,0},{2,1},{3,2},{4,7},{5,4},{6,5},{7,6},{8,11},{9,8},{10,9... | collective-permute-start | bytes 196616 | tf_op jit(solution)/shard_map/ppermute | solution.py:334
  63.2 1.2 %collective-permute-done.14.f1 = bf16[64,512]{1,0:T(8,128)(2,1)S(1)} collective-permute-done((bf16[64,512]{1,0:T(8,128)(2,1)S(1)}, bf16[64,512]{1,0:T(8,128)(2,1)S(1)}, u32[]{:S(2)}, u32[]{:S(2)}) %collective-permute-start.14) | collective-permute-done | bytes 65568 | tf_op jit(solution)/shard_map/ppermute | solution.py:334
  64.4 2.8 %collective-permute-done.15.f2 = bf16[64,512]{1,0:T(8,128)(2,1)S(1)} collective-permute-done((bf16[64,512]{1,0:T(8,128)(2,1)S(1)}, bf16[64,512]{1,0:T(8,128)(2,1)S(1)}, u32[]{:S(2)}, u32[]{:S(2)}) %collective-permute-start.15) | collective-permute-done | bytes 65568 | tf_op jit(solution)/shard_map/ppermute | solution.py:334
  69.6 1.5 %collective-permute-done.19.p3 = bf16[64,512]{1,0:T(8,128)(2,1)S(1)} collective-permute-done((bf16[64,512]{1,0:T(8,128)(2,1)S(1)}, bf16[64,512]{1,0:T(8,128)(2,1)S(1)}, u32[]{:S(2)}, u32[]{:S(2)}) %collective-permute-start.19) | collective-permute-done | bytes 65568 | tf_op jit(solution)/shard_map/ppermute | solution.py:334
  71.1 1.8 %collective-permute-done.18.p2 = bf16[64,512]{1,0:T(8,128)(2,1)S(1)} collective-permute-done((bf16[64,512]{1,0:T(8,128)(2,1)S(1)}, bf16[64,512]{1,0:T(8,128)(2,1)S(1)}, u32[]{:S(2)}, u32[]{:S(2)}) %collective-permute-start.18) | collective-permute-done | bytes 65568 | tf_op jit(solution)/shard_map/ppermute | solution.py:334
  74.8 9.4 %all-to-all-start.1 = ((bf16[16,64,512]{2,1,0:T(8,128)(2,1)}), bf16[16,64,512]{2,1,0:T(8,128)(2,1)S(1)}, u32[]{:S(2)}, u32[]{:S(2)}) async-start(bf16[16,64,512]{2,1,0:T(8,128)(2,1)} %spread.1), calls=%async_computation.1 | async-start | bytes 2097152 | tf_op jit(solution)/shard_map/all_to_all | solution.py:427
  84.2 4.4 %grid_grad.1 = bf16[2048,512]{1,0:T(8,128)(2,1)} custom-call(s32[1]{0:T(128)} %bitcast.1.sub_ref, s32[1]{0:T(128)} %bitcast.core_ref, bf16[256,512]{1,0:T(8,128)(2,1)S(1)} %collective-permute-done.9.near, bf16[256,512]{1,0:T(8,128)(2,1)S(1)} %collective-permute-done.10.block.far, bf16[256,512]{1,0:T(8,128)(2,1)S(1)} %get-tuple-element.95.own, ...), custom_call_target="tpu_custom_call" | custom-call | flops 1073741824 | bytes 5242880 | tf_op jit(solution)/shard_map/grid_grad/pallas_call | solution.py:48
  88.6 10.9 %all-to-all-done.1 = bf16[16,64,512]{2,1,0:T(8,128)(2,1)S(1)} async-done(((bf16[16,64,512]{2,1,0:T(8,128)(2,1)}), bf16[16,64,512]{2,1,0:T(8,128)(2,1)S(1)}, u32[]{:S(2)}, u32[]{:S(2)}) %all-to-all-start.1) | async-done | bytes 1048608 | tf_op jit(solution)/shard_map/all_to_all | solution.py:427
  99.4 3.2 %collective-permute-start.20 = (bf16[1024,512]{1,0:T(8,128)(2,1)S(1)}, bf16[1024,512]{1,0:T(8,128)(2,1)S(1)}, u32[]{:S(2)}, u32[]{:S(2)}) collective-permute-start(bf16[1024,512]{1,0:T(8,128)(2,1)S(1)} %bitcast.6), channel_id=1, source_target_pairs={{0,4},{4,0},{1,5},{5,1},{2,6},{6,2},{3,7},{7,3},{8,12},{12,8},{9,1... | collective-permute-start | bytes 3145736 | tf_op jit(solution)/shard_map/ppermute | solution.py:334
  102.7 1.4 %widen_own.1.refs_0_ = f32[4,512,512]{2,1,0:T(8,128)} custom-call(s32[1]{0:T(128)} %bitcast.core_ref, bf16[1024,512]{1,0:T(8,128)(2,1)S(1)} %bitcast.7), custom_call_target="tpu_custom_call" | custom-call | flops 1048576 | bytes 3145728 | tf_op jit(solution)/shard_map/widen_own/pallas_call | solution.py:48
  104.9 1.4 %widen_other.1 = f32[4,512,512]{2,1,0:T(8,128)} custom-call(s32[1]{0:T(128)} %bitcast.core_ref, bf16[1024,512]{1,0:T(8,128)(2,1)S(1)} %collective-permute-done.20.half_ref, f32[4,512,512]{2,1,0:T(8,128)} %widen_own.1.refs_0_), custom_call_target="tpu_custom_call", output_to_operand_aliasing={{}: (2, {})} | custom-call | flops 1048576 | bytes 3145728 | tf_op jit(solution)/shard_map/widen_other/pallas_call | solution.py:48
  (36 shorter events, 10.0 us)
Async XLA Ops:
  4.3 4.7 %collective-permute-start = (bf16[256,512]{1,0:T(8,128)(2,1)S(1)}, bf16[256,512]{1,0:T(8,128)(2,1)S(1)}, u32[]{:S(2)}, u32[]{:S(2)}) collective-permute-start(bf16[256,512]{1,0:T(8,128)(2,1)S(1)} %get-tuple-element.54), channel_id=1, source_target_pairs={{0,4},{4,0},{1,5},{5,1},{2,6},{6,2},{3,7},{7,3},{8,12},{12,8},{9,1... | collective-permute-start | bytes 786440 | tf_op jit(solution)/shard_map/ppermute | solution.py:334
  5.8 9.0 %collective-permute-start.1 = (bf16[256,512]{1,0:T(8,128)(2,1)S(1)}, bf16[256,512]{1,0:T(8,128)(2,1)S(1)}, u32[]{:S(2)}, u32[]{:S(2)}) collective-permute-start(bf16[256,512]{1,0:T(8,128)(2,1)S(1)} %get-tuple-element.55), channel_id=1, source_target_pairs={{4,8},{12,16},{20,24},{28,32},{36,40},{44,48},{52,56},{60,64},{68,... | collective-permute-start | bytes 786440 | tf_op jit(solution)/shard_map/ppermute | solution.py:340
  9.0 6.2 %collective-permute-start.2 = (bf16[128,512]{1,0:T(8,128)(2,1)S(1)}, bf16[128,512]{1,0:T(8,128)(2,1)S(1)}, u32[]{:S(2)}, u32[]{:S(2)}) collective-permute-start(bf16[128,512]{1,0:T(8,128)(2,1)S(1)} %get-tuple-element.57), channel_id=1, source_target_pairs={{0,1},{1,2},{2,3},{3,0},{4,5},{5,6},{6,7},{7,4},{8,9},{9,10},{10,1... | collective-permute-start | bytes 393224 | tf_op jit(solution)/shard_map/ppermute | solution.py:334
  10.8 11.7 %collective-permute-start.3 = (bf16[128,512]{1,0:T(8,128)(2,1)S(1)}, bf16[128,512]{1,0:T(8,128)(2,1)S(1)}, u32[]{:S(2)}, u32[]{:S(2)}) collective-permute-start(bf16[128,512]{1,0:T(8,128)(2,1)S(1)} %get-tuple-element.60), channel_id=1, source_target_pairs={{0,2},{1,3},{2,0},{3,1},{4,6},{5,7},{6,4},{7,5},{8,10},{9,11},{10,... | collective-permute-start | bytes 393224 | tf_op jit(solution)/shard_map/ppermute | solution.py:334
  14.1 8.4 %collective-permute-start.4 = (bf16[128,512]{1,0:T(8,128)(2,1)S(1)}, bf16[128,512]{1,0:T(8,128)(2,1)S(1)}, u32[]{:S(2)}, u32[]{:S(2)}) collective-permute-start(bf16[128,512]{1,0:T(8,128)(2,1)S(1)} %get-tuple-element.61), channel_id=1, source_target_pairs={{0,3},{1,0},{2,1},{3,2},{4,7},{5,4},{6,5},{7,6},{8,11},{9,8},{10,9... | collective-permute-start | bytes 393224 | tf_op jit(solution)/shard_map/ppermute | solution.py:334
  15.2 7.2 %collective-permute-start.5 = (bf16[64,512]{1,0:T(8,128)(2,1)S(1)}, bf16[64,512]{1,0:T(8,128)(2,1)S(1)}, u32[]{:S(2)}, u32[]{:S(2)}) collective-permute-start(bf16[64,512]{1,0:T(8,128)(2,1)S(1)} %get-tuple-element.62), channel_id=1, source_target_pairs={{0,1},{1,2},{2,3},{3,0},{4,5},{5,6},{6,7},{7,4},{8,9},{9,10},{10,1... | collective-permute-start | bytes 196616 | tf_op jit(solution)/shard_map/ppermute | solution.py:334
  15.6 6.9 %collective-permute-start.6 = (bf16[64,512]{1,0:T(8,128)(2,1)S(1)}, bf16[64,512]{1,0:T(8,128)(2,1)S(1)}, u32[]{:S(2)}, u32[]{:S(2)}) collective-permute-start(bf16[64,512]{1,0:T(8,128)(2,1)S(1)} %get-tuple-element.63), channel_id=1, source_target_pairs={{0,2},{1,3},{2,0},{3,1},{4,6},{5,7},{6,4},{7,5},{8,10},{9,11},{10,... | collective-permute-start | bytes 196616 | tf_op jit(solution)/shard_map/ppermute | solution.py:334
  19.7 3.1 %collective-permute-start.7 = (bf16[64,512]{1,0:T(8,128)(2,1)S(1)}, bf16[64,512]{1,0:T(8,128)(2,1)S(1)}, u32[]{:S(2)}, u32[]{:S(2)}) collective-permute-start(bf16[64,512]{1,0:T(8,128)(2,1)S(1)} %get-tuple-element.64), channel_id=1, source_target_pairs={{0,3},{1,0},{2,1},{3,2},{4,7},{5,4},{6,5},{7,6},{8,11},{9,8},{10,9... | collective-permute-start | bytes 196616 | tf_op jit(solution)/shard_map/ppermute | solution.py:334
  29.9 3.4 %collective-permute-start.8 = (bf16[1024,512]{1,0:T(8,128)(2,1)S(1)}, bf16[1024,512]{1,0:T(8,128)(2,1)S(1)}, u32[]{:S(2)}, u32[]{:S(2)}) collective-permute-start(bf16[1024,512]{1,0:T(8,128)(2,1)S(1)} %get-tuple-element.78), channel_id=1, source_target_pairs={{0,4},{4,0},{1,5},{5,1},{2,6},{6,2},{3,7},{7,3},{8,12},{12,8},{9,1... | collective-permute-start | bytes 3145736 | tf_op jit(solution)/shard_map/ppermute | solution.py:334
  34.4 33.4 %all-to-all-start = ((bf16[16,64,512]{2,1,0:T(8,128)(2,1)}), bf16[16,64,512]{2,1,0:T(8,128)(2,1)S(1)}, u32[]{:S(2)}, u32[]{:S(2)}) async-start(bf16[16,64,512]{2,1,0:T(8,128)(2,1)} %bitcast.4), calls=%async_computation | async-start | bytes 2097152 | tf_op jit(solution)/shard_map/all_to_all | solution.py:417
  43.7 3.8 %collective-permute-start.9 = (bf16[256,512]{1,0:T(8,128)(2,1)S(1)}, bf16[256,512]{1,0:T(8,128)(2,1)S(1)}, u32[]{:S(2)}, u32[]{:S(2)}) collective-permute-start(bf16[256,512]{1,0:T(8,128)(2,1)S(1)} %get-tuple-element.81), channel_id=1, source_target_pairs={{0,4},{4,0},{1,5},{5,1},{2,6},{6,2},{3,7},{7,3},{8,12},{12,8},{9,1... | collective-permute-start | bytes 786440 | tf_op jit(solution)/shard_map/ppermute | solution.py:334
  44.1 16.5 %collective-permute-start.10 = (bf16[256,512]{1,0:T(8,128)(2,1)S(1)}, bf16[256,512]{1,0:T(8,128)(2,1)S(1)}, u32[]{:S(2)}, u32[]{:S(2)}) collective-permute-start(bf16[256,512]{1,0:T(8,128)(2,1)S(1)} %get-tuple-element.82), channel_id=1, source_target_pairs={{4,8},{12,16},{20,24},{28,32},{36,40},{44,48},{52,56},{60,64},{68,... | collective-permute-start | bytes 786440 | tf_op jit(solution)/shard_map/ppermute | solution.py:340
  47.5 13.1 %collective-permute-start.11 = (bf16[128,512]{1,0:T(8,128)(2,1)S(1)}, bf16[128,512]{1,0:T(8,128)(2,1)S(1)}, u32[]{:S(2)}, u32[]{:S(2)}) collective-permute-start(bf16[128,512]{1,0:T(8,128)(2,1)S(1)} %get-tuple-element.84), channel_id=1, source_target_pairs={{0,3},{1,0},{2,1},{3,2},{4,7},{5,4},{6,5},{7,6},{8,11},{9,8},{10,9... | collective-permute-start | bytes 393224 | tf_op jit(solution)/shard_map/ppermute | solution.py:334
  49.6 13.5 %collective-permute-start.12 = (bf16[128,512]{1,0:T(8,128)(2,1)S(1)}, bf16[128,512]{1,0:T(8,128)(2,1)S(1)}, u32[]{:S(2)}, u32[]{:S(2)}) collective-permute-start(bf16[128,512]{1,0:T(8,128)(2,1)S(1)} %get-tuple-element.87), channel_id=1, source_target_pairs={{0,2},{1,3},{2,0},{3,1},{4,6},{5,7},{6,4},{7,5},{8,10},{9,11},{10,... | collective-permute-start | bytes 393224 | tf_op jit(solution)/shard_map/ppermute | solution.py:334
  49.9 13.3 %collective-permute-start.13 = (bf16[128,512]{1,0:T(8,128)(2,1)S(1)}, bf16[128,512]{1,0:T(8,128)(2,1)S(1)}, u32[]{:S(2)}, u32[]{:S(2)}) collective-permute-start(bf16[128,512]{1,0:T(8,128)(2,1)S(1)} %get-tuple-element.88), channel_id=1, source_target_pairs={{0,1},{1,2},{2,3},{3,0},{4,5},{5,6},{6,7},{7,4},{8,9},{9,10},{10,1... | collective-permute-start | bytes 393224 | tf_op jit(solution)/shard_map/ppermute | solution.py:334
  60.6 3.8 %collective-permute-start.14 = (bf16[64,512]{1,0:T(8,128)(2,1)S(1)}, bf16[64,512]{1,0:T(8,128)(2,1)S(1)}, u32[]{:S(2)}, u32[]{:S(2)}) collective-permute-start(bf16[64,512]{1,0:T(8,128)(2,1)S(1)} %get-tuple-element.89), channel_id=1, source_target_pairs={{0,3},{1,0},{2,1},{3,2},{4,7},{5,4},{6,5},{7,6},{8,11},{9,8},{10,9... | collective-permute-start | bytes 196616 | tf_op jit(solution)/shard_map/ppermute | solution.py:334
  62.5 4.7 %collective-permute-start.15 = (bf16[64,512]{1,0:T(8,128)(2,1)S(1)}, bf16[64,512]{1,0:T(8,128)(2,1)S(1)}, u32[]{:S(2)}, u32[]{:S(2)}) collective-permute-start(bf16[64,512]{1,0:T(8,128)(2,1)S(1)} %get-tuple-element.90), channel_id=1, source_target_pairs={{0,2},{1,3},{2,0},{3,1},{4,6},{5,7},{6,4},{7,5},{8,10},{9,11},{10,... | collective-permute-start | bytes 196616 | tf_op jit(solution)/shard_map/ppermute | solution.py:334
  62.8 5.0 %collective-permute-start.16 = (bf16[64,512]{1,0:T(8,128)(2,1)S(1)}, bf16[64,512]{1,0:T(8,128)(2,1)S(1)}, u32[]{:S(2)}, u32[]{:S(2)}) collective-permute-start(bf16[64,512]{1,0:T(8,128)(2,1)S(1)} %get-tuple-element.91), channel_id=1, source_target_pairs={{0,1},{1,2},{2,3},{3,0},{4,5},{5,6},{6,7},{7,4},{8,9},{9,10},{10,1... | collective-permute-start | bytes 196616 | tf_op jit(solution)/shard_map/ppermute | solution.py:334
  68.0 3.2 %collective-permute-start.19 = (bf16[64,512]{1,0:T(8,128)(2,1)S(1)}, bf16[64,512]{1,0:T(8,128)(2,1)S(1)}, u32[]{:S(2)}, u32[]{:S(2)}) collective-permute-start(bf16[64,512]{1,0:T(8,128)(2,1)S(1)} %reduce_sum.12.p0), channel_id=1, source_target_pairs={{0,3},{1,0},{2,1},{3,2},{4,7},{5,4},{6,5},{7,6},{8,11},{9,8},{10,9... | collective-permute-start | bytes 196616 | tf_op jit(solution)/shard_map/ppermute | solution.py:334
  68.3 4.6 %collective-permute-start.18 = (bf16[64,512]{1,0:T(8,128)(2,1)S(1)}, bf16[64,512]{1,0:T(8,128)(2,1)S(1)}, u32[]{:S(2)}, u32[]{:S(2)}) collective-permute-start(bf16[64,512]{1,0:T(8,128)(2,1)S(1)} %reduce_sum.12.p0), channel_id=1, source_target_pairs={{0,2},{1,3},{2,0},{3,1},{4,6},{5,7},{6,4},{7,5},{8,10},{9,11},{10,... | collective-permute-start | bytes 196616 | tf_op jit(solution)/shard_map/ppermute | solution.py:334
  69.3 4.3 %collective-permute-start.17 = (bf16[64,512]{1,0:T(8,128)(2,1)S(1)}, bf16[64,512]{1,0:T(8,128)(2,1)S(1)}, u32[]{:S(2)}, u32[]{:S(2)}) collective-permute-start(bf16[64,512]{1,0:T(8,128)(2,1)S(1)} %reduce_sum.12.p0), channel_id=1, source_target_pairs={{0,1},{1,2},{2,3},{3,0},{4,5},{5,6},{6,7},{7,4},{8,9},{9,10},{10,1... | collective-permute-start | bytes 196616 | tf_op jit(solution)/shard_map/ppermute | solution.py:334
  74.8 24.7 %all-to-all-start.1 = ((bf16[16,64,512]{2,1,0:T(8,128)(2,1)}), bf16[16,64,512]{2,1,0:T(8,128)(2,1)S(1)}, u32[]{:S(2)}, u32[]{:S(2)}) async-start(bf16[16,64,512]{2,1,0:T(8,128)(2,1)} %spread.1), calls=%async_computation.1 | async-start | bytes 2097152 | tf_op jit(solution)/shard_map/all_to_all | solution.py:427
  99.4 5.5 %collective-permute-start.20 = (bf16[1024,512]{1,0:T(8,128)(2,1)S(1)}, bf16[1024,512]{1,0:T(8,128)(2,1)S(1)}, u32[]{:S(2)}, u32[]{:S(2)}) collective-permute-start(bf16[1024,512]{1,0:T(8,128)(2,1)S(1)} %bitcast.6), channel_id=1, source_target_pairs={{0,4},{4,0},{1,5},{5,1},{2,6},{6,2},{3,7},{7,3},{8,12},{12,8},{9,1... | collective-permute-start | bytes 3145736 | tf_op jit(solution)/shard_map/ppermute | solution.py:334

commit v6 on v5

--- a/solution.py
+++ b/solution.py
@@ -70,7 +70,7 @@
     return [pltpu.VMEM(a.shape, a.dtype) for a in args] + [pltpu.SemaphoreType.DMA((len(args),))]
 
 
-def assemble(rows, near_first, near, far, own, m1, m2, m3, f1, f2, f3):
+def assemble(rows, near_first, near, far, own, *pieces):
     block = near.shape[0]
     cap = block // 4
     near_at = pl.multiple_of((1 - near_first) * (2 * block), block)
@@ -78,17 +78,20 @@
     rows[block : block + cap] = own[0:cap]
     rows[pl.ds(near_at, cap), :] = near[0:cap]
     rows[pl.ds(far_at, cap), :] = far[0:cap]
-    for k, (mixed, outer) in enumerate(((m1, f1), (m2, f2), (m3, f3)), 1):
+    for k in range(1, 4):
+        mixed, last = pieces[k - 1], pieces[len(pieces) - 4 + k]
         rows[block + k * cap : block + (k + 1) * cap] = mixed[0:cap]
         rows[pl.ds(near_at + k * cap, cap), :] = mixed[cap : 2 * cap]
-        rows[pl.ds(far_at + k * cap, cap), :] = outer[...]
+        rows[pl.ds(far_at + k * cap, cap), :] = last[last.shape[0] - cap :]
 
 
 def gather_body(sub_ref, core_ref, rows_hbm, gain_hbm, x_hbm, near_ref, far_ref, own_ref,
                 rows_ref, gain_ref, x_ref, sems):
     half = x_ref.shape[0] // 2
     cap = rows_ref.shape[3]
-    parts = [pl.ds(i * half, half) for i in range(2)]
+    core = core_ref[0]
+    firsts = [pl.multiple_of((1 - core) * half, half), pl.multiple_of(core * half, half)]
+    parts = [pl.ds(first, half) for first in firsts]
     copies = fetch(
         [rows_hbm, gain_hbm] + [x_hbm.at[p] for p in parts],
         [rows_ref, gain_ref] + [x_ref.at[p] for p in parts],
@@ -101,7 +104,12 @@
         jnp.int32, (cap, cap), 1
     )
     gain = gain_ref[...]
-    for step, (o, first, count) in enumerate(((0, 0, half), (2, half, half), (1, 0, 2 * half))):
+    steps = (
+        (2 - 2 * core, firsts[0], half, near_ref),
+        (2 * core, firsts[1], half, far_ref),
+        (1, 0, 2 * half, own_ref),
+    )
+    for step, (o, first, count, out_ref) in enumerate(steps):
         cols = []
         for k in range(4):
             s = lax.rem(me + k, 4)
@@ -112,20 +120,8 @@
         onehot = jnp.where(lanes == col, 1.0, 0.0).astype(BF16)
         if step < 2:
             copies[2 + step].wait()
-        wide = nn(onehot, x_ref[first : first + count, :])
-        normed = (wide * inv_rms(wide) * gain).astype(BF16)
-        if o == 1:
-            own_ref[...] = normed
-            continue
-        to_near = core_ref[0] == (2 - o) // 2
-
-        @pl.when(to_near)
-        def _():
-            near_ref[...] = normed
-
-        @pl.when(jnp.logical_not(to_near))
-        def _():
-            far_ref[...] = normed
+        wide = nn(onehot, x_ref[pl.ds(first, count), :])
+        out_ref[...] = (wide * inv_rms(wide) * gain).astype(BF16)
 
 
 def prep_body(sub_ref, mesh_hbm, gain_hbm, wq_hbm, wo_hbm, og_hbm, nbr_hbm, valid_hbm, bias_hbm,
@@ -218,18 +214,20 @@
     place(1, width, tn(att_ref[...], og_ref[...]).astype(BF16))
 
 
-def tail_body(core_ref, part_ref, att_ref, qg_ref, wkv_ref, og_ref, wo_hbm, wq_hbm, mesh_hbm,
-              gain_hbm, out_ref, grad_ref, near_ref, far_ref, own_ref, back_ref, wo_ref, wq_ref, mesh_ref, gain_ref, sems):
+def back_body(part_ref, wkv_ref, s0, s1, s2, s3):
+    cap = s0.shape[1]
+    for o in range(3):
+        rows = slice(o * 4 * cap, (o + 1) * 4 * cap)
+        back = nt(part_ref[rows, :], wkv_ref[...]).astype(BF16)
+        for k, piece in enumerate((s0, s1, s2, s3)):
+            piece[o] = back[k * cap : (k + 1) * cap]
+
+
+def mesh_body(att_ref, qg_ref, og_ref, wo_hbm, wq_hbm, mesh_hbm, gain_hbm, out_ref, grad_ref,
+              wo_ref, wq_ref, mesh_ref, gain_ref, sems):
     copies = fetch(
         (wo_hbm, wq_hbm, mesh_hbm, gain_hbm), (wo_ref, wq_ref, mesh_ref, gain_ref), sems
     )
-    block = own_ref.shape[0]
-    back_ref[...] = nt(part_ref[...], wkv_ref[...]).astype(BF16)
-    near_at = core_ref[0] * (2 * block)
-    far_at = (1 - core_ref[0]) * (2 * block)
-    near_ref[...] = back_ref[pl.ds(pl.multiple_of(near_at, block), block), :]
-    far_ref[...] = back_ref[pl.ds(pl.multiple_of(far_at, block), block), :]
-    own_ref[...] = back_ref[block : 2 * block, :]
     for copy in copies:
         copy.wait()
     wide = mesh_ref[...].astype(F32)
@@ -239,6 +237,14 @@
     grad_ref[...] = (og_ref[...].astype(F32) + back).astype(BF16)
 
 
+def pack_body(core_ref, p0, p1, p2, p3, near_ref, far_ref):
+    cap = p0.shape[1]
+    near = core_ref[0] * 2
+    for k, piece in enumerate((p0, p1, p2, p3)):
+        near_ref[k * cap : (k + 1) * cap, :] = piece[near]
+        far_ref[k * cap : (k + 1) * cap, :] = piece[2 - near]
+
+
 def mix_body(own, near, m1, m2, m3):
     cap = m1.shape[0] // 2
     for k, mixed in enumerate((m1, m2, m3), 1):
@@ -252,7 +258,7 @@
         piece[...] = block[k * cap : (k + 1) * cap]
 
 
-def grid_body(sub_ref, core_ref, near, far, own, m1, m2, m3, f1, f2, f3, rows_hbm, gain_hbm, x_hbm, out_hbm,
+def grid_body(sub_ref, core_ref, near, far, s0, s1, s2, s3, rows_hbm, gain_hbm, x_hbm, out_hbm,
               got, done_ref, done_sems, rows_ref, gain_ref, x_ref, sems):
     copies = fetch((rows_hbm, gain_hbm, x_hbm), (rows_ref, gain_ref, x_ref), sems)
     points = x_ref.shape[0]
@@ -260,7 +266,11 @@
     cap = rows_ref.shape[3]
     block = 4 * cap
     me = sub_ref[0]
-    assemble(got, core_ref[0], near, far, own, m1, m2, m3, f1, f2, f3)
+    core = core_ref[0]
+    got[pl.ds(pl.multiple_of((1 - core) * (2 * block), block), block), :] = near[...]
+    got[pl.ds(pl.multiple_of(core * (2 * block), block), block), :] = far[...]
+    for k, piece in enumerate((s0, s1, s2, s3)):
+        got[block + k * cap : block + (k + 1) * cap] = piece[1]
     for copy in copies:
         copy.wait()
     gain = gain_ref[...]
@@ -369,18 +379,15 @@
         held(send_rows, gain_g, grid_x)[:-1] + [pltpu.SemaphoreType.DMA((4,))],
     )
 
-    def exchange(near, far, own, sign):
-        far = swapped_far(far)
-        near = shifted(near, "gc", 1)
-        mixed = call(mix_body, [two] * 3, [VM] * 2, (own, near), 0, 1 << 20, "mix")
-        mixed = [shifted(m, "z", sign * k) for k, m in enumerate(mixed, 1)]
-        far, mixed[0] = lax.optimization_barrier((far, mixed[0]))
-        outer = call(split_body, [one] * 3, [VM], (far,), 0, 1 << 19, "split")
-        outer = [shifted(f, "z", sign * k) for k, f in enumerate(outer, 1)]
-        return near, far, own, *mixed, *outer
-
-    received = exchange(near, far, own, 1)
-    sub2, near = lax.optimization_barrier((sub1, received[1]))
+    far = swapped_far(far)
+    near = shifted(near, "gc", 1)
+    mixed = call(mix_body, [two] * 3, [VM] * 2, (own, near), 0, 1 << 20, "mix")
+    mixed = [shifted(m, "z", k) for k, m in enumerate(mixed, 1)]
+    far, mixed[0] = lax.optimization_barrier((far, mixed[0]))
+    outer = call(split_body, [one] * 3, [VM], (far,), 0, 1 << 19, "split")
+    outer = [shifted(f, "z", k) for k, f in enumerate(outer, 1)]
+    received = near, far, own, *mixed, *outer
+    sub2, far = lax.optimization_barrier((sub1, far))
     prep_args = (mesh_h, gain_m, w_query, w_out, out_grad, neighbours, valid, edge_bias)
     mesh_normed, queries, att_grad, dense = call(
         prep_body,
@@ -401,13 +408,11 @@
     )
 
     other = shifted(send, "gc", 1)
-    mesh_out, mesh_grad, near, far, back_own = call(
-        tail_body, [sds((nodes, width))] * 2 + [four] * 3, [SM] + [VM] * 5 + [HB] * 4,
-        (core1, part_grads, attended, query_grad, weights_near, og_near, w_out, w_query, mesh_h, gain_m),
-        1 << 30, 5 << 20, "tail",
-        [pltpu.VMEM((slots, width), BF16)] + held(w_out, w_query, mesh_h, gain_m),
-    )
-    other, near = lax.optimization_barrier((other, near))
+    s0, s1, s2, s3 = call(
+        back_body, [sds((3, cap, width))] * 4, [VM] * 2, (part_grads, weights_near),
+        1 << 30, 3 << 20, "back",
+    )
+    other, s1 = lax.optimization_barrier((other, s1))
     (own,) = call(
         pair_body, [sds((2 * width, width))], [VM] * 2, (keep, other), 1 << 20, 3 << 20, "pair",
         [pltpu.VMEM((2 * width, width), BF16), pltpu.SemaphoreType.DMA((4,))], [HB],
@@ -416,18 +421,31 @@
     share = 2 * width // plane
     parts = lax.all_to_all(own.reshape(plane, share, width), PLANE, 0, 0, tiled=True)
 
-    returned = exchange(near, far, back_own, -1)
-    parts, *returned = lax.optimization_barrier((parts, *returned))
+    attended, own = lax.optimization_barrier((attended, own))
+    mesh_out, mesh_grad = call(
+        mesh_body, [sds((nodes, width))] * 2, [VM] * 3 + [HB] * 4,
+        (attended, query_grad, og_near, w_out, w_query, mesh_h, gain_m), 1 << 28, 2 << 20, "mesh",
+        held(w_out, w_query, mesh_h, gain_m),
+    )
+    s1, s2, s3 = (shifted(s, "z", -k) for k, s in ((1, s1), (2, s2), (3, s3)))
+    s1, mesh_out = lax.optimization_barrier((s1, mesh_out))
+    near, far = call(
+        pack_body, [four] * 2, [SM] + [VM] * 4, (core1, s0, s1, s2, s3), 0, 1 << 20, "pack"
+    )
+    far = swapped_far(far)
+    near = shifted(near, "gc", 1)
+    parts, near = lax.optimization_barrier((parts, near))
     part = jnp.sum(parts.astype(F32), axis=0).astype(BF16)
     p1, p2, p3 = (shifted(part, "z", k) for k in (1, 2, 3))
+    p1, far = lax.optimization_barrier((p1, far))
     (spread,) = call(
         spread_body, [sds((plane, share, width))], [VM] * 4, (part, p1, p2, p3), 1 << 18, 1 << 20,
         "spread", [pltpu.VMEM((share, width), BF16), pltpu.SemaphoreType.DMA((plane,))], [HB],
     )
     mine = lax.all_to_all(spread, PLANE, 0, 0, tiled=True).reshape(2 * width, width)
     (grid_grad,) = call(
-        grid_body, [sds((points, width))], [SM] * 2 + [VM] * 9 + [HB] * 3,
-        (sub1, core1, *returned, send_rows, gain_g, grid_x),
+        grid_body, [sds((points, width))], [SM] * 2 + [VM] * 6 + [HB] * 3,
+        (sub1, core1, near, far, s0, s1, s2, s3, send_rows, gain_g, grid_x),
         1 << 30, 5 << 20, "grid_grad",
         [pltpu.VMEM((slots, width), BF16), pltpu.VMEM((points, width), BF16),
          pltpu.SemaphoreType.DMA((points // 256,))] + held(send_rows, gain_g, grid_x),

time: 107 us -> 97.3 us (0.909)
  starting transfers between devices: 47.6 us -> 42.1 us
  waiting for transfers between devices: 31.4 us -> 28 us
    ppermute x2, waiting for transfers between devices: 10.3 us -> 1.94 us  [swapped_far(): return lax.ppermute(block, SLAB, pairs + [(j, i) for i, j in pairs])]
    ppermute x19 -> x16, waiting for transfers between devices: 10.3 us -> 15.5 us  [shifted(): return lax.ppermute(block, axis, [(i, (i + k) % n) for i in range(n)])]
    all_to_all x1, starting transfers between devices: 9.39 us -> 6.19 us  [shards(): lax.all_to_all(spread, PLANE, 0, 0, tiled=True).reshape(2 * width, width)]
    ppermute x19 -> x16, starting transfers between devices: 22.4 us -> 20.7 us  [shifted(): return lax.ppermute(block, axis, [(i, (i + k) % n) for i in range(n)])]
  transfers between devices with their start and end apart: 23 -> 20, of which waited for: 11 -> 10; matrix products, arithmetic and copies ran while one was open for 0% -> 0% of each run, Pallas kernels for 11% -> 12%
where the time goes in v6:
time: 97.3 us; the launch traced here: 96.9 us
  starting transfers between devices  42.1 us (43%)
  waiting for transfers between devices  28 us (29%)
  Pallas kernels  25.6 us (26%)
  between operations  1.01 us (1%)
    pallas_call x13, Pallas kernels, call(): pl.pallas_call(body, out_shape=outs, in_specs=in_specs, out_specs=out_spe...  25.6 us
    ppermute x16, starting transfers between devices, shifted(): return lax.ppermute(block, axis, [(i, (i + k) % n) for i in range(n)])  20.7 us
    ppermute x16, waiting for transfers between devices, shifted(): return lax.ppermute(block, axis, [(i, (i + k) % n) for i in range(n)])  15.5 us
    all_to_all x1, waiting for transfers between devices, shards(): lax.all_to_all(spread, PLANE, 0, 0, tiled=True).reshape(2 * width, width)  10.6 us
    all_to_all x1, starting transfers between devices, shards(): lax.all_to_all(own.reshape(plane, share, width), PLANE, 0, 0, tiled=True)  8.94 us
    ppermute x2, starting transfers between devices, swapped_far(): return lax.ppermute(block, SLAB, pairs + [(j, i) for i, j in pairs])  6.29 us
    all_to_all x1, starting transfers between devices, shards(): lax.all_to_all(spread, PLANE, 0, 0, tiled=True).reshape(2 * width, width)  6.19 us
  transfers between devices with their start and end apart: 20, of which 10 were waited for; matrix products, arithmetic and copies ran while one was open for 0% of the time, Pallas kernels for 12%

profile of v6, /device:TPU:1, one launch (start us, length us, event | category | flops | bytes accessed | tf_op | source)
XLA Modules:
  0.0 96.9 jit_solution(13358066012147089261)
XLA Ops:
  0.6 3.0 %gather_rows.1 = (bf16[256,512]{1,0:T(8,128)(2,1)S(1)}, bf16[256,512]{1,0:T(8,128)(2,1)S(1)}, bf16[256,512]{1,0:T(8,128)(2,1)S(1)}) custom-call(s32[1]{0:T(128)} %bitcast.1.sub_ref, s32[1]{0:T(128)} %bitcast.core_ref, s32[1,3,4,64]{3,2,1,0:T(4,128)} %rows_hbm.3, f32[1,512]{1,0:T(1,128)} %bitcast.10, bf16[2048,512]{1,0:T(8,128)(2,1)} %x_hbm.3), custom_call_target="tpu_custom_call" | custom-call | flops 1073741824 | bytes 4194304 | tf_op jit(solution)/shard_map/gather_rows/pallas_call | solution.py:48
  3.6 1.5 %collective-permute-start = (bf16[256,512]{1,0:T(8,128)(2,1)S(1)}, bf16[256,512]{1,0:T(8,128)(2,1)S(1)}, u32[]{:S(2)}, u32[]{:S(2)}) collective-permute-start(bf16[256,512]{1,0:T(8,128)(2,1)S(1)} %get-tuple-element.46), channel_id=1, source_target_pairs={{0,4},{4,0},{1,5},{5,1},{2,6},{6,2},{3,7},{7,3},{8,12},{12,8},{9,1... | collective-permute-start | bytes 786440 | tf_op jit(solution)/shard_map/ppermute | solution.py:344
  5.1 3.2 %collective-permute-start.1 = (bf16[256,512]{1,0:T(8,128)(2,1)S(1)}, bf16[256,512]{1,0:T(8,128)(2,1)S(1)}, u32[]{:S(2)}, u32[]{:S(2)}) collective-permute-start(bf16[256,512]{1,0:T(8,128)(2,1)S(1)} %get-tuple-element.47), channel_id=1, source_target_pairs={{4,8},{12,16},{20,24},{28,32},{36,40},{44,48},{52,56},{60,64},{68,... | collective-permute-start | bytes 786440 | tf_op jit(solution)/shard_map/ppermute | solution.py:350
  8.3 1.7 %collective-permute-start.2 = (bf16[128,512]{1,0:T(8,128)(2,1)S(1)}, bf16[128,512]{1,0:T(8,128)(2,1)S(1)}, u32[]{:S(2)}, u32[]{:S(2)}) collective-permute-start(bf16[128,512]{1,0:T(8,128)(2,1)S(1)} %get-tuple-element.49), channel_id=1, source_target_pairs={{0,1},{1,2},{2,3},{3,0},{4,5},{5,6},{6,7},{7,4},{8,9},{9,10},{10,1... | collective-permute-start | bytes 393224 | tf_op jit(solution)/shard_map/ppermute | solution.py:344
  10.0 3.3 %collective-permute-start.3 = (bf16[128,512]{1,0:T(8,128)(2,1)S(1)}, bf16[128,512]{1,0:T(8,128)(2,1)S(1)}, u32[]{:S(2)}, u32[]{:S(2)}) collective-permute-start(bf16[128,512]{1,0:T(8,128)(2,1)S(1)} %get-tuple-element.52), channel_id=1, source_target_pairs={{0,2},{1,3},{2,0},{3,1},{4,6},{5,7},{6,4},{7,5},{8,10},{9,11},{10,... | collective-permute-start | bytes 393224 | tf_op jit(solution)/shard_map/ppermute | solution.py:344
  14.9 4.1 %collective-permute-start.6 = (bf16[64,512]{1,0:T(8,128)(2,1)S(1)}, bf16[64,512]{1,0:T(8,128)(2,1)S(1)}, u32[]{:S(2)}, u32[]{:S(2)}) collective-permute-start(bf16[64,512]{1,0:T(8,128)(2,1)S(1)} %get-tuple-element.55), channel_id=1, source_target_pairs={{0,2},{1,3},{2,0},{3,1},{4,6},{5,7},{6,4},{7,5},{8,10},{9,11},{10,... | collective-permute-start | bytes 196616 | tf_op jit(solution)/shard_map/ppermute | solution.py:344
  19.0 2.8 %prep.1 = (bf16[64,512]{1,0:T(8,128)(2,1)S(1)}, bf16[64,512]{1,0:T(8,128)(2,1)S(1)}, bf16[64,512]{1,0:T(8,128)(2,1)S(1)}, f32[4,64,768]{2,1,0:T(8,128)S(1)}) custom-call(s32[1]{0:T(128)} %bitcast.1.sub_ref, bf16[64,512]{1,0:T(8,128)(2,1)} %mesh_hbm.3, f32[1,512]{1,0:T(1,128)} %bitcast.8, bf16[512,512]{1,0:T(8,128)(2,1)} %wq_hbm.3, bf16[512,512]{1,0:T(8,128)(2,1)} %wo_hbm.3, ...), custom_call_target="tpu_custom_call" | custom-call | flops 1073741824 | bytes 8388608 | tf_op jit(solution)/shard_map/prep/pallas_call | solution.py:48
  22.1 7.2 %middle.1 = (bf16[1024,512]{1,0:T(8,128)(2,1)S(1)}, bf16[1024,512]{1,0:T(8,128)(2,1)S(1)}, bf16[768,1024]{1,0:T(8,128)(2,1)S(1)}, bf16[64,512]{1,0:T(8,128)(2,1)...) custom-call(s32[1]{0:T(128)} %bitcast.core_ref, ...), custom_call_target="tpu_custom_call" | custom-call | flops 3221225472 | bytes 8388608 | tf_op jit(solution)/shard_map/middle/pallas_call | solution.py:48
  30.4 1.6 %collective-permute-done.8.other_ref = bf16[1024,512]{1,0:T(8,128)(2,1)S(1)} collective-permute-done((bf16[1024,512]{1,0:T(8,128)(2,1)S(1)}, bf16[1024,512]{1,0:T(8,128)(2,1)S(1)}, u32[]{:S(2)}, u32[]{:S(2)}) %collective-permute-start.8) | collective-permute-done | bytes 1048608 | tf_op jit(solution)/shard_map/ppermute | solution.py:344
  33.1 8.9 %all-to-all-start = ((bf16[16,64,512]{2,1,0:T(8,128)(2,1)}), bf16[16,64,512]{2,1,0:T(8,128)(2,1)S(1)}, u32[]{:S(2)}, u32[]{:S(2)}) async-start(bf16[16,64,512]{2,1,0:T(8,128)(2,1)} %bitcast.4), calls=%async_computation | async-start | bytes 2097152 | tf_op jit(solution)/shard_map/all_to_all | solution.py:422
  42.0 1.9 %collective-permute-start.9 = (bf16[3,64,512]{2,1,0:T(8,128)(2,1)S(1)}, bf16[3,64,512]{2,1,0:T(8,128)(2,1)S(1)}, u32[]{:S(2)}, u32[]{:S(2)}) collective-permute-start(bf16[3,64,512]{2,1,0:T(8,128)(2,1)S(1)} %get-tuple-element.66), channel_id=1, source_target_pairs={{0,3},{1,0},{2,1},{3,2},{4,7},{5,4},{6,5},{7,6},{8,11},{9,8},{10,9... | collective-permute-start | bytes 589832 | tf_op jit(solution)/shard_map/ppermute | solution.py:344
  44.5 2.3 %mesh.1 = (bf16[64,512]{1,0:T(8,128)(2,1)}, bf16[64,512]{1,0:T(8,128)(2,1)}) custom-call(bf16[64,512]{1,0:T(8,128)(2,1)S(1)} %get-tuple-element.70.att_ref, bf16[64,512]{1,0:T(8,128)(2,1)S(1)} %get-tuple-element.71.qg_ref, bf16[64,512]{1,0:T(8,128)(2,1)S(1)} %get-tuple-element.72.og_ref, bf16[512,512]{1,0:T(8,128)(2,1)} %wo_hbm.3, bf16[512,512]{1,0:T(8,128)(2,1)} %wq_hbm.3, ...), custom_call_target="tpu_custom_call" | custom-call | flops 268435456 | bytes 2097152 | tf_op jit(solution)/shard_map/mesh/pallas_call | solution.py:48
  47.9 3.0 %collective-permute-done.10.p2.s2 = bf16[3,64,512]{2,1,0:T(8,128)(2,1)S(1)} collective-permute-done((bf16[3,64,512]{2,1,0:T(8,128)(2,1)S(1)}, bf16[3,64,512]{2,1,0:T(8,128)(2,1)S(1)}, u32[]{:S(2)}, u32[]{:S(2)}) %collective-permute-start.10) | collective-permute-done | bytes 196640 | tf_op jit(solution)/shard_map/ppermute | solution.py:344
  50.9 5.5 %collective-permute-done.11.p3.s3 = bf16[3,64,512]{2,1,0:T(8,128)(2,1)S(1)} collective-permute-done((bf16[3,64,512]{2,1,0:T(8,128)(2,1)S(1)}, bf16[3,64,512]{2,1,0:T(8,128)(2,1)S(1)}, u32[]{:S(2)}, u32[]{:S(2)}) %collective-permute-start.11) | collective-permute-done | bytes 196640 | tf_op jit(solution)/shard_map/ppermute | solution.py:344
  57.0 3.1 %collective-permute-start.14 = (bf16[256,512]{1,0:T(8,128)(2,1)S(1)}, bf16[256,512]{1,0:T(8,128)(2,1)S(1)}, u32[]{:S(2)}, u32[]{:S(2)}) collective-permute-start(bf16[256,512]{1,0:T(8,128)(2,1)S(1)} %get-tuple-element.82), channel_id=1, source_target_pairs={{4,8},{12,16},{20,24},{28,32},{36,40},{44,48},{52,56},{60,64},{68,... | collective-permute-start | bytes 786440 | tf_op jit(solution)/shard_map/ppermute | solution.py:350
  60.4 2.7 %collective-permute-start.16 = (bf16[64,512]{1,0:T(8,128)(2,1)S(1)}, bf16[64,512]{1,0:T(8,128)(2,1)S(1)}, u32[]{:S(2)}, u32[]{:S(2)}) collective-permute-start(bf16[64,512]{1,0:T(8,128)(2,1)S(1)} %reduce_sum.12.p0), channel_id=1, source_target_pairs={{0,3},{1,0},{2,1},{3,2},{4,7},{5,4},{6,5},{7,6},{8,11},{9,8},{10,9... | collective-permute-start | bytes 196616 | tf_op jit(solution)/shard_map/ppermute | solution.py:344
  63.0 1.9 %collective-permute-done.14.far = bf16[256,512]{1,0:T(8,128)(2,1)S(1)} collective-permute-done((bf16[256,512]{1,0:T(8,128)(2,1)S(1)}, bf16[256,512]{1,0:T(8,128)(2,1)S(1)}, u32[]{:S(2)}, u32[]{:S(2)}) %collective-permute-start.14) | collective-permute-done | bytes 262176 | tf_op jit(solution)/shard_map/ppermute | solution.py:350
  65.0 2.7 %collective-permute-done.15.p2 = bf16[64,512]{1,0:T(8,128)(2,1)S(1)} collective-permute-done((bf16[64,512]{1,0:T(8,128)(2,1)S(1)}, bf16[64,512]{1,0:T(8,128)(2,1)S(1)}, u32[]{:S(2)}, u32[]{:S(2)}) %collective-permute-start.15) | collective-permute-done | bytes 65568 | tf_op jit(solution)/shard_map/ppermute | solution.py:344
  68.8 6.2 %all-to-all-start.1 = ((bf16[16,64,512]{2,1,0:T(8,128)(2,1)}), bf16[16,64,512]{2,1,0:T(8,128)(2,1)S(1)}, u32[]{:S(2)}, u32[]{:S(2)}) async-start(bf16[16,64,512]{2,1,0:T(8,128)(2,1)} %spread.1), calls=%async_computation.1 | async-start | bytes 2097152 | tf_op jit(solution)/shard_map/all_to_all | solution.py:445
  75.0 4.4 %grid_grad.1 = bf16[2048,512]{1,0:T(8,128)(2,1)} custom-call(s32[1]{0:T(128)} %bitcast.1.sub_ref, s32[1]{0:T(128)} %bitcast.core_ref, bf16[256,512]{1,0:T(8,128)(2,1)S(1)} %collective-permute-done.12.near, bf16[256,512]{1,0:T(8,128)(2,1)S(1)} %collective-permute-done.14.far, bf16[3,64,512]{2,1,0:T(8,128)(2,1)S(1)} %get-tuple-element.76.p0.s0, ...), custom_call_target="tpu_custom_call" | custom-call | flops 1073741824 | bytes 5242880 | tf_op jit(solution)/shard_map/grid_grad/pallas_call | solution.py:48
  79.4 10.6 %all-to-all-done.1 = bf16[16,64,512]{2,1,0:T(8,128)(2,1)S(1)} async-done(((bf16[16,64,512]{2,1,0:T(8,128)(2,1)}), bf16[16,64,512]{2,1,0:T(8,128)(2,1)S(1)}, u32[]{:S(2)}, u32[]{:S(2)}) %all-to-all-start.1) | async-done | bytes 1048608 | tf_op jit(solution)/shard_map/all_to_all | solution.py:445
  90.0 3.1 %collective-permute-start.17 = (bf16[1024,512]{1,0:T(8,128)(2,1)S(1)}, bf16[1024,512]{1,0:T(8,128)(2,1)S(1)}, u32[]{:S(2)}, u32[]{:S(2)}) collective-permute-start(bf16[1024,512]{1,0:T(8,128)(2,1)S(1)} %bitcast.6), channel_id=1, source_target_pairs={{0,4},{4,0},{1,5},{5,1},{2,6},{6,2},{3,7},{7,3},{8,12},{12,8},{9,1... | collective-permute-start | bytes 3145736 | tf_op jit(solution)/shard_map/ppermute | solution.py:344
  93.1 1.4 %widen_own.1.refs_0_ = f32[4,512,512]{2,1,0:T(8,128)} custom-call(s32[1]{0:T(128)} %bitcast.core_ref, bf16[1024,512]{1,0:T(8,128)(2,1)S(1)} %bitcast.7), custom_call_target="tpu_custom_call" | custom-call | flops 1048576 | bytes 3145728 | tf_op jit(solution)/shard_map/widen_own/pallas_call | solution.py:48
  95.3 1.4 %widen_other.1 = f32[4,512,512]{2,1,0:T(8,128)} custom-call(s32[1]{0:T(128)} %bitcast.core_ref, bf16[1024,512]{1,0:T(8,128)(2,1)S(1)} %collective-permute-done.17.half_ref, f32[4,512,512]{2,1,0:T(8,128)} %widen_own.1.refs_0_), custom_call_target="tpu_custom_call", output_to_operand_aliasing={{}: (2, {})} | custom-call | flops 1048576 | bytes 3145728 | tf_op jit(solution)/shard_map/widen_other/pallas_call | solution.py:48
  (30 shorter events, 8.6 us)
Async XLA Ops:
  3.6 4.7 %collective-permute-start = (bf16[256,512]{1,0:T(8,128)(2,1)S(1)}, bf16[256,512]{1,0:T(8,128)(2,1)S(1)}, u32[]{:S(2)}, u32[]{:S(2)}) collective-permute-start(bf16[256,512]{1,0:T(8,128)(2,1)S(1)} %get-tuple-element.46), channel_id=1, source_target_pairs={{0,4},{4,0},{1,5},{5,1},{2,6},{6,2},{3,7},{7,3},{8,12},{12,8},{9,1... | collective-permute-start | bytes 786440 | tf_op jit(solution)/shard_map/ppermute | solution.py:344
  5.1 9.0 %collective-permute-start.1 = (bf16[256,512]{1,0:T(8,128)(2,1)S(1)}, bf16[256,512]{1,0:T(8,128)(2,1)S(1)}, u32[]{:S(2)}, u32[]{:S(2)}) collective-permute-start(bf16[256,512]{1,0:T(8,128)(2,1)S(1)} %get-tuple-element.47), channel_id=1, source_target_pairs={{4,8},{12,16},{20,24},{28,32},{36,40},{44,48},{52,56},{60,64},{68,... | collective-permute-start | bytes 786440 | tf_op jit(solution)/shard_map/ppermute | solution.py:350
  8.3 6.2 %collective-permute-start.2 = (bf16[128,512]{1,0:T(8,128)(2,1)S(1)}, bf16[128,512]{1,0:T(8,128)(2,1)S(1)}, u32[]{:S(2)}, u32[]{:S(2)}) collective-permute-start(bf16[128,512]{1,0:T(8,128)(2,1)S(1)} %get-tuple-element.49), channel_id=1, source_target_pairs={{0,1},{1,2},{2,3},{3,0},{4,5},{5,6},{6,7},{7,4},{8,9},{9,10},{10,1... | collective-permute-start | bytes 393224 | tf_op jit(solution)/shard_map/ppermute | solution.py:344
  10.0 11.7 %collective-permute-start.3 = (bf16[128,512]{1,0:T(8,128)(2,1)S(1)}, bf16[128,512]{1,0:T(8,128)(2,1)S(1)}, u32[]{:S(2)}, u32[]{:S(2)}) collective-permute-start(bf16[128,512]{1,0:T(8,128)(2,1)S(1)} %get-tuple-element.52), channel_id=1, source_target_pairs={{0,2},{1,3},{2,0},{3,1},{4,6},{5,7},{6,4},{7,5},{8,10},{9,11},{10,... | collective-permute-start | bytes 393224 | tf_op jit(solution)/shard_map/ppermute | solution.py:344
  13.3 8.4 %collective-permute-start.4 = (bf16[128,512]{1,0:T(8,128)(2,1)S(1)}, bf16[128,512]{1,0:T(8,128)(2,1)S(1)}, u32[]{:S(2)}, u32[]{:S(2)}) collective-permute-start(bf16[128,512]{1,0:T(8,128)(2,1)S(1)} %get-tuple-element.53), channel_id=1, source_target_pairs={{0,3},{1,0},{2,1},{3,2},{4,7},{5,4},{6,5},{7,6},{8,11},{9,8},{10,9... | collective-permute-start | bytes 393224 | tf_op jit(solution)/shard_map/ppermute | solution.py:344
  14.5 7.2 %collective-permute-start.5 = (bf16[64,512]{1,0:T(8,128)(2,1)S(1)}, bf16[64,512]{1,0:T(8,128)(2,1)S(1)}, u32[]{:S(2)}, u32[]{:S(2)}) collective-permute-start(bf16[64,512]{1,0:T(8,128)(2,1)S(1)} %get-tuple-element.54), channel_id=1, source_target_pairs={{0,1},{1,2},{2,3},{3,0},{4,5},{5,6},{6,7},{7,4},{8,9},{9,10},{10,1... | collective-permute-start | bytes 196616 | tf_op jit(solution)/shard_map/ppermute | solution.py:344
  14.9 6.9 %collective-permute-start.6 = (bf16[64,512]{1,0:T(8,128)(2,1)S(1)}, bf16[64,512]{1,0:T(8,128)(2,1)S(1)}, u32[]{:S(2)}, u32[]{:S(2)}) collective-permute-start(bf16[64,512]{1,0:T(8,128)(2,1)S(1)} %get-tuple-element.55), channel_id=1, source_target_pairs={{0,2},{1,3},{2,0},{3,1},{4,6},{5,7},{6,4},{7,5},{8,10},{9,11},{10,... | collective-permute-start | bytes 196616 | tf_op jit(solution)/shard_map/ppermute | solution.py:344
  19.0 3.1 %collective-permute-start.7 = (bf16[64,512]{1,0:T(8,128)(2,1)S(1)}, bf16[64,512]{1,0:T(8,128)(2,1)S(1)}, u32[]{:S(2)}, u32[]{:S(2)}) collective-permute-start(bf16[64,512]{1,0:T(8,128)(2,1)S(1)} %get-tuple-element.56), channel_id=1, source_target_pairs={{0,3},{1,0},{2,1},{3,2},{4,7},{5,4},{6,5},{7,6},{8,11},{9,8},{10,9... | collective-permute-start | bytes 196616 | tf_op jit(solution)/shard_map/ppermute | solution.py:344
  29.2 2.7 %collective-permute-start.8 = (bf16[1024,512]{1,0:T(8,128)(2,1)S(1)}, bf16[1024,512]{1,0:T(8,128)(2,1)S(1)}, u32[]{:S(2)}, u32[]{:S(2)}) collective-permute-start(bf16[1024,512]{1,0:T(8,128)(2,1)S(1)} %get-tuple-element.62), channel_id=1, source_target_pairs={{0,4},{4,0},{1,5},{5,1},{2,6},{6,2},{3,7},{7,3},{8,12},{12,8},{9,1... | collective-permute-start | bytes 3145736 | tf_op jit(solution)/shard_map/ppermute | solution.py:344
  33.1 27.1 %all-to-all-start = ((bf16[16,64,512]{2,1,0:T(8,128)(2,1)}), bf16[16,64,512]{2,1,0:T(8,128)(2,1)S(1)}, u32[]{:S(2)}, u32[]{:S(2)}) async-start(bf16[16,64,512]{2,1,0:T(8,128)(2,1)} %bitcast.4), calls=%async_computation | async-start | bytes 2097152 | tf_op jit(solution)/shard_map/all_to_all | solution.py:422
  42.0 5.9 %collective-permute-start.9 = (bf16[3,64,512]{2,1,0:T(8,128)(2,1)S(1)}, bf16[3,64,512]{2,1,0:T(8,128)(2,1)S(1)}, u32[]{:S(2)}, u32[]{:S(2)}) collective-permute-start(bf16[3,64,512]{2,1,0:T(8,128)(2,1)S(1)} %get-tuple-element.66), channel_id=1, source_target_pairs={{0,3},{1,0},{2,1},{3,2},{4,7},{5,4},{6,5},{7,6},{8,11},{9,8},{10,9... | collective-permute-start | bytes 589832 | tf_op jit(solution)/shard_map/ppermute | solution.py:344
  43.9 7.0 %collective-permute-start.10 = (bf16[3,64,512]{2,1,0:T(8,128)(2,1)S(1)}, bf16[3,64,512]{2,1,0:T(8,128)(2,1)S(1)}, u32[]{:S(2)}, u32[]{:S(2)}) collective-permute-start(bf16[3,64,512]{2,1,0:T(8,128)(2,1)S(1)} %get-tuple-element.78), channel_id=1, source_target_pairs={{0,2},{1,3},{2,0},{3,1},{4,6},{5,7},{6,4},{7,5},{8,10},{9,11},{10,... | collective-permute-start | bytes 589832 | tf_op jit(solution)/shard_map/ppermute | solution.py:344
  44.2 12.2 %collective-permute-start.11 = (bf16[3,64,512]{2,1,0:T(8,128)(2,1)S(1)}, bf16[3,64,512]{2,1,0:T(8,128)(2,1)S(1)}, u32[]{:S(2)}, u32[]{:S(2)}) collective-permute-start(bf16[3,64,512]{2,1,0:T(8,128)(2,1)S(1)} %get-tuple-element.79), channel_id=1, source_target_pairs={{0,1},{1,2},{2,3},{3,0},{4,5},{5,6},{6,7},{7,4},{8,9},{9,10},{10,1... | collective-permute-start | bytes 589832 | tf_op jit(solution)/shard_map/ppermute | solution.py:344
  56.4 3.7 %collective-permute-start.12 = (bf16[256,512]{1,0:T(8,128)(2,1)S(1)}, bf16[256,512]{1,0:T(8,128)(2,1)S(1)}, u32[]{:S(2)}, u32[]{:S(2)}) collective-permute-start(bf16[256,512]{1,0:T(8,128)(2,1)S(1)} %get-tuple-element.80), channel_id=1, source_target_pairs={{0,4},{4,0},{1,5},{5,1},{2,6},{6,2},{3,7},{7,3},{8,12},{12,8},{9,1... | collective-permute-start | bytes 786440 | tf_op jit(solution)/shard_map/ppermute | solution.py:344
  57.0 8.0 %collective-permute-start.14 = (bf16[256,512]{1,0:T(8,128)(2,1)S(1)}, bf16[256,512]{1,0:T(8,128)(2,1)S(1)}, u32[]{:S(2)}, u32[]{:S(2)}) collective-permute-start(bf16[256,512]{1,0:T(8,128)(2,1)S(1)} %get-tuple-element.82), channel_id=1, source_target_pairs={{4,8},{12,16},{20,24},{28,32},{36,40},{44,48},{52,56},{60,64},{68,... | collective-permute-start | bytes 786440 | tf_op jit(solution)/shard_map/ppermute | solution.py:350
  60.3 4.7 %collective-permute-start.13 = (bf16[64,512]{1,0:T(8,128)(2,1)S(1)}, bf16[64,512]{1,0:T(8,128)(2,1)S(1)}, u32[]{:S(2)}, u32[]{:S(2)}) collective-permute-start(bf16[64,512]{1,0:T(8,128)(2,1)S(1)} %reduce_sum.12.p0), channel_id=1, source_target_pairs={{0,1},{1,2},{2,3},{3,0},{4,5},{5,6},{6,7},{7,4},{8,9},{9,10},{10,1... | collective-permute-start | bytes 196616 | tf_op jit(solution)/shard_map/ppermute | solution.py:344
  60.4 4.6 %collective-permute-start.16 = (bf16[64,512]{1,0:T(8,128)(2,1)S(1)}, bf16[64,512]{1,0:T(8,128)(2,1)S(1)}, u32[]{:S(2)}, u32[]{:S(2)}) collective-permute-start(bf16[64,512]{1,0:T(8,128)(2,1)S(1)} %reduce_sum.12.p0), channel_id=1, source_target_pairs={{0,3},{1,0},{2,1},{3,2},{4,7},{5,4},{6,5},{7,6},{8,11},{9,8},{10,9... | collective-permute-start | bytes 196616 | tf_op jit(solution)/shard_map/ppermute | solution.py:344
  63.0 4.6 %collective-permute-start.15 = (bf16[64,512]{1,0:T(8,128)(2,1)S(1)}, bf16[64,512]{1,0:T(8,128)(2,1)S(1)}, u32[]{:S(2)}, u32[]{:S(2)}) collective-permute-start(bf16[64,512]{1,0:T(8,128)(2,1)S(1)} %reduce_sum.12.p0), channel_id=1, source_target_pairs={{0,2},{1,3},{2,0},{3,1},{4,6},{5,7},{6,4},{7,5},{8,10},{9,11},{10,... | collective-permute-start | bytes 196616 | tf_op jit(solution)/shard_map/ppermute | solution.py:344
  68.8 21.2 %all-to-all-start.1 = ((bf16[16,64,512]{2,1,0:T(8,128)(2,1)}), bf16[16,64,512]{2,1,0:T(8,128)(2,1)S(1)}, u32[]{:S(2)}, u32[]{:S(2)}) async-start(bf16[16,64,512]{2,1,0:T(8,128)(2,1)} %spread.1), calls=%async_computation.1 | async-start | bytes 2097152 | tf_op jit(solution)/shard_map/all_to_all | solution.py:445
  90.0 5.4 %collective-permute-start.17 = (bf16[1024,512]{1,0:T(8,128)(2,1)S(1)}, bf16[1024,512]{1,0:T(8,128)(2,1)S(1)}, u32[]{:S(2)}, u32[]{:S(2)}) collective-permute-start(bf16[1024,512]{1,0:T(8,128)(2,1)S(1)} %bitcast.6), channel_id=1, source_target_pairs={{0,4},{4,0},{1,5},{5,1},{2,6},{6,2},{3,7},{7,3},{8,12},{12,8},{9,1... | collective-permute-start | bytes 3145736 | tf_op jit(solution)/shard_map/ppermute | solution.py:344

commit v7 on v6

--- a/solution.py
+++ b/solution.py
@@ -124,17 +124,26 @@
         out_ref[...] = (wide * inv_rms(wide) * gain).astype(BF16)
 
 
-def prep_body(sub_ref, mesh_hbm, gain_hbm, wq_hbm, wo_hbm, og_hbm, nbr_hbm, valid_hbm, bias_hbm,
-              normed_ref, q_ref, ag_ref, dense_ref, inv_ref, edge_ref,
-              nbr_ref, valid_ref, bias_ref, mesh_ref, gain_ref, wq_ref, wo_ref, og_ref, sems):
+def mesh_in_body(mesh_hbm, gain_hbm, wq_hbm, wo_hbm, og_hbm, normed_ref, q_ref, ag_ref, og_ref,
+                 mesh_ref, gain_ref, wq_ref, wo_ref, sems):
     copies = fetch(
-        (nbr_hbm, valid_hbm, bias_hbm, mesh_hbm, gain_hbm, wq_hbm, wo_hbm, og_hbm),
-        (nbr_ref, valid_ref, bias_ref, mesh_ref, gain_ref, wq_ref, wo_ref, og_ref),
-        sems,
-    )
+        (mesh_hbm, gain_hbm, wq_hbm, wo_hbm, og_hbm), (mesh_ref, gain_ref, wq_ref, wo_ref, og_ref), sems
+    )
+    for copy in copies:
+        copy.wait()
+    wide = mesh_ref[...].astype(F32)
+    normed = (wide * inv_rms(wide) * gain_ref[...]).astype(BF16)
+    normed_ref[...] = normed
+    q_ref[...] = (nn(normed, wq_ref[...]) * (128 ** -0.5)).astype(BF16)
+    ag_ref[...] = nt(og_ref[...], wo_ref[...]).astype(BF16)
+
+
+def slots_body(sub_ref, nbr_hbm, valid_hbm, bias_hbm, dense_ref, inv_ref, edge_ref,
+               nbr_ref, valid_ref, bias_ref, sems):
+    copies = fetch((nbr_hbm, valid_hbm, bias_hbm), (nbr_ref, valid_ref, bias_ref), sems)
     heads, nodes, slots = dense_ref.shape
     fan = nbr_ref.shape[1]
-    for copy in copies[:3]:
+    for copy in copies:
         copy.wait()
     slot = nbr_ref[...]
     slot = (slot & ~192) | (((sub_ref[0] - (slot >> 6)) & 3) << 6)
@@ -156,23 +165,14 @@
         for h in range(heads):
             got = jnp.take_along_axis(edge_ref[h], at, axis=1, mode="promise_in_bounds")
             dense_ref[h, :, b * 128 : (b + 1) * 128] = jnp.where(here, got, ABSENT)
-    for copy in copies[3:]:
-        copy.wait()
-    wide = mesh_ref[...].astype(F32)
-    normed = (wide * inv_rms(wide) * gain_ref[...]).astype(BF16)
-    normed_ref[...] = normed
-    q_ref[...] = (nn(normed, wq_ref[...]) * (128 ** -0.5)).astype(BF16)
-    ag_ref[...] = nt(og_ref[...], wo_ref[...]).astype(BF16)
-
-
-def middle_body(core_ref, near, far, own, m1, m2, m3, f1, f2, f3, q_ref, ag_ref, mn_ref, bias_ref,
-                wk_hbm, wv_hbm, og_hbm, keep_ref, send_ref, part_ref, att_ref, qg_ref,
-                wkv_ref, og_ref, rows, keys, vals, sems):
+
+
+def middle_body(core_ref, near, far, own, m1, m2, m3, f1, f2, f3, q_ref, ag_ref, mn_ref, og_ref,
+                bias_ref, wk_hbm, wv_hbm, send_ref, part_ref, att_ref, qg_ref, wkv_ref, rows,
+                keys, vals, sems):
     width = q_ref.shape[1]
     copies = fetch(
-        (wk_hbm, wv_hbm, og_hbm),
-        (wkv_ref.at[:, pl.ds(0, width)], wkv_ref.at[:, pl.ds(width, width)], og_ref),
-        sems,
+        (wk_hbm, wv_hbm), (wkv_ref.at[:, pl.ds(0, width)], wkv_ref.at[:, pl.ds(width, width)]), sems
     )
     heads = bias_ref.shape[0]
     core = core_ref[0]
@@ -180,7 +180,6 @@
     copies[0].wait()
     keys[...] = nn(rows[...], wkv_ref[:, :width]).astype(BF16)
     copies[1].wait()
-    copies[2].wait()
     vals[...] = nn(rows[...], wkv_ref[:, width:]).astype(BF16)
     for h in range(heads):
         at = slice(h * 128, (h + 1) * 128)
@@ -197,21 +196,21 @@
         qg_ref[:, at] = (nn(sg, kh) * (128 ** -0.5)).astype(BF16)
         part_ref[:, at] = tn(sg, q).astype(BF16)
         part_ref[:, width + h * 128 : width + (h + 1) * 128] = tn(probs_b, ag).astype(BF16)
-
-    def place(half, row, value):
-        @pl.when(core == half)
-        def _():
-            keep_ref[row : row + width, :] = value
-
-        @pl.when(core != half)
-        def _():
-            send_ref[row : row + width, :] = value
-
-    both = tn(rows[...], part_ref[...]).astype(BF16)
-    place(0, 0, tn(mn_ref[...], qg_ref[...]).astype(BF16))
-    place(0, width, both[:, :width])
-    place(1, 0, both[:, width:])
-    place(1, width, tn(att_ref[...], og_ref[...]).astype(BF16))
+    half_grads(1 - core, send_ref, rows, part_ref, mn_ref, qg_ref, att_ref, og_ref)
+
+
+def half_grads(half, out_ref, rows, part_ref, mn_ref, qg_ref, att_ref, og_ref):
+    width = mn_ref.shape[1]
+    first = half == 0
+    left = jnp.where(first, mn_ref[...].astype(F32), att_ref[...].astype(F32)).astype(BF16)
+    right = jnp.where(first, qg_ref[...].astype(F32), og_ref[...].astype(F32)).astype(BF16)
+    columns = pl.ds(pl.multiple_of(half * width, width), width)
+    out_ref[0:width] = tn(left, right).astype(BF16)
+    out_ref[width : 2 * width] = tn(rows[...], part_ref[:, columns]).astype(BF16)
+
+
+def keep_body(core_ref, rows, part_ref, mn_ref, qg_ref, att_ref, og_ref, keep_ref):
+    half_grads(core_ref[0], keep_ref, rows, part_ref, mn_ref, qg_ref, att_ref, og_ref)
 
 
 def back_body(part_ref, wkv_ref, s0, s1, s2, s3):
@@ -301,14 +300,16 @@
 def widen_body(turn, core_ref, half_ref, *refs):
     out_hbm, wide, sems = refs[-3:]
     count, width, _ = wide.shape
-    first = (core_ref[0] ^ turn) * count
+    half = core_ref[0] ^ turn
     part = width // 2
     copies = []
     for i in range(2 * count):
         m, rows = i // 2, pl.ds((i % 2) * part, part)
         wide[m, rows, :] = half_ref[i * part : (i + 1) * part, :].astype(F32)
         copies.append(
-            pltpu.make_async_copy(wide.at[m, rows], out_hbm.at[first + m, rows], sems.at[i])
+            pltpu.make_async_copy(
+                wide.at[m, rows], out_hbm.at[lax.select(half == 0, m, 3 - m), rows], sems.at[i]
+            )
         )
         copies[-1].start()
     for copy in copies:
@@ -383,36 +384,41 @@
     near = shifted(near, "gc", 1)
     mixed = call(mix_body, [two] * 3, [VM] * 2, (own, near), 0, 1 << 20, "mix")
     mixed = [shifted(m, "z", k) for k, m in enumerate(mixed, 1)]
-    far, mixed[0] = lax.optimization_barrier((far, mixed[0]))
+    mesh_normed, queries, att_grad, og_near = call(
+        mesh_in_body, [sds((nodes, width))] * 4, [HB] * 5, (mesh_h, gain_m, w_query, w_out, out_grad),
+        1 << 28, 2 << 20, "mesh_in", held(mesh_h, gain_m, w_query, w_out)[:-1] + [pltpu.SemaphoreType.DMA((5,))],
+    )
+    far, mixed[0], queries = lax.optimization_barrier((far, mixed[0], queries))
     outer = call(split_body, [one] * 3, [VM], (far,), 0, 1 << 19, "split")
     outer = [shifted(f, "z", k) for k, f in enumerate(outer, 1)]
     received = near, far, own, *mixed, *outer
     sub2, far = lax.optimization_barrier((sub1, far))
-    prep_args = (mesh_h, gain_m, w_query, w_out, out_grad, neighbours, valid, edge_bias)
-    mesh_normed, queries, att_grad, dense = call(
-        prep_body,
-        [sds((nodes, width))] * 3 + [sds((heads, nodes, slots), F32)],
-        [SM] + [HB] * 8, (sub2, *prep_args), 1 << 30, 8 << 20, "prep",
+    (dense,) = call(
+        slots_body, [sds((heads, nodes, slots), F32)], [SM] + [HB] * 3,
+        (sub2, neighbours, valid, edge_bias), 1 << 30, 8 << 20, "slots",
         [pltpu.VMEM((nodes * 8, 128), F32), pltpu.VMEM((heads, nodes, 128), F32)]
-        + held(neighbours, valid, edge_bias, mesh_h, gain_m, w_query, w_out, out_grad),
-    )
-    keep, send, part_grads, attended, query_grad, weights_near, og_near = call(
+        + held(neighbours, valid, edge_bias),
+    )
+    send, part_grads, attended, query_grad, weights_near, rows = call(
         middle_body,
-        [sds((2 * width, width))] * 2 + [sds((slots, 2 * width))] + [sds((nodes, width))] * 2
-        + [sds((width, 2 * width)), sds((nodes, width))],
-        [SM] + [VM] * 13 + [HB] * 3,
-        (core1, *received, queries, att_grad, mesh_normed, dense, w_key, w_value,
-         out_grad),
+        [sds((2 * width, width)), sds((slots, 2 * width))] + [sds((nodes, width))] * 2
+        + [sds((width, 2 * width)), sds((slots, width))],
+        [SM] + [VM] * 14 + [HB] * 2,
+        (core1, *received, queries, att_grad, mesh_normed, og_near, dense, w_key, w_value),
         3 << 30, 8 << 20, "middle",
-        [pltpu.VMEM((slots, width), BF16)] * 3 + [pltpu.SemaphoreType.DMA((3,))],
+        [pltpu.VMEM((slots, width), BF16)] * 2 + [pltpu.SemaphoreType.DMA((2,))],
     )
 
     other = shifted(send, "gc", 1)
+    (keep,) = call(
+        keep_body, [sds((2 * width, width))], [SM] + [VM] * 6,
+        (core1, rows, part_grads, mesh_normed, query_grad, attended, og_near), 1 << 29, 3 << 20, "keep",
+    )
     s0, s1, s2, s3 = call(
         back_body, [sds((3, cap, width))] * 4, [VM] * 2, (part_grads, weights_near),
         1 << 30, 3 << 20, "back",
     )
-    other, s1 = lax.optimization_barrier((other, s1))
+    other, s1, keep = lax.optimization_barrier((other, s1, keep))
     (own,) = call(
         pair_body, [sds((2 * width, width))], [VM] * 2, (keep, other), 1 << 20, 3 << 20, "pair",
         [pltpu.VMEM((2 * width, width), BF16), pltpu.SemaphoreType.DMA((4,))], [HB],
@@ -428,16 +434,16 @@
         held(w_out, w_query, mesh_h, gain_m),
     )
     s1, s2, s3 = (shifted(s, "z", -k) for k, s in ((1, s1), (2, s2), (3, s3)))
-    s1, mesh_out = lax.optimization_barrier((s1, mesh_out))
+    s1, parts, mesh_out = lax.optimization_barrier((s1, parts, mesh_out))
+    part = jnp.sum(parts.astype(F32), axis=0).astype(BF16)
+    part, s0 = lax.optimization_barrier((part, s0))
     near, far = call(
         pack_body, [four] * 2, [SM] + [VM] * 4, (core1, s0, s1, s2, s3), 0, 1 << 20, "pack"
     )
     far = swapped_far(far)
     near = shifted(near, "gc", 1)
-    parts, near = lax.optimization_barrier((parts, near))
-    part = jnp.sum(parts.astype(F32), axis=0).astype(BF16)
     p1, p2, p3 = (shifted(part, "z", k) for k in (1, 2, 3))
-    p1, far = lax.optimization_barrier((p1, far))
+    p1, near, far = lax.optimization_barrier((p1, near, far))
     (spread,) = call(
         spread_body, [sds((plane, share, width))], [VM] * 4, (part, p1, p2, p3), 1 << 18, 1 << 20,
         "spread", [pltpu.VMEM((share, width), BF16), pltpu.SemaphoreType.DMA((plane,))], [HB],

time: 97.3 us -> 99.5 us (1.023)
  Pallas kernels: 25.6 us -> 26.6 us
    all_to_all x1, waiting for transfers between devices: 0.01 us -> 9.15 us  [shards(): lax.all_to_all(own.reshape(plane, share, width), PLANE, 0, 0, tiled=True)]
    ppermute x16, waiting for transfers between devices: 15.5 us -> 7.64 us  [shifted(): return lax.ppermute(block, axis, [(i, (i + k) % n) for i in range(n)])]
    ppermute x16, starting transfers between devices: 20.7 us -> 24.3 us  [shifted(): return lax.ppermute(block, axis, [(i, (i + k) % n) for i in range(n)])]
    all_to_all x1, starting transfers between devices: 8.94 us -> 7.79 us  [shards(): lax.all_to_all(own.reshape(plane, share, width), PLANE, 0, 0, tiled=True)]
    ppermute x2, starting transfers between devices: 6.29 us -> 5.28 us  [swapped_far(): return lax.ppermute(block, SLAB, pairs + [(j, i) for i, j in pairs])]
    pallas_call x13 -> x15, Pallas kernels: 25.6 us -> 26.6 us  [call(): pl.pallas_call(body, out_shape=outs, in_specs=in_specs, out_specs=out_spe...]
  transfers between devices with their start and end apart: 20 -> 20, of which waited for: 10 -> 10; matrix products, arithmetic and copies ran while one was open for 0% -> 0% of each run, Pallas kernels for 12% -> 14%
where the time goes in v7:
time: 99.5 us; the launch traced here: 99 us
  starting transfers between devices  42.6 us (43%)
  waiting for transfers between devices  28.6 us (29%)
  Pallas kernels  26.6 us (27%)
  between operations  1.02 us (1%)
    pallas_call x15, Pallas kernels, call(): pl.pallas_call(body, out_shape=outs, in_specs=in_specs, out_specs=out_spe...  26.6 us
    ppermute x16, starting transfers between devices, shifted(): return lax.ppermute(block, axis, [(i, (i + k) % n) for i in range(n)])  24.3 us
    all_to_all x1, waiting for transfers between devices, shards(): lax.all_to_all(spread, PLANE, 0, 0, tiled=True).reshape(2 * width, width)  10.6 us
    all_to_all x1, waiting for transfers between devices, shards(): lax.all_to_all(own.reshape(plane, share, width), PLANE, 0, 0, tiled=True)  9.15 us
    all_to_all x1, starting transfers between devices, shards(): lax.all_to_all(own.reshape(plane, share, width), PLANE, 0, 0, tiled=True)  7.79 us
    ppermute x16, waiting for transfers between devices, shifted(): return lax.ppermute(block, axis, [(i, (i + k) % n) for i in range(n)])  7.64 us
    ppermute x2, starting transfers between devices, swapped_far(): return lax.ppermute(block, SLAB, pairs + [(j, i) for i, j in pairs])  5.28 us
    all_to_all x1, starting transfers between devices, shards(): lax.all_to_all(spread, PLANE, 0, 0, tiled=True).reshape(2 * width, width)  5.27 us
  transfers between devices with their start and end apart: 20, of which 10 were waited for; matrix products, arithmetic and copies ran while one was open for 0% of the time, Pallas kernels for 14%

profile of v7, /device:TPU:1, one launch (start us, length us, event | category | flops | bytes accessed | tf_op | source)
XLA Modules:
  0.0 99.0 jit_solution(3173676521777849936)
XLA Ops:
  0.6 3.0 %gather_rows.1 = (bf16[256,512]{1,0:T(8,128)(2,1)S(1)}, bf16[256,512]{1,0:T(8,128)(2,1)S(1)}, bf16[256,512]{1,0:T(8,128)(2,1)S(1)}) custom-call(s32[1]{0:T(128)} %bitcast.1.sub_ref, s32[1]{0:T(128)} %bitcast.core_ref, s32[1,3,4,64]{3,2,1,0:T(4,128)} %rows_hbm.3, f32[1,512]{1,0:T(1,128)} %bitcast.10, bf16[2048,512]{1,0:T(8,128)(2,1)} %x_hbm.3), custom_call_target="tpu_custom_call" | custom-call | flops 1073741824 | bytes 4194304 | tf_op jit(solution)/shard_map/gather_rows/pallas_call | solution.py:48
  3.6 1.5 %collective-permute-start = (bf16[256,512]{1,0:T(8,128)(2,1)S(1)}, bf16[256,512]{1,0:T(8,128)(2,1)S(1)}, u32[]{:S(2)}, u32[]{:S(2)}) collective-permute-start(bf16[256,512]{1,0:T(8,128)(2,1)S(1)} %get-tuple-element.49), channel_id=1, source_target_pairs={{0,4},{4,0},{1,5},{5,1},{2,6},{6,2},{3,7},{7,3},{8,12},{12,8},{9,1... | collective-permute-start | bytes 786440 | tf_op jit(solution)/shard_map/ppermute | solution.py:345
  5.1 3.2 %collective-permute-start.1 = (bf16[256,512]{1,0:T(8,128)(2,1)S(1)}, bf16[256,512]{1,0:T(8,128)(2,1)S(1)}, u32[]{:S(2)}, u32[]{:S(2)}) collective-permute-start(bf16[256,512]{1,0:T(8,128)(2,1)S(1)} %get-tuple-element.50), channel_id=1, source_target_pairs={{4,8},{12,16},{20,24},{28,32},{36,40},{44,48},{52,56},{60,64},{68,... | collective-permute-start | bytes 786440 | tf_op jit(solution)/shard_map/ppermute | solution.py:351
  8.3 1.7 %collective-permute-start.2 = (bf16[128,512]{1,0:T(8,128)(2,1)S(1)}, bf16[128,512]{1,0:T(8,128)(2,1)S(1)}, u32[]{:S(2)}, u32[]{:S(2)}) collective-permute-start(bf16[128,512]{1,0:T(8,128)(2,1)S(1)} %get-tuple-element.52), channel_id=1, source_target_pairs={{0,1},{1,2},{2,3},{3,0},{4,5},{5,6},{6,7},{7,4},{8,9},{9,10},{10,1... | collective-permute-start | bytes 393224 | tf_op jit(solution)/shard_map/ppermute | solution.py:345
  10.0 3.3 %collective-permute-start.3 = (bf16[128,512]{1,0:T(8,128)(2,1)S(1)}, bf16[128,512]{1,0:T(8,128)(2,1)S(1)}, u32[]{:S(2)}, u32[]{:S(2)}) collective-permute-start(bf16[128,512]{1,0:T(8,128)(2,1)S(1)} %get-tuple-element.56), channel_id=1, source_target_pairs={{0,2},{1,3},{2,0},{3,1},{4,6},{5,7},{6,4},{7,5},{8,10},{9,11},{10,... | collective-permute-start | bytes 393224 | tf_op jit(solution)/shard_map/ppermute | solution.py:345
  14.1 1.7 %mesh_in.1 = (bf16[64,512]{1,0:T(8,128)(2,1)S(1)}, bf16[64,512]{1,0:T(8,128)(2,1)S(1)}, bf16[64,512]{1,0:T(8,128)(2,1)S(1)}, bf16[64,512]{1,0:T(8,128)(2,1)S(1)}) custom-call(bf16[64,512]{1,0:T(8,128)(2,1)} %mesh_hbm.3, f32[1,512]{1,0:T(1,128)} %bitcast.8, bf16[512,512]{1,0:T(8,128)(2,1)} %wq_hbm.3, bf16[512,512]{1,0:T(8,128)(2,1)} %wo_hbm.3, ...), custom_call_target="tpu_custom_call" | custom-call | flops 268435456 | bytes 2097152 | tf_op jit(solution)/shard_map/mesh_in/pallas_call | solution.py:48
  16.7 2.3 %collective-permute-start.6 = (bf16[64,512]{1,0:T(8,128)(2,1)S(1)}, bf16[64,512]{1,0:T(8,128)(2,1)S(1)}, u32[]{:S(2)}, u32[]{:S(2)}) collective-permute-start(bf16[64,512]{1,0:T(8,128)(2,1)S(1)} %get-tuple-element.59), channel_id=1, source_target_pairs={{0,2},{1,3},{2,0},{3,1},{4,6},{5,7},{6,4},{7,5},{8,10},{9,11},{10,... | collective-permute-start | bytes 196616 | tf_op jit(solution)/shard_map/ppermute | solution.py:345
  19.1 2.3 %slots.1.bias_ref = f32[4,64,768]{2,1,0:T(8,128)S(1)} custom-call(s32[1]{0:T(128)} %bitcast.1.sub_ref, s32[64,96]{1,0:T(8,128)} %nbr_hbm.1, s32[64,96]{1,0:T(8,128)} %valid_hbm.1, f32[64,384]{1,0:T(8,128)} %bias_hbm.1), custom_call_target="tpu_custom_call" | custom-call | flops 1073741824 | bytes 8388608 | tf_op jit(solution)/shard_map/slots/pallas_call | solution.py:48
  23.2 6.2 %middle.1 = (bf16[1024,512]{1,0:T(8,128)(2,1)S(1)}, bf16[768,1024]{1,0:T(8,128)(2,1)S(1)}, bf16[64,512]{1,0:T(8,128)(2,1)S(1)}, bf16[64,512]{1,0:T(8,128)(2,1)S(...) custom-call(s32[1]{0:T(128)} %bitcast.core_ref, bf16[256,512]{1,0:T(8,128)(2,1)S(1)} %collective-permute-done.near, ...), custom_call_target="tpu_custom_call" | custom-call | flops 3221225472 | bytes 8388608 | tf_op jit(solution)/shard_map/middle/pallas_call | solution.py:48
  33.2 7.8 %all-to-all-start = ((bf16[16,64,512]{2,1,0:T(8,128)(2,1)}), bf16[16,64,512]{2,1,0:T(8,128)(2,1)S(1)}, u32[]{:S(2)}, u32[]{:S(2)}) async-start(bf16[16,64,512]{2,1,0:T(8,128)(2,1)} %bitcast.4), calls=%async_computation | async-start | bytes 2097152 | tf_op jit(solution)/shard_map/all_to_all | solution.py:428
  41.0 1.9 %collective-permute-start.9 = (bf16[3,64,512]{2,1,0:T(8,128)(2,1)S(1)}, bf16[3,64,512]{2,1,0:T(8,128)(2,1)S(1)}, u32[]{:S(2)}, u32[]{:S(2)}) collective-permute-start(bf16[3,64,512]{2,1,0:T(8,128)(2,1)S(1)} %get-tuple-element.73), channel_id=1, source_target_pairs={{0,3},{1,0},{2,1},{3,2},{4,7},{5,4},{6,5},{7,6},{8,11},{9,8},{10,9... | collective-permute-start | bytes 589832 | tf_op jit(solution)/shard_map/ppermute | solution.py:345
  43.5 2.3 %mesh.1 = (bf16[64,512]{1,0:T(8,128)(2,1)}, bf16[64,512]{1,0:T(8,128)(2,1)}) custom-call(bf16[64,512]{1,0:T(8,128)(2,1)S(1)} %get-tuple-element.76.att_ref, bf16[64,512]{1,0:T(8,128)(2,1)S(1)} %get-tuple-element.71.qg_ref, bf16[64,512]{1,0:T(8,128)(2,1)S(1)} %get-tuple-element.64.og_ref, bf16[512,512]{1,0:T(8,128)(2,1)} %wo_hbm.3, bf16[512,512]{1,0:T(8,128)(2,1)} %wq_hbm.3, ...), custom_call_target="tpu_custom_call" | custom-call | flops 268435456 | bytes 2097152 | tf_op jit(solution)/shard_map/mesh/pallas_call | solution.py:48
  46.9 9.1 %all-to-all-done = bf16[16,64,512]{2,1,0:T(8,128)(2,1)S(1)} async-done(((bf16[16,64,512]{2,1,0:T(8,128)(2,1)}), bf16[16,64,512]{2,1,0:T(8,128)(2,1)S(1)}, u32[]{:S(2)}, u32[]{:S(2)}) %all-to-all-start) | async-done | bytes 1048608 | tf_op jit(solution)/shard_map/all_to_all | solution.py:428
  56.2 4.0 %collective-permute-start.13 = (bf16[256,512]{1,0:T(8,128)(2,1)S(1)}, bf16[256,512]{1,0:T(8,128)(2,1)S(1)}, u32[]{:S(2)}, u32[]{:S(2)}) collective-permute-start(bf16[256,512]{1,0:T(8,128)(2,1)S(1)} %get-tuple-element.87), channel_id=1, source_target_pairs={{0,4},{4,0},{1,5},{5,1},{2,6},{6,2},{3,7},{7,3},{8,12},{12,8},{9,1... | collective-permute-start | bytes 786440 | tf_op jit(solution)/shard_map/ppermute | solution.py:345
  60.3 2.1 %collective-permute-start.14 = (bf16[256,512]{1,0:T(8,128)(2,1)S(1)}, bf16[256,512]{1,0:T(8,128)(2,1)S(1)}, u32[]{:S(2)}, u32[]{:S(2)}) collective-permute-start(bf16[256,512]{1,0:T(8,128)(2,1)S(1)} %get-tuple-element.88), channel_id=1, source_target_pairs={{4,8},{12,16},{20,24},{28,32},{36,40},{44,48},{52,56},{60,64},{68,... | collective-permute-start | bytes 786440 | tf_op jit(solution)/shard_map/ppermute | solution.py:351
  62.7 2.4 %collective-permute-start.16 = (bf16[64,512]{1,0:T(8,128)(2,1)S(1)}, bf16[64,512]{1,0:T(8,128)(2,1)S(1)}, u32[]{:S(2)}, u32[]{:S(2)}) collective-permute-start(bf16[64,512]{1,0:T(8,128)(2,1)S(1)} %reduce_sum.12.p0), channel_id=1, source_target_pairs={{0,3},{1,0},{2,1},{3,2},{4,7},{5,4},{6,5},{7,6},{8,11},{9,8},{10,9... | collective-permute-start | bytes 196616 | tf_op jit(solution)/shard_map/ppermute | solution.py:345
  65.4 1.4 %collective-permute-done.10.p1 = bf16[64,512]{1,0:T(8,128)(2,1)S(1)} collective-permute-done((bf16[64,512]{1,0:T(8,128)(2,1)S(1)}, bf16[64,512]{1,0:T(8,128)(2,1)S(1)}, u32[]{:S(2)}, u32[]{:S(2)}) %collective-permute-start.10) | collective-permute-done | bytes 65568 | tf_op jit(solution)/shard_map/ppermute | solution.py:345
  67.9 2.1 %collective-permute-done.15.p2 = bf16[64,512]{1,0:T(8,128)(2,1)S(1)} collective-permute-done((bf16[64,512]{1,0:T(8,128)(2,1)S(1)}, bf16[64,512]{1,0:T(8,128)(2,1)S(1)}, u32[]{:S(2)}, u32[]{:S(2)}) %collective-permute-start.15) | collective-permute-done | bytes 65568 | tf_op jit(solution)/shard_map/ppermute | solution.py:345
  71.2 5.3 %all-to-all-start.1 = ((bf16[16,64,512]{2,1,0:T(8,128)(2,1)}), bf16[16,64,512]{2,1,0:T(8,128)(2,1)S(1)}, u32[]{:S(2)}, u32[]{:S(2)}) async-start(bf16[16,64,512]{2,1,0:T(8,128)(2,1)} %spread.1), calls=%async_computation.1 | async-start | bytes 2097152 | tf_op jit(solution)/shard_map/all_to_all | solution.py:451
  76.5 4.4 %grid_grad.1 = bf16[2048,512]{1,0:T(8,128)(2,1)} custom-call(s32[1]{0:T(128)} %bitcast.1.sub_ref, s32[1]{0:T(128)} %bitcast.core_ref, bf16[256,512]{1,0:T(8,128)(2,1)S(1)} %collective-permute-done.13.near, bf16[256,512]{1,0:T(8,128)(2,1)S(1)} %collective-permute-done.14.far, bf16[3,64,512]{2,1,0:T(8,128)(2,1)S(1)} %get-tuple-element.83.p0.s0, ...), custom_call_target="tpu_custom_call" | custom-call | flops 1073741824 | bytes 5242880 | tf_op jit(solution)/shard_map/grid_grad/pallas_call | solution.py:48
  80.8 10.6 %all-to-all-done.1 = bf16[16,64,512]{2,1,0:T(8,128)(2,1)S(1)} async-done(((bf16[16,64,512]{2,1,0:T(8,128)(2,1)}), bf16[16,64,512]{2,1,0:T(8,128)(2,1)S(1)}, u32[]{:S(2)}, u32[]{:S(2)}) %all-to-all-start.1) | async-done | bytes 1048608 | tf_op jit(solution)/shard_map/all_to_all | solution.py:451
  91.5 3.7 %collective-permute-start.17 = (bf16[1024,512]{1,0:T(8,128)(2,1)S(1)}, bf16[1024,512]{1,0:T(8,128)(2,1)S(1)}, u32[]{:S(2)}, u32[]{:S(2)}) collective-permute-start(bf16[1024,512]{1,0:T(8,128)(2,1)S(1)} %bitcast.6), channel_id=1, source_target_pairs={{0,4},{4,0},{1,5},{5,1},{2,6},{6,2},{3,7},{7,3},{8,12},{12,8},{9,1... | collective-permute-start | bytes 3145736 | tf_op jit(solution)/shard_map/ppermute | solution.py:345
  95.2 1.4 %widen_own.1.refs_0_ = f32[4,512,512]{2,1,0:T(8,128)} custom-call(s32[1]{0:T(128)} %bitcast.core_ref, bf16[1024,512]{1,0:T(8,128)(2,1)S(1)} %bitcast.7), custom_call_target="tpu_custom_call" | custom-call | flops 1048576 | bytes 3145728 | tf_op jit(solution)/shard_map/widen_own/pallas_call | solution.py:48
  97.5 1.4 %widen_other.1 = f32[4,512,512]{2,1,0:T(8,128)} custom-call(s32[1]{0:T(128)} %bitcast.core_ref, bf16[1024,512]{1,0:T(8,128)(2,1)S(1)} %collective-permute-done.17.half_ref, f32[4,512,512]{2,1,0:T(8,128)} %widen_own.1.refs_0_), custom_call_target="tpu_custom_call", output_to_operand_aliasing={{}: (2, {})} | custom-call | flops 1048576 | bytes 3145728 | tf_op jit(solution)/shard_map/widen_other/pallas_call | solution.py:48
  (32 shorter events, 13.1 us)
Async XLA Ops:
  3.6 4.7 %collective-permute-start = (bf16[256,512]{1,0:T(8,128)(2,1)S(1)}, bf16[256,512]{1,0:T(8,128)(2,1)S(1)}, u32[]{:S(2)}, u32[]{:S(2)}) collective-permute-start(bf16[256,512]{1,0:T(8,128)(2,1)S(1)} %get-tuple-element.49), channel_id=1, source_target_pairs={{0,4},{4,0},{1,5},{5,1},{2,6},{6,2},{3,7},{7,3},{8,12},{12,8},{9,1... | collective-permute-start | bytes 786440 | tf_op jit(solution)/shard_map/ppermute | solution.py:345
  5.1 10.7 %collective-permute-start.1 = (bf16[256,512]{1,0:T(8,128)(2,1)S(1)}, bf16[256,512]{1,0:T(8,128)(2,1)S(1)}, u32[]{:S(2)}, u32[]{:S(2)}) collective-permute-start(bf16[256,512]{1,0:T(8,128)(2,1)S(1)} %get-tuple-element.50), channel_id=1, source_target_pairs={{4,8},{12,16},{20,24},{28,32},{36,40},{44,48},{52,56},{60,64},{68,... | collective-permute-start | bytes 786440 | tf_op jit(solution)/shard_map/ppermute | solution.py:351
  8.3 7.5 %collective-permute-start.2 = (bf16[128,512]{1,0:T(8,128)(2,1)S(1)}, bf16[128,512]{1,0:T(8,128)(2,1)S(1)}, u32[]{:S(2)}, u32[]{:S(2)}) collective-permute-start(bf16[128,512]{1,0:T(8,128)(2,1)S(1)} %get-tuple-element.52), channel_id=1, source_target_pairs={{0,1},{1,2},{2,3},{3,0},{4,5},{5,6},{6,7},{7,4},{8,9},{9,10},{10,1... | collective-permute-start | bytes 393224 | tf_op jit(solution)/shard_map/ppermute | solution.py:345
  10.0 11.4 %collective-permute-start.3 = (bf16[128,512]{1,0:T(8,128)(2,1)S(1)}, bf16[128,512]{1,0:T(8,128)(2,1)S(1)}, u32[]{:S(2)}, u32[]{:S(2)}) collective-permute-start(bf16[128,512]{1,0:T(8,128)(2,1)S(1)} %get-tuple-element.56), channel_id=1, source_target_pairs={{0,2},{1,3},{2,0},{3,1},{4,6},{5,7},{6,4},{7,5},{8,10},{9,11},{10,... | collective-permute-start | bytes 393224 | tf_op jit(solution)/shard_map/ppermute | solution.py:345
  13.3 8.1 %collective-permute-start.4 = (bf16[128,512]{1,0:T(8,128)(2,1)S(1)}, bf16[128,512]{1,0:T(8,128)(2,1)S(1)}, u32[]{:S(2)}, u32[]{:S(2)}) collective-permute-start(bf16[128,512]{1,0:T(8,128)(2,1)S(1)} %get-tuple-element.57), channel_id=1, source_target_pairs={{0,3},{1,0},{2,1},{3,2},{4,7},{5,4},{6,5},{7,6},{8,11},{9,8},{10,9... | collective-permute-start | bytes 393224 | tf_op jit(solution)/shard_map/ppermute | solution.py:345
  15.9 5.6 %collective-permute-start.5 = (bf16[64,512]{1,0:T(8,128)(2,1)S(1)}, bf16[64,512]{1,0:T(8,128)(2,1)S(1)}, u32[]{:S(2)}, u32[]{:S(2)}) collective-permute-start(bf16[64,512]{1,0:T(8,128)(2,1)S(1)} %get-tuple-element.58), channel_id=1, source_target_pairs={{0,1},{1,2},{2,3},{3,0},{4,5},{5,6},{6,7},{7,4},{8,9},{9,10},{10,1... | collective-permute-start | bytes 196616 | tf_op jit(solution)/shard_map/ppermute | solution.py:345
  16.7 5.6 %collective-permute-start.6 = (bf16[64,512]{1,0:T(8,128)(2,1)S(1)}, bf16[64,512]{1,0:T(8,128)(2,1)S(1)}, u32[]{:S(2)}, u32[]{:S(2)}) collective-permute-start(bf16[64,512]{1,0:T(8,128)(2,1)S(1)} %get-tuple-element.59), channel_id=1, source_target_pairs={{0,2},{1,3},{2,0},{3,1},{4,6},{5,7},{6,4},{7,5},{8,10},{9,11},{10,... | collective-permute-start | bytes 196616 | tf_op jit(solution)/shard_map/ppermute | solution.py:345
  19.0 4.2 %collective-permute-start.7 = (bf16[64,512]{1,0:T(8,128)(2,1)S(1)}, bf16[64,512]{1,0:T(8,128)(2,1)S(1)}, u32[]{:S(2)}, u32[]{:S(2)}) collective-permute-start(bf16[64,512]{1,0:T(8,128)(2,1)S(1)} %get-tuple-element.60), channel_id=1, source_target_pairs={{0,3},{1,0},{2,1},{3,2},{4,7},{5,4},{6,5},{7,6},{8,11},{9,8},{10,9... | collective-permute-start | bytes 196616 | tf_op jit(solution)/shard_map/ppermute | solution.py:345
  29.4 2.8 %collective-permute-start.8 = (bf16[1024,512]{1,0:T(8,128)(2,1)S(1)}, bf16[1024,512]{1,0:T(8,128)(2,1)S(1)}, u32[]{:S(2)}, u32[]{:S(2)}) collective-permute-start(bf16[1024,512]{1,0:T(8,128)(2,1)S(1)} %get-tuple-element.66), channel_id=1, source_target_pairs={{0,4},{4,0},{1,5},{5,1},{2,6},{6,2},{3,7},{7,3},{8,12},{12,8},{9,1... | collective-permute-start | bytes 3145736 | tf_op jit(solution)/shard_map/ppermute | solution.py:345
  33.2 22.8 %all-to-all-start = ((bf16[16,64,512]{2,1,0:T(8,128)(2,1)}), bf16[16,64,512]{2,1,0:T(8,128)(2,1)S(1)}, u32[]{:S(2)}, u32[]{:S(2)}) async-start(bf16[16,64,512]{2,1,0:T(8,128)(2,1)} %bitcast.4), calls=%async_computation | async-start | bytes 2097152 | tf_op jit(solution)/shard_map/all_to_all | solution.py:428
  41.0 5.9 %collective-permute-start.9 = (bf16[3,64,512]{2,1,0:T(8,128)(2,1)S(1)}, bf16[3,64,512]{2,1,0:T(8,128)(2,1)S(1)}, u32[]{:S(2)}, u32[]{:S(2)}) collective-permute-start(bf16[3,64,512]{2,1,0:T(8,128)(2,1)S(1)} %get-tuple-element.73), channel_id=1, source_target_pairs={{0,3},{1,0},{2,1},{3,2},{4,7},{5,4},{6,5},{7,6},{8,11},{9,8},{10,9... | collective-permute-start | bytes 589832 | tf_op jit(solution)/shard_map/ppermute | solution.py:345
  42.9 13.3 %collective-permute-start.11 = (bf16[3,64,512]{2,1,0:T(8,128)(2,1)S(1)}, bf16[3,64,512]{2,1,0:T(8,128)(2,1)S(1)}, u32[]{:S(2)}, u32[]{:S(2)}) collective-permute-start(bf16[3,64,512]{2,1,0:T(8,128)(2,1)S(1)} %get-tuple-element.85), channel_id=1, source_target_pairs={{0,2},{1,3},{2,0},{3,1},{4,6},{5,7},{6,4},{7,5},{8,10},{9,11},{10,... | collective-permute-start | bytes 589832 | tf_op jit(solution)/shard_map/ppermute | solution.py:345
  43.2 13.0 %collective-permute-start.12 = (bf16[3,64,512]{2,1,0:T(8,128)(2,1)S(1)}, bf16[3,64,512]{2,1,0:T(8,128)(2,1)S(1)}, u32[]{:S(2)}, u32[]{:S(2)}) collective-permute-start(bf16[3,64,512]{2,1,0:T(8,128)(2,1)S(1)} %get-tuple-element.86), channel_id=1, source_target_pairs={{0,1},{1,2},{2,3},{3,0},{4,5},{5,6},{6,7},{7,4},{8,9},{9,10},{10,1... | collective-permute-start | bytes 589832 | tf_op jit(solution)/shard_map/ppermute | solution.py:345
  56.2 10.5 %collective-permute-start.13 = (bf16[256,512]{1,0:T(8,128)(2,1)S(1)}, bf16[256,512]{1,0:T(8,128)(2,1)S(1)}, u32[]{:S(2)}, u32[]{:S(2)}) collective-permute-start(bf16[256,512]{1,0:T(8,128)(2,1)S(1)} %get-tuple-element.87), channel_id=1, source_target_pairs={{0,4},{4,0},{1,5},{5,1},{2,6},{6,2},{3,7},{7,3},{8,12},{12,8},{9,1... | collective-permute-start | bytes 786440 | tf_op jit(solution)/shard_map/ppermute | solution.py:345
  60.3 7.7 %collective-permute-start.14 = (bf16[256,512]{1,0:T(8,128)(2,1)S(1)}, bf16[256,512]{1,0:T(8,128)(2,1)S(1)}, u32[]{:S(2)}, u32[]{:S(2)}) collective-permute-start(bf16[256,512]{1,0:T(8,128)(2,1)S(1)} %get-tuple-element.88), channel_id=1, source_target_pairs={{4,8},{12,16},{20,24},{28,32},{36,40},{44,48},{52,56},{60,64},{68,... | collective-permute-start | bytes 786440 | tf_op jit(solution)/shard_map/ppermute | solution.py:351
  62.4 4.4 %collective-permute-start.10 = (bf16[64,512]{1,0:T(8,128)(2,1)S(1)}, bf16[64,512]{1,0:T(8,128)(2,1)S(1)}, u32[]{:S(2)}, u32[]{:S(2)}) collective-permute-start(bf16[64,512]{1,0:T(8,128)(2,1)S(1)} %reduce_sum.12.p0), channel_id=1, source_target_pairs={{0,1},{1,2},{2,3},{3,0},{4,5},{5,6},{6,7},{7,4},{8,9},{9,10},{10,1... | collective-permute-start | bytes 196616 | tf_op jit(solution)/shard_map/ppermute | solution.py:345
  62.7 5.2 %collective-permute-start.16 = (bf16[64,512]{1,0:T(8,128)(2,1)S(1)}, bf16[64,512]{1,0:T(8,128)(2,1)S(1)}, u32[]{:S(2)}, u32[]{:S(2)}) collective-permute-start(bf16[64,512]{1,0:T(8,128)(2,1)S(1)} %reduce_sum.12.p0), channel_id=1, source_target_pairs={{0,3},{1,0},{2,1},{3,2},{4,7},{5,4},{6,5},{7,6},{8,11},{9,8},{10,9... | collective-permute-start | bytes 196616 | tf_op jit(solution)/shard_map/ppermute | solution.py:345
  65.1 4.9 %collective-permute-start.15 = (bf16[64,512]{1,0:T(8,128)(2,1)S(1)}, bf16[64,512]{1,0:T(8,128)(2,1)S(1)}, u32[]{:S(2)}, u32[]{:S(2)}) collective-permute-start(bf16[64,512]{1,0:T(8,128)(2,1)S(1)} %reduce_sum.12.p0), channel_id=1, source_target_pairs={{0,2},{1,3},{2,0},{3,1},{4,6},{5,7},{6,4},{7,5},{8,10},{9,11},{10,... | collective-permute-start | bytes 196616 | tf_op jit(solution)/shard_map/ppermute | solution.py:345
  71.2 20.3 %all-to-all-start.1 = ((bf16[16,64,512]{2,1,0:T(8,128)(2,1)}), bf16[16,64,512]{2,1,0:T(8,128)(2,1)S(1)}, u32[]{:S(2)}, u32[]{:S(2)}) async-start(bf16[16,64,512]{2,1,0:T(8,128)(2,1)} %spread.1), calls=%async_computation.1 | async-start | bytes 2097152 | tf_op jit(solution)/shard_map/all_to_all | solution.py:451
  91.5 6.0 %collective-permute-start.17 = (bf16[1024,512]{1,0:T(8,128)(2,1)S(1)}, bf16[1024,512]{1,0:T(8,128)(2,1)S(1)}, u32[]{:S(2)}, u32[]{:S(2)}) collective-permute-start(bf16[1024,512]{1,0:T(8,128)(2,1)S(1)} %bitcast.6), channel_id=1, source_target_pairs={{0,4},{4,0},{1,5},{5,1},{2,6},{6,2},{3,7},{7,3},{8,12},{12,8},{9,1... | collective-permute-start | bytes 3145736 | tf_op jit(solution)/shard_map/ppermute | solution.py:345

commit v8 on v7

--- a/solution.py
+++ b/solution.py
@@ -70,22 +70,21 @@
     return [pltpu.VMEM(a.shape, a.dtype) for a in args] + [pltpu.SemaphoreType.DMA((len(args),))]
 
 
-def assemble(rows, near_first, near, far, own, *pieces):
+def assemble(rows, near_first, near, own, m1, m2, m3, f0, f1, f2, f3):
     block = near.shape[0]
     cap = block // 4
     near_at = pl.multiple_of((1 - near_first) * (2 * block), block)
     far_at = pl.multiple_of(near_first * (2 * block), block)
     rows[block : block + cap] = own[0:cap]
     rows[pl.ds(near_at, cap), :] = near[0:cap]
-    rows[pl.ds(far_at, cap), :] = far[0:cap]
-    for k in range(1, 4):
-        mixed, last = pieces[k - 1], pieces[len(pieces) - 4 + k]
+    for k, mixed in enumerate((m1, m2, m3), 1):
         rows[block + k * cap : block + (k + 1) * cap] = mixed[0:cap]
         rows[pl.ds(near_at + k * cap, cap), :] = mixed[cap : 2 * cap]
-        rows[pl.ds(far_at + k * cap, cap), :] = last[last.shape[0] - cap :]
-
-
-def gather_body(sub_ref, core_ref, rows_hbm, gain_hbm, x_hbm, near_ref, far_ref, own_ref,
+    for k, far in enumerate((f0, f1, f2, f3)):
+        rows[pl.ds(far_at + k * cap, cap), :] = far[...]
+
+
+def gather_body(sub_ref, core_ref, rows_hbm, gain_hbm, x_hbm, near_ref, own_ref, f0, f1, f2, f3,
                 rows_ref, gain_ref, x_ref, sems):
     half = x_ref.shape[0] // 2
     cap = rows_ref.shape[3]
@@ -105,11 +104,11 @@
     )
     gain = gain_ref[...]
     steps = (
-        (2 - 2 * core, firsts[0], half, near_ref),
-        (2 * core, firsts[1], half, far_ref),
-        (1, 0, 2 * half, own_ref),
-    )
-    for step, (o, first, count, out_ref) in enumerate(steps):
+        (2 - 2 * core, firsts[0], half, (near_ref,)),
+        (2 * core, firsts[1], half, (f0, f1, f2, f3)),
+        (1, 0, 2 * half, (own_ref,)),
+    )
+    for step, (o, first, count, outs) in enumerate(steps):
         cols = []
         for k in range(4):
             s = lax.rem(me + k, 4)
@@ -121,7 +120,10 @@
         if step < 2:
             copies[2 + step].wait()
         wide = nn(onehot, x_ref[pl.ds(first, count), :])
-        out_ref[...] = (wide * inv_rms(wide) * gain).astype(BF16)
+        normed = (wide * inv_rms(wide) * gain).astype(BF16)
+        for i, out_ref in enumerate(outs):
+            size = out_ref.shape[0]
+            out_ref[...] = normed[i * size : (i + 1) * size]
 
 
 def mesh_in_body(mesh_hbm, gain_hbm, wq_hbm, wo_hbm, og_hbm, normed_ref, q_ref, ag_ref, og_ref,
@@ -167,7 +169,7 @@
             dense_ref[h, :, b * 128 : (b + 1) * 128] = jnp.where(here, got, ABSENT)
 
 
-def middle_body(core_ref, near, far, own, m1, m2, m3, f1, f2, f3, q_ref, ag_ref, mn_ref, og_ref,
+def middle_body(core_ref, near, own, m1, m2, m3, f0, f1, f2, f3, q_ref, ag_ref, mn_ref, og_ref,
                 bias_ref, wk_hbm, wv_hbm, send_ref, part_ref, att_ref, qg_ref, wkv_ref, rows,
                 keys, vals, sems):
     width = q_ref.shape[1]
@@ -176,7 +178,7 @@
     )
     heads = bias_ref.shape[0]
     core = core_ref[0]
-    assemble(rows, 1 - core, near, far, own, m1, m2, m3, f1, f2, f3)
+    assemble(rows, 1 - core, near, own, m1, m2, m3, f0, f1, f2, f3)
     copies[0].wait()
     keys[...] = nn(rows[...], wkv_ref[:, :width]).astype(BF16)
     copies[1].wait()
@@ -213,13 +215,15 @@
     half_grads(core_ref[0], keep_ref, rows, part_ref, mn_ref, qg_ref, att_ref, og_ref)
 
 
-def back_body(part_ref, wkv_ref, s0, s1, s2, s3):
-    cap = s0.shape[1]
-    for o in range(3):
-        rows = slice(o * 4 * cap, (o + 1) * 4 * cap)
-        back = nt(part_ref[rows, :], wkv_ref[...]).astype(BF16)
-        for k, piece in enumerate((s0, s1, s2, s3)):
-            piece[o] = back[k * cap : (k + 1) * cap]
+def back_body(core_ref, part_ref, wkv_ref, near_ref, own_ref, f0, f1, f2, f3):
+    block = own_ref.shape[0]
+    near_at = pl.multiple_of(core_ref[0] * (2 * block), block)
+    far_at = pl.multiple_of((1 - core_ref[0]) * (2 * block), block)
+    for first, outs in ((near_at, (near_ref,)), (far_at, (f0, f1, f2, f3)), (block, (own_ref,))):
+        back = nt(part_ref[pl.ds(first, block), :], wkv_ref[...]).astype(BF16)
+        for i, out_ref in enumerate(outs):
+            size = out_ref.shape[0]
+            out_ref[...] = back[i * size : (i + 1) * size]
 
 
 def mesh_body(att_ref, qg_ref, og_ref, wo_hbm, wq_hbm, mesh_hbm, gain_hbm, out_ref, grad_ref,
@@ -236,14 +240,6 @@
     grad_ref[...] = (og_ref[...].astype(F32) + back).astype(BF16)
 
 
-def pack_body(core_ref, p0, p1, p2, p3, near_ref, far_ref):
-    cap = p0.shape[1]
-    near = core_ref[0] * 2
-    for k, piece in enumerate((p0, p1, p2, p3)):
-        near_ref[k * cap : (k + 1) * cap, :] = piece[near]
-        far_ref[k * cap : (k + 1) * cap, :] = piece[2 - near]
-
-
 def mix_body(own, near, m1, m2, m3):
     cap = m1.shape[0] // 2
     for k, mixed in enumerate((m1, m2, m3), 1):
@@ -251,13 +247,7 @@
         mixed[cap : 2 * cap] = near[k * cap : (k + 1) * cap]
 
 
-def split_body(block, f1, f2, f3):
-    cap = f1.shape[0]
-    for k, piece in enumerate((f1, f2, f3), 1):
-        piece[...] = block[k * cap : (k + 1) * cap]
-
-
-def grid_body(sub_ref, core_ref, near, far, s0, s1, s2, s3, rows_hbm, gain_hbm, x_hbm, out_hbm,
+def grid_body(sub_ref, core_ref, near, own, m1, m2, m3, f0, f1, f2, f3, rows_hbm, gain_hbm, x_hbm, out_hbm,
               got, done_ref, done_sems, rows_ref, gain_ref, x_ref, sems):
     copies = fetch((rows_hbm, gain_hbm, x_hbm), (rows_ref, gain_ref, x_ref), sems)
     points = x_ref.shape[0]
@@ -265,11 +255,7 @@
     cap = rows_ref.shape[3]
     block = 4 * cap
     me = sub_ref[0]
-    core = core_ref[0]
-    got[pl.ds(pl.multiple_of((1 - core) * (2 * block), block), block), :] = near[...]
-    got[pl.ds(pl.multiple_of(core * (2 * block), block), block), :] = far[...]
-    for k, piece in enumerate((s0, s1, s2, s3)):
-        got[block + k * cap : block + (k + 1) * cap] = piece[1]
+    assemble(got, core_ref[0], near, own, m1, m2, m3, f0, f1, f2, f3)
     for copy in copies:
         copy.wait()
     gain = gain_ref[...]
@@ -345,10 +331,12 @@
     return lax.ppermute(block, axis, [(i, (i + k) % n) for i in range(n)])
 
 
-def swapped_far(block):
-    n = lax.axis_size(SLAB)
-    pairs = [(i, i + 1) for i in range(1, n - 1, 2)]
-    return lax.ppermute(block, SLAB, pairs + [(j, i) for i, j in pairs])
+def to_far(block, k):
+    slabs, subs = lax.axis_size(SLAB), lax.axis_size("z")
+    pairs = [(i, i + 1) for i in range(1, slabs - 1, 2)]
+    pairs += [(j, i) for i, j in pairs]
+    route = [(i * subs + c, j * subs + (c + k) % subs) for i, j in pairs for c in range(subs)]
+    return lax.ppermute(block, ALL, route)
 
 
 def sds(shape, dtype=BF16):
@@ -374,25 +362,25 @@
     )
 
     one, two, four = sds((cap, width)), sds((2 * cap, width)), sds((block, width))
-    near, far, own = call(
-        gather_body, [four] * 3, [SM, SM, HB, HB, HB],
+
+    def exchange(near, own, far, sign):
+        near = shifted(near, "gc", 1)
+        far = [to_far(f, sign * k) for k, f in enumerate(far)]
+        mixed = call(mix_body, [two] * 3, [VM] * 2, (own, near), 0, 1 << 20, "mix")
+        mixed = [shifted(m, "z", sign * k) for k, m in enumerate(mixed, 1)]
+        return near, own, *mixed, *far
+
+    near, own, *far = call(
+        gather_body, [four] * 2 + [one] * 4, [SM, SM, HB, HB, HB],
         (sub1, core1, send_rows, gain_g, grid_x), 1 << 30, 4 << 20, "gather_rows",
         held(send_rows, gain_g, grid_x)[:-1] + [pltpu.SemaphoreType.DMA((4,))],
     )
-
-    far = swapped_far(far)
-    near = shifted(near, "gc", 1)
-    mixed = call(mix_body, [two] * 3, [VM] * 2, (own, near), 0, 1 << 20, "mix")
-    mixed = [shifted(m, "z", k) for k, m in enumerate(mixed, 1)]
+    received = exchange(near, own, far, 1)
     mesh_normed, queries, att_grad, og_near = call(
         mesh_in_body, [sds((nodes, width))] * 4, [HB] * 5, (mesh_h, gain_m, w_query, w_out, out_grad),
         1 << 28, 2 << 20, "mesh_in", held(mesh_h, gain_m, w_query, w_out)[:-1] + [pltpu.SemaphoreType.DMA((5,))],
     )
-    far, mixed[0], queries = lax.optimization_barrier((far, mixed[0], queries))
-    outer = call(split_body, [one] * 3, [VM], (far,), 0, 1 << 19, "split")
-    outer = [shifted(f, "z", k) for k, f in enumerate(outer, 1)]
-    received = near, far, own, *mixed, *outer
-    sub2, far = lax.optimization_barrier((sub1, far))
+    sub2, near = lax.optimization_barrier((sub1, received[0]))
     (dense,) = call(
         slots_body, [sds((heads, nodes, slots), F32)], [SM] + [HB] * 3,
         (sub2, neighbours, valid, edge_bias), 1 << 30, 8 << 20, "slots",
@@ -414,44 +402,37 @@
         keep_body, [sds((2 * width, width))], [SM] + [VM] * 6,
         (core1, rows, part_grads, mesh_normed, query_grad, attended, og_near), 1 << 29, 3 << 20, "keep",
     )
-    s0, s1, s2, s3 = call(
-        back_body, [sds((3, cap, width))] * 4, [VM] * 2, (part_grads, weights_near),
+    near, own, *far = call(
+        back_body, [four] * 2 + [one] * 4, [SM] + [VM] * 2, (core1, part_grads, weights_near),
         1 << 30, 3 << 20, "back",
     )
-    other, s1, keep = lax.optimization_barrier((other, s1, keep))
-    (own,) = call(
+    other, near, keep = lax.optimization_barrier((other, near, keep))
+    returned = exchange(near, own, far, -1)
+    (sums,) = call(
         pair_body, [sds((2 * width, width))], [VM] * 2, (keep, other), 1 << 20, 3 << 20, "pair",
         [pltpu.VMEM((2 * width, width), BF16), pltpu.SemaphoreType.DMA((4,))], [HB],
     )
     plane = lax.axis_size(PLANE)
     share = 2 * width // plane
-    parts = lax.all_to_all(own.reshape(plane, share, width), PLANE, 0, 0, tiled=True)
-
-    attended, own = lax.optimization_barrier((attended, own))
+    parts = lax.all_to_all(sums.reshape(plane, share, width), PLANE, 0, 0, tiled=True)
+
+    attended, sums = lax.optimization_barrier((attended, sums))
     mesh_out, mesh_grad = call(
         mesh_body, [sds((nodes, width))] * 2, [VM] * 3 + [HB] * 4,
         (attended, query_grad, og_near, w_out, w_query, mesh_h, gain_m), 1 << 28, 2 << 20, "mesh",
         held(w_out, w_query, mesh_h, gain_m),
     )
-    s1, s2, s3 = (shifted(s, "z", -k) for k, s in ((1, s1), (2, s2), (3, s3)))
-    s1, parts, mesh_out = lax.optimization_barrier((s1, parts, mesh_out))
+    parts, mesh_out, *returned = lax.optimization_barrier((parts, mesh_out, *returned))
     part = jnp.sum(parts.astype(F32), axis=0).astype(BF16)
-    part, s0 = lax.optimization_barrier((part, s0))
-    near, far = call(
-        pack_body, [four] * 2, [SM] + [VM] * 4, (core1, s0, s1, s2, s3), 0, 1 << 20, "pack"
-    )
-    far = swapped_far(far)
-    near = shifted(near, "gc", 1)
     p1, p2, p3 = (shifted(part, "z", k) for k in (1, 2, 3))
-    p1, near, far = lax.optimization_barrier((p1, near, far))
     (spread,) = call(
         spread_body, [sds((plane, share, width))], [VM] * 4, (part, p1, p2, p3), 1 << 18, 1 << 20,
         "spread", [pltpu.VMEM((share, width), BF16), pltpu.SemaphoreType.DMA((plane,))], [HB],
     )
     mine = lax.all_to_all(spread, PLANE, 0, 0, tiled=True).reshape(2 * width, width)
     (grid_grad,) = call(
-        grid_body, [sds((points, width))], [SM] * 2 + [VM] * 6 + [HB] * 3,
-        (sub1, core1, near, far, s0, s1, s2, s3, send_rows, gain_g, grid_x),
+        grid_body, [sds((points, width))], [SM] * 2 + [VM] * 9 + [HB] * 3,
+        (sub1, core1, *returned, send_rows, gain_g, grid_x),
         1 << 30, 5 << 20, "grid_grad",
         [pltpu.VMEM((slots, width), BF16), pltpu.VMEM((points, width), BF16),
          pltpu.SemaphoreType.DMA((points // 256,))] + held(send_rows, gain_g, grid_x),

time: 99.5 us -> 118 us (1.19)
  starting transfers between devices: 42.6 us -> 68.1 us
  waiting for transfers between devices: 28.6 us -> 21.2 us
    ppermute x2 -> x8, starting transfers between devices: 5.28 us -> 32.3 us  [to_far(): return lax.ppermute(block, ALL, route)]
    ppermute x16 -> x13, starting transfers between devices: 24.3 us -> 13.1 us  [shifted(): return lax.ppermute(block, axis, [(i, (i + k) % n) for i in range(n)])]
    all_to_all x1, waiting for transfers between devices: 9.15 us -> 0.01 us  [shards(): lax.all_to_all(sums.reshape(plane, share, width), PLANE, 0, 0, tiled=True)]
    all_to_all x1, starting transfers between devices: 5.27 us -> 12.6 us  [shards(): lax.all_to_all(spread, PLANE, 0, 0, tiled=True).reshape(2 * width, width)]
    all_to_all x1, starting transfers between devices: 7.79 us -> 10.2 us  [shards(): lax.all_to_all(sums.reshape(plane, share, width), PLANE, 0, 0, tiled=True)]
    ppermute x2 -> x8, waiting for transfers between devices: 1.18 us -> 3.3 us  [to_far(): return lax.ppermute(block, ALL, route)]
    ppermute x16 -> x13, waiting for transfers between devices: 7.64 us -> 5.84 us  [shifted(): return lax.ppermute(block, axis, [(i, (i + k) % n) for i in range(n)])]
    all_to_all x1, waiting for transfers between devices: 10.6 us -> 12.1 us  [shards(): lax.all_to_all(spread, PLANE, 0, 0, tiled=True).reshape(2 * width, width)]
  transfers between devices with their start and end apart: 20 -> 23, of which waited for: 10 -> 8; matrix products, arithmetic and copies ran while one was open for 0% -> 0% of each run, Pallas kernels for 14% -> 12%
where the time goes in v8:
time: 118 us; the launch traced here: 117 us
  starting transfers between devices  68.1 us (58%)
  Pallas kernels  26.6 us (23%)
  waiting for transfers between devices  21.2 us (18%)
    ppermute x8, starting transfers between devices, to_far(): return lax.ppermute(block, ALL, route)  32.3 us
    pallas_call x14, Pallas kernels, call(): pl.pallas_call(body, out_shape=outs, in_specs=in_specs, out_specs=out_spe...  26.6 us
    ppermute x13, starting transfers between devices, shifted(): return lax.ppermute(block, axis, [(i, (i + k) % n) for i in range(n)])  13.1 us
    all_to_all x1, starting transfers between devices, shards(): lax.all_to_all(spread, PLANE, 0, 0, tiled=True).reshape(2 * width, width)  12.6 us
    all_to_all x1, waiting for transfers between devices, shards(): lax.all_to_all(spread, PLANE, 0, 0, tiled=True).reshape(2 * width, width)  12.1 us
    all_to_all x1, starting transfers between devices, shards(): lax.all_to_all(sums.reshape(plane, share, width), PLANE, 0, 0, tiled=True)  10.2 us
    ppermute x13, waiting for transfers between devices, shifted(): return lax.ppermute(block, axis, [(i, (i + k) % n) for i in range(n)])  5.84 us
    ppermute x8, waiting for transfers between devices, to_far(): return lax.ppermute(block, ALL, route)  3.3 us
  transfers between devices with their start and end apart: 23, of which 8 were waited for; matrix products, arithmetic and copies ran while one was open for 0% of the time, Pallas kernels for 12%

profile of v8, /device:TPU:1, one launch (start us, length us, event | category | flops | bytes accessed | tf_op | source)
XLA Modules:
  0.0 117.2 jit_solution(12846773810072682694)
XLA Ops:
  0.6 3.0 %gather_rows.1 = (bf16[256,512]{1,0:T(8,128)(2,1)S(1)}, bf16[256,512]{1,0:T(8,128)(2,1)S(1)}, bf16[64,512]{1,0:T(8,128)(2,1)S(1)}, bf16[64,512]{1,0:T(8,128)(2,1...) custom-call(s32[1]{0:T(128)} %bitcast.1.sub_ref, s32[1]{0:T(128)} %bitcast.core_ref, ...), custom_call_target="tpu_custom_call" | custom-call | flops 1073741824 | bytes 4194304 | tf_op jit(solution)/shard_map/gather_rows/pallas_call | solution.py:48
  5.1 3.2 %collective-permute-start.4 = (bf16[64,512]{1,0:T(8,128)(2,1)S(1)}, bf16[64,512]{1,0:T(8,128)(2,1)S(1)}, u32[]{:S(2)}, u32[]{:S(2)}) collective-permute-start(bf16[64,512]{1,0:T(8,128)(2,1)S(1)} %get-tuple-element.57), channel_id=1, source_target_pairs={{4,8},{5,9},{6,10},{7,11},{12,16},{13,17},{14,18},{15,19},{20,24},... | collective-permute-start | bytes 196616 | tf_op jit(solution)/shard_map/ppermute | solution.py:339
  8.3 3.8 %collective-permute-start.5 = (bf16[64,512]{1,0:T(8,128)(2,1)S(1)}, bf16[64,512]{1,0:T(8,128)(2,1)S(1)}, u32[]{:S(2)}, u32[]{:S(2)}) collective-permute-start(bf16[64,512]{1,0:T(8,128)(2,1)S(1)} %get-tuple-element.58), channel_id=1, source_target_pairs={{4,9},{5,10},{6,11},{7,8},{12,17},{13,18},{14,19},{15,16},{20,25},... | collective-permute-start | bytes 196616 | tf_op jit(solution)/shard_map/ppermute | solution.py:339
  12.2 1.7 %collective-permute-start.1 = (bf16[128,512]{1,0:T(8,128)(2,1)S(1)}, bf16[128,512]{1,0:T(8,128)(2,1)S(1)}, u32[]{:S(2)}, u32[]{:S(2)}) collective-permute-start(bf16[128,512]{1,0:T(8,128)(2,1)S(1)} %get-tuple-element.54), channel_id=1, source_target_pairs={{0,1},{1,2},{2,3},{3,0},{4,5},{5,6},{6,7},{7,4},{8,9},{9,10},{10,1... | collective-permute-start | bytes 393224 | tf_op jit(solution)/shard_map/ppermute | solution.py:331
  13.9 1.8 %collective-permute-start.2 = (bf16[128,512]{1,0:T(8,128)(2,1)S(1)}, bf16[128,512]{1,0:T(8,128)(2,1)S(1)}, u32[]{:S(2)}, u32[]{:S(2)}) collective-permute-start(bf16[128,512]{1,0:T(8,128)(2,1)S(1)} %get-tuple-element.55), channel_id=1, source_target_pairs={{0,2},{1,3},{2,0},{3,1},{4,6},{5,7},{6,4},{7,5},{8,10},{9,11},{10,... | collective-permute-start | bytes 393224 | tf_op jit(solution)/shard_map/ppermute | solution.py:331
  15.6 2.0 %collective-permute-start.3 = (bf16[128,512]{1,0:T(8,128)(2,1)S(1)}, bf16[128,512]{1,0:T(8,128)(2,1)S(1)}, u32[]{:S(2)}, u32[]{:S(2)}) collective-permute-start(bf16[128,512]{1,0:T(8,128)(2,1)S(1)} %get-tuple-element.56), channel_id=1, source_target_pairs={{0,3},{1,0},{2,1},{3,2},{4,7},{5,4},{6,5},{7,6},{8,11},{9,8},{10,9... | collective-permute-start | bytes 393224 | tf_op jit(solution)/shard_map/ppermute | solution.py:331
  17.6 1.7 %mesh_in.1 = (bf16[64,512]{1,0:T(8,128)(2,1)S(1)}, bf16[64,512]{1,0:T(8,128)(2,1)S(1)}, bf16[64,512]{1,0:T(8,128)(2,1)S(1)}, bf16[64,512]{1,0:T(8,128)(2,1)S(1)}) custom-call(bf16[64,512]{1,0:T(8,128)(2,1)} %mesh_hbm.3, f32[1,512]{1,0:T(1,128)} %bitcast.8, bf16[512,512]{1,0:T(8,128)(2,1)} %wq_hbm.3, bf16[512,512]{1,0:T(8,128)(2,1)} %wo_hbm.3, ...), custom_call_target="tpu_custom_call" | custom-call | flops 268435456 | bytes 2097152 | tf_op jit(solution)/shard_map/mesh_in/pallas_call | solution.py:48
  19.3 3.3 %collective-permute-start.6 = (bf16[64,512]{1,0:T(8,128)(2,1)S(1)}, bf16[64,512]{1,0:T(8,128)(2,1)S(1)}, u32[]{:S(2)}, u32[]{:S(2)}) collective-permute-start(bf16[64,512]{1,0:T(8,128)(2,1)S(1)} %get-tuple-element.59), channel_id=1, source_target_pairs={{4,10},{5,11},{6,8},{7,9},{12,18},{13,19},{14,16},{15,17},{20,26},... | collective-permute-start | bytes 196616 | tf_op jit(solution)/shard_map/ppermute | solution.py:339
  22.7 3.5 %collective-permute-start.7 = (bf16[64,512]{1,0:T(8,128)(2,1)S(1)}, bf16[64,512]{1,0:T(8,128)(2,1)S(1)}, u32[]{:S(2)}, u32[]{:S(2)}) collective-permute-start(bf16[64,512]{1,0:T(8,128)(2,1)S(1)} %get-tuple-element.60), channel_id=1, source_target_pairs={{4,11},{5,8},{6,9},{7,10},{12,19},{13,16},{14,17},{15,18},{20,27},... | collective-permute-start | bytes 196616 | tf_op jit(solution)/shard_map/ppermute | solution.py:339
  26.2 2.3 %slots.1.bias_ref = f32[4,64,768]{2,1,0:T(8,128)S(1)} custom-call(s32[1]{0:T(128)} %bitcast.1.sub_ref, s32[64,96]{1,0:T(8,128)} %nbr_hbm.1, s32[64,96]{1,0:T(8,128)} %valid_hbm.1, f32[64,384]{1,0:T(8,128)} %bias_hbm.1), custom_call_target="tpu_custom_call" | custom-call | flops 1073741824 | bytes 8388608 | tf_op jit(solution)/shard_map/slots/pallas_call | solution.py:48
  29.2 6.2 %middle.1 = (bf16[1024,512]{1,0:T(8,128)(2,1)S(1)}, bf16[768,1024]{1,0:T(8,128)(2,1)S(1)}, bf16[64,512]{1,0:T(8,128)(2,1)S(1)}, bf16[64,512]{1,0:T(8,128)(2,1)S(...) custom-call(s32[1]{0:T(128)} %bitcast.core_ref, bf16[256,512]{1,0:T(8,128)(2,1)S(1)} %collective-permute-done.near, ...), custom_call_target="tpu_custom_call" | custom-call | flops 3221225472 | bytes 8388608 | tf_op jit(solution)/shard_map/middle/pallas_call | solution.py:48
  39.2 10.2 %all-to-all-start = ((bf16[16,64,512]{2,1,0:T(8,128)(2,1)}), bf16[16,64,512]{2,1,0:T(8,128)(2,1)S(1)}, u32[]{:S(2)}, u32[]{:S(2)}) async-start(bf16[16,64,512]{2,1,0:T(8,128)(2,1)} %bitcast.4), calls=%async_computation | async-start | bytes 2097152 | tf_op jit(solution)/shard_map/all_to_all | solution.py:417
  49.9 3.4 %collective-permute-start.13 = (bf16[64,512]{1,0:T(8,128)(2,1)S(1)}, bf16[64,512]{1,0:T(8,128)(2,1)S(1)}, u32[]{:S(2)}, u32[]{:S(2)}) collective-permute-start(bf16[64,512]{1,0:T(8,128)(2,1)S(1)} %get-tuple-element.82), channel_id=1, source_target_pairs={{4,8},{5,9},{6,10},{7,11},{12,16},{13,17},{14,18},{15,19},{20,24},... | collective-permute-start | bytes 196616 | tf_op jit(solution)/shard_map/ppermute | solution.py:339
  53.3 4.9 %collective-permute-start.14 = (bf16[64,512]{1,0:T(8,128)(2,1)S(1)}, bf16[64,512]{1,0:T(8,128)(2,1)S(1)}, u32[]{:S(2)}, u32[]{:S(2)}) collective-permute-start(bf16[64,512]{1,0:T(8,128)(2,1)S(1)} %get-tuple-element.83), channel_id=1, source_target_pairs={{4,11},{5,8},{6,9},{7,10},{12,19},{13,16},{14,17},{15,18},{20,27},... | collective-permute-start | bytes 196616 | tf_op jit(solution)/shard_map/ppermute | solution.py:339
  59.8 7.5 %collective-permute-start.15 = (bf16[64,512]{1,0:T(8,128)(2,1)S(1)}, bf16[64,512]{1,0:T(8,128)(2,1)S(1)}, u32[]{:S(2)}, u32[]{:S(2)}) collective-permute-start(bf16[64,512]{1,0:T(8,128)(2,1)S(1)} %get-tuple-element.84), channel_id=1, source_target_pairs={{4,10},{5,11},{6,8},{7,9},{12,18},{13,19},{14,16},{15,17},{20,26},... | collective-permute-start | bytes 196616 | tf_op jit(solution)/shard_map/ppermute | solution.py:339
  67.3 2.7 %collective-permute-start.16 = (bf16[64,512]{1,0:T(8,128)(2,1)S(1)}, bf16[64,512]{1,0:T(8,128)(2,1)S(1)}, u32[]{:S(2)}, u32[]{:S(2)}) collective-permute-start(bf16[64,512]{1,0:T(8,128)(2,1)S(1)} %get-tuple-element.85), channel_id=1, source_target_pairs={{4,9},{5,10},{6,11},{7,8},{12,17},{13,18},{14,19},{15,16},{20,25},... | collective-permute-start | bytes 196616 | tf_op jit(solution)/shard_map/ppermute | solution.py:339
  70.0 2.3 %mesh.1 = (bf16[64,512]{1,0:T(8,128)(2,1)}, bf16[64,512]{1,0:T(8,128)(2,1)}) custom-call(bf16[64,512]{1,0:T(8,128)(2,1)S(1)} %get-tuple-element.75.att_ref, bf16[64,512]{1,0:T(8,128)(2,1)S(1)} %get-tuple-element.71.qg_ref, bf16[64,512]{1,0:T(8,128)(2,1)S(1)} %get-tuple-element.64.og_ref, bf16[512,512]{1,0:T(8,128)(2,1)} %wo_hbm.3, bf16[512,512]{1,0:T(8,128)(2,1)} %wq_hbm.3, ...), custom_call_target="tpu_custom_call" | custom-call | flops 268435456 | bytes 2097152 | tf_op jit(solution)/shard_map/mesh/pallas_call | solution.py:48
  72.3 2.7 %collective-permute-done.16.f3 = bf16[64,512]{1,0:T(8,128)(2,1)S(1)} collective-permute-done((bf16[64,512]{1,0:T(8,128)(2,1)S(1)}, bf16[64,512]{1,0:T(8,128)(2,1)S(1)}, u32[]{:S(2)}, u32[]{:S(2)}) %collective-permute-start.16) | collective-permute-done | bytes 65568 | tf_op jit(solution)/shard_map/ppermute | solution.py:339
  76.9 1.6 %collective-permute-done.19.p3 = bf16[64,512]{1,0:T(8,128)(2,1)S(1)} collective-permute-done((bf16[64,512]{1,0:T(8,128)(2,1)S(1)}, bf16[64,512]{1,0:T(8,128)(2,1)S(1)}, u32[]{:S(2)}, u32[]{:S(2)}) %collective-permute-start.19) | collective-permute-done | bytes 65568 | tf_op jit(solution)/shard_map/ppermute | solution.py:331
  78.6 1.6 %collective-permute-done.18.p2 = bf16[64,512]{1,0:T(8,128)(2,1)S(1)} collective-permute-done((bf16[64,512]{1,0:T(8,128)(2,1)S(1)}, bf16[64,512]{1,0:T(8,128)(2,1)S(1)}, u32[]{:S(2)}, u32[]{:S(2)}) %collective-permute-start.18) | collective-permute-done | bytes 65568 | tf_op jit(solution)/shard_map/ppermute | solution.py:331
  82.1 12.6 %all-to-all-start.1 = ((bf16[16,64,512]{2,1,0:T(8,128)(2,1)}), bf16[16,64,512]{2,1,0:T(8,128)(2,1)S(1)}, u32[]{:S(2)}, u32[]{:S(2)}) async-start(bf16[16,64,512]{2,1,0:T(8,128)(2,1)} %spread.1), calls=%async_computation.1 | async-start | bytes 2097152 | tf_op jit(solution)/shard_map/all_to_all | solution.py:432
  94.6 4.4 %grid_grad.1 = bf16[2048,512]{1,0:T(8,128)(2,1)} custom-call(s32[1]{0:T(128)} %bitcast.1.sub_ref, s32[1]{0:T(128)} %bitcast.core_ref, bf16[256,512]{1,0:T(8,128)(2,1)S(1)} %collective-permute-done.9.near, bf16[256,512]{1,0:T(8,128)(2,1)S(1)} %get-tuple-element.90.own, bf16[128,512]{1,0:T(8,128)(2,1)S(1)} %collective-permute-done.10.m1, ...), custom_call_target="tpu_custom_call" | custom-call | flops 1073741824 | bytes 5242880 | tf_op jit(solution)/shard_map/grid_grad/pallas_call | solution.py:48
  99.0 12.1 %all-to-all-done.1 = bf16[16,64,512]{2,1,0:T(8,128)(2,1)S(1)} async-done(((bf16[16,64,512]{2,1,0:T(8,128)(2,1)}), bf16[16,64,512]{2,1,0:T(8,128)(2,1)S(1)}, u32[]{:S(2)}, u32[]{:S(2)}) %all-to-all-start.1) | async-done | bytes 1048608 | tf_op jit(solution)/shard_map/all_to_all | solution.py:432
  111.1 2.3 %collective-permute-start.20 = (bf16[1024,512]{1,0:T(8,128)(2,1)S(1)}, bf16[1024,512]{1,0:T(8,128)(2,1)S(1)}, u32[]{:S(2)}, u32[]{:S(2)}) collective-permute-start(bf16[1024,512]{1,0:T(8,128)(2,1)S(1)} %bitcast.6), channel_id=1, source_target_pairs={{0,4},{4,0},{1,5},{5,1},{2,6},{6,2},{3,7},{7,3},{8,12},{12,8},{9,1... | collective-permute-start | bytes 3145736 | tf_op jit(solution)/shard_map/ppermute | solution.py:331
  (37 shorter events, 15.5 us)
Async XLA Ops:
  3.6 8.5 %collective-permute-start = (bf16[256,512]{1,0:T(8,128)(2,1)S(1)}, bf16[256,512]{1,0:T(8,128)(2,1)S(1)}, u32[]{:S(2)}, u32[]{:S(2)}) collective-permute-start(bf16[256,512]{1,0:T(8,128)(2,1)S(1)} %get-tuple-element.52), channel_id=1, source_target_pairs={{0,4},{4,0},{1,5},{5,1},{2,6},{6,2},{3,7},{7,3},{8,12},{12,8},{9,1... | collective-permute-start | bytes 786440 | tf_op jit(solution)/shard_map/ppermute | solution.py:331
  5.1 14.2 %collective-permute-start.4 = (bf16[64,512]{1,0:T(8,128)(2,1)S(1)}, bf16[64,512]{1,0:T(8,128)(2,1)S(1)}, u32[]{:S(2)}, u32[]{:S(2)}) collective-permute-start(bf16[64,512]{1,0:T(8,128)(2,1)S(1)} %get-tuple-element.57), channel_id=1, source_target_pairs={{4,8},{5,9},{6,10},{7,11},{12,16},{13,17},{14,18},{15,19},{20,24},... | collective-permute-start | bytes 196616 | tf_op jit(solution)/shard_map/ppermute | solution.py:339
  8.3 14.4 %collective-permute-start.5 = (bf16[64,512]{1,0:T(8,128)(2,1)S(1)}, bf16[64,512]{1,0:T(8,128)(2,1)S(1)}, u32[]{:S(2)}, u32[]{:S(2)}) collective-permute-start(bf16[64,512]{1,0:T(8,128)(2,1)S(1)} %get-tuple-element.58), channel_id=1, source_target_pairs={{4,9},{5,10},{6,11},{7,8},{12,17},{13,18},{14,19},{15,16},{20,25},... | collective-permute-start | bytes 196616 | tf_op jit(solution)/shard_map/ppermute | solution.py:339
  12.2 17.0 %collective-permute-start.1 = (bf16[128,512]{1,0:T(8,128)(2,1)S(1)}, bf16[128,512]{1,0:T(8,128)(2,1)S(1)}, u32[]{:S(2)}, u32[]{:S(2)}) collective-permute-start(bf16[128,512]{1,0:T(8,128)(2,1)S(1)} %get-tuple-element.54), channel_id=1, source_target_pairs={{0,1},{1,2},{2,3},{3,0},{4,5},{5,6},{6,7},{7,4},{8,9},{9,10},{10,1... | collective-permute-start | bytes 393224 | tf_op jit(solution)/shard_map/ppermute | solution.py:331
  13.9 15.3 %collective-permute-start.2 = (bf16[128,512]{1,0:T(8,128)(2,1)S(1)}, bf16[128,512]{1,0:T(8,128)(2,1)S(1)}, u32[]{:S(2)}, u32[]{:S(2)}) collective-permute-start(bf16[128,512]{1,0:T(8,128)(2,1)S(1)} %get-tuple-element.55), channel_id=1, source_target_pairs={{0,2},{1,3},{2,0},{3,1},{4,6},{5,7},{6,4},{7,5},{8,10},{9,11},{10,... | collective-permute-start | bytes 393224 | tf_op jit(solution)/shard_map/ppermute | solution.py:331
  15.6 13.6 %collective-permute-start.3 = (bf16[128,512]{1,0:T(8,128)(2,1)S(1)}, bf16[128,512]{1,0:T(8,128)(2,1)S(1)}, u32[]{:S(2)}, u32[]{:S(2)}) collective-permute-start(bf16[128,512]{1,0:T(8,128)(2,1)S(1)} %get-tuple-element.56), channel_id=1, source_target_pairs={{0,3},{1,0},{2,1},{3,2},{4,7},{5,4},{6,5},{7,6},{8,11},{9,8},{10,9... | collective-permute-start | bytes 393224 | tf_op jit(solution)/shard_map/ppermute | solution.py:331
  19.3 9.2 %collective-permute-start.6 = (bf16[64,512]{1,0:T(8,128)(2,1)S(1)}, bf16[64,512]{1,0:T(8,128)(2,1)S(1)}, u32[]{:S(2)}, u32[]{:S(2)}) collective-permute-start(bf16[64,512]{1,0:T(8,128)(2,1)S(1)} %get-tuple-element.59), channel_id=1, source_target_pairs={{4,10},{5,11},{6,8},{7,9},{12,18},{13,19},{14,16},{15,17},{20,26},... | collective-permute-start | bytes 196616 | tf_op jit(solution)/shard_map/ppermute | solution.py:339
  22.7 6.5 %collective-permute-start.7 = (bf16[64,512]{1,0:T(8,128)(2,1)S(1)}, bf16[64,512]{1,0:T(8,128)(2,1)S(1)}, u32[]{:S(2)}, u32[]{:S(2)}) collective-permute-start(bf16[64,512]{1,0:T(8,128)(2,1)S(1)} %get-tuple-element.60), channel_id=1, source_target_pairs={{4,11},{5,8},{6,9},{7,10},{12,19},{13,16},{14,17},{15,18},{20,27},... | collective-permute-start | bytes 196616 | tf_op jit(solution)/shard_map/ppermute | solution.py:339
  35.4 2.7 %collective-permute-start.8 = (bf16[1024,512]{1,0:T(8,128)(2,1)S(1)}, bf16[1024,512]{1,0:T(8,128)(2,1)S(1)}, u32[]{:S(2)}, u32[]{:S(2)}) collective-permute-start(bf16[1024,512]{1,0:T(8,128)(2,1)S(1)} %get-tuple-element.66), channel_id=1, source_target_pairs={{0,4},{4,0},{1,5},{5,1},{2,6},{6,2},{3,7},{7,3},{8,12},{12,8},{9,1... | collective-permute-start | bytes 3145736 | tf_op jit(solution)/shard_map/ppermute | solution.py:331
  39.2 35.8 %all-to-all-start = ((bf16[16,64,512]{2,1,0:T(8,128)(2,1)}), bf16[16,64,512]{2,1,0:T(8,128)(2,1)S(1)}, u32[]{:S(2)}, u32[]{:S(2)}) async-start(bf16[16,64,512]{2,1,0:T(8,128)(2,1)} %bitcast.4), calls=%async_computation | async-start | bytes 2097152 | tf_op jit(solution)/shard_map/all_to_all | solution.py:417
  49.4 8.8 %collective-permute-start.9 = (bf16[256,512]{1,0:T(8,128)(2,1)S(1)}, bf16[256,512]{1,0:T(8,128)(2,1)S(1)}, u32[]{:S(2)}, u32[]{:S(2)}) collective-permute-start(bf16[256,512]{1,0:T(8,128)(2,1)S(1)} %get-tuple-element.77), channel_id=1, source_target_pairs={{0,4},{4,0},{1,5},{5,1},{2,6},{6,2},{3,7},{7,3},{8,12},{12,8},{9,1... | collective-permute-start | bytes 786440 | tf_op jit(solution)/shard_map/ppermute | solution.py:331
  49.9 9.9 %collective-permute-start.13 = (bf16[64,512]{1,0:T(8,128)(2,1)S(1)}, bf16[64,512]{1,0:T(8,128)(2,1)S(1)}, u32[]{:S(2)}, u32[]{:S(2)}) collective-permute-start(bf16[64,512]{1,0:T(8,128)(2,1)S(1)} %get-tuple-element.82), channel_id=1, source_target_pairs={{4,8},{5,9},{6,10},{7,11},{12,16},{13,17},{14,18},{15,19},{20,24},... | collective-permute-start | bytes 196616 | tf_op jit(solution)/shard_map/ppermute | solution.py:339
  53.3 14.0 %collective-permute-start.14 = (bf16[64,512]{1,0:T(8,128)(2,1)S(1)}, bf16[64,512]{1,0:T(8,128)(2,1)S(1)}, u32[]{:S(2)}, u32[]{:S(2)}) collective-permute-start(bf16[64,512]{1,0:T(8,128)(2,1)S(1)} %get-tuple-element.83), channel_id=1, source_target_pairs={{4,11},{5,8},{6,9},{7,10},{12,19},{13,16},{14,17},{15,18},{20,27},... | collective-permute-start | bytes 196616 | tf_op jit(solution)/shard_map/ppermute | solution.py:339
  58.3 16.8 %collective-permute-start.10 = (bf16[128,512]{1,0:T(8,128)(2,1)S(1)}, bf16[128,512]{1,0:T(8,128)(2,1)S(1)}, u32[]{:S(2)}, u32[]{:S(2)}) collective-permute-start(bf16[128,512]{1,0:T(8,128)(2,1)S(1)} %get-tuple-element.79), channel_id=1, source_target_pairs={{0,3},{1,0},{2,1},{3,2},{4,7},{5,4},{6,5},{7,6},{8,11},{9,8},{10,9... | collective-permute-start | bytes 393224 | tf_op jit(solution)/shard_map/ppermute | solution.py:331
  58.8 16.2 %collective-permute-start.11 = (bf16[128,512]{1,0:T(8,128)(2,1)S(1)}, bf16[128,512]{1,0:T(8,128)(2,1)S(1)}, u32[]{:S(2)}, u32[]{:S(2)}) collective-permute-start(bf16[128,512]{1,0:T(8,128)(2,1)S(1)} %get-tuple-element.80), channel_id=1, source_target_pairs={{0,2},{1,3},{2,0},{3,1},{4,6},{5,7},{6,4},{7,5},{8,10},{9,11},{10,... | collective-permute-start | bytes 393224 | tf_op jit(solution)/shard_map/ppermute | solution.py:331
  58.8 16.2 %collective-permute-start.12 = (bf16[128,512]{1,0:T(8,128)(2,1)S(1)}, bf16[128,512]{1,0:T(8,128)(2,1)S(1)}, u32[]{:S(2)}, u32[]{:S(2)}) collective-permute-start(bf16[128,512]{1,0:T(8,128)(2,1)S(1)} %get-tuple-element.81), channel_id=1, source_target_pairs={{0,1},{1,2},{2,3},{3,0},{4,5},{5,6},{6,7},{7,4},{8,9},{9,10},{10,1... | collective-permute-start | bytes 393224 | tf_op jit(solution)/shard_map/ppermute | solution.py:331
  59.8 12.5 %collective-permute-start.15 = (bf16[64,512]{1,0:T(8,128)(2,1)S(1)}, bf16[64,512]{1,0:T(8,128)(2,1)S(1)}, u32[]{:S(2)}, u32[]{:S(2)}) collective-permute-start(bf16[64,512]{1,0:T(8,128)(2,1)S(1)} %get-tuple-element.84), channel_id=1, source_target_pairs={{4,10},{5,11},{6,8},{7,9},{12,18},{13,19},{14,16},{15,17},{20,26},... | collective-permute-start | bytes 196616 | tf_op jit(solution)/shard_map/ppermute | solution.py:339
  67.3 7.7 %collective-permute-start.16 = (bf16[64,512]{1,0:T(8,128)(2,1)S(1)}, bf16[64,512]{1,0:T(8,128)(2,1)S(1)}, u32[]{:S(2)}, u32[]{:S(2)}) collective-permute-start(bf16[64,512]{1,0:T(8,128)(2,1)S(1)} %get-tuple-element.85), channel_id=1, source_target_pairs={{4,9},{5,10},{6,11},{7,8},{12,17},{13,18},{14,19},{15,16},{20,25},... | collective-permute-start | bytes 196616 | tf_op jit(solution)/shard_map/ppermute | solution.py:339
  75.2 3.4 %collective-permute-start.19 = (bf16[64,512]{1,0:T(8,128)(2,1)S(1)}, bf16[64,512]{1,0:T(8,128)(2,1)S(1)}, u32[]{:S(2)}, u32[]{:S(2)}) collective-permute-start(bf16[64,512]{1,0:T(8,128)(2,1)S(1)} %reduce_sum.12.p0), channel_id=1, source_target_pairs={{0,3},{1,0},{2,1},{3,2},{4,7},{5,4},{6,5},{7,6},{8,11},{9,8},{10,9... | collective-permute-start | bytes 196616 | tf_op jit(solution)/shard_map/ppermute | solution.py:331
  75.5 4.7 %collective-permute-start.18 = (bf16[64,512]{1,0:T(8,128)(2,1)S(1)}, bf16[64,512]{1,0:T(8,128)(2,1)S(1)}, u32[]{:S(2)}, u32[]{:S(2)}) collective-permute-start(bf16[64,512]{1,0:T(8,128)(2,1)S(1)} %reduce_sum.12.p0), channel_id=1, source_target_pairs={{0,2},{1,3},{2,0},{3,1},{4,6},{5,7},{6,4},{7,5},{8,10},{9,11},{10,... | collective-permute-start | bytes 196616 | tf_op jit(solution)/shard_map/ppermute | solution.py:331
  75.6 5.3 %collective-permute-start.17 = (bf16[64,512]{1,0:T(8,128)(2,1)S(1)}, bf16[64,512]{1,0:T(8,128)(2,1)S(1)}, u32[]{:S(2)}, u32[]{:S(2)}) collective-permute-start(bf16[64,512]{1,0:T(8,128)(2,1)S(1)} %reduce_sum.12.p0), channel_id=1, source_target_pairs={{0,1},{1,2},{2,3},{3,0},{4,5},{5,6},{6,7},{7,4},{8,9},{9,10},{10,1... | collective-permute-start | bytes 196616 | tf_op jit(solution)/shard_map/ppermute | solution.py:331
  82.1 29.0 %all-to-all-start.1 = ((bf16[16,64,512]{2,1,0:T(8,128)(2,1)}), bf16[16,64,512]{2,1,0:T(8,128)(2,1)S(1)}, u32[]{:S(2)}, u32[]{:S(2)}) async-start(bf16[16,64,512]{2,1,0:T(8,128)(2,1)} %spread.1), calls=%async_computation.1 | async-start | bytes 2097152 | tf_op jit(solution)/shard_map/all_to_all | solution.py:432
  111.1 4.6 %collective-permute-start.20 = (bf16[1024,512]{1,0:T(8,128)(2,1)S(1)}, bf16[1024,512]{1,0:T(8,128)(2,1)S(1)}, u32[]{:S(2)}, u32[]{:S(2)}) collective-permute-start(bf16[1024,512]{1,0:T(8,128)(2,1)S(1)} %bitcast.6), channel_id=1, source_target_pairs={{0,4},{4,0},{1,5},{5,1},{2,6},{6,2},{3,7},{7,3},{8,12},{12,8},{9,1... | collective-permute-start | bytes 3145736 | tf_op jit(solution)/shard_map/ppermute | solution.py:331

commit v9 on v7

--- a/solution.py
+++ b/solution.py
@@ -257,40 +257,39 @@
         piece[...] = block[k * cap : (k + 1) * cap]
 
 
-def grid_body(sub_ref, core_ref, near, far, s0, s1, s2, s3, rows_hbm, gain_hbm, x_hbm, out_hbm,
-              got, done_ref, done_sems, rows_ref, gain_ref, x_ref, sems):
-    copies = fetch((rows_hbm, gain_hbm, x_hbm), (rows_ref, gain_ref, x_ref), sems)
-    points = x_ref.shape[0]
-    half = points // 2
+def grid_body(turn, sub_ref, core_ref, outer, s0, s1, s2, s3, rows_hbm, gain_hbm, x_hbm, *refs):
+    out_hbm, got, done_ref, done_sems, rows_ref, gain_ref, x_ref, sems = refs[-8:]
+    half = x_ref.shape[0]
+    upper = (1 - core_ref[0]) if turn == 0 else core_ref[0]
+    base = pl.multiple_of(upper * half, half)
+    copies = fetch((rows_hbm, gain_hbm, x_hbm.at[pl.ds(base, half)]), (rows_ref, gain_ref, x_ref), sems)
     cap = rows_ref.shape[3]
     block = 4 * cap
     me = sub_ref[0]
-    core = core_ref[0]
-    got[pl.ds(pl.multiple_of((1 - core) * (2 * block), block), block), :] = near[...]
-    got[pl.ds(pl.multiple_of(core * (2 * block), block), block), :] = far[...]
+    got[0:block] = outer[...]
     for k, piece in enumerate((s0, s1, s2, s3)):
         got[block + k * cap : block + (k + 1) * cap] = piece[1]
     for copy in copies:
         copy.wait()
     gain = gain_ref[...]
     idx = []
-    for o in range(3):
+    for o in (2 * upper, 1):
         for k in range(4):
             idx.append(rows_ref[0, o, pl.ds(lax.rem(me + k, 4), 1), :])
-    idx = jnp.concatenate(idx, axis=1)
+    idx = jnp.concatenate(idx, axis=1) - base
     tile = 256
     stores = []
-    for t in range(points // tile):
-        first = t * tile
-        low = 0 if first < half else block
-        ids = lax.broadcasted_iota(jnp.int32, (tile, 2 * block), 0) + first
-        onehot = jnp.where(ids == idx[:, low : low + 2 * block], 1.0, 0.0).astype(BF16)
-        upstream = nn(onehot, got[low : low + 2 * block, :])
-        wide = x_ref[first : first + tile, :].astype(F32)
-        part = slice(first, first + tile)
+    for t in range(half // tile):
+        part = slice(t * tile, (t + 1) * tile)
+        ids = lax.broadcasted_iota(jnp.int32, (tile, 2 * block), 0) + t * tile
+        onehot = jnp.where(ids == idx, 1.0, 0.0).astype(BF16)
+        upstream = nn(onehot, got[...])
+        wide = x_ref[part, :].astype(F32)
         done_ref[part, :] = norm_back(wide, inv_rms(wide), gain, upstream).astype(BF16)
         stores.append(
-            pltpu.make_async_copy(done_ref.at[part], out_hbm.at[part], done_sems.at[t])
+            pltpu.make_async_copy(
+                done_ref.at[part], out_hbm.at[pl.ds(base + t * tile, tile)], done_sems.at[t]
+            )
         )
         stores[-1].start()
     for store in stores:
@@ -434,7 +433,7 @@
         held(w_out, w_query, mesh_h, gain_m),
     )
     s1, s2, s3 = (shifted(s, "z", -k) for k, s in ((1, s1), (2, s2), (3, s3)))
-    s1, parts, mesh_out = lax.optimization_barrier((s1, parts, mesh_out))
+    s1, s2, s3, parts, mesh_out = lax.optimization_barrier((s1, s2, s3, parts, mesh_out))
     part = jnp.sum(parts.astype(F32), axis=0).astype(BF16)
     part, s0 = lax.optimization_barrier((part, s0))
     near, far = call(
@@ -443,19 +442,27 @@
     far = swapped_far(far)
     near = shifted(near, "gc", 1)
     p1, p2, p3 = (shifted(part, "z", k) for k in (1, 2, 3))
-    p1, near, far = lax.optimization_barrier((p1, near, far))
     (spread,) = call(
         spread_body, [sds((plane, share, width))], [VM] * 4, (part, p1, p2, p3), 1 << 18, 1 << 20,
         "spread", [pltpu.VMEM((share, width), BF16), pltpu.SemaphoreType.DMA((plane,))], [HB],
     )
     mine = lax.all_to_all(spread, PLANE, 0, 0, tiled=True).reshape(2 * width, width)
+    half = points // 2
+    grid_scratch = [
+        pltpu.VMEM((2 * block, width), BF16), pltpu.VMEM((half, width), BF16),
+        pltpu.SemaphoreType.DMA((half // 256,)), pltpu.VMEM(send_rows.shape, send_rows.dtype),
+        pltpu.VMEM(gain_g.shape, F32), pltpu.VMEM((half, width), BF16), pltpu.SemaphoreType.DMA((3,)),
+    ]
+    grid_specs = [SM] * 2 + [VM] * 5 + [HB] * 3
     (grid_grad,) = call(
-        grid_body, [sds((points, width))], [SM] * 2 + [VM] * 6 + [HB] * 3,
-        (sub1, core1, near, far, s0, s1, s2, s3, send_rows, gain_g, grid_x),
-        1 << 30, 5 << 20, "grid_grad",
-        [pltpu.VMEM((slots, width), BF16), pltpu.VMEM((points, width), BF16),
-         pltpu.SemaphoreType.DMA((points // 256,))] + held(send_rows, gain_g, grid_x),
-        [HB],
+        functools.partial(grid_body, 0), [sds((points, width))], grid_specs,
+        (sub1, core1, near, s0, s1, s2, s3, send_rows, gain_g, grid_x),
+        1 << 29, 3 << 20, "grid_near", grid_scratch, [HB],
+    )
+    (grid_grad,) = call(
+        functools.partial(grid_body, 1), [sds((points, width))], grid_specs + [HB],
+        (sub1, core1, far, s0, s1, s2, s3, send_rows, gain_g, grid_x, grid_grad),
+        1 << 29, 3 << 20, "grid_far", grid_scratch, [HB], {10: 0},
     )
     mine, grid_grad = lax.optimization_barrier((mine, grid_grad))
     theirs = shifted(mine, "gc", 1)

time: 99.5 us -> 96 us (0.965)
  waiting for transfers between devices: 28.6 us -> 24.9 us
  Pallas kernels: 26.6 us -> 28.5 us
  starting transfers between devices: 42.6 us -> 41 us
    all_to_all x1, waiting for transfers between devices: 10.6 us -> 0.01 us  [shards(): lax.all_to_all(spread, PLANE, 0, 0, tiled=True).reshape(2 * width, width)]
    ppermute x2, waiting for transfers between devices: 1.18 us -> 8.02 us  [swapped_far(): return lax.ppermute(block, SLAB, pairs + [(j, i) for i, j in pairs])]
    ppermute x16, waiting for transfers between devices: 7.64 us -> 14.5 us  [shifted(): return lax.ppermute(block, axis, [(i, (i + k) % n) for i in range(n)])]
    all_to_all x1, waiting for transfers between devices: 9.15 us -> 2.38 us  [shards(): lax.all_to_all(own.reshape(plane, share, width), PLANE, 0, 0, tiled=True)]
    ppermute x16, starting transfers between devices: 24.3 us -> 21.6 us  [shifted(): return lax.ppermute(block, axis, [(i, (i + k) % n) for i in range(n)])]
    pallas_call x15 -> x16, Pallas kernels: 26.6 us -> 28.5 us  [call(): pl.pallas_call(body, out_shape=outs, in_specs=in_specs, out_specs=out_spe...]
    ppermute x2, starting transfers between devices: 5.28 us -> 6.51 us  [swapped_far(): return lax.ppermute(block, SLAB, pairs + [(j, i) for i, j in pairs])]
  transfers between devices with their start and end apart: 20 -> 20, of which waited for: 10 -> 11; matrix products, arithmetic and copies ran while one was open for 0% -> 0% of each run, Pallas kernels for 14% -> 17%
where the time goes in v9:
time: 96 us; the launch traced here: 95.5 us
  starting transfers between devices  41 us (43%)
  Pallas kernels  28.5 us (30%)
  waiting for transfers between devices  24.9 us (26%)
  between operations  1.03 us (1%)
    pallas_call x16, Pallas kernels, call(): pl.pallas_call(body, out_shape=outs, in_specs=in_specs, out_specs=out_spe...  28.5 us
    ppermute x16, starting transfers between devices, shifted(): return lax.ppermute(block, axis, [(i, (i + k) % n) for i in range(n)])  21.6 us
    ppermute x16, waiting for transfers between devices, shifted(): return lax.ppermute(block, axis, [(i, (i + k) % n) for i in range(n)])  14.5 us
    ppermute x2, waiting for transfers between devices, swapped_far(): return lax.ppermute(block, SLAB, pairs + [(j, i) for i, j in pairs])  8.02 us
    all_to_all x1, starting transfers between devices, shards(): lax.all_to_all(own.reshape(plane, share, width), PLANE, 0, 0, tiled=True)  7.79 us
    ppermute x2, starting transfers between devices, swapped_far(): return lax.ppermute(block, SLAB, pairs + [(j, i) for i, j in pairs])  6.51 us
    all_to_all x1, starting transfers between devices, shards(): lax.all_to_all(spread, PLANE, 0, 0, tiled=True).reshape(2 * width, width)  5.14 us
    all_to_all x1, waiting for transfers between devices, shards(): lax.all_to_all(own.reshape(plane, share, width), PLANE, 0, 0, tiled=True)  2.38 us
  transfers between devices with their start and end apart: 20, of which 11 were waited for; matrix products, arithmetic and copies ran while one was open for 0% of the time, Pallas kernels for 17%

profile of v9, /device:TPU:1, one launch (start us, length us, event | category | flops | bytes accessed | tf_op | source)
XLA Modules:
  0.0 95.5 jit_solution(10624656113491252879)
XLA Ops:
  0.6 3.0 %gather_rows.1 = (bf16[256,512]{1,0:T(8,128)(2,1)S(1)}, bf16[256,512]{1,0:T(8,128)(2,1)S(1)}, bf16[256,512]{1,0:T(8,128)(2,1)S(1)}) custom-call(s32[1]{0:T(128)} %bitcast.1.sub_ref, s32[1]{0:T(128)} %bitcast.core_ref, s32[1,3,4,64]{3,2,1,0:T(4,128)} %rows_hbm.5, f32[1,512]{1,0:T(1,128)} %bitcast.10, bf16[2048,512]{1,0:T(8,128)(2,1)} %x_hbm.5), custom_call_target="tpu_custom_call" | custom-call | flops 1073741824 | bytes 4194304 | tf_op jit(solution)/shard_map/gather_rows/pallas_call | solution.py:48
  3.6 1.5 %collective-permute-start = (bf16[256,512]{1,0:T(8,128)(2,1)S(1)}, bf16[256,512]{1,0:T(8,128)(2,1)S(1)}, u32[]{:S(2)}, u32[]{:S(2)}) collective-permute-start(bf16[256,512]{1,0:T(8,128)(2,1)S(1)} %get-tuple-element.48), channel_id=1, source_target_pairs={{0,4},{4,0},{1,5},{5,1},{2,6},{6,2},{3,7},{7,3},{8,12},{12,8},{9,1... | collective-permute-start | bytes 786440 | tf_op jit(solution)/shard_map/ppermute | solution.py:344
  5.1 3.2 %collective-permute-start.1 = (bf16[256,512]{1,0:T(8,128)(2,1)S(1)}, bf16[256,512]{1,0:T(8,128)(2,1)S(1)}, u32[]{:S(2)}, u32[]{:S(2)}) collective-permute-start(bf16[256,512]{1,0:T(8,128)(2,1)S(1)} %get-tuple-element.49), channel_id=1, source_target_pairs={{4,8},{12,16},{20,24},{28,32},{36,40},{44,48},{52,56},{60,64},{68,... | collective-permute-start | bytes 786440 | tf_op jit(solution)/shard_map/ppermute | solution.py:350
  8.3 1.7 %collective-permute-start.2 = (bf16[128,512]{1,0:T(8,128)(2,1)S(1)}, bf16[128,512]{1,0:T(8,128)(2,1)S(1)}, u32[]{:S(2)}, u32[]{:S(2)}) collective-permute-start(bf16[128,512]{1,0:T(8,128)(2,1)S(1)} %get-tuple-element.51), channel_id=1, source_target_pairs={{0,1},{1,2},{2,3},{3,0},{4,5},{5,6},{6,7},{7,4},{8,9},{9,10},{10,1... | collective-permute-start | bytes 393224 | tf_op jit(solution)/shard_map/ppermute | solution.py:344
  10.0 3.3 %collective-permute-start.3 = (bf16[128,512]{1,0:T(8,128)(2,1)S(1)}, bf16[128,512]{1,0:T(8,128)(2,1)S(1)}, u32[]{:S(2)}, u32[]{:S(2)}) collective-permute-start(bf16[128,512]{1,0:T(8,128)(2,1)S(1)} %get-tuple-element.55), channel_id=1, source_target_pairs={{0,2},{1,3},{2,0},{3,1},{4,6},{5,7},{6,4},{7,5},{8,10},{9,11},{10,... | collective-permute-start | bytes 393224 | tf_op jit(solution)/shard_map/ppermute | solution.py:344
  14.1 1.7 %mesh_in.1 = (bf16[64,512]{1,0:T(8,128)(2,1)S(1)}, bf16[64,512]{1,0:T(8,128)(2,1)S(1)}, bf16[64,512]{1,0:T(8,128)(2,1)S(1)}, bf16[64,512]{1,0:T(8,128)(2,1)S(1)}) custom-call(bf16[64,512]{1,0:T(8,128)(2,1)} %mesh_hbm.3, f32[1,512]{1,0:T(1,128)} %bitcast.8, bf16[512,512]{1,0:T(8,128)(2,1)} %wq_hbm.3, bf16[512,512]{1,0:T(8,128)(2,1)} %wo_hbm.3, ...), custom_call_target="tpu_custom_call" | custom-call | flops 268435456 | bytes 2097152 | tf_op jit(solution)/shard_map/mesh_in/pallas_call | solution.py:48
  16.7 2.3 %collective-permute-start.6 = (bf16[64,512]{1,0:T(8,128)(2,1)S(1)}, bf16[64,512]{1,0:T(8,128)(2,1)S(1)}, u32[]{:S(2)}, u32[]{:S(2)}) collective-permute-start(bf16[64,512]{1,0:T(8,128)(2,1)S(1)} %get-tuple-element.58), channel_id=1, source_target_pairs={{0,2},{1,3},{2,0},{3,1},{4,6},{5,7},{6,4},{7,5},{8,10},{9,11},{10,... | collective-permute-start | bytes 196616 | tf_op jit(solution)/shard_map/ppermute | solution.py:344
  19.1 2.3 %slots.1.bias_ref = f32[4,64,768]{2,1,0:T(8,128)S(1)} custom-call(s32[1]{0:T(128)} %bitcast.1.sub_ref, s32[64,96]{1,0:T(8,128)} %nbr_hbm.1, s32[64,96]{1,0:T(8,128)} %valid_hbm.1, f32[64,384]{1,0:T(8,128)} %bias_hbm.1), custom_call_target="tpu_custom_call" | custom-call | flops 1073741824 | bytes 8388608 | tf_op jit(solution)/shard_map/slots/pallas_call | solution.py:48
  23.2 6.2 %middle.1 = (bf16[1024,512]{1,0:T(8,128)(2,1)S(1)}, bf16[768,1024]{1,0:T(8,128)(2,1)S(1)}, bf16[64,512]{1,0:T(8,128)(2,1)S(1)}, bf16[64,512]{1,0:T(8,128)(2,1)S(...) custom-call(s32[1]{0:T(128)} %bitcast.core_ref, bf16[256,512]{1,0:T(8,128)(2,1)S(1)} %collective-permute-done.near, ...), custom_call_target="tpu_custom_call" | custom-call | flops 3221225472 | bytes 8388608 | tf_op jit(solution)/shard_map/middle/pallas_call | solution.py:48
  33.2 7.8 %all-to-all-start = ((bf16[16,64,512]{2,1,0:T(8,128)(2,1)}), bf16[16,64,512]{2,1,0:T(8,128)(2,1)S(1)}, u32[]{:S(2)}, u32[]{:S(2)}) async-start(bf16[16,64,512]{2,1,0:T(8,128)(2,1)} %bitcast.4), calls=%async_computation | async-start | bytes 2097152 | tf_op jit(solution)/shard_map/all_to_all | solution.py:427
  43.5 1.6 %collective-permute-start.9 = (bf16[3,64,512]{2,1,0:T(8,128)(2,1)S(1)}, bf16[3,64,512]{2,1,0:T(8,128)(2,1)S(1)}, u32[]{:S(2)}, u32[]{:S(2)}) collective-permute-start(bf16[3,64,512]{2,1,0:T(8,128)(2,1)S(1)} %get-tuple-element.72), channel_id=1, source_target_pairs={{0,3},{1,0},{2,1},{3,2},{4,7},{5,4},{6,5},{7,6},{8,11},{9,8},{10,9... | collective-permute-start | bytes 589832 | tf_op jit(solution)/shard_map/ppermute | solution.py:344
  45.0 2.3 %mesh.1 = (bf16[64,512]{1,0:T(8,128)(2,1)}, bf16[64,512]{1,0:T(8,128)(2,1)}) custom-call(bf16[64,512]{1,0:T(8,128)(2,1)S(1)} %get-tuple-element.77.att_ref, bf16[64,512]{1,0:T(8,128)(2,1)S(1)} %get-tuple-element.70.qg_ref, bf16[64,512]{1,0:T(8,128)(2,1)S(1)} %get-tuple-element.63.og_ref, bf16[512,512]{1,0:T(8,128)(2,1)} %wo_hbm.3, bf16[512,512]{1,0:T(8,128)(2,1)} %wq_hbm.3, ...), custom_call_target="tpu_custom_call" | custom-call | flops 268435456 | bytes 2097152 | tf_op jit(solution)/shard_map/mesh/pallas_call | solution.py:48
  48.4 5.2 %collective-permute-done.11.p3.s3 = bf16[3,64,512]{2,1,0:T(8,128)(2,1)S(1)} collective-permute-done((bf16[3,64,512]{2,1,0:T(8,128)(2,1)S(1)}, bf16[3,64,512]{2,1,0:T(8,128)(2,1)S(1)}, u32[]{:S(2)}, u32[]{:S(2)}) %collective-permute-start.11) | collective-permute-done | bytes 196640 | tf_op jit(solution)/shard_map/ppermute | solution.py:344
  53.6 2.4 %all-to-all-done = bf16[16,64,512]{2,1,0:T(8,128)(2,1)S(1)} async-done(((bf16[16,64,512]{2,1,0:T(8,128)(2,1)}), bf16[16,64,512]{2,1,0:T(8,128)(2,1)S(1)}, u32[]{:S(2)}, u32[]{:S(2)}) %all-to-all-start) | async-done | bytes 1048608 | tf_op jit(solution)/shard_map/all_to_all | solution.py:427
  56.2 2.0 %collective-permute-start.14 = (bf16[64,512]{1,0:T(8,128)(2,1)S(1)}, bf16[64,512]{1,0:T(8,128)(2,1)S(1)}, u32[]{:S(2)}, u32[]{:S(2)}) collective-permute-start(bf16[64,512]{1,0:T(8,128)(2,1)S(1)} %reduce_sum.12.p0), channel_id=1, source_target_pairs={{0,3},{1,0},{2,1},{3,2},{4,7},{5,4},{6,5},{7,6},{8,11},{9,8},{10,9... | collective-permute-start | bytes 196616 | tf_op jit(solution)/shard_map/ppermute | solution.py:344
  60.1 2.8 %collective-permute-done.13.p2 = bf16[64,512]{1,0:T(8,128)(2,1)S(1)} collective-permute-done((bf16[64,512]{1,0:T(8,128)(2,1)S(1)}, bf16[64,512]{1,0:T(8,128)(2,1)S(1)}, u32[]{:S(2)}, u32[]{:S(2)}) %collective-permute-start.13) | collective-permute-done | bytes 65568 | tf_op jit(solution)/shard_map/ppermute | solution.py:344
  64.7 5.1 %all-to-all-start.1 = ((bf16[16,64,512]{2,1,0:T(8,128)(2,1)}), bf16[16,64,512]{2,1,0:T(8,128)(2,1)S(1)}, u32[]{:S(2)}, u32[]{:S(2)}) async-start(bf16[16,64,512]{2,1,0:T(8,128)(2,1)} %spread.1), calls=%async_computation.1 | async-start | bytes 2097152 | tf_op jit(solution)/shard_map/all_to_all | solution.py:449
  69.9 3.8 %collective-permute-start.16 = (bf16[256,512]{1,0:T(8,128)(2,1)S(1)}, bf16[256,512]{1,0:T(8,128)(2,1)S(1)}, u32[]{:S(2)}, u32[]{:S(2)}) collective-permute-start(bf16[256,512]{1,0:T(8,128)(2,1)S(1)} %get-tuple-element.89), channel_id=1, source_target_pairs={{0,4},{4,0},{1,5},{5,1},{2,6},{6,2},{3,7},{7,3},{8,12},{12,8},{9,1... | collective-permute-start | bytes 786440 | tf_op jit(solution)/shard_map/ppermute | solution.py:344
  73.6 3.3 %collective-permute-start.15 = (bf16[256,512]{1,0:T(8,128)(2,1)S(1)}, bf16[256,512]{1,0:T(8,128)(2,1)S(1)}, u32[]{:S(2)}, u32[]{:S(2)}) collective-permute-start(bf16[256,512]{1,0:T(8,128)(2,1)S(1)} %get-tuple-element.88), channel_id=1, source_target_pairs={{4,8},{12,16},{20,24},{28,32},{36,40},{44,48},{52,56},{60,64},{68,... | collective-permute-start | bytes 786440 | tf_op jit(solution)/shard_map/ppermute | solution.py:350
  77.0 3.1 %grid_near.1.refs_0_ = bf16[2048,512]{1,0:T(8,128)(2,1)} custom-call(s32[1]{0:T(128)} %bitcast.1.sub_ref, s32[1]{0:T(128)} %bitcast.core_ref, bf16[256,512]{1,0:T(8,128)(2,1)S(1)} %collective-permute-done.16.outer, bf16[3,64,512]{2,1,0:T(8,128)(2,1)S(1)} %get-tuple-element.84.p0.s0, bf16[3,64,512]{2,1,0:T(8,128)(2,1)S(1)} %collective-permute-done.9.p1.s1, ...), custom_call_target="tpu_custom_call" | custom-call | flops 536870912 | bytes 3145728 | tf_op jit(solution)/shard_map/grid_near/pallas_call | solution.py:48
  80.1 8.0 %collective-permute-done.15.outer = bf16[256,512]{1,0:T(8,128)(2,1)S(1)} collective-permute-done((bf16[256,512]{1,0:T(8,128)(2,1)S(1)}, bf16[256,512]{1,0:T(8,128)(2,1)S(1)}, u32[]{:S(2)}, u32[]{:S(2)}) %collective-permute-start.15) | collective-permute-done | bytes 262176 | tf_op jit(solution)/shard_map/ppermute | solution.py:350
  88.1 3.1 %grid_far.1 = bf16[2048,512]{1,0:T(8,128)(2,1)} custom-call(s32[1]{0:T(128)} %bitcast.1.sub_ref, s32[1]{0:T(128)} %bitcast.core_ref, bf16[256,512]{1,0:T(8,128)(2,1)S(1)} %collective-permute-done.15.outer, bf16[3,64,512]{2,1,0:T(8,128)(2,1)S(1)} %get-tuple-element.84.p0.s0, ...), custom_call_target="tpu_custom_call", output_to_operand_aliasing={{}: (10, {})} | custom-call | flops 536870912 | bytes 3145728 | tf_op jit(solution)/shard_map/grid_far/pallas_call | solution.py:48
  91.3 1.4 %widen_own.1.refs_0_ = f32[4,512,512]{2,1,0:T(8,128)} custom-call(s32[1]{0:T(128)} %bitcast.core_ref, bf16[1024,512]{1,0:T(8,128)(2,1)S(1)} %bitcast.7), custom_call_target="tpu_custom_call" | custom-call | flops 1048576 | bytes 3145728 | tf_op jit(solution)/shard_map/widen_own/pallas_call | solution.py:48
  94.0 1.4 %widen_other.1 = f32[4,512,512]{2,1,0:T(8,128)} custom-call(s32[1]{0:T(128)} %bitcast.core_ref, bf16[1024,512]{1,0:T(8,128)(2,1)S(1)} %collective-permute-done.17.half_ref, f32[4,512,512]{2,1,0:T(8,128)} %widen_own.1.refs_0_), custom_call_target="tpu_custom_call", output_to_operand_aliasing={{}: (2, {})} | custom-call | flops 1048576 | bytes 3145728 | tf_op jit(solution)/shard_map/widen_other/pallas_call | solution.py:48
  (33 shorter events, 16.0 us)
Async XLA Ops:
  3.6 4.7 %collective-permute-start = (bf16[256,512]{1,0:T(8,128)(2,1)S(1)}, bf16[256,512]{1,0:T(8,128)(2,1)S(1)}, u32[]{:S(2)}, u32[]{:S(2)}) collective-permute-start(bf16[256,512]{1,0:T(8,128)(2,1)S(1)} %get-tuple-element.48), channel_id=1, source_target_pairs={{0,4},{4,0},{1,5},{5,1},{2,6},{6,2},{3,7},{7,3},{8,12},{12,8},{9,1... | collective-permute-start | bytes 786440 | tf_op jit(solution)/shard_map/ppermute | solution.py:344
  5.1 10.7 %collective-permute-start.1 = (bf16[256,512]{1,0:T(8,128)(2,1)S(1)}, bf16[256,512]{1,0:T(8,128)(2,1)S(1)}, u32[]{:S(2)}, u32[]{:S(2)}) collective-permute-start(bf16[256,512]{1,0:T(8,128)(2,1)S(1)} %get-tuple-element.49), channel_id=1, source_target_pairs={{4,8},{12,16},{20,24},{28,32},{36,40},{44,48},{52,56},{60,64},{68,... | collective-permute-start | bytes 786440 | tf_op jit(solution)/shard_map/ppermute | solution.py:350
  8.3 7.5 %collective-permute-start.2 = (bf16[128,512]{1,0:T(8,128)(2,1)S(1)}, bf16[128,512]{1,0:T(8,128)(2,1)S(1)}, u32[]{:S(2)}, u32[]{:S(2)}) collective-permute-start(bf16[128,512]{1,0:T(8,128)(2,1)S(1)} %get-tuple-element.51), channel_id=1, source_target_pairs={{0,1},{1,2},{2,3},{3,0},{4,5},{5,6},{6,7},{7,4},{8,9},{9,10},{10,1... | collective-permute-start | bytes 393224 | tf_op jit(solution)/shard_map/ppermute | solution.py:344
  10.0 11.4 %collective-permute-start.3 = (bf16[128,512]{1,0:T(8,128)(2,1)S(1)}, bf16[128,512]{1,0:T(8,128)(2,1)S(1)}, u32[]{:S(2)}, u32[]{:S(2)}) collective-permute-start(bf16[128,512]{1,0:T(8,128)(2,1)S(1)} %get-tuple-element.55), channel_id=1, source_target_pairs={{0,2},{1,3},{2,0},{3,1},{4,6},{5,7},{6,4},{7,5},{8,10},{9,11},{10,... | collective-permute-start | bytes 393224 | tf_op jit(solution)/shard_map/ppermute | solution.py:344
  13.3 8.1 %collective-permute-start.4 = (bf16[128,512]{1,0:T(8,128)(2,1)S(1)}, bf16[128,512]{1,0:T(8,128)(2,1)S(1)}, u32[]{:S(2)}, u32[]{:S(2)}) collective-permute-start(bf16[128,512]{1,0:T(8,128)(2,1)S(1)} %get-tuple-element.56), channel_id=1, source_target_pairs={{0,3},{1,0},{2,1},{3,2},{4,7},{5,4},{6,5},{7,6},{8,11},{9,8},{10,9... | collective-permute-start | bytes 393224 | tf_op jit(solution)/shard_map/ppermute | solution.py:344
  15.9 5.6 %collective-permute-start.5 = (bf16[64,512]{1,0:T(8,128)(2,1)S(1)}, bf16[64,512]{1,0:T(8,128)(2,1)S(1)}, u32[]{:S(2)}, u32[]{:S(2)}) collective-permute-start(bf16[64,512]{1,0:T(8,128)(2,1)S(1)} %get-tuple-element.57), channel_id=1, source_target_pairs={{0,1},{1,2},{2,3},{3,0},{4,5},{5,6},{6,7},{7,4},{8,9},{9,10},{10,1... | collective-permute-start | bytes 196616 | tf_op jit(solution)/shard_map/ppermute | solution.py:344
  16.7 5.6 %collective-permute-start.6 = (bf16[64,512]{1,0:T(8,128)(2,1)S(1)}, bf16[64,512]{1,0:T(8,128)(2,1)S(1)}, u32[]{:S(2)}, u32[]{:S(2)}) collective-permute-start(bf16[64,512]{1,0:T(8,128)(2,1)S(1)} %get-tuple-element.58), channel_id=1, source_target_pairs={{0,2},{1,3},{2,0},{3,1},{4,6},{5,7},{6,4},{7,5},{8,10},{9,11},{10,... | collective-permute-start | bytes 196616 | tf_op jit(solution)/shard_map/ppermute | solution.py:344
  19.0 4.2 %collective-permute-start.7 = (bf16[64,512]{1,0:T(8,128)(2,1)S(1)}, bf16[64,512]{1,0:T(8,128)(2,1)S(1)}, u32[]{:S(2)}, u32[]{:S(2)}) collective-permute-start(bf16[64,512]{1,0:T(8,128)(2,1)S(1)} %get-tuple-element.59), channel_id=1, source_target_pairs={{0,3},{1,0},{2,1},{3,2},{4,7},{5,4},{6,5},{7,6},{8,11},{9,8},{10,9... | collective-permute-start | bytes 196616 | tf_op jit(solution)/shard_map/ppermute | solution.py:344
  29.4 2.8 %collective-permute-start.8 = (bf16[1024,512]{1,0:T(8,128)(2,1)S(1)}, bf16[1024,512]{1,0:T(8,128)(2,1)S(1)}, u32[]{:S(2)}, u32[]{:S(2)}) collective-permute-start(bf16[1024,512]{1,0:T(8,128)(2,1)S(1)} %get-tuple-element.65), channel_id=1, source_target_pairs={{0,4},{4,0},{1,5},{5,1},{2,6},{6,2},{3,7},{7,3},{8,12},{12,8},{9,1... | collective-permute-start | bytes 3145736 | tf_op jit(solution)/shard_map/ppermute | solution.py:344
  33.2 22.8 %all-to-all-start = ((bf16[16,64,512]{2,1,0:T(8,128)(2,1)}), bf16[16,64,512]{2,1,0:T(8,128)(2,1)S(1)}, u32[]{:S(2)}, u32[]{:S(2)}) async-start(bf16[16,64,512]{2,1,0:T(8,128)(2,1)} %bitcast.4), calls=%async_computation | async-start | bytes 2097152 | tf_op jit(solution)/shard_map/all_to_all | solution.py:427
  41.0 7.4 %collective-permute-start.10 = (bf16[3,64,512]{2,1,0:T(8,128)(2,1)S(1)}, bf16[3,64,512]{2,1,0:T(8,128)(2,1)S(1)}, u32[]{:S(2)}, u32[]{:S(2)}) collective-permute-start(bf16[3,64,512]{2,1,0:T(8,128)(2,1)S(1)} %get-tuple-element.73), channel_id=1, source_target_pairs={{0,2},{1,3},{2,0},{3,1},{4,6},{5,7},{6,4},{7,5},{8,10},{9,11},{10,... | collective-permute-start | bytes 589832 | tf_op jit(solution)/shard_map/ppermute | solution.py:344
  42.3 11.3 %collective-permute-start.11 = (bf16[3,64,512]{2,1,0:T(8,128)(2,1)S(1)}, bf16[3,64,512]{2,1,0:T(8,128)(2,1)S(1)}, u32[]{:S(2)}, u32[]{:S(2)}) collective-permute-start(bf16[3,64,512]{2,1,0:T(8,128)(2,1)S(1)} %get-tuple-element.74), channel_id=1, source_target_pairs={{0,1},{1,2},{2,3},{3,0},{4,5},{5,6},{6,7},{7,4},{8,9},{9,10},{10,1... | collective-permute-start | bytes 589832 | tf_op jit(solution)/shard_map/ppermute | solution.py:344
  43.5 10.2 %collective-permute-start.9 = (bf16[3,64,512]{2,1,0:T(8,128)(2,1)S(1)}, bf16[3,64,512]{2,1,0:T(8,128)(2,1)S(1)}, u32[]{:S(2)}, u32[]{:S(2)}) collective-permute-start(bf16[3,64,512]{2,1,0:T(8,128)(2,1)S(1)} %get-tuple-element.72), channel_id=1, source_target_pairs={{0,3},{1,0},{2,1},{3,2},{4,7},{5,4},{6,5},{7,6},{8,11},{9,8},{10,9... | collective-permute-start | bytes 589832 | tf_op jit(solution)/shard_map/ppermute | solution.py:344
  56.2 3.9 %collective-permute-start.14 = (bf16[64,512]{1,0:T(8,128)(2,1)S(1)}, bf16[64,512]{1,0:T(8,128)(2,1)S(1)}, u32[]{:S(2)}, u32[]{:S(2)}) collective-permute-start(bf16[64,512]{1,0:T(8,128)(2,1)S(1)} %reduce_sum.12.p0), channel_id=1, source_target_pairs={{0,3},{1,0},{2,1},{3,2},{4,7},{5,4},{6,5},{7,6},{8,11},{9,8},{10,9... | collective-permute-start | bytes 196616 | tf_op jit(solution)/shard_map/ppermute | solution.py:344
  58.2 4.7 %collective-permute-start.13 = (bf16[64,512]{1,0:T(8,128)(2,1)S(1)}, bf16[64,512]{1,0:T(8,128)(2,1)S(1)}, u32[]{:S(2)}, u32[]{:S(2)}) collective-permute-start(bf16[64,512]{1,0:T(8,128)(2,1)S(1)} %reduce_sum.12.p0), channel_id=1, source_target_pairs={{0,2},{1,3},{2,0},{3,1},{4,6},{5,7},{6,4},{7,5},{8,10},{9,11},{10,... | collective-permute-start | bytes 196616 | tf_op jit(solution)/shard_map/ppermute | solution.py:344
  58.5 5.0 %collective-permute-start.12 = (bf16[64,512]{1,0:T(8,128)(2,1)S(1)}, bf16[64,512]{1,0:T(8,128)(2,1)S(1)}, u32[]{:S(2)}, u32[]{:S(2)}) collective-permute-start(bf16[64,512]{1,0:T(8,128)(2,1)S(1)} %reduce_sum.12.p0), channel_id=1, source_target_pairs={{0,1},{1,2},{2,3},{3,0},{4,5},{5,6},{6,7},{7,4},{8,9},{9,10},{10,1... | collective-permute-start | bytes 196616 | tf_op jit(solution)/shard_map/ppermute | solution.py:344
  64.7 26.6 %all-to-all-start.1 = ((bf16[16,64,512]{2,1,0:T(8,128)(2,1)}), bf16[16,64,512]{2,1,0:T(8,128)(2,1)S(1)}, u32[]{:S(2)}, u32[]{:S(2)}) async-start(bf16[16,64,512]{2,1,0:T(8,128)(2,1)} %spread.1), calls=%async_computation.1 | async-start | bytes 2097152 | tf_op jit(solution)/shard_map/all_to_all | solution.py:449
  69.9 7.1 %collective-permute-start.16 = (bf16[256,512]{1,0:T(8,128)(2,1)S(1)}, bf16[256,512]{1,0:T(8,128)(2,1)S(1)}, u32[]{:S(2)}, u32[]{:S(2)}) collective-permute-start(bf16[256,512]{1,0:T(8,128)(2,1)S(1)} %get-tuple-element.89), channel_id=1, source_target_pairs={{0,4},{4,0},{1,5},{5,1},{2,6},{6,2},{3,7},{7,3},{8,12},{12,8},{9,1... | collective-permute-start | bytes 786440 | tf_op jit(solution)/shard_map/ppermute | solution.py:344
  73.6 14.5 %collective-permute-start.15 = (bf16[256,512]{1,0:T(8,128)(2,1)S(1)}, bf16[256,512]{1,0:T(8,128)(2,1)S(1)}, u32[]{:S(2)}, u32[]{:S(2)}) collective-permute-start(bf16[256,512]{1,0:T(8,128)(2,1)S(1)} %get-tuple-element.88), channel_id=1, source_target_pairs={{4,8},{12,16},{20,24},{28,32},{36,40},{44,48},{52,56},{60,64},{68,... | collective-permute-start | bytes 786440 | tf_op jit(solution)/shard_map/ppermute | solution.py:350
  91.2 2.7 %collective-permute-start.17 = (bf16[1024,512]{1,0:T(8,128)(2,1)S(1)}, bf16[1024,512]{1,0:T(8,128)(2,1)S(1)}, u32[]{:S(2)}, u32[]{:S(2)}) collective-permute-start(bf16[1024,512]{1,0:T(8,128)(2,1)S(1)} %bitcast.6), channel_id=1, source_target_pairs={{0,4},{4,0},{1,5},{5,1},{2,6},{6,2},{3,7},{7,3},{8,12},{12,8},{9,1... | collective-permute-start | bytes 3145736 | tf_op jit(solution)/shard_map/ppermute | solution.py:344

commit v10 on v9

--- a/solution.py
+++ b/solution.py
@@ -262,28 +262,35 @@
     half = x_ref.shape[0]
     upper = (1 - core_ref[0]) if turn == 0 else core_ref[0]
     base = pl.multiple_of(upper * half, half)
-    copies = fetch((rows_hbm, gain_hbm, x_hbm.at[pl.ds(base, half)]), (rows_ref, gain_ref, x_ref), sems)
+    tile = 256
+    tiles = half // tile
+    spans = [pl.ds(t * tile, tile) for t in range(tiles)]
+    copies = fetch(
+        [rows_hbm, gain_hbm] + [x_hbm.at[pl.ds(base + t * tile, tile)] for t in range(tiles)],
+        [rows_ref, gain_ref] + [x_ref.at[span] for span in spans],
+        sems,
+    )
     cap = rows_ref.shape[3]
     block = 4 * cap
     me = sub_ref[0]
     got[0:block] = outer[...]
     for k, piece in enumerate((s0, s1, s2, s3)):
         got[block + k * cap : block + (k + 1) * cap] = piece[1]
-    for copy in copies:
-        copy.wait()
+    copies[0].wait()
+    copies[1].wait()
     gain = gain_ref[...]
     idx = []
     for o in (2 * upper, 1):
         for k in range(4):
             idx.append(rows_ref[0, o, pl.ds(lax.rem(me + k, 4), 1), :])
     idx = jnp.concatenate(idx, axis=1) - base
-    tile = 256
     stores = []
-    for t in range(half // tile):
+    for t in range(tiles):
         part = slice(t * tile, (t + 1) * tile)
         ids = lax.broadcasted_iota(jnp.int32, (tile, 2 * block), 0) + t * tile
         onehot = jnp.where(ids == idx, 1.0, 0.0).astype(BF16)
         upstream = nn(onehot, got[...])
+        copies[2 + t].wait()
         wide = x_ref[part, :].astype(F32)
         done_ref[part, :] = norm_back(wide, inv_rms(wide), gain, upstream).astype(BF16)
         stores.append(
@@ -300,10 +307,10 @@
     out_hbm, wide, sems = refs[-3:]
     count, width, _ = wide.shape
     half = core_ref[0] ^ turn
-    part = width // 2
+    part = width // 4
     copies = []
-    for i in range(2 * count):
-        m, rows = i // 2, pl.ds((i % 2) * part, part)
+    for i in range(4 * count):
+        m, rows = i // 4, pl.ds((i % 4) * part, part)
         wide[m, rows, :] = half_ref[i * part : (i + 1) * part, :].astype(F32)
         copies.append(
             pltpu.make_async_copy(
@@ -451,7 +458,7 @@
     grid_scratch = [
         pltpu.VMEM((2 * block, width), BF16), pltpu.VMEM((half, width), BF16),
         pltpu.SemaphoreType.DMA((half // 256,)), pltpu.VMEM(send_rows.shape, send_rows.dtype),
-        pltpu.VMEM(gain_g.shape, F32), pltpu.VMEM((half, width), BF16), pltpu.SemaphoreType.DMA((3,)),
+        pltpu.VMEM(gain_g.shape, F32), pltpu.VMEM((half, width), BF16), pltpu.SemaphoreType.DMA((2 + half // 256,)),
     ]
     grid_specs = [SM] * 2 + [VM] * 5 + [HB] * 3
     (grid_grad,) = call(
@@ -459,15 +466,15 @@
         (sub1, core1, near, s0, s1, s2, s3, send_rows, gain_g, grid_x),
         1 << 29, 3 << 20, "grid_near", grid_scratch, [HB],
     )
+    mine, far, grid_grad = lax.optimization_barrier((mine, far, grid_grad))
+    theirs = shifted(mine, "gc", 1)
     (grid_grad,) = call(
         functools.partial(grid_body, 1), [sds((points, width))], grid_specs + [HB],
         (sub1, core1, far, s0, s1, s2, s3, send_rows, gain_g, grid_x, grid_grad),
         1 << 29, 3 << 20, "grid_far", grid_scratch, [HB], {10: 0},
     )
-    mine, grid_grad = lax.optimization_barrier((mine, grid_grad))
-    theirs = shifted(mine, "gc", 1)
     whole = sds((4, width, width), F32)
-    wide = [pltpu.VMEM((2, width, width), F32), pltpu.SemaphoreType.DMA((4,))]
+    wide = [pltpu.VMEM((2, width, width), F32), pltpu.SemaphoreType.DMA((8,))]
     (weight_grads,) = call(
         functools.partial(widen_body, 0), [whole], [SM, VM], (core1, mine), 1 << 20, 3 << 20, "widen_own",
         wide, [HB],

time: 96 us -> 96.8 us (level)
  starting transfers between devices: 41 us -> 43.1 us
  waiting for transfers between devices: 24.9 us -> 23.7 us
    ppermute x16, starting transfers between devices: 21.6 us -> 23.7 us  [shifted(): return lax.ppermute(block, axis, [(i, (i + k) % n) for i in range(n)])]
    ppermute x16, waiting for transfers between devices: 14.5 us -> 13.2 us  [shifted(): return lax.ppermute(block, axis, [(i, (i + k) % n) for i in range(n)])]
  transfers between devices with their start and end apart: 20 -> 20, of which waited for: 11 -> 10; matrix products, arithmetic and copies ran while one was open for 0% -> 0% of each run, Pallas kernels for 17% -> 16%
where the time goes in v10:
time: 96.8 us; the launch traced here: 96.3 us
  starting transfers between devices  43.1 us (45%)
  Pallas kernels  28.3 us (29%)
  waiting for transfers between devices  23.7 us (24%)
  between operations  1.02 us (1%)
    pallas_call x16, Pallas kernels, call(): pl.pallas_call(body, out_shape=outs, in_specs=in_specs, out_specs=out_spe...  28.3 us
    ppermute x16, starting transfers between devices, shifted(): return lax.ppermute(block, axis, [(i, (i + k) % n) for i in range(n)])  23.7 us
    ppermute x16, waiting for transfers between devices, shifted(): return lax.ppermute(block, axis, [(i, (i + k) % n) for i in range(n)])  13.2 us
    ppermute x2, waiting for transfers between devices, swapped_far(): return lax.ppermute(block, SLAB, pairs + [(j, i) for i, j in pairs])  8.09 us
    all_to_all x1, starting transfers between devices, shards(): lax.all_to_all(own.reshape(plane, share, width), PLANE, 0, 0, tiled=True)  7.79 us
    ppermute x2, starting transfers between devices, swapped_far(): return lax.ppermute(block, SLAB, pairs + [(j, i) for i, j in pairs])  6.51 us
    all_to_all x1, starting transfers between devices, shards(): lax.all_to_all(spread, PLANE, 0, 0, tiled=True).reshape(2 * width, width)  5.14 us
    all_to_all x1, waiting for transfers between devices, shards(): lax.all_to_all(own.reshape(plane, share, width), PLANE, 0, 0, tiled=True)  2.38 us
  transfers between devices with their start and end apart: 20, of which 10 were waited for; matrix products, arithmetic and copies ran while one was open for 0% of the time, Pallas kernels for 16%

profile of v10, /device:TPU:1, one launch (start us, length us, event | category | flops | bytes accessed | tf_op | source)
XLA Modules:
  0.0 96.3 jit_solution(12329453569698060102)
XLA Ops:
  0.6 3.0 %gather_rows.1 = (bf16[256,512]{1,0:T(8,128)(2,1)S(1)}, bf16[256,512]{1,0:T(8,128)(2,1)S(1)}, bf16[256,512]{1,0:T(8,128)(2,1)S(1)}) custom-call(s32[1]{0:T(128)} %bitcast.1.sub_ref, s32[1]{0:T(128)} %bitcast.core_ref, s32[1,3,4,64]{3,2,1,0:T(4,128)} %rows_hbm.5, f32[1,512]{1,0:T(1,128)} %bitcast.10, bf16[2048,512]{1,0:T(8,128)(2,1)} %x_hbm.5), custom_call_target="tpu_custom_call" | custom-call | flops 1073741824 | bytes 4194304 | tf_op jit(solution)/shard_map/gather_rows/pallas_call | solution.py:48
  3.6 1.5 %collective-permute-start = (bf16[256,512]{1,0:T(8,128)(2,1)S(1)}, bf16[256,512]{1,0:T(8,128)(2,1)S(1)}, u32[]{:S(2)}, u32[]{:S(2)}) collective-permute-start(bf16[256,512]{1,0:T(8,128)(2,1)S(1)} %get-tuple-element.49), channel_id=1, source_target_pairs={{0,4},{4,0},{1,5},{5,1},{2,6},{6,2},{3,7},{7,3},{8,12},{12,8},{9,1... | collective-permute-start | bytes 786440 | tf_op jit(solution)/shard_map/ppermute | solution.py:351
  5.1 3.2 %collective-permute-start.1 = (bf16[256,512]{1,0:T(8,128)(2,1)S(1)}, bf16[256,512]{1,0:T(8,128)(2,1)S(1)}, u32[]{:S(2)}, u32[]{:S(2)}) collective-permute-start(bf16[256,512]{1,0:T(8,128)(2,1)S(1)} %get-tuple-element.50), channel_id=1, source_target_pairs={{4,8},{12,16},{20,24},{28,32},{36,40},{44,48},{52,56},{60,64},{68,... | collective-permute-start | bytes 786440 | tf_op jit(solution)/shard_map/ppermute | solution.py:357
  8.3 1.7 %collective-permute-start.2 = (bf16[128,512]{1,0:T(8,128)(2,1)S(1)}, bf16[128,512]{1,0:T(8,128)(2,1)S(1)}, u32[]{:S(2)}, u32[]{:S(2)}) collective-permute-start(bf16[128,512]{1,0:T(8,128)(2,1)S(1)} %get-tuple-element.52), channel_id=1, source_target_pairs={{0,1},{1,2},{2,3},{3,0},{4,5},{5,6},{6,7},{7,4},{8,9},{9,10},{10,1... | collective-permute-start | bytes 393224 | tf_op jit(solution)/shard_map/ppermute | solution.py:351
  10.0 3.3 %collective-permute-start.3 = (bf16[128,512]{1,0:T(8,128)(2,1)S(1)}, bf16[128,512]{1,0:T(8,128)(2,1)S(1)}, u32[]{:S(2)}, u32[]{:S(2)}) collective-permute-start(bf16[128,512]{1,0:T(8,128)(2,1)S(1)} %get-tuple-element.56), channel_id=1, source_target_pairs={{0,2},{1,3},{2,0},{3,1},{4,6},{5,7},{6,4},{7,5},{8,10},{9,11},{10,... | collective-permute-start | bytes 393224 | tf_op jit(solution)/shard_map/ppermute | solution.py:351
  14.1 1.7 %mesh_in.1 = (bf16[64,512]{1,0:T(8,128)(2,1)S(1)}, bf16[64,512]{1,0:T(8,128)(2,1)S(1)}, bf16[64,512]{1,0:T(8,128)(2,1)S(1)}, bf16[64,512]{1,0:T(8,128)(2,1)S(1)}) custom-call(bf16[64,512]{1,0:T(8,128)(2,1)} %mesh_hbm.3, f32[1,512]{1,0:T(1,128)} %bitcast.8, bf16[512,512]{1,0:T(8,128)(2,1)} %wq_hbm.3, bf16[512,512]{1,0:T(8,128)(2,1)} %wo_hbm.3, ...), custom_call_target="tpu_custom_call" | custom-call | flops 268435456 | bytes 2097152 | tf_op jit(solution)/shard_map/mesh_in/pallas_call | solution.py:48
  16.7 2.3 %collective-permute-start.6 = (bf16[64,512]{1,0:T(8,128)(2,1)S(1)}, bf16[64,512]{1,0:T(8,128)(2,1)S(1)}, u32[]{:S(2)}, u32[]{:S(2)}) collective-permute-start(bf16[64,512]{1,0:T(8,128)(2,1)S(1)} %get-tuple-element.59), channel_id=1, source_target_pairs={{0,2},{1,3},{2,0},{3,1},{4,6},{5,7},{6,4},{7,5},{8,10},{9,11},{10,... | collective-permute-start | bytes 196616 | tf_op jit(solution)/shard_map/ppermute | solution.py:351
  19.1 2.3 %slots.1.bias_ref = f32[4,64,768]{2,1,0:T(8,128)S(1)} custom-call(s32[1]{0:T(128)} %bitcast.1.sub_ref, s32[64,96]{1,0:T(8,128)} %nbr_hbm.1, s32[64,96]{1,0:T(8,128)} %valid_hbm.1, f32[64,384]{1,0:T(8,128)} %bias_hbm.1), custom_call_target="tpu_custom_call" | custom-call | flops 1073741824 | bytes 8388608 | tf_op jit(solution)/shard_map/slots/pallas_call | solution.py:48
  23.2 6.2 %middle.1 = (bf16[1024,512]{1,0:T(8,128)(2,1)S(1)}, bf16[768,1024]{1,0:T(8,128)(2,1)S(1)}, bf16[64,512]{1,0:T(8,128)(2,1)S(1)}, bf16[64,512]{1,0:T(8,128)(2,1)S(...) custom-call(s32[1]{0:T(128)} %bitcast.core_ref, bf16[256,512]{1,0:T(8,128)(2,1)S(1)} %collective-permute-done.near, ...), custom_call_target="tpu_custom_call" | custom-call | flops 3221225472 | bytes 8388608 | tf_op jit(solution)/shard_map/middle/pallas_call | solution.py:48
  33.2 7.8 %all-to-all-start = ((bf16[16,64,512]{2,1,0:T(8,128)(2,1)}), bf16[16,64,512]{2,1,0:T(8,128)(2,1)S(1)}, u32[]{:S(2)}, u32[]{:S(2)}) async-start(bf16[16,64,512]{2,1,0:T(8,128)(2,1)} %bitcast.4), calls=%async_computation | async-start | bytes 2097152 | tf_op jit(solution)/shard_map/all_to_all | solution.py:434
  43.5 1.6 %collective-permute-start.9 = (bf16[3,64,512]{2,1,0:T(8,128)(2,1)S(1)}, bf16[3,64,512]{2,1,0:T(8,128)(2,1)S(1)}, u32[]{:S(2)}, u32[]{:S(2)}) collective-permute-start(bf16[3,64,512]{2,1,0:T(8,128)(2,1)S(1)} %get-tuple-element.73), channel_id=1, source_target_pairs={{0,3},{1,0},{2,1},{3,2},{4,7},{5,4},{6,5},{7,6},{8,11},{9,8},{10,9... | collective-permute-start | bytes 589832 | tf_op jit(solution)/shard_map/ppermute | solution.py:351
  45.0 2.3 %mesh.1 = (bf16[64,512]{1,0:T(8,128)(2,1)}, bf16[64,512]{1,0:T(8,128)(2,1)}) custom-call(bf16[64,512]{1,0:T(8,128)(2,1)S(1)} %get-tuple-element.78.att_ref, bf16[64,512]{1,0:T(8,128)(2,1)S(1)} %get-tuple-element.71.qg_ref, bf16[64,512]{1,0:T(8,128)(2,1)S(1)} %get-tuple-element.64.og_ref, bf16[512,512]{1,0:T(8,128)(2,1)} %wo_hbm.3, bf16[512,512]{1,0:T(8,128)(2,1)} %wq_hbm.3, ...), custom_call_target="tpu_custom_call" | custom-call | flops 268435456 | bytes 2097152 | tf_op jit(solution)/shard_map/mesh/pallas_call | solution.py:48
  48.4 5.2 %collective-permute-done.11.p3.s3 = bf16[3,64,512]{2,1,0:T(8,128)(2,1)S(1)} collective-permute-done((bf16[3,64,512]{2,1,0:T(8,128)(2,1)S(1)}, bf16[3,64,512]{2,1,0:T(8,128)(2,1)S(1)}, u32[]{:S(2)}, u32[]{:S(2)}) %collective-permute-start.11) | collective-permute-done | bytes 196640 | tf_op jit(solution)/shard_map/ppermute | solution.py:351
  53.6 2.4 %all-to-all-done = bf16[16,64,512]{2,1,0:T(8,128)(2,1)S(1)} async-done(((bf16[16,64,512]{2,1,0:T(8,128)(2,1)}), bf16[16,64,512]{2,1,0:T(8,128)(2,1)S(1)}, u32[]{:S(2)}, u32[]{:S(2)}) %all-to-all-start) | async-done | bytes 1048608 | tf_op jit(solution)/shard_map/all_to_all | solution.py:434
  56.2 2.0 %collective-permute-start.14 = (bf16[64,512]{1,0:T(8,128)(2,1)S(1)}, bf16[64,512]{1,0:T(8,128)(2,1)S(1)}, u32[]{:S(2)}, u32[]{:S(2)}) collective-permute-start(bf16[64,512]{1,0:T(8,128)(2,1)S(1)} %reduce_sum.12.p0), channel_id=1, source_target_pairs={{0,3},{1,0},{2,1},{3,2},{4,7},{5,4},{6,5},{7,6},{8,11},{9,8},{10,9... | collective-permute-start | bytes 196616 | tf_op jit(solution)/shard_map/ppermute | solution.py:351
  60.1 2.8 %collective-permute-done.13.p2 = bf16[64,512]{1,0:T(8,128)(2,1)S(1)} collective-permute-done((bf16[64,512]{1,0:T(8,128)(2,1)S(1)}, bf16[64,512]{1,0:T(8,128)(2,1)S(1)}, u32[]{:S(2)}, u32[]{:S(2)}) %collective-permute-start.13) | collective-permute-done | bytes 65568 | tf_op jit(solution)/shard_map/ppermute | solution.py:351
  64.7 5.1 %all-to-all-start.1 = ((bf16[16,64,512]{2,1,0:T(8,128)(2,1)}), bf16[16,64,512]{2,1,0:T(8,128)(2,1)S(1)}, u32[]{:S(2)}, u32[]{:S(2)}) async-start(bf16[16,64,512]{2,1,0:T(8,128)(2,1)} %spread.1), calls=%async_computation.1 | async-start | bytes 2097152 | tf_op jit(solution)/shard_map/all_to_all | solution.py:456
  69.9 3.8 %collective-permute-start.16 = (bf16[256,512]{1,0:T(8,128)(2,1)S(1)}, bf16[256,512]{1,0:T(8,128)(2,1)S(1)}, u32[]{:S(2)}, u32[]{:S(2)}) collective-permute-start(bf16[256,512]{1,0:T(8,128)(2,1)S(1)} %get-tuple-element.90), channel_id=1, source_target_pairs={{0,4},{4,0},{1,5},{5,1},{2,6},{6,2},{3,7},{7,3},{8,12},{12,8},{9,1... | collective-permute-start | bytes 786440 | tf_op jit(solution)/shard_map/ppermute | solution.py:351
  73.6 3.3 %collective-permute-start.15 = (bf16[256,512]{1,0:T(8,128)(2,1)S(1)}, bf16[256,512]{1,0:T(8,128)(2,1)S(1)}, u32[]{:S(2)}, u32[]{:S(2)}) collective-permute-start(bf16[256,512]{1,0:T(8,128)(2,1)S(1)} %get-tuple-element.89), channel_id=1, source_target_pairs={{4,8},{12,16},{20,24},{28,32},{36,40},{44,48},{52,56},{60,64},{68,... | collective-permute-start | bytes 786440 | tf_op jit(solution)/shard_map/ppermute | solution.py:357
  77.0 3.0 %grid_near.1.refs_0_ = bf16[2048,512]{1,0:T(8,128)(2,1)} custom-call(s32[1]{0:T(128)} %bitcast.1.sub_ref, s32[1]{0:T(128)} %bitcast.core_ref, bf16[256,512]{1,0:T(8,128)(2,1)S(1)} %collective-permute-done.16.outer, bf16[3,64,512]{2,1,0:T(8,128)(2,1)S(1)} %get-tuple-element.85.p0.s0, bf16[3,64,512]{2,1,0:T(8,128)(2,1)S(1)} %collective-permute-done.9.p1.s1, ...), custom_call_target="tpu_custom_call" | custom-call | flops 536870912 | bytes 3145728 | tf_op jit(solution)/shard_map/grid_near/pallas_call | solution.py:48
  80.0 8.1 %collective-permute-done.15.outer = bf16[256,512]{1,0:T(8,128)(2,1)S(1)} collective-permute-done((bf16[256,512]{1,0:T(8,128)(2,1)S(1)}, bf16[256,512]{1,0:T(8,128)(2,1)S(1)}, u32[]{:S(2)}, u32[]{:S(2)}) %collective-permute-start.15) | collective-permute-done | bytes 262176 | tf_op jit(solution)/shard_map/ppermute | solution.py:357
  88.1 2.2 %collective-permute-start.17 = (bf16[1024,512]{1,0:T(8,128)(2,1)S(1)}, bf16[1024,512]{1,0:T(8,128)(2,1)S(1)}, u32[]{:S(2)}, u32[]{:S(2)}) collective-permute-start(bf16[1024,512]{1,0:T(8,128)(2,1)S(1)} %bitcast.6), channel_id=1, source_target_pairs={{0,4},{4,0},{1,5},{5,1},{2,6},{6,2},{3,7},{7,3},{8,12},{12,8},{9,1... | collective-permute-start | bytes 3145736 | tf_op jit(solution)/shard_map/ppermute | solution.py:351
  91.7 3.0 %grid_far.1 = bf16[2048,512]{1,0:T(8,128)(2,1)} custom-call(s32[1]{0:T(128)} %bitcast.1.sub_ref, s32[1]{0:T(128)} %bitcast.core_ref, bf16[256,512]{1,0:T(8,128)(2,1)S(1)} %collective-permute-done.15.outer, bf16[3,64,512]{2,1,0:T(8,128)(2,1)S(1)} %get-tuple-element.85.p0.s0, ...), custom_call_target="tpu_custom_call", output_to_operand_aliasing={{}: (10, {})} | custom-call | flops 536870912 | bytes 3145728 | tf_op jit(solution)/shard_map/grid_far/pallas_call | solution.py:48
  94.8 1.4 %widen_other.1 = f32[4,512,512]{2,1,0:T(8,128)} custom-call(s32[1]{0:T(128)} %bitcast.core_ref, bf16[1024,512]{1,0:T(8,128)(2,1)S(1)} %collective-permute-done.17.half_ref, f32[4,512,512]{2,1,0:T(8,128)} %widen_own.1.refs_0_), custom_call_target="tpu_custom_call", output_to_operand_aliasing={{}: (2, {})} | custom-call | flops 1048576 | bytes 3145728 | tf_op jit(solution)/shard_map/widen_other/pallas_call | solution.py:48
  (33 shorter events, 16.1 us)
Async XLA Ops:
  3.6 4.7 %collective-permute-start = (bf16[256,512]{1,0:T(8,128)(2,1)S(1)}, bf16[256,512]{1,0:T(8,128)(2,1)S(1)}, u32[]{:S(2)}, u32[]{:S(2)}) collective-permute-start(bf16[256,512]{1,0:T(8,128)(2,1)S(1)} %get-tuple-element.49), channel_id=1, source_target_pairs={{0,4},{4,0},{1,5},{5,1},{2,6},{6,2},{3,7},{7,3},{8,12},{12,8},{9,1... | collective-permute-start | bytes 786440 | tf_op jit(solution)/shard_map/ppermute | solution.py:351
  5.1 10.7 %collective-permute-start.1 = (bf16[256,512]{1,0:T(8,128)(2,1)S(1)}, bf16[256,512]{1,0:T(8,128)(2,1)S(1)}, u32[]{:S(2)}, u32[]{:S(2)}) collective-permute-start(bf16[256,512]{1,0:T(8,128)(2,1)S(1)} %get-tuple-element.50), channel_id=1, source_target_pairs={{4,8},{12,16},{20,24},{28,32},{36,40},{44,48},{52,56},{60,64},{68,... | collective-permute-start | bytes 786440 | tf_op jit(solution)/shard_map/ppermute | solution.py:357
  8.3 7.5 %collective-permute-start.2 = (bf16[128,512]{1,0:T(8,128)(2,1)S(1)}, bf16[128,512]{1,0:T(8,128)(2,1)S(1)}, u32[]{:S(2)}, u32[]{:S(2)}) collective-permute-start(bf16[128,512]{1,0:T(8,128)(2,1)S(1)} %get-tuple-element.52), channel_id=1, source_target_pairs={{0,1},{1,2},{2,3},{3,0},{4,5},{5,6},{6,7},{7,4},{8,9},{9,10},{10,1... | collective-permute-start | bytes 393224 | tf_op jit(solution)/shard_map/ppermute | solution.py:351
  10.0 11.4 %collective-permute-start.3 = (bf16[128,512]{1,0:T(8,128)(2,1)S(1)}, bf16[128,512]{1,0:T(8,128)(2,1)S(1)}, u32[]{:S(2)}, u32[]{:S(2)}) collective-permute-start(bf16[128,512]{1,0:T(8,128)(2,1)S(1)} %get-tuple-element.56), channel_id=1, source_target_pairs={{0,2},{1,3},{2,0},{3,1},{4,6},{5,7},{6,4},{7,5},{8,10},{9,11},{10,... | collective-permute-start | bytes 393224 | tf_op jit(solution)/shard_map/ppermute | solution.py:351
  13.3 8.1 %collective-permute-start.4 = (bf16[128,512]{1,0:T(8,128)(2,1)S(1)}, bf16[128,512]{1,0:T(8,128)(2,1)S(1)}, u32[]{:S(2)}, u32[]{:S(2)}) collective-permute-start(bf16[128,512]{1,0:T(8,128)(2,1)S(1)} %get-tuple-element.57), channel_id=1, source_target_pairs={{0,3},{1,0},{2,1},{3,2},{4,7},{5,4},{6,5},{7,6},{8,11},{9,8},{10,9... | collective-permute-start | bytes 393224 | tf_op jit(solution)/shard_map/ppermute | solution.py:351
  15.9 5.6 %collective-permute-start.5 = (bf16[64,512]{1,0:T(8,128)(2,1)S(1)}, bf16[64,512]{1,0:T(8,128)(2,1)S(1)}, u32[]{:S(2)}, u32[]{:S(2)}) collective-permute-start(bf16[64,512]{1,0:T(8,128)(2,1)S(1)} %get-tuple-element.58), channel_id=1, source_target_pairs={{0,1},{1,2},{2,3},{3,0},{4,5},{5,6},{6,7},{7,4},{8,9},{9,10},{10,1... | collective-permute-start | bytes 196616 | tf_op jit(solution)/shard_map/ppermute | solution.py:351
  16.7 5.6 %collective-permute-start.6 = (bf16[64,512]{1,0:T(8,128)(2,1)S(1)}, bf16[64,512]{1,0:T(8,128)(2,1)S(1)}, u32[]{:S(2)}, u32[]{:S(2)}) collective-permute-start(bf16[64,512]{1,0:T(8,128)(2,1)S(1)} %get-tuple-element.59), channel_id=1, source_target_pairs={{0,2},{1,3},{2,0},{3,1},{4,6},{5,7},{6,4},{7,5},{8,10},{9,11},{10,... | collective-permute-start | bytes 196616 | tf_op jit(solution)/shard_map/ppermute | solution.py:351
  19.0 4.2 %collective-permute-start.7 = (bf16[64,512]{1,0:T(8,128)(2,1)S(1)}, bf16[64,512]{1,0:T(8,128)(2,1)S(1)}, u32[]{:S(2)}, u32[]{:S(2)}) collective-permute-start(bf16[64,512]{1,0:T(8,128)(2,1)S(1)} %get-tuple-element.60), channel_id=1, source_target_pairs={{0,3},{1,0},{2,1},{3,2},{4,7},{5,4},{6,5},{7,6},{8,11},{9,8},{10,9... | collective-permute-start | bytes 196616 | tf_op jit(solution)/shard_map/ppermute | solution.py:351
  29.4 2.8 %collective-permute-start.8 = (bf16[1024,512]{1,0:T(8,128)(2,1)S(1)}, bf16[1024,512]{1,0:T(8,128)(2,1)S(1)}, u32[]{:S(2)}, u32[]{:S(2)}) collective-permute-start(bf16[1024,512]{1,0:T(8,128)(2,1)S(1)} %get-tuple-element.66), channel_id=1, source_target_pairs={{0,4},{4,0},{1,5},{5,1},{2,6},{6,2},{3,7},{7,3},{8,12},{12,8},{9,1... | collective-permute-start | bytes 3145736 | tf_op jit(solution)/shard_map/ppermute | solution.py:351
  33.2 22.8 %all-to-all-start = ((bf16[16,64,512]{2,1,0:T(8,128)(2,1)}), bf16[16,64,512]{2,1,0:T(8,128)(2,1)S(1)}, u32[]{:S(2)}, u32[]{:S(2)}) async-start(bf16[16,64,512]{2,1,0:T(8,128)(2,1)} %bitcast.4), calls=%async_computation | async-start | bytes 2097152 | tf_op jit(solution)/shard_map/all_to_all | solution.py:434
  41.0 7.4 %collective-permute-start.10 = (bf16[3,64,512]{2,1,0:T(8,128)(2,1)S(1)}, bf16[3,64,512]{2,1,0:T(8,128)(2,1)S(1)}, u32[]{:S(2)}, u32[]{:S(2)}) collective-permute-start(bf16[3,64,512]{2,1,0:T(8,128)(2,1)S(1)} %get-tuple-element.74), channel_id=1, source_target_pairs={{0,2},{1,3},{2,0},{3,1},{4,6},{5,7},{6,4},{7,5},{8,10},{9,11},{10,... | collective-permute-start | bytes 589832 | tf_op jit(solution)/shard_map/ppermute | solution.py:351
  42.3 11.3 %collective-permute-start.11 = (bf16[3,64,512]{2,1,0:T(8,128)(2,1)S(1)}, bf16[3,64,512]{2,1,0:T(8,128)(2,1)S(1)}, u32[]{:S(2)}, u32[]{:S(2)}) collective-permute-start(bf16[3,64,512]{2,1,0:T(8,128)(2,1)S(1)} %get-tuple-element.75), channel_id=1, source_target_pairs={{0,1},{1,2},{2,3},{3,0},{4,5},{5,6},{6,7},{7,4},{8,9},{9,10},{10,1... | collective-permute-start | bytes 589832 | tf_op jit(solution)/shard_map/ppermute | solution.py:351
  43.5 10.2 %collective-permute-start.9 = (bf16[3,64,512]{2,1,0:T(8,128)(2,1)S(1)}, bf16[3,64,512]{2,1,0:T(8,128)(2,1)S(1)}, u32[]{:S(2)}, u32[]{:S(2)}) collective-permute-start(bf16[3,64,512]{2,1,0:T(8,128)(2,1)S(1)} %get-tuple-element.73), channel_id=1, source_target_pairs={{0,3},{1,0},{2,1},{3,2},{4,7},{5,4},{6,5},{7,6},{8,11},{9,8},{10,9... | collective-permute-start | bytes 589832 | tf_op jit(solution)/shard_map/ppermute | solution.py:351
  56.2 3.9 %collective-permute-start.14 = (bf16[64,512]{1,0:T(8,128)(2,1)S(1)}, bf16[64,512]{1,0:T(8,128)(2,1)S(1)}, u32[]{:S(2)}, u32[]{:S(2)}) collective-permute-start(bf16[64,512]{1,0:T(8,128)(2,1)S(1)} %reduce_sum.12.p0), channel_id=1, source_target_pairs={{0,3},{1,0},{2,1},{3,2},{4,7},{5,4},{6,5},{7,6},{8,11},{9,8},{10,9... | collective-permute-start | bytes 196616 | tf_op jit(solution)/shard_map/ppermute | solution.py:351
  58.2 4.7 %collective-permute-start.13 = (bf16[64,512]{1,0:T(8,128)(2,1)S(1)}, bf16[64,512]{1,0:T(8,128)(2,1)S(1)}, u32[]{:S(2)}, u32[]{:S(2)}) collective-permute-start(bf16[64,512]{1,0:T(8,128)(2,1)S(1)} %reduce_sum.12.p0), channel_id=1, source_target_pairs={{0,2},{1,3},{2,0},{3,1},{4,6},{5,7},{6,4},{7,5},{8,10},{9,11},{10,... | collective-permute-start | bytes 196616 | tf_op jit(solution)/shard_map/ppermute | solution.py:351
  58.5 5.0 %collective-permute-start.12 = (bf16[64,512]{1,0:T(8,128)(2,1)S(1)}, bf16[64,512]{1,0:T(8,128)(2,1)S(1)}, u32[]{:S(2)}, u32[]{:S(2)}) collective-permute-start(bf16[64,512]{1,0:T(8,128)(2,1)S(1)} %reduce_sum.12.p0), channel_id=1, source_target_pairs={{0,1},{1,2},{2,3},{3,0},{4,5},{5,6},{6,7},{7,4},{8,9},{9,10},{10,1... | collective-permute-start | bytes 196616 | tf_op jit(solution)/shard_map/ppermute | solution.py:351
  64.7 23.5 %all-to-all-start.1 = ((bf16[16,64,512]{2,1,0:T(8,128)(2,1)}), bf16[16,64,512]{2,1,0:T(8,128)(2,1)S(1)}, u32[]{:S(2)}, u32[]{:S(2)}) async-start(bf16[16,64,512]{2,1,0:T(8,128)(2,1)} %spread.1), calls=%async_computation.1 | async-start | bytes 2097152 | tf_op jit(solution)/shard_map/all_to_all | solution.py:456
  69.9 7.1 %collective-permute-start.16 = (bf16[256,512]{1,0:T(8,128)(2,1)S(1)}, bf16[256,512]{1,0:T(8,128)(2,1)S(1)}, u32[]{:S(2)}, u32[]{:S(2)}) collective-permute-start(bf16[256,512]{1,0:T(8,128)(2,1)S(1)} %get-tuple-element.90), channel_id=1, source_target_pairs={{0,4},{4,0},{1,5},{5,1},{2,6},{6,2},{3,7},{7,3},{8,12},{12,8},{9,1... | collective-permute-start | bytes 786440 | tf_op jit(solution)/shard_map/ppermute | solution.py:351
  73.6 14.5 %collective-permute-start.15 = (bf16[256,512]{1,0:T(8,128)(2,1)S(1)}, bf16[256,512]{1,0:T(8,128)(2,1)S(1)}, u32[]{:S(2)}, u32[]{:S(2)}) collective-permute-start(bf16[256,512]{1,0:T(8,128)(2,1)S(1)} %get-tuple-element.89), channel_id=1, source_target_pairs={{4,8},{12,16},{20,24},{28,32},{36,40},{44,48},{52,56},{60,64},{68,... | collective-permute-start | bytes 786440 | tf_op jit(solution)/shard_map/ppermute | solution.py:357
  88.1 6.6 %collective-permute-start.17 = (bf16[1024,512]{1,0:T(8,128)(2,1)S(1)}, bf16[1024,512]{1,0:T(8,128)(2,1)S(1)}, u32[]{:S(2)}, u32[]{:S(2)}) collective-permute-start(bf16[1024,512]{1,0:T(8,128)(2,1)S(1)} %bitcast.6), channel_id=1, source_target_pairs={{0,4},{4,0},{1,5},{5,1},{2,6},{6,2},{3,7},{7,3},{8,12},{12,8},{9,1... | collective-permute-start | bytes 3145736 | tf_op jit(solution)/shard_map/ppermute | solution.py:351

commit v11 on v10

--- a/solution.py
+++ b/solution.py
@@ -52,7 +52,7 @@
         out_specs=out_specs or [VM] * len(outs),
         scratch_shapes=list(scratch),
         input_output_aliases=aliases or {},
-        compiler_params=pltpu.CompilerParams(vmem_limit_bytes=24 << 20),
+        compiler_params=pltpu.CompilerParams(vmem_limit_bytes=16 << 20),
         cost_estimate=pl.CostEstimate(flops=flops, bytes_accessed=nbytes, transcendentals=0),
         name=name,
     )(*args)
@@ -85,8 +85,12 @@
         rows[pl.ds(far_at + k * cap, cap), :] = last[last.shape[0] - cap :]
 
 
-def gather_body(sub_ref, core_ref, rows_hbm, gain_hbm, x_hbm, near_ref, far_ref, own_ref,
-                rows_ref, gain_ref, x_ref, sems):
+def gather_body(sub_ref, core_ref, rows_hbm, gain_hbm, x_hbm, *refs):
+    later = (len(refs) - 7) // 2
+    later_hbm, refs = refs[:later], refs[later:]
+    near_ref, far_ref, own_ref = refs[:3]
+    later_refs = refs[3 : 3 + later - 1]
+    rows_ref, gain_ref, x_ref, sems, later_sems = refs[-5:]
     half = x_ref.shape[0] // 2
     cap = rows_ref.shape[3]
     core = core_ref[0]
@@ -97,6 +101,10 @@
         [rows_ref, gain_ref] + [x_ref.at[p] for p in parts],
         sems,
     )
+    wkv_ref = later_refs[-1]
+    width = x_ref.shape[1]
+    later_refs = (*later_refs[:-1], wkv_ref.at[:, pl.ds(0, width)], wkv_ref.at[:, pl.ds(width, width)])
+    later_copies = fetch(later_hbm, later_refs, later_sems)
     copies[0].wait()
     copies[1].wait()
     me = sub_ref[0]
@@ -122,15 +130,11 @@
             copies[2 + step].wait()
         wide = nn(onehot, x_ref[pl.ds(first, count), :])
         out_ref[...] = (wide * inv_rms(wide) * gain).astype(BF16)
-
-
-def mesh_in_body(mesh_hbm, gain_hbm, wq_hbm, wo_hbm, og_hbm, normed_ref, q_ref, ag_ref, og_ref,
-                 mesh_ref, gain_ref, wq_ref, wo_ref, sems):
-    copies = fetch(
-        (mesh_hbm, gain_hbm, wq_hbm, wo_hbm, og_hbm), (mesh_ref, gain_ref, wq_ref, wo_ref, og_ref), sems
-    )
-    for copy in copies:
+    for copy in later_copies:
         copy.wait()
+
+
+def mesh_in_body(mesh_ref, gain_ref, wq_ref, wo_ref, og_ref, normed_ref, q_ref, ag_ref):
     wide = mesh_ref[...].astype(F32)
     normed = (wide * inv_rms(wide) * gain_ref[...]).astype(BF16)
     normed_ref[...] = normed
@@ -138,13 +142,9 @@
     ag_ref[...] = nt(og_ref[...], wo_ref[...]).astype(BF16)
 
 
-def slots_body(sub_ref, nbr_hbm, valid_hbm, bias_hbm, dense_ref, inv_ref, edge_ref,
-               nbr_ref, valid_ref, bias_ref, sems):
-    copies = fetch((nbr_hbm, valid_hbm, bias_hbm), (nbr_ref, valid_ref, bias_ref), sems)
+def slots_body(sub_ref, nbr_ref, valid_ref, bias_ref, dense_ref, inv_ref, edge_ref):
     heads, nodes, slots = dense_ref.shape
     fan = nbr_ref.shape[1]
-    for copy in copies:
-        copy.wait()
     slot = nbr_ref[...]
     slot = (slot & ~192) | (((sub_ref[0] - (slot >> 6)) & 3) << 6)
     high, low = slot >> 7, slot & 127
@@ -168,18 +168,12 @@
 
 
 def middle_body(core_ref, near, far, own, m1, m2, m3, f1, f2, f3, q_ref, ag_ref, mn_ref, og_ref,
-                bias_ref, wk_hbm, wv_hbm, send_ref, part_ref, att_ref, qg_ref, wkv_ref, rows,
-                keys, vals, sems):
+                bias_ref, wkv_ref, send_ref, part_ref, att_ref, qg_ref, rows, keys, vals):
     width = q_ref.shape[1]
-    copies = fetch(
-        (wk_hbm, wv_hbm), (wkv_ref.at[:, pl.ds(0, width)], wkv_ref.at[:, pl.ds(width, width)]), sems
-    )
     heads = bias_ref.shape[0]
     core = core_ref[0]
     assemble(rows, 1 - core, near, far, own, m1, m2, m3, f1, f2, f3)
-    copies[0].wait()
     keys[...] = nn(rows[...], wkv_ref[:, :width]).astype(BF16)
-    copies[1].wait()
     vals[...] = nn(rows[...], wkv_ref[:, width:]).astype(BF16)
     for h in range(heads):
         at = slice(h * 128, (h + 1) * 128)
@@ -222,13 +216,7 @@
             piece[o] = back[k * cap : (k + 1) * cap]
 
 
-def mesh_body(att_ref, qg_ref, og_ref, wo_hbm, wq_hbm, mesh_hbm, gain_hbm, out_ref, grad_ref,
-              wo_ref, wq_ref, mesh_ref, gain_ref, sems):
-    copies = fetch(
-        (wo_hbm, wq_hbm, mesh_hbm, gain_hbm), (wo_ref, wq_ref, mesh_ref, gain_ref), sems
-    )
-    for copy in copies:
-        copy.wait()
+def mesh_body(att_ref, qg_ref, og_ref, wo_ref, wq_ref, mesh_ref, gain_ref, out_ref, grad_ref):
     wide = mesh_ref[...].astype(F32)
     out_ref[...] = (wide + nn(att_ref[...], wo_ref[...])).astype(BF16)
     upstream = nt(qg_ref[...], wq_ref[...])
@@ -380,19 +368,23 @@
     )
 
     one, two, four = sds((cap, width)), sds((2 * cap, width)), sds((block, width))
-    near, far, own = call(
-        gather_body, [four] * 3, [SM, SM, HB, HB, HB],
-        (sub1, core1, send_rows, gain_g, grid_x), 1 << 30, 4 << 20, "gather_rows",
-        held(send_rows, gain_g, grid_x)[:-1] + [pltpu.SemaphoreType.DMA((4,))],
-    )
-
+    later = (mesh_h, gain_m, w_query, w_out, out_grad, neighbours, valid, edge_bias)
+    weights = sds((width, 2 * width))
+    near, far, own, *later, weights_near = call(
+        gather_body, [four] * 3 + [sds(a.shape, a.dtype) for a in later] + [weights],
+        [SM, SM] + [HB] * (5 + len(later)),
+        (sub1, core1, send_rows, gain_g, grid_x, *later, w_key, w_value), 1 << 30, 6 << 20, "gather_rows",
+        held(send_rows, gain_g, grid_x)[:-1]
+        + [pltpu.SemaphoreType.DMA((4,)), pltpu.SemaphoreType.DMA((len(later) + 2,))],
+    )
+    mesh_near, gain_near, wq_near, wo_near, og_near, nbr_near, valid_near, bias_near = later
     far = swapped_far(far)
     near = shifted(near, "gc", 1)
     mixed = call(mix_body, [two] * 3, [VM] * 2, (own, near), 0, 1 << 20, "mix")
     mixed = [shifted(m, "z", k) for k, m in enumerate(mixed, 1)]
-    mesh_normed, queries, att_grad, og_near = call(
-        mesh_in_body, [sds((nodes, width))] * 4, [HB] * 5, (mesh_h, gain_m, w_query, w_out, out_grad),
-        1 << 28, 2 << 20, "mesh_in", held(mesh_h, gain_m, w_query, w_out)[:-1] + [pltpu.SemaphoreType.DMA((5,))],
+    mesh_normed, queries, att_grad = call(
+        mesh_in_body, [sds((nodes, width))] * 3, [VM] * 5,
+        (mesh_near, gain_near, wq_near, wo_near, og_near), 1 << 28, 2 << 20, "mesh_in",
     )
     far, mixed[0], queries = lax.optimization_barrier((far, mixed[0], queries))
     outer = call(split_body, [one] * 3, [VM], (far,), 0, 1 << 19, "split")
@@ -400,19 +392,17 @@
     received = near, far, own, *mixed, *outer
     sub2, far = lax.optimization_barrier((sub1, far))
     (dense,) = call(
-        slots_body, [sds((heads, nodes, slots), F32)], [SM] + [HB] * 3,
-        (sub2, neighbours, valid, edge_bias), 1 << 30, 8 << 20, "slots",
-        [pltpu.VMEM((nodes * 8, 128), F32), pltpu.VMEM((heads, nodes, 128), F32)]
-        + held(neighbours, valid, edge_bias),
-    )
-    send, part_grads, attended, query_grad, weights_near, rows = call(
+        slots_body, [sds((heads, nodes, slots), F32)], [SM] + [VM] * 3,
+        (sub2, nbr_near, valid_near, bias_near), 1 << 30, 8 << 20, "slots",
+        [pltpu.VMEM((nodes * 8, 128), F32), pltpu.VMEM((heads, nodes, 128), F32)],
+    )
+    send, part_grads, attended, query_grad, rows = call(
         middle_body,
         [sds((2 * width, width)), sds((slots, 2 * width))] + [sds((nodes, width))] * 2
-        + [sds((width, 2 * width)), sds((slots, width))],
-        [SM] + [VM] * 14 + [HB] * 2,
-        (core1, *received, queries, att_grad, mesh_normed, og_near, dense, w_key, w_value),
-        3 << 30, 8 << 20, "middle",
-        [pltpu.VMEM((slots, width), BF16)] * 2 + [pltpu.SemaphoreType.DMA((2,))],
+        + [sds((slots, width))],
+        [SM] + [VM] * 15,
+        (core1, *received, queries, att_grad, mesh_normed, og_near, dense, weights_near),
+        3 << 30, 8 << 20, "middle", [pltpu.VMEM((slots, width), BF16)] * 2,
     )
 
     other = shifted(send, "gc", 1)
@@ -435,9 +425,8 @@
 
     attended, own = lax.optimization_barrier((attended, own))
     mesh_out, mesh_grad = call(
-        mesh_body, [sds((nodes, width))] * 2, [VM] * 3 + [HB] * 4,
-        (attended, query_grad, og_near, w_out, w_query, mesh_h, gain_m), 1 << 28, 2 << 20, "mesh",
-        held(w_out, w_query, mesh_h, gain_m),
+        mesh_body, [sds((nodes, width))] * 2, [VM] * 7,
+        (attended, query_grad, og_near, wo_near, wq_near, mesh_near, gain_near), 1 << 28, 2 << 20, "mesh",
     )
     s1, s2, s3 = (shifted(s, "z", -k) for k, s in ((1, s1), (2, s2), (3, s3)))
     s1, s2, s3, parts, mesh_out = lax.optimization_barrier((s1, s2, s3, parts, mesh_out))

time: 96.8 us -> 97.3 us (level)
  Pallas kernels: 28.3 us -> 24.2 us
  starting transfers between devices: 43.1 us -> 45 us
  waiting for transfers between devices: 23.7 us -> 25.4 us
  other arithmetic: 0.15 us -> 1.37 us
    pallas_call x16, Pallas kernels: 28.3 us -> 24.2 us  [call(): pl.pallas_call(body, out_shape=outs, in_specs=in_specs, out_specs=out_spe...]
    ppermute x16, waiting for transfers between devices: 13.2 us -> 14.9 us  [shifted(): return lax.ppermute(block, axis, [(i, (i + k) % n) for i in range(n)])]
    reduce_sum x1, other arithmetic: 0.15 us -> 1.37 us  [shards(): part = jnp.sum(parts.astype(F32), axis=0).astype(BF16)]
    all_to_all x1, starting transfers between devices: 7.79 us -> 8.98 us  [shards(): lax.all_to_all(own.reshape(plane, share, width), PLANE, 0, 0, tiled=True)]
  transfers between devices with their start and end apart: 20 -> 20, of which waited for: 10 -> 11; matrix products, arithmetic and copies ran while one was open for 0% -> 0% of each run, Pallas kernels for 16% -> 13%
where the time goes in v11:
time: 97.3 us; the launch traced here: 96.9 us
  starting transfers between devices  45 us (46%)
  waiting for transfers between devices  25.4 us (26%)
  Pallas kernels  24.2 us (25%)
  other arithmetic  1.37 us (1%)
  between operations  1 us (1%)
    ppermute x16, starting transfers between devices, shifted(): return lax.ppermute(block, axis, [(i, (i + k) % n) for i in range(n)])  24.4 us
    pallas_call x16, Pallas kernels, call(): pl.pallas_call(body, out_shape=outs, in_specs=in_specs, out_specs=out_spe...  24.2 us
    ppermute x16, waiting for transfers between devices, shifted(): return lax.ppermute(block, axis, [(i, (i + k) % n) for i in range(n)])  14.9 us
    all_to_all x1, starting transfers between devices, shards(): lax.all_to_all(own.reshape(plane, share, width), PLANE, 0, 0, tiled=True)  8.98 us
    ppermute x2, waiting for transfers between devices, swapped_far(): return lax.ppermute(block, SLAB, pairs + [(j, i) for i, j in pairs])  8.08 us
    ppermute x2, starting transfers between devices, swapped_far(): return lax.ppermute(block, SLAB, pairs + [(j, i) for i, j in pairs])  6.51 us
    all_to_all x1, starting transfers between devices, shards(): lax.all_to_all(spread, PLANE, 0, 0, tiled=True).reshape(2 * width, width)  5.14 us
    all_to_all x1, waiting for transfers between devices, shards(): lax.all_to_all(own.reshape(plane, share, width), PLANE, 0, 0, tiled=True)  2.33 us
  transfers between devices with their start and end apart: 20, of which 11 were waited for; matrix products, arithmetic and copies ran while one was open for 0% of the time, Pallas kernels for 13%

profile of v11, /device:TPU:1, one launch (start us, length us, event | category | flops | bytes accessed | tf_op | source)
XLA Modules:
  0.0 96.9 jit_solution(7645299913227332774)
XLA Ops:
  0.6 3.5 %gather_rows.1 = (bf16[256,512]{1,0:T(8,128)(2,1)S(1)}, bf16[256,512]{1,0:T(8,128)(2,1)S(1)}, bf16[256,512]{1,0:T(8,128)(2,1)S(1)}, bf16[64,512]{1,0:T(8,128)(2,...) custom-call(s32[1]{0:T(128)} %bitcast.1.sub_ref, ...), custom_call_target="tpu_custom_call" | custom-call | flops 1073741824 | bytes 6291456 | tf_op jit(solution)/shard_map/gather_rows/pallas_call | solution.py:48
  4.2 1.5 %collective-permute-start = (bf16[256,512]{1,0:T(8,128)(2,1)S(1)}, bf16[256,512]{1,0:T(8,128)(2,1)S(1)}, u32[]{:S(2)}, u32[]{:S(2)}) collective-permute-start(bf16[256,512]{1,0:T(8,128)(2,1)S(1)} %get-tuple-element.56), channel_id=1, source_target_pairs={{0,4},{4,0},{1,5},{5,1},{2,6},{6,2},{3,7},{7,3},{8,12},{12,8},{9,1... | collective-permute-start | bytes 786440 | tf_op jit(solution)/shard_map/ppermute | solution.py:339
  5.7 3.2 %collective-permute-start.1 = (bf16[256,512]{1,0:T(8,128)(2,1)S(1)}, bf16[256,512]{1,0:T(8,128)(2,1)S(1)}, u32[]{:S(2)}, u32[]{:S(2)}) collective-permute-start(bf16[256,512]{1,0:T(8,128)(2,1)S(1)} %get-tuple-element.57), channel_id=1, source_target_pairs={{4,8},{12,16},{20,24},{28,32},{36,40},{44,48},{52,56},{60,64},{68,... | collective-permute-start | bytes 786440 | tf_op jit(solution)/shard_map/ppermute | solution.py:345
  8.9 1.7 %collective-permute-start.2 = (bf16[128,512]{1,0:T(8,128)(2,1)S(1)}, bf16[128,512]{1,0:T(8,128)(2,1)S(1)}, u32[]{:S(2)}, u32[]{:S(2)}) collective-permute-start(bf16[128,512]{1,0:T(8,128)(2,1)S(1)} %get-tuple-element.59), channel_id=1, source_target_pairs={{0,1},{1,2},{2,3},{3,0},{4,5},{5,6},{6,7},{7,4},{8,9},{9,10},{10,1... | collective-permute-start | bytes 393224 | tf_op jit(solution)/shard_map/ppermute | solution.py:339
  10.6 3.3 %collective-permute-start.3 = (bf16[128,512]{1,0:T(8,128)(2,1)S(1)}, bf16[128,512]{1,0:T(8,128)(2,1)S(1)}, u32[]{:S(2)}, u32[]{:S(2)}) collective-permute-start(bf16[128,512]{1,0:T(8,128)(2,1)S(1)} %get-tuple-element.68), channel_id=1, source_target_pairs={{0,2},{1,3},{2,0},{3,1},{4,6},{5,7},{6,4},{7,5},{8,10},{9,11},{10,... | collective-permute-start | bytes 393224 | tf_op jit(solution)/shard_map/ppermute | solution.py:339
  15.9 3.6 %collective-permute-start.6 = (bf16[64,512]{1,0:T(8,128)(2,1)S(1)}, bf16[64,512]{1,0:T(8,128)(2,1)S(1)}, u32[]{:S(2)}, u32[]{:S(2)}) collective-permute-start(bf16[64,512]{1,0:T(8,128)(2,1)S(1)} %get-tuple-element.71), channel_id=1, source_target_pairs={{0,2},{1,3},{2,0},{3,1},{4,6},{5,7},{6,4},{7,5},{8,10},{9,11},{10,... | collective-permute-start | bytes 196616 | tf_op jit(solution)/shard_map/ppermute | solution.py:339
  22.6 4.9 %middle.1 = (bf16[1024,512]{1,0:T(8,128)(2,1)S(1)}, bf16[768,1024]{1,0:T(8,128)(2,1)S(1)}, bf16[64,512]{1,0:T(8,128)(2,1)S(1)}, bf16[64,512]{1,0:T(8,128)(2,1)S(1)}, bf16[768,512]{1,0:T(8,128)(2,1)S(1)}) custom-call(s32[1]{0:T(128)} %bitcast.core_ref, bf16[256,512]{1,0:T(8,128)(2,1)S(1)} %collective-permute-done.near, ...), custom_call_target="tpu_custom_call" | custom-call | flops 3221225472 | bytes 8388608 | tf_op jit(solution)/shard_map/middle/pallas_call | solution.py:48
  31.4 9.0 %all-to-all-start = ((bf16[16,64,512]{2,1,0:T(8,128)(2,1)}), bf16[16,64,512]{2,1,0:T(8,128)(2,1)}, u32[]{:S(2)}, u32[]{:S(2)}) async-start(bf16[16,64,512]{2,1,0:T(8,128)(2,1)} %bitcast.4), calls=%async_computation | async-start | bytes 2097152 | tf_op jit(solution)/shard_map/all_to_all | solution.py:424
  42.8 1.6 %collective-permute-start.9 = (bf16[3,64,512]{2,1,0:T(8,128)(2,1)S(1)}, bf16[3,64,512]{2,1,0:T(8,128)(2,1)S(1)}, u32[]{:S(2)}, u32[]{:S(2)}) collective-permute-start(bf16[3,64,512]{2,1,0:T(8,128)(2,1)S(1)} %get-tuple-element.87), channel_id=1, source_target_pairs={{0,3},{1,0},{2,1},{3,2},{4,7},{5,4},{6,5},{7,6},{8,11},{9,8},{10,9... | collective-permute-start | bytes 589832 | tf_op jit(solution)/shard_map/ppermute | solution.py:339
  45.5 2.3 %collective-permute-done.10.p2.s2 = bf16[3,64,512]{2,1,0:T(8,128)(2,1)S(1)} collective-permute-done((bf16[3,64,512]{2,1,0:T(8,128)(2,1)S(1)}, bf16[3,64,512]{2,1,0:T(8,128)(2,1)S(1)}, u32[]{:S(2)}, u32[]{:S(2)}) %collective-permute-start.10) | collective-permute-done | bytes 196640 | tf_op jit(solution)/shard_map/ppermute | solution.py:339
  47.8 5.3 %collective-permute-done.11.p3.s3 = bf16[3,64,512]{2,1,0:T(8,128)(2,1)S(1)} collective-permute-done((bf16[3,64,512]{2,1,0:T(8,128)(2,1)S(1)}, bf16[3,64,512]{2,1,0:T(8,128)(2,1)S(1)}, u32[]{:S(2)}, u32[]{:S(2)}) %collective-permute-start.11) | collective-permute-done | bytes 196640 | tf_op jit(solution)/shard_map/ppermute | solution.py:339
  53.1 2.3 %all-to-all-done = bf16[16,64,512]{2,1,0:T(8,128)(2,1)} async-done(((bf16[16,64,512]{2,1,0:T(8,128)(2,1)}), bf16[16,64,512]{2,1,0:T(8,128)(2,1)}, u32[]{:S(2)}, u32[]{:S(2)}) %all-to-all-start) | async-done | bytes 1048608 | tf_op jit(solution)/shard_map/all_to_all | solution.py:424
  55.4 1.4 %reduce_sum.12.p0 = bf16[64,512]{1,0:T(8,128)(2,1)S(1)} reduce(bf16[16,64,512]{2,1,0:T(8,128)(2,1)} %all-to-all-done, bf16[]{:T(256)} %constant.11.clone.1), dimensions={0}, to_apply=%region_0.0 | reduce | flops 491520 | bytes 1114114 | tf_op jit(solution)/shard_map/reduce_sum | solution.py:433
  56.8 2.0 %collective-permute-start.14 = (bf16[64,512]{1,0:T(8,128)(2,1)S(1)}, bf16[64,512]{1,0:T(8,128)(2,1)S(1)}, u32[]{:S(2)}, u32[]{:S(2)}) collective-permute-start(bf16[64,512]{1,0:T(8,128)(2,1)S(1)} %reduce_sum.12.p0), channel_id=1, source_target_pairs={{0,3},{1,0},{2,1},{3,2},{4,7},{5,4},{6,5},{7,6},{8,11},{9,8},{10,9... | collective-permute-start | bytes 196616 | tf_op jit(solution)/shard_map/ppermute | solution.py:339
  60.7 2.8 %collective-permute-done.13.p2 = bf16[64,512]{1,0:T(8,128)(2,1)S(1)} collective-permute-done((bf16[64,512]{1,0:T(8,128)(2,1)S(1)}, bf16[64,512]{1,0:T(8,128)(2,1)S(1)}, u32[]{:S(2)}, u32[]{:S(2)}) %collective-permute-start.13) | collective-permute-done | bytes 65568 | tf_op jit(solution)/shard_map/ppermute | solution.py:339
  65.3 5.1 %all-to-all-start.1 = ((bf16[16,64,512]{2,1,0:T(8,128)(2,1)}), bf16[16,64,512]{2,1,0:T(8,128)(2,1)S(1)}, u32[]{:S(2)}, u32[]{:S(2)}) async-start(bf16[16,64,512]{2,1,0:T(8,128)(2,1)} %spread.1), calls=%async_computation.1 | async-start | bytes 2097152 | tf_op jit(solution)/shard_map/all_to_all | solution.py:445
  70.5 3.8 %collective-permute-start.16 = (bf16[256,512]{1,0:T(8,128)(2,1)S(1)}, bf16[256,512]{1,0:T(8,128)(2,1)S(1)}, u32[]{:S(2)}, u32[]{:S(2)}) collective-permute-start(bf16[256,512]{1,0:T(8,128)(2,1)S(1)} %get-tuple-element.104), channel_id=1, source_target_pairs={{0,4},{4,0},{1,5},{5,1},{2,6},{6,2},{3,7},{7,3},{8,12},{12,8},{9,1... | collective-permute-start | bytes 786440 | tf_op jit(solution)/shard_map/ppermute | solution.py:339
  74.3 3.3 %collective-permute-start.15 = (bf16[256,512]{1,0:T(8,128)(2,1)S(1)}, bf16[256,512]{1,0:T(8,128)(2,1)S(1)}, u32[]{:S(2)}, u32[]{:S(2)}) collective-permute-start(bf16[256,512]{1,0:T(8,128)(2,1)S(1)} %get-tuple-element.103), channel_id=1, source_target_pairs={{4,8},{12,16},{20,24},{28,32},{36,40},{44,48},{52,56},{60,64},{68,... | collective-permute-start | bytes 786440 | tf_op jit(solution)/shard_map/ppermute | solution.py:345
  77.6 3.0 %grid_near.1.refs_0_ = bf16[2048,512]{1,0:T(8,128)(2,1)} custom-call(s32[1]{0:T(128)} %bitcast.1.sub_ref, s32[1]{0:T(128)} %bitcast.core_ref, bf16[256,512]{1,0:T(8,128)(2,1)S(1)} %collective-permute-done.16.outer, bf16[3,64,512]{2,1,0:T(8,128)(2,1)S(1)} %get-tuple-element.99.p0.s0, bf16[3,64,512]{2,1,0:T(8,128)(2,1)S(1)} %collective-permute-done.9.p1.s1, ...), custom_call_target="tpu_custom_call" | custom-call | flops 536870912 | bytes 3145728 | tf_op jit(solution)/shard_map/grid_near/pallas_call | solution.py:48
  80.7 8.1 %collective-permute-done.15.outer = bf16[256,512]{1,0:T(8,128)(2,1)S(1)} collective-permute-done((bf16[256,512]{1,0:T(8,128)(2,1)S(1)}, bf16[256,512]{1,0:T(8,128)(2,1)S(1)}, u32[]{:S(2)}, u32[]{:S(2)}) %collective-permute-start.15) | collective-permute-done | bytes 262176 | tf_op jit(solution)/shard_map/ppermute | solution.py:345
  88.8 2.2 %collective-permute-start.17 = (bf16[1024,512]{1,0:T(8,128)(2,1)S(1)}, bf16[1024,512]{1,0:T(8,128)(2,1)S(1)}, u32[]{:S(2)}, u32[]{:S(2)}) collective-permute-start(bf16[1024,512]{1,0:T(8,128)(2,1)S(1)} %bitcast.6), channel_id=1, source_target_pairs={{0,4},{4,0},{1,5},{5,1},{2,6},{6,2},{3,7},{7,3},{8,12},{12,8},{9,1... | collective-permute-start | bytes 3145736 | tf_op jit(solution)/shard_map/ppermute | solution.py:339
  90.9 1.4 %widen_own.1.refs_0_ = f32[4,512,512]{2,1,0:T(8,128)} custom-call(s32[1]{0:T(128)} %bitcast.core_ref, bf16[1024,512]{1,0:T(8,128)(2,1)S(1)} %bitcast.7), custom_call_target="tpu_custom_call" | custom-call | flops 1048576 | bytes 3145728 | tf_op jit(solution)/shard_map/widen_own/pallas_call | solution.py:48
  92.3 3.0 %grid_far.1 = bf16[2048,512]{1,0:T(8,128)(2,1)} custom-call(s32[1]{0:T(128)} %bitcast.1.sub_ref, s32[1]{0:T(128)} %bitcast.core_ref, bf16[256,512]{1,0:T(8,128)(2,1)S(1)} %collective-permute-done.15.outer, bf16[3,64,512]{2,1,0:T(8,128)(2,1)S(1)} %get-tuple-element.99.p0.s0, ...), custom_call_target="tpu_custom_call", output_to_operand_aliasing={{}: (10, {})} | custom-call | flops 536870912 | bytes 3145728 | tf_op jit(solution)/shard_map/grid_far/pallas_call | solution.py:48
  95.4 1.4 %widen_other.1 = f32[4,512,512]{2,1,0:T(8,128)} custom-call(s32[1]{0:T(128)} %bitcast.core_ref, bf16[1024,512]{1,0:T(8,128)(2,1)S(1)} %collective-permute-done.17.half_ref, f32[4,512,512]{2,1,0:T(8,128)} %widen_own.1.refs_0_), custom_call_target="tpu_custom_call", output_to_operand_aliasing={{}: (2, {})} | custom-call | flops 1048576 | bytes 3145728 | tf_op jit(solution)/shard_map/widen_other/pallas_call | solution.py:48
  (33 shorter events, 16.1 us)
Async XLA Ops:
  4.2 4.7 %collective-permute-start = (bf16[256,512]{1,0:T(8,128)(2,1)S(1)}, bf16[256,512]{1,0:T(8,128)(2,1)S(1)}, u32[]{:S(2)}, u32[]{:S(2)}) collective-permute-start(bf16[256,512]{1,0:T(8,128)(2,1)S(1)} %get-tuple-element.56), channel_id=1, source_target_pairs={{0,4},{4,0},{1,5},{5,1},{2,6},{6,2},{3,7},{7,3},{8,12},{12,8},{9,1... | collective-permute-start | bytes 786440 | tf_op jit(solution)/shard_map/ppermute | solution.py:339
  5.7 9.4 %collective-permute-start.1 = (bf16[256,512]{1,0:T(8,128)(2,1)S(1)}, bf16[256,512]{1,0:T(8,128)(2,1)S(1)}, u32[]{:S(2)}, u32[]{:S(2)}) collective-permute-start(bf16[256,512]{1,0:T(8,128)(2,1)S(1)} %get-tuple-element.57), channel_id=1, source_target_pairs={{4,8},{12,16},{20,24},{28,32},{36,40},{44,48},{52,56},{60,64},{68,... | collective-permute-start | bytes 786440 | tf_op jit(solution)/shard_map/ppermute | solution.py:345
  8.9 6.2 %collective-permute-start.2 = (bf16[128,512]{1,0:T(8,128)(2,1)S(1)}, bf16[128,512]{1,0:T(8,128)(2,1)S(1)}, u32[]{:S(2)}, u32[]{:S(2)}) collective-permute-start(bf16[128,512]{1,0:T(8,128)(2,1)S(1)} %get-tuple-element.59), channel_id=1, source_target_pairs={{0,1},{1,2},{2,3},{3,0},{4,5},{5,6},{6,7},{7,4},{8,9},{9,10},{10,1... | collective-permute-start | bytes 393224 | tf_op jit(solution)/shard_map/ppermute | solution.py:339
  10.6 10.3 %collective-permute-start.3 = (bf16[128,512]{1,0:T(8,128)(2,1)S(1)}, bf16[128,512]{1,0:T(8,128)(2,1)S(1)}, u32[]{:S(2)}, u32[]{:S(2)}) collective-permute-start(bf16[128,512]{1,0:T(8,128)(2,1)S(1)} %get-tuple-element.68), channel_id=1, source_target_pairs={{0,2},{1,3},{2,0},{3,1},{4,6},{5,7},{6,4},{7,5},{8,10},{9,11},{10,... | collective-permute-start | bytes 393224 | tf_op jit(solution)/shard_map/ppermute | solution.py:339
  13.9 7.0 %collective-permute-start.4 = (bf16[128,512]{1,0:T(8,128)(2,1)S(1)}, bf16[128,512]{1,0:T(8,128)(2,1)S(1)}, u32[]{:S(2)}, u32[]{:S(2)}) collective-permute-start(bf16[128,512]{1,0:T(8,128)(2,1)S(1)} %get-tuple-element.69), channel_id=1, source_target_pairs={{0,3},{1,0},{2,1},{3,2},{4,7},{5,4},{6,5},{7,6},{8,11},{9,8},{10,9... | collective-permute-start | bytes 393224 | tf_op jit(solution)/shard_map/ppermute | solution.py:339
  15.1 6.5 %collective-permute-start.5 = (bf16[64,512]{1,0:T(8,128)(2,1)S(1)}, bf16[64,512]{1,0:T(8,128)(2,1)S(1)}, u32[]{:S(2)}, u32[]{:S(2)}) collective-permute-start(bf16[64,512]{1,0:T(8,128)(2,1)S(1)} %get-tuple-element.70), channel_id=1, source_target_pairs={{0,1},{1,2},{2,3},{3,0},{4,5},{5,6},{6,7},{7,4},{8,9},{9,10},{10,1... | collective-permute-start | bytes 196616 | tf_op jit(solution)/shard_map/ppermute | solution.py:339
  15.9 6.2 %collective-permute-start.6 = (bf16[64,512]{1,0:T(8,128)(2,1)S(1)}, bf16[64,512]{1,0:T(8,128)(2,1)S(1)}, u32[]{:S(2)}, u32[]{:S(2)}) collective-permute-start(bf16[64,512]{1,0:T(8,128)(2,1)S(1)} %get-tuple-element.71), channel_id=1, source_target_pairs={{0,2},{1,3},{2,0},{3,1},{4,6},{5,7},{6,4},{7,5},{8,10},{9,11},{10,... | collective-permute-start | bytes 196616 | tf_op jit(solution)/shard_map/ppermute | solution.py:339
  19.5 3.1 %collective-permute-start.7 = (bf16[64,512]{1,0:T(8,128)(2,1)S(1)}, bf16[64,512]{1,0:T(8,128)(2,1)S(1)}, u32[]{:S(2)}, u32[]{:S(2)}) collective-permute-start(bf16[64,512]{1,0:T(8,128)(2,1)S(1)} %get-tuple-element.72), channel_id=1, source_target_pairs={{0,3},{1,0},{2,1},{3,2},{4,7},{5,4},{6,5},{7,6},{8,11},{9,8},{10,9... | collective-permute-start | bytes 196616 | tf_op jit(solution)/shard_map/ppermute | solution.py:339
  27.6 2.7 %collective-permute-start.8 = (bf16[1024,512]{1,0:T(8,128)(2,1)S(1)}, bf16[1024,512]{1,0:T(8,128)(2,1)S(1)}, u32[]{:S(2)}, u32[]{:S(2)}) collective-permute-start(bf16[1024,512]{1,0:T(8,128)(2,1)S(1)} %get-tuple-element.81), channel_id=1, source_target_pairs={{0,4},{4,0},{1,5},{5,1},{2,6},{6,2},{3,7},{7,3},{8,12},{12,8},{9,1... | collective-permute-start | bytes 3145736 | tf_op jit(solution)/shard_map/ppermute | solution.py:339
  31.4 24.0 %all-to-all-start = ((bf16[16,64,512]{2,1,0:T(8,128)(2,1)}), bf16[16,64,512]{2,1,0:T(8,128)(2,1)}, u32[]{:S(2)}, u32[]{:S(2)}) async-start(bf16[16,64,512]{2,1,0:T(8,128)(2,1)} %bitcast.4), calls=%async_computation | async-start | bytes 2097152 | tf_op jit(solution)/shard_map/all_to_all | solution.py:424
  40.4 7.4 %collective-permute-start.10 = (bf16[3,64,512]{2,1,0:T(8,128)(2,1)S(1)}, bf16[3,64,512]{2,1,0:T(8,128)(2,1)S(1)}, u32[]{:S(2)}, u32[]{:S(2)}) collective-permute-start(bf16[3,64,512]{2,1,0:T(8,128)(2,1)S(1)} %get-tuple-element.88), channel_id=1, source_target_pairs={{0,2},{1,3},{2,0},{3,1},{4,6},{5,7},{6,4},{7,5},{8,10},{9,11},{10,... | collective-permute-start | bytes 589832 | tf_op jit(solution)/shard_map/ppermute | solution.py:339
  41.7 11.4 %collective-permute-start.11 = (bf16[3,64,512]{2,1,0:T(8,128)(2,1)S(1)}, bf16[3,64,512]{2,1,0:T(8,128)(2,1)S(1)}, u32[]{:S(2)}, u32[]{:S(2)}) collective-permute-start(bf16[3,64,512]{2,1,0:T(8,128)(2,1)S(1)} %get-tuple-element.89), channel_id=1, source_target_pairs={{0,1},{1,2},{2,3},{3,0},{4,5},{5,6},{6,7},{7,4},{8,9},{9,10},{10,1... | collective-permute-start | bytes 589832 | tf_op jit(solution)/shard_map/ppermute | solution.py:339
  42.8 10.3 %collective-permute-start.9 = (bf16[3,64,512]{2,1,0:T(8,128)(2,1)S(1)}, bf16[3,64,512]{2,1,0:T(8,128)(2,1)S(1)}, u32[]{:S(2)}, u32[]{:S(2)}) collective-permute-start(bf16[3,64,512]{2,1,0:T(8,128)(2,1)S(1)} %get-tuple-element.87), channel_id=1, source_target_pairs={{0,3},{1,0},{2,1},{3,2},{4,7},{5,4},{6,5},{7,6},{8,11},{9,8},{10,9... | collective-permute-start | bytes 589832 | tf_op jit(solution)/shard_map/ppermute | solution.py:339
  56.8 3.9 %collective-permute-start.14 = (bf16[64,512]{1,0:T(8,128)(2,1)S(1)}, bf16[64,512]{1,0:T(8,128)(2,1)S(1)}, u32[]{:S(2)}, u32[]{:S(2)}) collective-permute-start(bf16[64,512]{1,0:T(8,128)(2,1)S(1)} %reduce_sum.12.p0), channel_id=1, source_target_pairs={{0,3},{1,0},{2,1},{3,2},{4,7},{5,4},{6,5},{7,6},{8,11},{9,8},{10,9... | collective-permute-start | bytes 196616 | tf_op jit(solution)/shard_map/ppermute | solution.py:339
  58.8 4.7 %collective-permute-start.13 = (bf16[64,512]{1,0:T(8,128)(2,1)S(1)}, bf16[64,512]{1,0:T(8,128)(2,1)S(1)}, u32[]{:S(2)}, u32[]{:S(2)}) collective-permute-start(bf16[64,512]{1,0:T(8,128)(2,1)S(1)} %reduce_sum.12.p0), channel_id=1, source_target_pairs={{0,2},{1,3},{2,0},{3,1},{4,6},{5,7},{6,4},{7,5},{8,10},{9,11},{10,... | collective-permute-start | bytes 196616 | tf_op jit(solution)/shard_map/ppermute | solution.py:339
  59.2 5.0 %collective-permute-start.12 = (bf16[64,512]{1,0:T(8,128)(2,1)S(1)}, bf16[64,512]{1,0:T(8,128)(2,1)S(1)}, u32[]{:S(2)}, u32[]{:S(2)}) collective-permute-start(bf16[64,512]{1,0:T(8,128)(2,1)S(1)} %reduce_sum.12.p0), channel_id=1, source_target_pairs={{0,1},{1,2},{2,3},{3,0},{4,5},{5,6},{6,7},{7,4},{8,9},{9,10},{10,1... | collective-permute-start | bytes 196616 | tf_op jit(solution)/shard_map/ppermute | solution.py:339
  65.3 23.5 %all-to-all-start.1 = ((bf16[16,64,512]{2,1,0:T(8,128)(2,1)}), bf16[16,64,512]{2,1,0:T(8,128)(2,1)S(1)}, u32[]{:S(2)}, u32[]{:S(2)}) async-start(bf16[16,64,512]{2,1,0:T(8,128)(2,1)} %spread.1), calls=%async_computation.1 | async-start | bytes 2097152 | tf_op jit(solution)/shard_map/all_to_all | solution.py:445
  70.5 7.1 %collective-permute-start.16 = (bf16[256,512]{1,0:T(8,128)(2,1)S(1)}, bf16[256,512]{1,0:T(8,128)(2,1)S(1)}, u32[]{:S(2)}, u32[]{:S(2)}) collective-permute-start(bf16[256,512]{1,0:T(8,128)(2,1)S(1)} %get-tuple-element.104), channel_id=1, source_target_pairs={{0,4},{4,0},{1,5},{5,1},{2,6},{6,2},{3,7},{7,3},{8,12},{12,8},{9,1... | collective-permute-start | bytes 786440 | tf_op jit(solution)/shard_map/ppermute | solution.py:339
  74.3 14.5 %collective-permute-start.15 = (bf16[256,512]{1,0:T(8,128)(2,1)S(1)}, bf16[256,512]{1,0:T(8,128)(2,1)S(1)}, u32[]{:S(2)}, u32[]{:S(2)}) collective-permute-start(bf16[256,512]{1,0:T(8,128)(2,1)S(1)} %get-tuple-element.103), channel_id=1, source_target_pairs={{4,8},{12,16},{20,24},{28,32},{36,40},{44,48},{52,56},{60,64},{68,... | collective-permute-start | bytes 786440 | tf_op jit(solution)/shard_map/ppermute | solution.py:345
  88.8 6.6 %collective-permute-start.17 = (bf16[1024,512]{1,0:T(8,128)(2,1)S(1)}, bf16[1024,512]{1,0:T(8,128)(2,1)S(1)}, u32[]{:S(2)}, u32[]{:S(2)}) collective-permute-start(bf16[1024,512]{1,0:T(8,128)(2,1)S(1)} %bitcast.6), channel_id=1, source_target_pairs={{0,4},{4,0},{1,5},{5,1},{2,6},{6,2},{3,7},{7,3},{8,12},{12,8},{9,1... | collective-permute-start | bytes 3145736 | tf_op jit(solution)/shard_map/ppermute | solution.py:339

commit v12 on v11

--- a/solution.py
+++ b/solution.py
@@ -86,11 +86,11 @@
 
 
 def gather_body(sub_ref, core_ref, rows_hbm, gain_hbm, x_hbm, *refs):
-    later = (len(refs) - 7) // 2
+    later = (len(refs) - 8) // 2
     later_hbm, refs = refs[:later], refs[later:]
-    near_ref, far_ref, own_ref = refs[:3]
-    later_refs = refs[3 : 3 + later - 1]
-    rows_ref, gain_ref, x_ref, sems, later_sems = refs[-5:]
+    near_ref, far_ref, own_ref, rows_ref, gain_ref = refs[:5]
+    later_refs = refs[5 : 5 + later]
+    x_ref, sems, later_sems = refs[-3:]
     half = x_ref.shape[0] // 2
     cap = rows_ref.shape[3]
     core = core_ref[0]
@@ -101,9 +101,6 @@
         [rows_ref, gain_ref] + [x_ref.at[p] for p in parts],
         sems,
     )
-    wkv_ref = later_refs[-1]
-    width = x_ref.shape[1]
-    later_refs = (*later_refs[:-1], wkv_ref.at[:, pl.ds(0, width)], wkv_ref.at[:, pl.ds(width, width)])
     later_copies = fetch(later_hbm, later_refs, later_sems)
     copies[0].wait()
     copies[1].wait()
@@ -142,7 +139,12 @@
     ag_ref[...] = nt(og_ref[...], wo_ref[...]).astype(BF16)
 
 
-def slots_body(sub_ref, nbr_ref, valid_ref, bias_ref, dense_ref, inv_ref, edge_ref):
+def slots_body(sub_ref, nbr_ref, valid_ref, bias_ref, wk_hbm, wv_hbm, dense_ref, wkv_ref,
+               inv_ref, edge_ref, sems):
+    width = wk_hbm.shape[0]
+    copies = fetch(
+        (wk_hbm, wv_hbm), (wkv_ref.at[:, pl.ds(0, width)], wkv_ref.at[:, pl.ds(width, width)]), sems
+    )
     heads, nodes, slots = dense_ref.shape
     fan = nbr_ref.shape[1]
     slot = nbr_ref[...]
@@ -165,6 +167,8 @@
         for h in range(heads):
             got = jnp.take_along_axis(edge_ref[h], at, axis=1, mode="promise_in_bounds")
             dense_ref[h, :, b * 128 : (b + 1) * 128] = jnp.where(here, got, ABSENT)
+    for copy in copies:
+        copy.wait()
 
 
 def middle_body(core_ref, near, far, own, m1, m2, m3, f1, f2, f3, q_ref, ag_ref, mn_ref, og_ref,
@@ -245,50 +249,61 @@
         piece[...] = block[k * cap : (k + 1) * cap]
 
 
-def grid_body(turn, sub_ref, core_ref, outer, s0, s1, s2, s3, rows_hbm, gain_hbm, x_hbm, *refs):
-    out_hbm, got, done_ref, done_sems, rows_ref, gain_ref, x_ref, sems = refs[-8:]
+def grid_half(upper, sub_ref, outer, s0, s1, s2, s3, rows_ref, gain_ref, x_ref, out_hbm, got, done_ref,
+              sems, ready):
     half = x_ref.shape[0]
-    upper = (1 - core_ref[0]) if turn == 0 else core_ref[0]
     base = pl.multiple_of(upper * half, half)
-    tile = 256
-    tiles = half // tile
-    spans = [pl.ds(t * tile, tile) for t in range(tiles)]
-    copies = fetch(
-        [rows_hbm, gain_hbm] + [x_hbm.at[pl.ds(base + t * tile, tile)] for t in range(tiles)],
-        [rows_ref, gain_ref] + [x_ref.at[span] for span in spans],
-        sems,
-    )
     cap = rows_ref.shape[3]
     block = 4 * cap
     me = sub_ref[0]
     got[0:block] = outer[...]
     for k, piece in enumerate((s0, s1, s2, s3)):
         got[block + k * cap : block + (k + 1) * cap] = piece[1]
-    copies[0].wait()
-    copies[1].wait()
     gain = gain_ref[...]
     idx = []
     for o in (2 * upper, 1):
         for k in range(4):
             idx.append(rows_ref[0, o, pl.ds(lax.rem(me + k, 4), 1), :])
     idx = jnp.concatenate(idx, axis=1) - base
+    tile = 256
     stores = []
-    for t in range(tiles):
+    for t in range(half // tile):
         part = slice(t * tile, (t + 1) * tile)
         ids = lax.broadcasted_iota(jnp.int32, (tile, 2 * block), 0) + t * tile
         onehot = jnp.where(ids == idx, 1.0, 0.0).astype(BF16)
         upstream = nn(onehot, got[...])
-        copies[2 + t].wait()
+        if t == 0:
+            ready()
         wide = x_ref[part, :].astype(F32)
         done_ref[part, :] = norm_back(wide, inv_rms(wide), gain, upstream).astype(BF16)
         stores.append(
             pltpu.make_async_copy(
-                done_ref.at[part], out_hbm.at[pl.ds(base + t * tile, tile)], done_sems.at[t]
+                done_ref.at[part], out_hbm.at[pl.ds(base + t * tile, tile)], sems.at[t]
             )
         )
         stores[-1].start()
     for store in stores:
         store.wait()
+
+
+def grid_near_body(sub_ref, core_ref, near, s0, s1, s2, s3, rows_ref, gain_ref, x_hbm,
+                   out_hbm, far_x_ref, got, done_ref, done_sems, x_ref, sems):
+    half = x_ref.shape[0]
+    upper = 1 - core_ref[0]
+    copies = fetch(
+        [x_hbm.at[pl.ds(pl.multiple_of(u * half, half), half)] for u in (upper, core_ref[0])],
+        [x_ref, far_x_ref],
+        sems,
+    )
+    grid_half(upper, sub_ref, near, s0, s1, s2, s3, rows_ref, gain_ref, x_ref, out_hbm, got, done_ref,
+              done_sems, copies[0].wait)
+    copies[1].wait()
+
+
+def grid_far_body(sub_ref, core_ref, far, s0, s1, s2, s3, rows_ref, gain_ref, x_ref, prior_hbm,
+                  out_hbm, got, done_ref, done_sems):
+    grid_half(core_ref[0], sub_ref, far, s0, s1, s2, s3, rows_ref, gain_ref, x_ref, out_hbm, got,
+              done_ref, done_sems, lambda: None)
 
 
 def widen_body(turn, core_ref, half_ref, *refs):
@@ -322,6 +337,13 @@
         copy.wait()
 
 
+def plane_body(parts_ref, out_ref):
+    total = parts_ref[0].astype(F32)
+    for i in range(1, parts_ref.shape[0]):
+        total = total + parts_ref[i].astype(F32)
+    out_ref[...] = total.astype(BF16)
+
+
 def spread_body(p0, p1, p2, p3, out_hbm, total, sems):
     even = p0[...].astype(F32) + p2[...].astype(F32)
     odd = p1[...].astype(F32) + p3[...].astype(F32)
@@ -369,13 +391,13 @@
 
     one, two, four = sds((cap, width)), sds((2 * cap, width)), sds((block, width))
     later = (mesh_h, gain_m, w_query, w_out, out_grad, neighbours, valid, edge_bias)
-    weights = sds((width, 2 * width))
-    near, far, own, *later, weights_near = call(
-        gather_body, [four] * 3 + [sds(a.shape, a.dtype) for a in later] + [weights],
-        [SM, SM] + [HB] * (5 + len(later)),
-        (sub1, core1, send_rows, gain_g, grid_x, *later, w_key, w_value), 1 << 30, 6 << 20, "gather_rows",
-        held(send_rows, gain_g, grid_x)[:-1]
-        + [pltpu.SemaphoreType.DMA((4,)), pltpu.SemaphoreType.DMA((len(later) + 2,))],
+    near, far, own, rows_near, gain_g_near, *later = call(
+        gather_body,
+        [four] * 3 + [sds(a.shape, a.dtype) for a in (send_rows, gain_g, *later)],
+        [SM, SM] + [HB] * (3 + len(later)),
+        (sub1, core1, send_rows, gain_g, grid_x, *later), 1 << 30, 5 << 20, "gather_rows",
+        [pltpu.VMEM((points, width), BF16), pltpu.SemaphoreType.DMA((4,)),
+         pltpu.SemaphoreType.DMA((len(later),))],
     )
     mesh_near, gain_near, wq_near, wo_near, og_near, nbr_near, valid_near, bias_near = later
     far = swapped_far(far)
@@ -391,10 +413,12 @@
     outer = [shifted(f, "z", k) for k, f in enumerate(outer, 1)]
     received = near, far, own, *mixed, *outer
     sub2, far = lax.optimization_barrier((sub1, far))
-    (dense,) = call(
-        slots_body, [sds((heads, nodes, slots), F32)], [SM] + [VM] * 3,
-        (sub2, nbr_near, valid_near, bias_near), 1 << 30, 8 << 20, "slots",
-        [pltpu.VMEM((nodes * 8, 128), F32), pltpu.VMEM((heads, nodes, 128), F32)],
+    dense, weights_near = call(
+        slots_body, [sds((heads, nodes, slots), F32), sds((width, 2 * width))],
+        [SM] + [VM] * 3 + [HB] * 2,
+        (sub2, nbr_near, valid_near, bias_near, w_key, w_value), 1 << 30, 8 << 20, "slots",
+        [pltpu.VMEM((nodes * 8, 128), F32), pltpu.VMEM((heads, nodes, 128), F32),
+         pltpu.SemaphoreType.DMA((2,))],
     )
     send, part_grads, attended, query_grad, rows = call(
         middle_body,
@@ -430,7 +454,7 @@
     )
     s1, s2, s3 = (shifted(s, "z", -k) for k, s in ((1, s1), (2, s2), (3, s3)))
     s1, s2, s3, parts, mesh_out = lax.optimization_barrier((s1, s2, s3, parts, mesh_out))
-    part = jnp.sum(parts.astype(F32), axis=0).astype(BF16)
+    (part,) = call(plane_body, [sds((share, width))], [VM], (parts,), 1 << 20, 1 << 20, "plane")
     part, s0 = lax.optimization_barrier((part, s0))
     near, far = call(
         pack_body, [four] * 2, [SM] + [VM] * 4, (core1, s0, s1, s2, s3), 0, 1 << 20, "pack"
@@ -446,20 +470,19 @@
     half = points // 2
     grid_scratch = [
         pltpu.VMEM((2 * block, width), BF16), pltpu.VMEM((half, width), BF16),
-        pltpu.SemaphoreType.DMA((half // 256,)), pltpu.VMEM(send_rows.shape, send_rows.dtype),
-        pltpu.VMEM(gain_g.shape, F32), pltpu.VMEM((half, width), BF16), pltpu.SemaphoreType.DMA((2 + half // 256,)),
+        pltpu.SemaphoreType.DMA((half // 256,)),
     ]
-    grid_specs = [SM] * 2 + [VM] * 5 + [HB] * 3
-    (grid_grad,) = call(
-        functools.partial(grid_body, 0), [sds((points, width))], grid_specs,
-        (sub1, core1, near, s0, s1, s2, s3, send_rows, gain_g, grid_x),
-        1 << 29, 3 << 20, "grid_near", grid_scratch, [HB],
+    grid_grad, far_x = call(
+        grid_near_body, [sds((points, width)), sds((half, width))], [SM] * 2 + [VM] * 7 + [HB],
+        (sub1, core1, near, s0, s1, s2, s3, rows_near, gain_g_near, grid_x),
+        1 << 29, 3 << 20, "grid_near",
+        grid_scratch + [pltpu.VMEM((half, width), BF16), pltpu.SemaphoreType.DMA((2,))], [HB, VM],
     )
     mine, far, grid_grad = lax.optimization_barrier((mine, far, grid_grad))
     theirs = shifted(mine, "gc", 1)
     (grid_grad,) = call(
-        functools.partial(grid_body, 1), [sds((points, width))], grid_specs + [HB],
-        (sub1, core1, far, s0, s1, s2, s3, send_rows, gain_g, grid_x, grid_grad),
+        grid_far_body, [sds((points, width))], [SM] * 2 + [VM] * 8 + [HB],
+        (sub1, core1, far, s0, s1, s2, s3, rows_near, gain_g_near, far_x, grid_grad),
         1 << 29, 3 << 20, "grid_far", grid_scratch, [HB], {10: 0},
     )
     whole = sds((4, width, width), F32)

time: 97.3 us -> 94.7 us (0.973)
  other arithmetic: 1.37 us -> 0 us
  starting transfers between devices: 45 us -> 43.9 us
    reduce_sum x1 -> x0, other arithmetic: 1.37 us -> none  [shards(): part = jnp.sum(parts.astype(F32), axis=0).astype(BF16)]
    pallas_call x16 -> x17, Pallas kernels: 24.2 us -> 23.8 us  [call(): pl.pallas_call(body, out_shape=outs, in_specs=in_specs, out_specs=out_spe...]
  transfers between devices with their start and end apart: 20 -> 20, of which waited for: 11 -> 11; matrix products, arithmetic and copies ran while one was open for 0% -> 0% of each run, Pallas kernels for 13% -> 12%
where the time goes in v12:
time: 94.7 us; the launch traced here: 94.3 us
  starting transfers between devices  43.9 us (46%)
  waiting for transfers between devices  24.6 us (26%)
  Pallas kernels  23.8 us (25%)
  between operations  1.02 us (1%)
  local copies, waits for them, and re-layouts  0.97 us (1%)
    ppermute x16, starting transfers between devices, shifted(): return lax.ppermute(block, axis, [(i, (i + k) % n) for i in range(n)])  23.8 us
    pallas_call x17, Pallas kernels, call(): pl.pallas_call(body, out_shape=outs, in_specs=in_specs, out_specs=out_spe...  23.8 us
    ppermute x16, waiting for transfers between devices, shifted(): return lax.ppermute(block, axis, [(i, (i + k) % n) for i in range(n)])  14.3 us
    all_to_all x1, starting transfers between devices, shards(): lax.all_to_all(own.reshape(plane, share, width), PLANE, 0, 0, tiled=True)  9.07 us
    ppermute x2, waiting for transfers between devices, swapped_far(): return lax.ppermute(block, SLAB, pairs + [(j, i) for i, j in pairs])  7.26 us
    ppermute x2, starting transfers between devices, swapped_far(): return lax.ppermute(block, SLAB, pairs + [(j, i) for i, j in pairs])  6.53 us
    all_to_all x1, starting transfers between devices, shards(): lax.all_to_all(spread, PLANE, 0, 0, tiled=True).reshape(2 * width, width)  4.51 us
    all_to_all x1, waiting for transfers between devices, shards(): lax.all_to_all(own.reshape(plane, share, width), PLANE, 0, 0, tiled=True)  2.99 us
  transfers between devices with their start and end apart: 20, of which 11 were waited for; matrix products, arithmetic and copies ran while one was open for 0% of the time, Pallas kernels for 12%

profile of v12, /device:TPU:1, one launch (start us, length us, event | category | flops | bytes accessed | tf_op | source)
XLA Modules:
  0.0 94.3 jit_solution(3752032911870724825)
XLA Ops:
  0.6 3.5 %gather_rows.1 = (bf16[256,512]{1,0:T(8,128)(2,1)S(1)}, bf16[256,512]{1,0:T(8,128)(2,1)S(1)}, bf16[256,512]{1,0:T(8,128)(2,1)S(1)}, s32[1,3,4,64]{3,2,1,0:T(4,12...) custom-call(s32[1]{0:T(128)} %bitcast.1.sub_ref, ...), custom_call_target="tpu_custom_call" | custom-call | flops 1073741824 | bytes 5242880 | tf_op jit(solution)/shard_map/gather_rows/pallas_call | solution.py:48
  4.1 1.5 %collective-permute-start = (bf16[256,512]{1,0:T(8,128)(2,1)S(1)}, bf16[256,512]{1,0:T(8,128)(2,1)S(1)}, u32[]{:S(2)}, u32[]{:S(2)}) collective-permute-start(bf16[256,512]{1,0:T(8,128)(2,1)S(1)} %get-tuple-element.61), channel_id=1, source_target_pairs={{0,4},{4,0},{1,5},{5,1},{2,6},{6,2},{3,7},{7,3},{8,12},{12,8},{9,1... | collective-permute-start | bytes 786440 | tf_op jit(solution)/shard_map/ppermute | solution.py:361
  5.6 3.2 %collective-permute-start.1 = (bf16[256,512]{1,0:T(8,128)(2,1)S(1)}, bf16[256,512]{1,0:T(8,128)(2,1)S(1)}, u32[]{:S(2)}, u32[]{:S(2)}) collective-permute-start(bf16[256,512]{1,0:T(8,128)(2,1)S(1)} %get-tuple-element.62), channel_id=1, source_target_pairs={{4,8},{12,16},{20,24},{28,32},{36,40},{44,48},{52,56},{60,64},{68,... | collective-permute-start | bytes 786440 | tf_op jit(solution)/shard_map/ppermute | solution.py:367
  8.8 1.7 %collective-permute-start.2 = (bf16[128,512]{1,0:T(8,128)(2,1)S(1)}, bf16[128,512]{1,0:T(8,128)(2,1)S(1)}, u32[]{:S(2)}, u32[]{:S(2)}) collective-permute-start(bf16[128,512]{1,0:T(8,128)(2,1)S(1)} %get-tuple-element.64), channel_id=1, source_target_pairs={{0,1},{1,2},{2,3},{3,0},{4,5},{5,6},{6,7},{7,4},{8,9},{9,10},{10,1... | collective-permute-start | bytes 393224 | tf_op jit(solution)/shard_map/ppermute | solution.py:361
  10.5 3.3 %collective-permute-start.3 = (bf16[128,512]{1,0:T(8,128)(2,1)S(1)}, bf16[128,512]{1,0:T(8,128)(2,1)S(1)}, u32[]{:S(2)}, u32[]{:S(2)}) collective-permute-start(bf16[128,512]{1,0:T(8,128)(2,1)S(1)} %get-tuple-element.73), channel_id=1, source_target_pairs={{0,2},{1,3},{2,0},{3,1},{4,6},{5,7},{6,4},{7,5},{8,10},{9,11},{10,... | collective-permute-start | bytes 393224 | tf_op jit(solution)/shard_map/ppermute | solution.py:361
  15.9 3.6 %collective-permute-start.6 = (bf16[64,512]{1,0:T(8,128)(2,1)S(1)}, bf16[64,512]{1,0:T(8,128)(2,1)S(1)}, u32[]{:S(2)}, u32[]{:S(2)}) collective-permute-start(bf16[64,512]{1,0:T(8,128)(2,1)S(1)} %get-tuple-element.76), channel_id=1, source_target_pairs={{0,2},{1,3},{2,0},{3,1},{4,6},{5,7},{6,4},{7,5},{8,10},{9,11},{10,... | collective-permute-start | bytes 196616 | tf_op jit(solution)/shard_map/ppermute | solution.py:361
  22.6 4.9 %middle.1 = (bf16[1024,512]{1,0:T(8,128)(2,1)S(1)}, bf16[768,1024]{1,0:T(8,128)(2,1)S(1)}, bf16[64,512]{1,0:T(8,128)(2,1)S(1)}, bf16[64,512]{1,0:T(8,128)(2,1)S(1)}, bf16[768,512]{1,0:T(8,128)(2,1)S(1)}) custom-call(s32[1]{0:T(128)} %bitcast.core_ref, bf16[256,512]{1,0:T(8,128)(2,1)S(1)} %collective-permute-done.near, ...), custom_call_target="tpu_custom_call" | custom-call | flops 3221225472 | bytes 8388608 | tf_op jit(solution)/shard_map/middle/pallas_call | solution.py:48
  28.3 1.7 %back.1 = (bf16[3,64,512]{2,1,0:T(8,128)(2,1)S(1)}, bf16[3,64,512]{2,1,0:T(8,128)(2,1)S(1)}, bf16[3,64,512]{2,1,0:T(8,128)(2,1)}, bf16[3,64,512]{2,1,0:T(8,128)(2,1)S(1)}) custom-call(bf16[768,1024]{1,0:T(8,128)(2,1)S(1)} %get-tuple-element.88.part_ref, bf16[512,1024]{1,0:T(8,128)(2,1)S(1)} %get-tuple-element.86.wkv_ref), custom_call_target="tpu_custom_call" | custom-call | flops 1073741824 | bytes 3145728 | tf_op jit(solution)/shard_map/back/pallas_call | solution.py:48
  31.3 9.1 %all-to-all-start = ((bf16[16,64,512]{2,1,0:T(8,128)(2,1)}), bf16[16,64,512]{2,1,0:T(8,128)(2,1)S(1)}, u32[]{:S(2)}, u32[]{:S(2)}) async-start(bf16[16,64,512]{2,1,0:T(8,128)(2,1)} %bitcast.4), calls=%async_computation | async-start | bytes 2097152 | tf_op jit(solution)/shard_map/all_to_all | solution.py:448
  42.8 1.6 %collective-permute-start.9 = (bf16[3,64,512]{2,1,0:T(8,128)(2,1)S(1)}, bf16[3,64,512]{2,1,0:T(8,128)(2,1)S(1)}, u32[]{:S(2)}, u32[]{:S(2)}) collective-permute-start(bf16[3,64,512]{2,1,0:T(8,128)(2,1)S(1)} %get-tuple-element.93), channel_id=1, source_target_pairs={{0,3},{1,0},{2,1},{3,2},{4,7},{5,4},{6,5},{7,6},{8,11},{9,8},{10,9... | collective-permute-start | bytes 589832 | tf_op jit(solution)/shard_map/ppermute | solution.py:361
  45.5 2.7 %collective-permute-done.10.p2.s2 = bf16[3,64,512]{2,1,0:T(8,128)(2,1)S(1)} collective-permute-done((bf16[3,64,512]{2,1,0:T(8,128)(2,1)}, bf16[3,64,512]{2,1,0:T(8,128)(2,1)S(1)}, u32[]{:S(2)}, u32[]{:S(2)}) %collective-permute-start.10) | collective-permute-done | bytes 196640 | tf_op jit(solution)/shard_map/ppermute | solution.py:361
  48.2 5.0 %collective-permute-done.11.p3.s3 = bf16[3,64,512]{2,1,0:T(8,128)(2,1)S(1)} collective-permute-done((bf16[3,64,512]{2,1,0:T(8,128)(2,1)S(1)}, bf16[3,64,512]{2,1,0:T(8,128)(2,1)S(1)}, u32[]{:S(2)}, u32[]{:S(2)}) %collective-permute-start.11) | collective-permute-done | bytes 196640 | tf_op jit(solution)/shard_map/ppermute | solution.py:361
  53.2 3.0 %all-to-all-done.parts_ref = bf16[16,64,512]{2,1,0:T(8,128)(2,1)S(1)} async-done(((bf16[16,64,512]{2,1,0:T(8,128)(2,1)}), bf16[16,64,512]{2,1,0:T(8,128)(2,1)S(1)}, u32[]{:S(2)}, u32[]{:S(2)}) %all-to-all-start) | async-done | bytes 1048608 | tf_op jit(solution)/shard_map/all_to_all | solution.py:448
  56.4 2.0 %collective-permute-start.14 = (bf16[64,512]{1,0:T(8,128)(2,1)S(1)}, bf16[64,512]{1,0:T(8,128)(2,1)S(1)}, u32[]{:S(2)}, u32[]{:S(2)}) collective-permute-start(bf16[64,512]{1,0:T(8,128)(2,1)S(1)} %plane.1.p0), channel_id=1, source_target_pairs={{0,3},{1,0},{2,1},{3,2},{4,7},{5,4},{6,5},{7,6},{8,11},{9,8},{10,9... | collective-permute-start | bytes 196616 | tf_op jit(solution)/shard_map/ppermute | solution.py:361
  60.3 2.8 %collective-permute-done.13.p2 = bf16[64,512]{1,0:T(8,128)(2,1)S(1)} collective-permute-done((bf16[64,512]{1,0:T(8,128)(2,1)S(1)}, bf16[64,512]{1,0:T(8,128)(2,1)S(1)}, u32[]{:S(2)}, u32[]{:S(2)}) %collective-permute-start.13) | collective-permute-done | bytes 65568 | tf_op jit(solution)/shard_map/ppermute | solution.py:361
  64.8 4.5 %all-to-all-start.1 = ((bf16[16,64,512]{2,1,0:T(8,128)(2,1)}), bf16[16,64,512]{2,1,0:T(8,128)(2,1)S(1)}, u32[]{:S(2)}, u32[]{:S(2)}) async-start(bf16[16,64,512]{2,1,0:T(8,128)(2,1)} %spread.1), calls=%async_computation.1 | async-start | bytes 2097152 | tf_op jit(solution)/shard_map/all_to_all | solution.py:469
  69.4 3.6 %collective-permute-start.16 = (bf16[256,512]{1,0:T(8,128)(2,1)S(1)}, bf16[256,512]{1,0:T(8,128)(2,1)S(1)}, u32[]{:S(2)}, u32[]{:S(2)}) collective-permute-start(bf16[256,512]{1,0:T(8,128)(2,1)S(1)} %get-tuple-element.110), channel_id=1, source_target_pairs={{0,4},{4,0},{1,5},{5,1},{2,6},{6,2},{3,7},{7,3},{8,12},{12,8},{9,1... | collective-permute-start | bytes 786440 | tf_op jit(solution)/shard_map/ppermute | solution.py:361
  73.0 3.3 %collective-permute-start.15 = (bf16[256,512]{1,0:T(8,128)(2,1)S(1)}, bf16[256,512]{1,0:T(8,128)(2,1)S(1)}, u32[]{:S(2)}, u32[]{:S(2)}) collective-permute-start(bf16[256,512]{1,0:T(8,128)(2,1)S(1)} %get-tuple-element.109), channel_id=1, source_target_pairs={{4,8},{12,16},{20,24},{28,32},{36,40},{44,48},{52,56},{60,64},{68,... | collective-permute-start | bytes 786440 | tf_op jit(solution)/shard_map/ppermute | solution.py:367
  76.4 3.1 %grid_near.1 = (bf16[2048,512]{1,0:T(8,128)(2,1)}, bf16[1024,512]{1,0:T(8,128)(2,1)S(1)}) custom-call(s32[1]{0:T(128)} %bitcast.1.sub_ref, s32[1]{0:T(128)} %bitcast.core_ref, bf16[256,512]{1,0:T(8,128)(2,1)S(1)} %collective-permute-done.16.near, bf16[3,64,512]{2,1,0:T(8,128)(2,1)S(1)} %get-tuple-element.105.p0.s0, ...), custom_call_target="tpu_custom_call" | custom-call | flops 536870912 | bytes 3145728 | tf_op jit(solution)/shard_map/grid_near/pallas_call | solution.py:48
  80.4 7.3 %collective-permute-done.15.far = bf16[256,512]{1,0:T(8,128)(2,1)S(1)} collective-permute-done((bf16[256,512]{1,0:T(8,128)(2,1)S(1)}, bf16[256,512]{1,0:T(8,128)(2,1)S(1)}, u32[]{:S(2)}, u32[]{:S(2)}) %collective-permute-start.15) | collective-permute-done | bytes 262176 | tf_op jit(solution)/shard_map/ppermute | solution.py:367
  87.7 1.8 %collective-permute-start.17 = (bf16[1024,512]{1,0:T(8,128)(2,1)S(1)}, bf16[1024,512]{1,0:T(8,128)(2,1)S(1)}, u32[]{:S(2)}, u32[]{:S(2)}) collective-permute-start(bf16[1024,512]{1,0:T(8,128)(2,1)S(1)} %bitcast.6), channel_id=1, source_target_pairs={{0,4},{4,0},{1,5},{5,1},{2,6},{6,2},{3,7},{7,3},{8,12},{12,8},{9,1... | collective-permute-start | bytes 3145736 | tf_op jit(solution)/shard_map/ppermute | solution.py:361
  89.5 1.4 %widen_own.1.refs_0_ = f32[4,512,512]{2,1,0:T(8,128)} custom-call(s32[1]{0:T(128)} %bitcast.core_ref, bf16[1024,512]{1,0:T(8,128)(2,1)S(1)} %bitcast.7), custom_call_target="tpu_custom_call" | custom-call | flops 1048576 | bytes 3145728 | tf_op jit(solution)/shard_map/widen_own/pallas_call | solution.py:48
  90.9 1.8 %grid_far.1 = bf16[2048,512]{1,0:T(8,128)(2,1)} custom-call(s32[1]{0:T(128)} %bitcast.1.sub_ref, s32[1]{0:T(128)} %bitcast.core_ref, bf16[256,512]{1,0:T(8,128)(2,1)S(1)} %collective-permute-done.15.far, bf16[3,64,512]{2,1,0:T(8,128)(2,1)S(1)} %get-tuple-element.105.p0.s0, ...), custom_call_target="tpu_custom_call", output_to_operand_aliasing={{}: (10, {})} | custom-call | flops 536870912 | bytes 3145728 | tf_op jit(solution)/shard_map/grid_far/pallas_call | solution.py:48
  92.8 1.4 %widen_other.1 = f32[4,512,512]{2,1,0:T(8,128)} custom-call(s32[1]{0:T(128)} %bitcast.core_ref, bf16[1024,512]{1,0:T(8,128)(2,1)S(1)} %collective-permute-done.17.half_ref, f32[4,512,512]{2,1,0:T(8,128)} %widen_own.1.refs_0_), custom_call_target="tpu_custom_call", output_to_operand_aliasing={{}: (2, {})} | custom-call | flops 1048576 | bytes 3145728 | tf_op jit(solution)/shard_map/widen_other/pallas_call | solution.py:48
  (37 shorter events, 15.6 us)
Async XLA Ops:
  4.1 4.7 %collective-permute-start = (bf16[256,512]{1,0:T(8,128)(2,1)S(1)}, bf16[256,512]{1,0:T(8,128)(2,1)S(1)}, u32[]{:S(2)}, u32[]{:S(2)}) collective-permute-start(bf16[256,512]{1,0:T(8,128)(2,1)S(1)} %get-tuple-element.61), channel_id=1, source_target_pairs={{0,4},{4,0},{1,5},{5,1},{2,6},{6,2},{3,7},{7,3},{8,12},{12,8},{9,1... | collective-permute-start | bytes 786440 | tf_op jit(solution)/shard_map/ppermute | solution.py:361
  5.6 9.4 %collective-permute-start.1 = (bf16[256,512]{1,0:T(8,128)(2,1)S(1)}, bf16[256,512]{1,0:T(8,128)(2,1)S(1)}, u32[]{:S(2)}, u32[]{:S(2)}) collective-permute-start(bf16[256,512]{1,0:T(8,128)(2,1)S(1)} %get-tuple-element.62), channel_id=1, source_target_pairs={{4,8},{12,16},{20,24},{28,32},{36,40},{44,48},{52,56},{60,64},{68,... | collective-permute-start | bytes 786440 | tf_op jit(solution)/shard_map/ppermute | solution.py:367
  8.8 6.2 %collective-permute-start.2 = (bf16[128,512]{1,0:T(8,128)(2,1)S(1)}, bf16[128,512]{1,0:T(8,128)(2,1)S(1)}, u32[]{:S(2)}, u32[]{:S(2)}) collective-permute-start(bf16[128,512]{1,0:T(8,128)(2,1)S(1)} %get-tuple-element.64), channel_id=1, source_target_pairs={{0,1},{1,2},{2,3},{3,0},{4,5},{5,6},{6,7},{7,4},{8,9},{9,10},{10,1... | collective-permute-start | bytes 393224 | tf_op jit(solution)/shard_map/ppermute | solution.py:361
  10.5 10.3 %collective-permute-start.3 = (bf16[128,512]{1,0:T(8,128)(2,1)S(1)}, bf16[128,512]{1,0:T(8,128)(2,1)S(1)}, u32[]{:S(2)}, u32[]{:S(2)}) collective-permute-start(bf16[128,512]{1,0:T(8,128)(2,1)S(1)} %get-tuple-element.73), channel_id=1, source_target_pairs={{0,2},{1,3},{2,0},{3,1},{4,6},{5,7},{6,4},{7,5},{8,10},{9,11},{10,... | collective-permute-start | bytes 393224 | tf_op jit(solution)/shard_map/ppermute | solution.py:361
  13.8 7.0 %collective-permute-start.4 = (bf16[128,512]{1,0:T(8,128)(2,1)S(1)}, bf16[128,512]{1,0:T(8,128)(2,1)S(1)}, u32[]{:S(2)}, u32[]{:S(2)}) collective-permute-start(bf16[128,512]{1,0:T(8,128)(2,1)S(1)} %get-tuple-element.74), channel_id=1, source_target_pairs={{0,3},{1,0},{2,1},{3,2},{4,7},{5,4},{6,5},{7,6},{8,11},{9,8},{10,9... | collective-permute-start | bytes 393224 | tf_op jit(solution)/shard_map/ppermute | solution.py:361
  15.1 6.5 %collective-permute-start.5 = (bf16[64,512]{1,0:T(8,128)(2,1)S(1)}, bf16[64,512]{1,0:T(8,128)(2,1)S(1)}, u32[]{:S(2)}, u32[]{:S(2)}) collective-permute-start(bf16[64,512]{1,0:T(8,128)(2,1)S(1)} %get-tuple-element.75), channel_id=1, source_target_pairs={{0,1},{1,2},{2,3},{3,0},{4,5},{5,6},{6,7},{7,4},{8,9},{9,10},{10,1... | collective-permute-start | bytes 196616 | tf_op jit(solution)/shard_map/ppermute | solution.py:361
  15.9 6.2 %collective-permute-start.6 = (bf16[64,512]{1,0:T(8,128)(2,1)S(1)}, bf16[64,512]{1,0:T(8,128)(2,1)S(1)}, u32[]{:S(2)}, u32[]{:S(2)}) collective-permute-start(bf16[64,512]{1,0:T(8,128)(2,1)S(1)} %get-tuple-element.76), channel_id=1, source_target_pairs={{0,2},{1,3},{2,0},{3,1},{4,6},{5,7},{6,4},{7,5},{8,10},{9,11},{10,... | collective-permute-start | bytes 196616 | tf_op jit(solution)/shard_map/ppermute | solution.py:361
  19.5 3.1 %collective-permute-start.7 = (bf16[64,512]{1,0:T(8,128)(2,1)S(1)}, bf16[64,512]{1,0:T(8,128)(2,1)S(1)}, u32[]{:S(2)}, u32[]{:S(2)}) collective-permute-start(bf16[64,512]{1,0:T(8,128)(2,1)S(1)} %get-tuple-element.77), channel_id=1, source_target_pairs={{0,3},{1,0},{2,1},{3,2},{4,7},{5,4},{6,5},{7,6},{8,11},{9,8},{10,9... | collective-permute-start | bytes 196616 | tf_op jit(solution)/shard_map/ppermute | solution.py:361
  27.5 2.7 %collective-permute-start.8 = (bf16[1024,512]{1,0:T(8,128)(2,1)S(1)}, bf16[1024,512]{1,0:T(8,128)(2,1)S(1)}, u32[]{:S(2)}, u32[]{:S(2)}) collective-permute-start(bf16[1024,512]{1,0:T(8,128)(2,1)S(1)} %get-tuple-element.87), channel_id=1, source_target_pairs={{0,4},{4,0},{1,5},{5,1},{2,6},{6,2},{3,7},{7,3},{8,12},{12,8},{9,1... | collective-permute-start | bytes 3145736 | tf_op jit(solution)/shard_map/ppermute | solution.py:361
  31.3 24.9 %all-to-all-start = ((bf16[16,64,512]{2,1,0:T(8,128)(2,1)}), bf16[16,64,512]{2,1,0:T(8,128)(2,1)S(1)}, u32[]{:S(2)}, u32[]{:S(2)}) async-start(bf16[16,64,512]{2,1,0:T(8,128)(2,1)} %bitcast.4), calls=%async_computation | async-start | bytes 2097152 | tf_op jit(solution)/shard_map/all_to_all | solution.py:448
  40.4 7.8 %collective-permute-start.10 = (bf16[3,64,512]{2,1,0:T(8,128)(2,1)}, bf16[3,64,512]{2,1,0:T(8,128)(2,1)S(1)}, u32[]{:S(2)}, u32[]{:S(2)}) collective-permute-start(bf16[3,64,512]{2,1,0:T(8,128)(2,1)} %get-tuple-element.94), channel_id=1, source_target_pairs={{0,2},{1,3},{2,0},{3,1},{4,6},{5,7},{6,4},{7,5},{8,10},{9,11},{10,... | collective-permute-start | bytes 589832 | tf_op jit(solution)/shard_map/ppermute | solution.py:361
  41.7 11.5 %collective-permute-start.11 = (bf16[3,64,512]{2,1,0:T(8,128)(2,1)S(1)}, bf16[3,64,512]{2,1,0:T(8,128)(2,1)S(1)}, u32[]{:S(2)}, u32[]{:S(2)}) collective-permute-start(bf16[3,64,512]{2,1,0:T(8,128)(2,1)S(1)} %get-tuple-element.95), channel_id=1, source_target_pairs={{0,1},{1,2},{2,3},{3,0},{4,5},{5,6},{6,7},{7,4},{8,9},{9,10},{10,1... | collective-permute-start | bytes 589832 | tf_op jit(solution)/shard_map/ppermute | solution.py:361
  42.8 10.4 %collective-permute-start.9 = (bf16[3,64,512]{2,1,0:T(8,128)(2,1)S(1)}, bf16[3,64,512]{2,1,0:T(8,128)(2,1)S(1)}, u32[]{:S(2)}, u32[]{:S(2)}) collective-permute-start(bf16[3,64,512]{2,1,0:T(8,128)(2,1)S(1)} %get-tuple-element.93), channel_id=1, source_target_pairs={{0,3},{1,0},{2,1},{3,2},{4,7},{5,4},{6,5},{7,6},{8,11},{9,8},{10,9... | collective-permute-start | bytes 589832 | tf_op jit(solution)/shard_map/ppermute | solution.py:361
  56.4 3.9 %collective-permute-start.14 = (bf16[64,512]{1,0:T(8,128)(2,1)S(1)}, bf16[64,512]{1,0:T(8,128)(2,1)S(1)}, u32[]{:S(2)}, u32[]{:S(2)}) collective-permute-start(bf16[64,512]{1,0:T(8,128)(2,1)S(1)} %plane.1.p0), channel_id=1, source_target_pairs={{0,3},{1,0},{2,1},{3,2},{4,7},{5,4},{6,5},{7,6},{8,11},{9,8},{10,9... | collective-permute-start | bytes 196616 | tf_op jit(solution)/shard_map/ppermute | solution.py:361
  58.4 4.7 %collective-permute-start.13 = (bf16[64,512]{1,0:T(8,128)(2,1)S(1)}, bf16[64,512]{1,0:T(8,128)(2,1)S(1)}, u32[]{:S(2)}, u32[]{:S(2)}) collective-permute-start(bf16[64,512]{1,0:T(8,128)(2,1)S(1)} %plane.1.p0), channel_id=1, source_target_pairs={{0,2},{1,3},{2,0},{3,1},{4,6},{5,7},{6,4},{7,5},{8,10},{9,11},{10,... | collective-permute-start | bytes 196616 | tf_op jit(solution)/shard_map/ppermute | solution.py:361
  58.7 5.0 %collective-permute-start.12 = (bf16[64,512]{1,0:T(8,128)(2,1)S(1)}, bf16[64,512]{1,0:T(8,128)(2,1)S(1)}, u32[]{:S(2)}, u32[]{:S(2)}) collective-permute-start(bf16[64,512]{1,0:T(8,128)(2,1)S(1)} %plane.1.p0), channel_id=1, source_target_pairs={{0,1},{1,2},{2,3},{3,0},{4,5},{5,6},{6,7},{7,4},{8,9},{9,10},{10,1... | collective-permute-start | bytes 196616 | tf_op jit(solution)/shard_map/ppermute | solution.py:361
  64.8 22.8 %all-to-all-start.1 = ((bf16[16,64,512]{2,1,0:T(8,128)(2,1)}), bf16[16,64,512]{2,1,0:T(8,128)(2,1)S(1)}, u32[]{:S(2)}, u32[]{:S(2)}) async-start(bf16[16,64,512]{2,1,0:T(8,128)(2,1)} %spread.1), calls=%async_computation.1 | async-start | bytes 2097152 | tf_op jit(solution)/shard_map/all_to_all | solution.py:469
  69.4 6.9 %collective-permute-start.16 = (bf16[256,512]{1,0:T(8,128)(2,1)S(1)}, bf16[256,512]{1,0:T(8,128)(2,1)S(1)}, u32[]{:S(2)}, u32[]{:S(2)}) collective-permute-start(bf16[256,512]{1,0:T(8,128)(2,1)S(1)} %get-tuple-element.110), channel_id=1, source_target_pairs={{0,4},{4,0},{1,5},{5,1},{2,6},{6,2},{3,7},{7,3},{8,12},{12,8},{9,1... | collective-permute-start | bytes 786440 | tf_op jit(solution)/shard_map/ppermute | solution.py:361
  73.0 14.7 %collective-permute-start.15 = (bf16[256,512]{1,0:T(8,128)(2,1)S(1)}, bf16[256,512]{1,0:T(8,128)(2,1)S(1)}, u32[]{:S(2)}, u32[]{:S(2)}) collective-permute-start(bf16[256,512]{1,0:T(8,128)(2,1)S(1)} %get-tuple-element.109), channel_id=1, source_target_pairs={{4,8},{12,16},{20,24},{28,32},{36,40},{44,48},{52,56},{60,64},{68,... | collective-permute-start | bytes 786440 | tf_op jit(solution)/shard_map/ppermute | solution.py:367
  79.5 1.0 %copy-start = (bf16[1024,512]{1,0:T(8,128)(2,1)}, bf16[1024,512]{1,0:T(8,128)(2,1)S(1)}, u32[]{:S(2)}) copy-start(bf16[1024,512]{1,0:T(8,128)(2,1)S(1)} %get-tuple-element.115.x_ref) | copy-start | bytes 3145732
  87.7 3.2 %copy-start.1 = (bf16[1024,512]{1,0:T(8,128)(2,1)S(1)}, bf16[1024,512]{1,0:T(8,128)(2,1)}, u32[]{:S(2)}) copy-start(bf16[1024,512]{1,0:T(8,128)(2,1)} %copy-done) | copy-start | bytes 3145732
  87.7 5.1 %collective-permute-start.17 = (bf16[1024,512]{1,0:T(8,128)(2,1)S(1)}, bf16[1024,512]{1,0:T(8,128)(2,1)S(1)}, u32[]{:S(2)}, u32[]{:S(2)}) collective-permute-start(bf16[1024,512]{1,0:T(8,128)(2,1)S(1)} %bitcast.6), channel_id=1, source_target_pairs={{0,4},{4,0},{1,5},{5,1},{2,6},{6,2},{3,7},{7,3},{8,12},{12,8},{9,1... | collective-permute-start | bytes 3145736 | tf_op jit(solution)/shard_map/ppermute | solution.py:361

commit v13 on v12

--- a/solution.py
+++ b/solution.py
@@ -85,14 +85,9 @@
         rows[pl.ds(far_at + k * cap, cap), :] = last[last.shape[0] - cap :]
 
 
-def gather_body(sub_ref, core_ref, rows_hbm, gain_hbm, x_hbm, *refs):
-    later = (len(refs) - 8) // 2
-    later_hbm, refs = refs[:later], refs[later:]
-    near_ref, far_ref, own_ref, rows_ref, gain_ref = refs[:5]
-    later_refs = refs[5 : 5 + later]
-    x_ref, sems, later_sems = refs[-3:]
+def gather_body(sub_ref, core_ref, rows_hbm, gain_hbm, x_hbm, near_ref, far_ref, rows_ref, gain_ref,
+                x_ref, sems):
     half = x_ref.shape[0] // 2
-    cap = rows_ref.shape[3]
     core = core_ref[0]
     firsts = [pl.multiple_of((1 - core) * half, half), pl.multiple_of(core * half, half)]
     parts = [pl.ds(first, half) for first in firsts]
@@ -101,34 +96,42 @@
         [rows_ref, gain_ref] + [x_ref.at[p] for p in parts],
         sems,
     )
-    later_copies = fetch(later_hbm, later_refs, later_sems)
     copies[0].wait()
     copies[1].wait()
-    me = sub_ref[0]
+    steps = ((2 - 2 * core, firsts[0], near_ref), (2 * core, firsts[1], far_ref))
+    for step, (o, first, out_ref) in enumerate(steps):
+        onehot = picks(sub_ref, rows_ref, o, first, half)
+        copies[2 + step].wait()
+        out_ref[...] = normed_rows(onehot, x_ref[pl.ds(first, half), :], gain_ref)
+
+
+def own_body(sub_ref, rows_ref, gain_ref, x_ref, *refs):
+    later = (len(refs) - 2) // 2
+    own_ref = refs[later]
+    copies = fetch(refs[:later], refs[later + 1 : -1], refs[-1])
+    onehot = picks(sub_ref, rows_ref, 1, 0, x_ref.shape[0])
+    own_ref[...] = normed_rows(onehot, x_ref[...], gain_ref)
+    for copy in copies:
+        copy.wait()
+
+
+def picks(sub_ref, rows_ref, o, first, count):
+    cap = rows_ref.shape[3]
     eye = lax.broadcasted_iota(jnp.int32, (cap, cap), 0) == lax.broadcasted_iota(
         jnp.int32, (cap, cap), 1
     )
-    gain = gain_ref[...]
-    steps = (
-        (2 - 2 * core, firsts[0], half, near_ref),
-        (2 * core, firsts[1], half, far_ref),
-        (1, 0, 2 * half, own_ref),
-    )
-    for step, (o, first, count, out_ref) in enumerate(steps):
-        cols = []
-        for k in range(4):
-            s = lax.rem(me + k, 4)
-            row = rows_ref[0, o, pl.ds(s, 1), :].astype(F32)
-            cols.append(jnp.sum(jnp.where(eye, row, 0.0), axis=1, keepdims=True))
-        col = jnp.concatenate(cols, axis=0).astype(jnp.int32) - first
-        lanes = lax.broadcasted_iota(jnp.int32, (4 * cap, count), 1)
-        onehot = jnp.where(lanes == col, 1.0, 0.0).astype(BF16)
-        if step < 2:
-            copies[2 + step].wait()
-        wide = nn(onehot, x_ref[pl.ds(first, count), :])
-        out_ref[...] = (wide * inv_rms(wide) * gain).astype(BF16)
-    for copy in later_copies:
-        copy.wait()
+    cols = []
+    for k in range(4):
+        row = rows_ref[0, o, pl.ds(lax.rem(sub_ref[0] + k, 4), 1), :].astype(F32)
+        cols.append(jnp.sum(jnp.where(eye, row, 0.0), axis=1, keepdims=True))
+    col = jnp.concatenate(cols, axis=0).astype(jnp.int32) - first
+    lanes = lax.broadcasted_iota(jnp.int32, (4 * cap, count), 1)
+    return jnp.where(lanes == col, 1.0, 0.0).astype(BF16)
+
+
+def normed_rows(onehot, points, gain_ref):
+    wide = nn(onehot, points)
+    return (wide * inv_rms(wide) * gain_ref[...]).astype(BF16)
 
 
 def mesh_in_body(mesh_ref, gain_ref, wq_ref, wo_ref, og_ref, normed_ref, q_ref, ag_ref):
@@ -186,7 +189,7 @@
         scores = nt(q, kh) + bias_ref[h]
         peak = jnp.max(scores, axis=1, keepdims=True)
         terms = jnp.exp(scores - peak)
-        probs = terms / jnp.sum(terms, axis=1, keepdims=True)
+        probs = terms * (1.0 / jnp.sum(terms, axis=1, keepdims=True))
         probs_b = probs.astype(BF16)
         att_ref[:, at] = nn(probs_b, vh).astype(BF16)
         pg = nt(ag, vh)
@@ -300,16 +303,17 @@
     copies[1].wait()
 
 
-def grid_far_body(sub_ref, core_ref, far, s0, s1, s2, s3, rows_ref, gain_ref, x_ref, prior_hbm,
-                  out_hbm, got, done_ref, done_sems):
+def grid_far_body(sub_ref, core_ref, far, s0, s1, s2, s3, rows_ref, gain_ref, x_ref, mine_ref, prior_hbm,
+                  out_hbm, weights_hbm, got, done_ref, done_sems, wide, wide_sems):
+    copies = widen(core_ref[0], mine_ref, weights_hbm, wide, wide_sems)
     grid_half(core_ref[0], sub_ref, far, s0, s1, s2, s3, rows_ref, gain_ref, x_ref, out_hbm, got,
               done_ref, done_sems, lambda: None)
-
-
-def widen_body(turn, core_ref, half_ref, *refs):
-    out_hbm, wide, sems = refs[-3:]
+    for copy in copies:
+        copy.wait()
+
+
+def widen(half, half_ref, out_hbm, wide, sems):
     count, width, _ = wide.shape
-    half = core_ref[0] ^ turn
     part = width // 4
     copies = []
     for i in range(4 * count):
@@ -321,7 +325,11 @@
             )
         )
         copies[-1].start()
-    for copy in copies:
+    return copies
+
+
+def widen_body(core_ref, half_ref, prior_hbm, out_hbm, wide, sems):
+    for copy in widen(1 - core_ref[0], half_ref, out_hbm, wide, sems):
         copy.wait()
 
 
@@ -391,13 +399,16 @@
 
     one, two, four = sds((cap, width)), sds((2 * cap, width)), sds((block, width))
     later = (mesh_h, gain_m, w_query, w_out, out_grad, neighbours, valid, edge_bias)
-    near, far, own, rows_near, gain_g_near, *later = call(
+    near, far, rows_near, gain_g_near, x_near = call(
         gather_body,
-        [four] * 3 + [sds(a.shape, a.dtype) for a in (send_rows, gain_g, *later)],
-        [SM, SM] + [HB] * (3 + len(later)),
-        (sub1, core1, send_rows, gain_g, grid_x, *later), 1 << 30, 5 << 20, "gather_rows",
-        [pltpu.VMEM((points, width), BF16), pltpu.SemaphoreType.DMA((4,)),
-         pltpu.SemaphoreType.DMA((len(later),))],
+        [four] * 2 + [sds(a.shape, a.dtype) for a in (send_rows, gain_g, grid_x)],
+        [SM, SM] + [HB] * 3, (sub1, core1, send_rows, gain_g, grid_x), 1 << 30, 3 << 20, "gather_rows",
+        [pltpu.SemaphoreType.DMA((4,))],
+    )
+    own, *later = call(
+        own_body, [four] + [sds(a.shape, a.dtype) for a in later], [SM] + [VM] * 3 + [HB] * len(later),
+        (sub1, rows_near, gain_g_near, x_near, *later), 1 << 29, 4 << 20, "own_rows",
+        [pltpu.SemaphoreType.DMA((len(later),))],
     )
     mesh_near, gain_near, wq_near, wo_near, og_near, nbr_near, valid_near, bias_near = later
     far = swapped_far(far)
@@ -480,20 +491,16 @@
     )
     mine, far, grid_grad = lax.optimization_barrier((mine, far, grid_grad))
     theirs = shifted(mine, "gc", 1)
-    (grid_grad,) = call(
-        grid_far_body, [sds((points, width))], [SM] * 2 + [VM] * 8 + [HB],
-        (sub1, core1, far, s0, s1, s2, s3, rows_near, gain_g_near, far_x, grid_grad),
-        1 << 29, 3 << 20, "grid_far", grid_scratch, [HB], {10: 0},
-    )
     whole = sds((4, width, width), F32)
     wide = [pltpu.VMEM((2, width, width), F32), pltpu.SemaphoreType.DMA((8,))]
+    grid_grad, weight_grads = call(
+        grid_far_body, [sds((points, width)), whole], [SM] * 2 + [VM] * 9 + [HB],
+        (sub1, core1, far, s0, s1, s2, s3, rows_near, gain_g_near, far_x, mine, grid_grad),
+        1 << 29, 5 << 20, "grid_far", grid_scratch + wide, [HB, HB], {11: 0},
+    )
     (weight_grads,) = call(
-        functools.partial(widen_body, 0), [whole], [SM, VM], (core1, mine), 1 << 20, 3 << 20, "widen_own",
-        wide, [HB],
-    )
-    (weight_grads,) = call(
-        functools.partial(widen_body, 1), [whole], [SM, VM, HB], (core1, theirs, weight_grads),
-        1 << 20, 3 << 20, "widen_other", wide, [HB], {2: 0},
+        widen_body, [whole], [SM, VM, HB], (core1, theirs, weight_grads), 1 << 20, 3 << 20, "widen", wide,
+        [HB], {2: 0},
     )
     return mesh_out, mesh_grad, grid_grad, weight_grads
 

time: 94.7 us -> 96.9 us (1.023)
  starting transfers between devices: 43.9 us -> 45.8 us
  local copies, waits for them, and re-layouts: 0.97 us -> 2.19 us
  waiting for transfers between devices: 24.6 us -> 23.6 us
    ppermute x16, waiting for transfers between devices: 14.3 us -> 13 us  [shifted(): return lax.ppermute(block, axis, [(i, (i + k) % n) for i in range(n)])]
    unnamed x4, local copies, waits for them, and re-layouts: 0.97 us -> 2.19 us
  transfers between devices with their start and end apart: 20 -> 20, of which waited for: 11 -> 12; matrix products, arithmetic and copies ran while one was open for 0% -> 0% of each run, Pallas kernels for 12% -> 13%
where the time goes in v13:
time: 96.9 us; the launch traced here: 96.5 us
  starting transfers between devices  45.8 us (47%)
  Pallas kernels  23.9 us (25%)
  waiting for transfers between devices  23.6 us (24%)
  local copies, waits for them, and re-layouts  2.19 us (2%)
  between operations  1.01 us (1%)
    ppermute x16, starting transfers between devices, shifted(): return lax.ppermute(block, axis, [(i, (i + k) % n) for i in range(n)])  24.4 us
    pallas_call x17, Pallas kernels, call(): pl.pallas_call(body, out_shape=outs, in_specs=in_specs, out_specs=out_spe...  23.9 us
    ppermute x16, waiting for transfers between devices, shifted(): return lax.ppermute(block, axis, [(i, (i + k) % n) for i in range(n)])  13 us
    all_to_all x1, starting transfers between devices, shards(): lax.all_to_all(own.reshape(plane, share, width), PLANE, 0, 0, tiled=True)  9.82 us
    ppermute x2, waiting for transfers between devices, swapped_far(): return lax.ppermute(block, SLAB, pairs + [(j, i) for i, j in pairs])  7.75 us
    ppermute x2, starting transfers between devices, swapped_far(): return lax.ppermute(block, SLAB, pairs + [(j, i) for i, j in pairs])  6.54 us
    all_to_all x1, starting transfers between devices, shards(): lax.all_to_all(spread, PLANE, 0, 0, tiled=True).reshape(2 * width, width)  5.03 us
    all_to_all x1, waiting for transfers between devices, shards(): lax.all_to_all(own.reshape(plane, share, width), PLANE, 0, 0, tiled=True)  2.93 us
  transfers between devices with their start and end apart: 20, of which 12 were waited for; matrix products, arithmetic and copies ran while one was open for 0% of the time, Pallas kernels for 13%

profile of v13, /device:TPU:1, one launch (start us, length us, event | category | flops | bytes accessed | tf_op | source)
XLA Modules:
  0.0 96.5 jit_solution(5855007171948186229)
XLA Ops:
  0.6 2.4 %gather_rows.1 = (bf16[256,512]{1,0:T(8,128)(2,1)S(1)}, bf16[256,512]{1,0:T(8,128)(2,1)S(1)}, s32[1,3,4,64]{3,2,1,0:T(4,128)S(1)}, f32[1,512]{1,0:T(1,128)S(1)}, bf16[2048,512]{1,0:T(8,128)(2,1)S(1)}) custom-call(s32[1]{0:T(128)} %bitcast.1.sub_ref, s32[1]{0:T(128)} %bitcast.core_ref, s32[1,3,4,64]{3,2,1,0:T(4,128)} %rows_hbm.1, f32[1,512]{1,0:T(1,128)} %bitcast.9, ...), custom_call_target="tpu_custom_call" | custom-call | flops 1073741824 | bytes 3145728 | tf_op jit(solution)/shard_map/gather_rows/pallas_call | solution.py:48
  3.0 1.5 %collective-permute-start = (bf16[256,512]{1,0:T(8,128)(2,1)S(1)}, bf16[256,512]{1,0:T(8,128)(2,1)S(1)}, u32[]{:S(2)}, u32[]{:S(2)}) collective-permute-start(bf16[256,512]{1,0:T(8,128)(2,1)S(1)} %get-tuple-element.64), channel_id=1, source_target_pairs={{0,4},{4,0},{1,5},{5,1},{2,6},{6,2},{3,7},{7,3},{8,12},{12,8},{9,1... | collective-permute-start | bytes 786440 | tf_op jit(solution)/shard_map/ppermute | solution.py:369
  4.5 3.2 %collective-permute-start.1 = (bf16[256,512]{1,0:T(8,128)(2,1)S(1)}, bf16[256,512]{1,0:T(8,128)(2,1)S(1)}, u32[]{:S(2)}, u32[]{:S(2)}) collective-permute-start(bf16[256,512]{1,0:T(8,128)(2,1)S(1)} %get-tuple-element.65), channel_id=1, source_target_pairs={{4,8},{12,16},{20,24},{28,32},{36,40},{44,48},{52,56},{60,64},{68,... | collective-permute-start | bytes 786440 | tf_op jit(solution)/shard_map/ppermute | solution.py:375
  7.7 1.8 %own_rows.1 = (bf16[256,512]{1,0:T(8,128)(2,1)S(1)}, bf16[64,512]{1,0:T(8,128)(2,1)S(1)}, f32[1,512]{1,0:T(1,128)S(1)}, bf16[512,512]{1,0:T(8,128)(2,1)S(1)}, bf...) custom-call(s32[1]{0:T(128)} %bitcast.1.sub_ref, ...), custom_call_target="tpu_custom_call" | custom-call | flops 536870912 | bytes 4194304 | tf_op jit(solution)/shard_map/own_rows/pallas_call | solution.py:48
  9.5 1.7 %collective-permute-start.2 = (bf16[128,512]{1,0:T(8,128)(2,1)S(1)}, bf16[128,512]{1,0:T(8,128)(2,1)S(1)}, u32[]{:S(2)}, u32[]{:S(2)}) collective-permute-start(bf16[128,512]{1,0:T(8,128)(2,1)S(1)} %get-tuple-element.70), channel_id=1, source_target_pairs={{0,1},{1,2},{2,3},{3,0},{4,5},{5,6},{6,7},{7,4},{8,9},{9,10},{10,1... | collective-permute-start | bytes 393224 | tf_op jit(solution)/shard_map/ppermute | solution.py:369
  11.3 3.3 %collective-permute-start.3 = (bf16[128,512]{1,0:T(8,128)(2,1)S(1)}, bf16[128,512]{1,0:T(8,128)(2,1)S(1)}, u32[]{:S(2)}, u32[]{:S(2)}) collective-permute-start(bf16[128,512]{1,0:T(8,128)(2,1)S(1)} %get-tuple-element.79), channel_id=1, source_target_pairs={{0,2},{1,3},{2,0},{3,1},{4,6},{5,7},{6,4},{7,5},{8,10},{9,11},{10,... | collective-permute-start | bytes 393224 | tf_op jit(solution)/shard_map/ppermute | solution.py:369
  15.7 1.7 %collective-permute-done.2.m1 = bf16[128,512]{1,0:T(8,128)(2,1)S(1)} collective-permute-done((bf16[128,512]{1,0:T(8,128)(2,1)S(1)}, bf16[128,512]{1,0:T(8,128)(2,1)S(1)}, u32[]{:S(2)}, u32[]{:S(2)}) %collective-permute-start.2) | collective-permute-done | bytes 131104 | tf_op jit(solution)/shard_map/ppermute | solution.py:369
  17.5 2.1 %collective-permute-start.6 = (bf16[64,512]{1,0:T(8,128)(2,1)S(1)}, bf16[64,512]{1,0:T(8,128)(2,1)S(1)}, u32[]{:S(2)}, u32[]{:S(2)}) collective-permute-start(bf16[64,512]{1,0:T(8,128)(2,1)S(1)} %get-tuple-element.82), channel_id=1, source_target_pairs={{0,2},{1,3},{2,0},{3,1},{4,6},{5,7},{6,4},{7,5},{8,10},{9,11},{10,... | collective-permute-start | bytes 196616 | tf_op jit(solution)/shard_map/ppermute | solution.py:369
  23.1 4.9 %middle.1 = (bf16[1024,512]{1,0:T(8,128)(2,1)S(1)}, bf16[768,1024]{1,0:T(8,128)(2,1)S(1)}, bf16[64,512]{1,0:T(8,128)(2,1)S(1)}, bf16[64,512]{1,0:T(8,128)(2,1)S(1)}, bf16[768,512]{1,0:T(8,128)(2,1)S(1)}) custom-call(s32[1]{0:T(128)} %bitcast.core_ref, bf16[256,512]{1,0:T(8,128)(2,1)S(1)} %collective-permute-done.near, ...), custom_call_target="tpu_custom_call" | custom-call | flops 3221225472 | bytes 8388608 | tf_op jit(solution)/shard_map/middle/pallas_call | solution.py:48
  28.8 1.7 %back.1 = (bf16[3,64,512]{2,1,0:T(8,128)(2,1)S(1)}, bf16[3,64,512]{2,1,0:T(8,128)(2,1)S(1)}, bf16[3,64,512]{2,1,0:T(8,128)(2,1)}, bf16[3,64,512]{2,1,0:T(8,128)(2,1)S(1)}) custom-call(bf16[768,1024]{1,0:T(8,128)(2,1)S(1)} %get-tuple-element.94.part_ref, bf16[512,1024]{1,0:T(8,128)(2,1)S(1)} %get-tuple-element.92.wkv_ref), custom_call_target="tpu_custom_call" | custom-call | flops 1073741824 | bytes 3145728 | tf_op jit(solution)/shard_map/back/pallas_call | solution.py:48
  31.8 9.8 %all-to-all-start = ((bf16[16,64,512]{2,1,0:T(8,128)(2,1)}), bf16[16,64,512]{2,1,0:T(8,128)(2,1)S(1)}, u32[]{:S(2)}, u32[]{:S(2)}) async-start(bf16[16,64,512]{2,1,0:T(8,128)(2,1)} %bitcast.4), calls=%async_computation | async-start | bytes 2097152 | tf_op jit(solution)/shard_map/all_to_all | solution.py:459
  41.6 2.3 %collective-permute-start.10 = (bf16[3,64,512]{2,1,0:T(8,128)(2,1)}, bf16[3,64,512]{2,1,0:T(8,128)(2,1)S(1)}, u32[]{:S(2)}, u32[]{:S(2)}) collective-permute-start(bf16[3,64,512]{2,1,0:T(8,128)(2,1)} %get-tuple-element.100), channel_id=1, source_target_pairs={{0,2},{1,3},{2,0},{3,1},{4,6},{5,7},{6,4},{7,5},{8,10},{9,11},{10,... | collective-permute-start | bytes 589832 | tf_op jit(solution)/shard_map/ppermute | solution.py:369
  44.0 1.6 %collective-permute-start.11 = (bf16[3,64,512]{2,1,0:T(8,128)(2,1)S(1)}, bf16[3,64,512]{2,1,0:T(8,128)(2,1)S(1)}, u32[]{:S(2)}, u32[]{:S(2)}) collective-permute-start(bf16[3,64,512]{2,1,0:T(8,128)(2,1)S(1)} %get-tuple-element.101), channel_id=1, source_target_pairs={{0,1},{1,2},{2,3},{3,0},{4,5},{5,6},{6,7},{7,4},{8,9},{9,10},{10,1... | collective-permute-start | bytes 589832 | tf_op jit(solution)/shard_map/ppermute | solution.py:369
  47.7 1.7 %collective-permute-done.10.p2.s2 = bf16[3,64,512]{2,1,0:T(8,128)(2,1)S(1)} collective-permute-done((bf16[3,64,512]{2,1,0:T(8,128)(2,1)}, bf16[3,64,512]{2,1,0:T(8,128)(2,1)S(1)}, u32[]{:S(2)}, u32[]{:S(2)}) %collective-permute-start.10) | collective-permute-done | bytes 196640 | tf_op jit(solution)/shard_map/ppermute | solution.py:369
  49.4 5.1 %collective-permute-done.11.p3.s3 = bf16[3,64,512]{2,1,0:T(8,128)(2,1)S(1)} collective-permute-done((bf16[3,64,512]{2,1,0:T(8,128)(2,1)S(1)}, bf16[3,64,512]{2,1,0:T(8,128)(2,1)S(1)}, u32[]{:S(2)}, u32[]{:S(2)}) %collective-permute-start.11) | collective-permute-done | bytes 196640 | tf_op jit(solution)/shard_map/ppermute | solution.py:369
  54.5 2.9 %all-to-all-done.parts_ref = bf16[16,64,512]{2,1,0:T(8,128)(2,1)S(1)} async-done(((bf16[16,64,512]{2,1,0:T(8,128)(2,1)}), bf16[16,64,512]{2,1,0:T(8,128)(2,1)S(1)}, u32[]{:S(2)}, u32[]{:S(2)}) %all-to-all-start) | async-done | bytes 1048608 | tf_op jit(solution)/shard_map/all_to_all | solution.py:459
  58.8 3.6 %collective-permute-start.13 = (bf16[64,512]{1,0:T(8,128)(2,1)S(1)}, bf16[64,512]{1,0:T(8,128)(2,1)S(1)}, u32[]{:S(2)}, u32[]{:S(2)}) collective-permute-start(bf16[64,512]{1,0:T(8,128)(2,1)S(1)} %plane.1.p0), channel_id=1, source_target_pairs={{0,2},{1,3},{2,0},{3,1},{4,6},{5,7},{6,4},{7,5},{8,10},{9,11},{10,... | collective-permute-start | bytes 196616 | tf_op jit(solution)/shard_map/ppermute | solution.py:369
  62.8 1.9 %collective-permute-done.13.p2 = bf16[64,512]{1,0:T(8,128)(2,1)S(1)} collective-permute-done((bf16[64,512]{1,0:T(8,128)(2,1)S(1)}, bf16[64,512]{1,0:T(8,128)(2,1)S(1)}, u32[]{:S(2)}, u32[]{:S(2)}) %collective-permute-start.13) | collective-permute-done | bytes 65568 | tf_op jit(solution)/shard_map/ppermute | solution.py:369
  66.9 5.0 %all-to-all-start.1 = ((bf16[16,64,512]{2,1,0:T(8,128)(2,1)}), bf16[16,64,512]{2,1,0:T(8,128)(2,1)S(1)}, u32[]{:S(2)}, u32[]{:S(2)}) async-start(bf16[16,64,512]{2,1,0:T(8,128)(2,1)} %spread.1), calls=%async_computation.1 | async-start | bytes 2097152 | tf_op jit(solution)/shard_map/all_to_all | solution.py:480
  72.0 3.0 %collective-permute-start.16 = (bf16[256,512]{1,0:T(8,128)(2,1)S(1)}, bf16[256,512]{1,0:T(8,128)(2,1)S(1)}, u32[]{:S(2)}, u32[]{:S(2)}) collective-permute-start(bf16[256,512]{1,0:T(8,128)(2,1)S(1)} %get-tuple-element.116), channel_id=1, source_target_pairs={{0,4},{4,0},{1,5},{5,1},{2,6},{6,2},{3,7},{7,3},{8,12},{12,8},{9,1... | collective-permute-start | bytes 786440 | tf_op jit(solution)/shard_map/ppermute | solution.py:369
  75.1 3.4 %collective-permute-start.15 = (bf16[256,512]{1,0:T(8,128)(2,1)S(1)}, bf16[256,512]{1,0:T(8,128)(2,1)S(1)}, u32[]{:S(2)}, u32[]{:S(2)}) collective-permute-start(bf16[256,512]{1,0:T(8,128)(2,1)S(1)} %get-tuple-element.115), channel_id=1, source_target_pairs={{4,8},{12,16},{20,24},{28,32},{36,40},{44,48},{52,56},{60,64},{68,... | collective-permute-start | bytes 786440 | tf_op jit(solution)/shard_map/ppermute | solution.py:375
  78.4 3.1 %grid_near.1 = (bf16[2048,512]{1,0:T(8,128)(2,1)}, bf16[1024,512]{1,0:T(8,128)(2,1)S(1)}) custom-call(s32[1]{0:T(128)} %bitcast.1.sub_ref, s32[1]{0:T(128)} %bitcast.core_ref, bf16[256,512]{1,0:T(8,128)(2,1)S(1)} %collective-permute-done.16.near, bf16[3,64,512]{2,1,0:T(8,128)(2,1)S(1)} %get-tuple-element.111.p0.s0, ...), custom_call_target="tpu_custom_call" | custom-call | flops 536870912 | bytes 3145728 | tf_op jit(solution)/shard_map/grid_near/pallas_call | solution.py:48
  82.5 7.7 %collective-permute-done.15.far = bf16[256,512]{1,0:T(8,128)(2,1)S(1)} collective-permute-done((bf16[256,512]{1,0:T(8,128)(2,1)S(1)}, bf16[256,512]{1,0:T(8,128)(2,1)S(1)}, u32[]{:S(2)}, u32[]{:S(2)}) %collective-permute-start.15) | collective-permute-done | bytes 262176 | tf_op jit(solution)/shard_map/ppermute | solution.py:375
  92.3 2.6 %grid_far.1 = (bf16[2048,512]{1,0:T(8,128)(2,1)}, f32[4,512,512]{2,1,0:T(8,128)}) custom-call(s32[1]{0:T(128)} %bitcast.1.sub_ref, s32[1]{0:T(128)} %bitcast.core_ref, bf16[256,512]{1,0:T(8,128)(2,1)S(1)} %collective-permute-done.15.far, bf16[3,64,512]{2,1,0:T(8,128)(2,1)S(1)} %get-tuple-element.111.p0.s0, ...), custom_call_target="tpu_custom_call", output_to_operand_aliasing={{0}: (11, {})} | custom-call | flops 536870912 | bytes 5242880 | tf_op jit(solution)/shard_map/grid_far/pallas_call | solution.py:48
  (37 shorter events, 17.5 us)
Async XLA Ops:
  3.0 6.5 %collective-permute-start = (bf16[256,512]{1,0:T(8,128)(2,1)S(1)}, bf16[256,512]{1,0:T(8,128)(2,1)S(1)}, u32[]{:S(2)}, u32[]{:S(2)}) collective-permute-start(bf16[256,512]{1,0:T(8,128)(2,1)S(1)} %get-tuple-element.64), channel_id=1, source_target_pairs={{0,4},{4,0},{1,5},{5,1},{2,6},{6,2},{3,7},{7,3},{8,12},{12,8},{9,1... | collective-permute-start | bytes 786440 | tf_op jit(solution)/shard_map/ppermute | solution.py:369
  4.5 11.2 %collective-permute-start.1 = (bf16[256,512]{1,0:T(8,128)(2,1)S(1)}, bf16[256,512]{1,0:T(8,128)(2,1)S(1)}, u32[]{:S(2)}, u32[]{:S(2)}) collective-permute-start(bf16[256,512]{1,0:T(8,128)(2,1)S(1)} %get-tuple-element.65), channel_id=1, source_target_pairs={{4,8},{12,16},{20,24},{28,32},{36,40},{44,48},{52,56},{60,64},{68,... | collective-permute-start | bytes 786440 | tf_op jit(solution)/shard_map/ppermute | solution.py:375
  9.5 7.9 %collective-permute-start.2 = (bf16[128,512]{1,0:T(8,128)(2,1)S(1)}, bf16[128,512]{1,0:T(8,128)(2,1)S(1)}, u32[]{:S(2)}, u32[]{:S(2)}) collective-permute-start(bf16[128,512]{1,0:T(8,128)(2,1)S(1)} %get-tuple-element.70), channel_id=1, source_target_pairs={{0,1},{1,2},{2,3},{3,0},{4,5},{5,6},{6,7},{7,4},{8,9},{9,10},{10,1... | collective-permute-start | bytes 393224 | tf_op jit(solution)/shard_map/ppermute | solution.py:369
  11.3 11.0 %collective-permute-start.3 = (bf16[128,512]{1,0:T(8,128)(2,1)S(1)}, bf16[128,512]{1,0:T(8,128)(2,1)S(1)}, u32[]{:S(2)}, u32[]{:S(2)}) collective-permute-start(bf16[128,512]{1,0:T(8,128)(2,1)S(1)} %get-tuple-element.79), channel_id=1, source_target_pairs={{0,2},{1,3},{2,0},{3,1},{4,6},{5,7},{6,4},{7,5},{8,10},{9,11},{10,... | collective-permute-start | bytes 393224 | tf_op jit(solution)/shard_map/ppermute | solution.py:369
  14.6 7.7 %collective-permute-start.4 = (bf16[128,512]{1,0:T(8,128)(2,1)S(1)}, bf16[128,512]{1,0:T(8,128)(2,1)S(1)}, u32[]{:S(2)}, u32[]{:S(2)}) collective-permute-start(bf16[128,512]{1,0:T(8,128)(2,1)S(1)} %get-tuple-element.80), channel_id=1, source_target_pairs={{0,3},{1,0},{2,1},{3,2},{4,7},{5,4},{6,5},{7,6},{8,11},{9,8},{10,9... | collective-permute-start | bytes 393224 | tf_op jit(solution)/shard_map/ppermute | solution.py:369
  17.4 5.1 %collective-permute-start.5 = (bf16[64,512]{1,0:T(8,128)(2,1)S(1)}, bf16[64,512]{1,0:T(8,128)(2,1)S(1)}, u32[]{:S(2)}, u32[]{:S(2)}) collective-permute-start(bf16[64,512]{1,0:T(8,128)(2,1)S(1)} %get-tuple-element.81), channel_id=1, source_target_pairs={{0,1},{1,2},{2,3},{3,0},{4,5},{5,6},{6,7},{7,4},{8,9},{9,10},{10,1... | collective-permute-start | bytes 196616 | tf_op jit(solution)/shard_map/ppermute | solution.py:369
  17.5 5.0 %collective-permute-start.6 = (bf16[64,512]{1,0:T(8,128)(2,1)S(1)}, bf16[64,512]{1,0:T(8,128)(2,1)S(1)}, u32[]{:S(2)}, u32[]{:S(2)}) collective-permute-start(bf16[64,512]{1,0:T(8,128)(2,1)S(1)} %get-tuple-element.82), channel_id=1, source_target_pairs={{0,2},{1,3},{2,0},{3,1},{4,6},{5,7},{6,4},{7,5},{8,10},{9,11},{10,... | collective-permute-start | bytes 196616 | tf_op jit(solution)/shard_map/ppermute | solution.py:369
  19.6 3.5 %collective-permute-start.7 = (bf16[64,512]{1,0:T(8,128)(2,1)S(1)}, bf16[64,512]{1,0:T(8,128)(2,1)S(1)}, u32[]{:S(2)}, u32[]{:S(2)}) collective-permute-start(bf16[64,512]{1,0:T(8,128)(2,1)S(1)} %get-tuple-element.83), channel_id=1, source_target_pairs={{0,3},{1,0},{2,1},{3,2},{4,7},{5,4},{6,5},{7,6},{8,11},{9,8},{10,9... | collective-permute-start | bytes 196616 | tf_op jit(solution)/shard_map/ppermute | solution.py:369
  28.0 2.7 %collective-permute-start.8 = (bf16[1024,512]{1,0:T(8,128)(2,1)S(1)}, bf16[1024,512]{1,0:T(8,128)(2,1)S(1)}, u32[]{:S(2)}, u32[]{:S(2)}) collective-permute-start(bf16[1024,512]{1,0:T(8,128)(2,1)S(1)} %get-tuple-element.93), channel_id=1, source_target_pairs={{0,4},{4,0},{1,5},{5,1},{2,6},{6,2},{3,7},{7,3},{8,12},{12,8},{9,1... | collective-permute-start | bytes 3145736 | tf_op jit(solution)/shard_map/ppermute | solution.py:369
  31.8 25.7 %all-to-all-start = ((bf16[16,64,512]{2,1,0:T(8,128)(2,1)}), bf16[16,64,512]{2,1,0:T(8,128)(2,1)S(1)}, u32[]{:S(2)}, u32[]{:S(2)}) async-start(bf16[16,64,512]{2,1,0:T(8,128)(2,1)} %bitcast.4), calls=%async_computation | async-start | bytes 2097152 | tf_op jit(solution)/shard_map/all_to_all | solution.py:459
  41.6 7.7 %collective-permute-start.10 = (bf16[3,64,512]{2,1,0:T(8,128)(2,1)}, bf16[3,64,512]{2,1,0:T(8,128)(2,1)S(1)}, u32[]{:S(2)}, u32[]{:S(2)}) collective-permute-start(bf16[3,64,512]{2,1,0:T(8,128)(2,1)} %get-tuple-element.100), channel_id=1, source_target_pairs={{0,2},{1,3},{2,0},{3,1},{4,6},{5,7},{6,4},{7,5},{8,10},{9,11},{10,... | collective-permute-start | bytes 589832 | tf_op jit(solution)/shard_map/ppermute | solution.py:369
  44.0 10.5 %collective-permute-start.11 = (bf16[3,64,512]{2,1,0:T(8,128)(2,1)S(1)}, bf16[3,64,512]{2,1,0:T(8,128)(2,1)S(1)}, u32[]{:S(2)}, u32[]{:S(2)}) collective-permute-start(bf16[3,64,512]{2,1,0:T(8,128)(2,1)S(1)} %get-tuple-element.101), channel_id=1, source_target_pairs={{0,1},{1,2},{2,3},{3,0},{4,5},{5,6},{6,7},{7,4},{8,9},{9,10},{10,1... | collective-permute-start | bytes 589832 | tf_op jit(solution)/shard_map/ppermute | solution.py:369
  45.6 8.9 %collective-permute-start.9 = (bf16[3,64,512]{2,1,0:T(8,128)(2,1)S(1)}, bf16[3,64,512]{2,1,0:T(8,128)(2,1)S(1)}, u32[]{:S(2)}, u32[]{:S(2)}) collective-permute-start(bf16[3,64,512]{2,1,0:T(8,128)(2,1)S(1)} %get-tuple-element.99), channel_id=1, source_target_pairs={{0,3},{1,0},{2,1},{3,2},{4,7},{5,4},{6,5},{7,6},{8,11},{9,8},{10,9... | collective-permute-start | bytes 589832 | tf_op jit(solution)/shard_map/ppermute | solution.py:369
  57.6 5.2 %collective-permute-start.12 = (bf16[64,512]{1,0:T(8,128)(2,1)S(1)}, bf16[64,512]{1,0:T(8,128)(2,1)S(1)}, u32[]{:S(2)}, u32[]{:S(2)}) collective-permute-start(bf16[64,512]{1,0:T(8,128)(2,1)S(1)} %plane.1.p0), channel_id=1, source_target_pairs={{0,1},{1,2},{2,3},{3,0},{4,5},{5,6},{6,7},{7,4},{8,9},{9,10},{10,1... | collective-permute-start | bytes 196616 | tf_op jit(solution)/shard_map/ppermute | solution.py:369
  58.8 5.9 %collective-permute-start.13 = (bf16[64,512]{1,0:T(8,128)(2,1)S(1)}, bf16[64,512]{1,0:T(8,128)(2,1)S(1)}, u32[]{:S(2)}, u32[]{:S(2)}) collective-permute-start(bf16[64,512]{1,0:T(8,128)(2,1)S(1)} %plane.1.p0), channel_id=1, source_target_pairs={{0,2},{1,3},{2,0},{3,1},{4,6},{5,7},{6,4},{7,5},{8,10},{9,11},{10,... | collective-permute-start | bytes 196616 | tf_op jit(solution)/shard_map/ppermute | solution.py:369
  62.3 3.4 %collective-permute-start.14 = (bf16[64,512]{1,0:T(8,128)(2,1)S(1)}, bf16[64,512]{1,0:T(8,128)(2,1)S(1)}, u32[]{:S(2)}, u32[]{:S(2)}) collective-permute-start(bf16[64,512]{1,0:T(8,128)(2,1)S(1)} %plane.1.p0), channel_id=1, source_target_pairs={{0,3},{1,0},{2,1},{3,2},{4,7},{5,4},{6,5},{7,6},{8,11},{9,8},{10,9... | collective-permute-start | bytes 196616 | tf_op jit(solution)/shard_map/ppermute | solution.py:369
  66.9 23.3 %all-to-all-start.1 = ((bf16[16,64,512]{2,1,0:T(8,128)(2,1)}), bf16[16,64,512]{2,1,0:T(8,128)(2,1)S(1)}, u32[]{:S(2)}, u32[]{:S(2)}) async-start(bf16[16,64,512]{2,1,0:T(8,128)(2,1)} %spread.1), calls=%async_computation.1 | async-start | bytes 2097152 | tf_op jit(solution)/shard_map/all_to_all | solution.py:480
  72.0 6.4 %collective-permute-start.16 = (bf16[256,512]{1,0:T(8,128)(2,1)S(1)}, bf16[256,512]{1,0:T(8,128)(2,1)S(1)}, u32[]{:S(2)}, u32[]{:S(2)}) collective-permute-start(bf16[256,512]{1,0:T(8,128)(2,1)S(1)} %get-tuple-element.116), channel_id=1, source_target_pairs={{0,4},{4,0},{1,5},{5,1},{2,6},{6,2},{3,7},{7,3},{8,12},{12,8},{9,1... | collective-permute-start | bytes 786440 | tf_op jit(solution)/shard_map/ppermute | solution.py:369
  75.1 15.2 %collective-permute-start.15 = (bf16[256,512]{1,0:T(8,128)(2,1)S(1)}, bf16[256,512]{1,0:T(8,128)(2,1)S(1)}, u32[]{:S(2)}, u32[]{:S(2)}) collective-permute-start(bf16[256,512]{1,0:T(8,128)(2,1)S(1)} %get-tuple-element.115), channel_id=1, source_target_pairs={{4,8},{12,16},{20,24},{28,32},{36,40},{44,48},{52,56},{60,64},{68,... | collective-permute-start | bytes 786440 | tf_op jit(solution)/shard_map/ppermute | solution.py:375
  81.5 1.0 %copy-start = (bf16[1024,512]{1,0:T(8,128)(2,1)}, bf16[1024,512]{1,0:T(8,128)(2,1)S(1)}, u32[]{:S(2)}) copy-start(bf16[1024,512]{1,0:T(8,128)(2,1)S(1)} %get-tuple-element.119.x_ref) | copy-start | bytes 3145732
  90.2 4.7 %collective-permute-start.17 = (bf16[1024,512]{1,0:T(8,128)(2,1)S(1)}, bf16[1024,512]{1,0:T(8,128)(2,1)S(1)}, u32[]{:S(2)}, u32[]{:S(2)}) collective-permute-start(bf16[1024,512]{1,0:T(8,128)(2,1)S(1)} %bitcast.6), channel_id=1, source_target_pairs={{0,4},{4,0},{1,5},{5,1},{2,6},{6,2},{3,7},{7,3},{8,12},{12,8},{9,1... | collective-permute-start | bytes 3145736 | tf_op jit(solution)/shard_map/ppermute | solution.py:369
  91.1 1.2 %copy-start.1 = (bf16[1024,512]{1,0:T(8,128)(2,1)S(1)}, bf16[1024,512]{1,0:T(8,128)(2,1)}, u32[]{:S(2)}) copy-start(bf16[1024,512]{1,0:T(8,128)(2,1)} %copy-done) | copy-start | bytes 3145732

commit v14 on v12

--- a/solution.py
+++ b/solution.py
@@ -101,7 +101,6 @@
         [rows_ref, gain_ref] + [x_ref.at[p] for p in parts],
         sems,
     )
-    later_copies = fetch(later_hbm, later_refs, later_sems)
     copies[0].wait()
     copies[1].wait()
     me = sub_ref[0]
@@ -125,6 +124,8 @@
         onehot = jnp.where(lanes == col, 1.0, 0.0).astype(BF16)
         if step < 2:
             copies[2 + step].wait()
+        if step == 1:
+            later_copies = fetch(later_hbm, later_refs, later_sems)
         wide = nn(onehot, x_ref[pl.ds(first, count), :])
         out_ref[...] = (wide * inv_rms(wide) * gain).astype(BF16)
     for copy in later_copies:
@@ -186,7 +187,7 @@
         scores = nt(q, kh) + bias_ref[h]
         peak = jnp.max(scores, axis=1, keepdims=True)
         terms = jnp.exp(scores - peak)
-        probs = terms / jnp.sum(terms, axis=1, keepdims=True)
+        probs = terms * (1.0 / jnp.sum(terms, axis=1, keepdims=True))
         probs_b = probs.astype(BF16)
         att_ref[:, at] = nn(probs_b, vh).astype(BF16)
         pg = nt(ag, vh)
@@ -286,30 +287,29 @@
         store.wait()
 
 
-def grid_near_body(sub_ref, core_ref, near, s0, s1, s2, s3, rows_ref, gain_ref, x_hbm,
-                   out_hbm, far_x_ref, got, done_ref, done_sems, x_ref, sems):
+def grid_near_body(sub_ref, core_ref, near, s0, s1, s2, s3, rows_ref, gain_ref, x_hbm, out_hbm,
+                   got, done_ref, done_sems, x_ref, sems):
     half = x_ref.shape[0]
     upper = 1 - core_ref[0]
-    copies = fetch(
-        [x_hbm.at[pl.ds(pl.multiple_of(u * half, half), half)] for u in (upper, core_ref[0])],
-        [x_ref, far_x_ref],
-        sems,
-    )
+    (copy,) = fetch([x_hbm.at[pl.ds(pl.multiple_of(upper * half, half), half)]], [x_ref], sems)
     grid_half(upper, sub_ref, near, s0, s1, s2, s3, rows_ref, gain_ref, x_ref, out_hbm, got, done_ref,
-              done_sems, copies[0].wait)
-    copies[1].wait()
-
-
-def grid_far_body(sub_ref, core_ref, far, s0, s1, s2, s3, rows_ref, gain_ref, x_ref, prior_hbm,
-                  out_hbm, got, done_ref, done_sems):
-    grid_half(core_ref[0], sub_ref, far, s0, s1, s2, s3, rows_ref, gain_ref, x_ref, out_hbm, got,
-              done_ref, done_sems, lambda: None)
-
-
-def widen_body(turn, core_ref, half_ref, *refs):
-    out_hbm, wide, sems = refs[-3:]
+              done_sems, copy.wait)
+
+
+def grid_far_body(sub_ref, core_ref, far, s0, s1, s2, s3, rows_ref, gain_ref, mine_ref, x_hbm, prior_hbm,
+                  out_hbm, weights_hbm, got, done_ref, done_sems, x_ref, sems, wide, wide_sems):
+    half = x_ref.shape[0]
+    upper = core_ref[0]
+    (copy,) = fetch([x_hbm.at[pl.ds(pl.multiple_of(upper * half, half), half)]], [x_ref], sems)
+    copies = widen(upper, mine_ref, weights_hbm, wide, wide_sems)
+    grid_half(upper, sub_ref, far, s0, s1, s2, s3, rows_ref, gain_ref, x_ref, out_hbm, got, done_ref,
+              done_sems, copy.wait)
+    for copy in copies:
+        copy.wait()
+
+
+def widen(half, half_ref, out_hbm, wide, sems):
     count, width, _ = wide.shape
-    half = core_ref[0] ^ turn
     part = width // 4
     copies = []
     for i in range(4 * count):
@@ -321,7 +321,11 @@
             )
         )
         copies[-1].start()
-    for copy in copies:
+    return copies
+
+
+def widen_body(core_ref, half_ref, prior_hbm, out_hbm, wide, sems):
+    for copy in widen(1 - core_ref[0], half_ref, out_hbm, wide, sems):
         copy.wait()
 
 
@@ -470,30 +474,26 @@
     half = points // 2
     grid_scratch = [
         pltpu.VMEM((2 * block, width), BF16), pltpu.VMEM((half, width), BF16),
-        pltpu.SemaphoreType.DMA((half // 256,)),
+        pltpu.SemaphoreType.DMA((half // 256,)), pltpu.VMEM((half, width), BF16),
+        pltpu.SemaphoreType.DMA((1,)),
     ]
-    grid_grad, far_x = call(
-        grid_near_body, [sds((points, width)), sds((half, width))], [SM] * 2 + [VM] * 7 + [HB],
+    (grid_grad,) = call(
+        grid_near_body, [sds((points, width))], [SM] * 2 + [VM] * 7 + [HB],
         (sub1, core1, near, s0, s1, s2, s3, rows_near, gain_g_near, grid_x),
-        1 << 29, 3 << 20, "grid_near",
-        grid_scratch + [pltpu.VMEM((half, width), BF16), pltpu.SemaphoreType.DMA((2,))], [HB, VM],
+        1 << 29, 3 << 20, "grid_near", grid_scratch, [HB],
     )
     mine, far, grid_grad = lax.optimization_barrier((mine, far, grid_grad))
     theirs = shifted(mine, "gc", 1)
-    (grid_grad,) = call(
-        grid_far_body, [sds((points, width))], [SM] * 2 + [VM] * 8 + [HB],
-        (sub1, core1, far, s0, s1, s2, s3, rows_near, gain_g_near, far_x, grid_grad),
-        1 << 29, 3 << 20, "grid_far", grid_scratch, [HB], {10: 0},
-    )
     whole = sds((4, width, width), F32)
     wide = [pltpu.VMEM((2, width, width), F32), pltpu.SemaphoreType.DMA((8,))]
+    grid_grad, weight_grads = call(
+        grid_far_body, [sds((points, width)), whole], [SM] * 2 + [VM] * 8 + [HB] * 2,
+        (sub1, core1, far, s0, s1, s2, s3, rows_near, gain_g_near, mine, grid_x, grid_grad),
+        1 << 29, 5 << 20, "grid_far", grid_scratch + wide, [HB, HB], {11: 0},
+    )
     (weight_grads,) = call(
-        functools.partial(widen_body, 0), [whole], [SM, VM], (core1, mine), 1 << 20, 3 << 20, "widen_own",
-        wide, [HB],
-    )
-    (weight_grads,) = call(
-        functools.partial(widen_body, 1), [whole], [SM, VM, HB], (core1, theirs, weight_grads),
-        1 << 20, 3 << 20, "widen_other", wide, [HB], {2: 0},
+        widen_body, [whole], [SM, VM, HB], (core1, theirs, weight_grads), 1 << 20, 3 << 20, "widen", wide,
+        [HB], {2: 0},
     )
     return mesh_out, mesh_grad, grid_grad, weight_grads
 

time: 94.7 us -> 94 us (level)
  starting transfers between devices: 43.9 us -> 45 us
  local copies, waits for them, and re-layouts: 0.97 us -> 0 us
    ppermute x16, waiting for transfers between devices: 14.3 us -> 12.5 us  [shifted(): return lax.ppermute(block, axis, [(i, (i + k) % n) for i in range(n)])]
    ppermute x2, waiting for transfers between devices: 7.26 us -> 8.26 us  [swapped_far(): return lax.ppermute(block, SLAB, pairs + [(j, i) for i, j in pairs])]
    unnamed x4 -> x0, local copies, waits for them, and re-layouts: 0.97 us -> none
    pallas_call x17 -> x16, Pallas kernels: 23.8 us -> 23.8 us  [call(): pl.pallas_call(body, out_shape=outs, in_specs=in_specs, out_specs=out_spe...]
where the time goes in v14:
time: 94 us; the launch traced here: 93.6 us
  starting transfers between devices  45 us (48%)
  Pallas kernels  23.8 us (25%)
  waiting for transfers between devices  23.7 us (25%)
  between operations  1 us (1%)
    ppermute x16, starting transfers between devices, shifted(): return lax.ppermute(block, axis, [(i, (i + k) % n) for i in range(n)])  24.6 us
    pallas_call x16, Pallas kernels, call(): pl.pallas_call(body, out_shape=outs, in_specs=in_specs, out_specs=out_spe...  23.8 us
    ppermute x16, waiting for transfers between devices, shifted(): return lax.ppermute(block, axis, [(i, (i + k) % n) for i in range(n)])  12.5 us
    all_to_all x1, starting transfers between devices, shards(): lax.all_to_all(own.reshape(plane, share, width), PLANE, 0, 0, tiled=True)  9.05 us
    ppermute x2, waiting for transfers between devices, swapped_far(): return lax.ppermute(block, SLAB, pairs + [(j, i) for i, j in pairs])  8.26 us
    ppermute x2, starting transfers between devices, swapped_far(): return lax.ppermute(block, SLAB, pairs + [(j, i) for i, j in pairs])  6.53 us
    all_to_all x1, starting transfers between devices, shards(): lax.all_to_all(spread, PLANE, 0, 0, tiled=True).reshape(2 * width, width)  4.81 us
    all_to_all x1, waiting for transfers between devices, shards(): lax.all_to_all(own.reshape(plane, share, width), PLANE, 0, 0, tiled=True)  2.99 us
  transfers between devices with their start and end apart: 20, of which 11 were waited for; matrix products, arithmetic and copies ran while one was open for 0% of the time, Pallas kernels for 12%

profile of v14, /device:TPU:1, one launch (start us, length us, event | category | flops | bytes accessed | tf_op | source)
XLA Modules:
  0.0 93.6 jit_solution(4699193512260270653)
XLA Ops:
  0.6 3.5 %gather_rows.1 = (bf16[256,512]{1,0:T(8,128)(2,1)S(1)}, bf16[256,512]{1,0:T(8,128)(2,1)S(1)}, bf16[256,512]{1,0:T(8,128)(2,1)S(1)}, s32[1,3,4,64]{3,2,1,0:T(4,12...) custom-call(s32[1]{0:T(128)} %bitcast.1.sub_ref, ...), custom_call_target="tpu_custom_call" | custom-call | flops 1073741824 | bytes 5242880 | tf_op jit(solution)/shard_map/gather_rows/pallas_call | solution.py:48
  4.2 1.5 %collective-permute-start = (bf16[256,512]{1,0:T(8,128)(2,1)S(1)}, bf16[256,512]{1,0:T(8,128)(2,1)S(1)}, u32[]{:S(2)}, u32[]{:S(2)}) collective-permute-start(bf16[256,512]{1,0:T(8,128)(2,1)S(1)} %get-tuple-element.61), channel_id=1, source_target_pairs={{0,4},{4,0},{1,5},{5,1},{2,6},{6,2},{3,7},{7,3},{8,12},{12,8},{9,1... | collective-permute-start | bytes 786440 | tf_op jit(solution)/shard_map/ppermute | solution.py:365
  5.7 3.2 %collective-permute-start.1 = (bf16[256,512]{1,0:T(8,128)(2,1)S(1)}, bf16[256,512]{1,0:T(8,128)(2,1)S(1)}, u32[]{:S(2)}, u32[]{:S(2)}) collective-permute-start(bf16[256,512]{1,0:T(8,128)(2,1)S(1)} %get-tuple-element.62), channel_id=1, source_target_pairs={{4,8},{12,16},{20,24},{28,32},{36,40},{44,48},{52,56},{60,64},{68,... | collective-permute-start | bytes 786440 | tf_op jit(solution)/shard_map/ppermute | solution.py:371
  8.9 1.7 %collective-permute-start.2 = (bf16[128,512]{1,0:T(8,128)(2,1)S(1)}, bf16[128,512]{1,0:T(8,128)(2,1)S(1)}, u32[]{:S(2)}, u32[]{:S(2)}) collective-permute-start(bf16[128,512]{1,0:T(8,128)(2,1)S(1)} %get-tuple-element.64), channel_id=1, source_target_pairs={{0,1},{1,2},{2,3},{3,0},{4,5},{5,6},{6,7},{7,4},{8,9},{9,10},{10,1... | collective-permute-start | bytes 393224 | tf_op jit(solution)/shard_map/ppermute | solution.py:365
  10.6 3.3 %collective-permute-start.3 = (bf16[128,512]{1,0:T(8,128)(2,1)S(1)}, bf16[128,512]{1,0:T(8,128)(2,1)S(1)}, u32[]{:S(2)}, u32[]{:S(2)}) collective-permute-start(bf16[128,512]{1,0:T(8,128)(2,1)S(1)} %get-tuple-element.73), channel_id=1, source_target_pairs={{0,2},{1,3},{2,0},{3,1},{4,6},{5,7},{6,4},{7,5},{8,10},{9,11},{10,... | collective-permute-start | bytes 393224 | tf_op jit(solution)/shard_map/ppermute | solution.py:365
  15.9 3.6 %collective-permute-start.6 = (bf16[64,512]{1,0:T(8,128)(2,1)S(1)}, bf16[64,512]{1,0:T(8,128)(2,1)S(1)}, u32[]{:S(2)}, u32[]{:S(2)}) collective-permute-start(bf16[64,512]{1,0:T(8,128)(2,1)S(1)} %get-tuple-element.76), channel_id=1, source_target_pairs={{0,2},{1,3},{2,0},{3,1},{4,6},{5,7},{6,4},{7,5},{8,10},{9,11},{10,... | collective-permute-start | bytes 196616 | tf_op jit(solution)/shard_map/ppermute | solution.py:365
  19.5 1.4 %slots.1 = (f32[4,64,768]{2,1,0:T(8,128)S(1)}, bf16[512,1024]{1,0:T(8,128)(2,1)S(1)}) custom-call(s32[1]{0:T(128)} %bitcast.1.sub_ref, s32[64,96]{1,0:T(8,128)S(1)} %get-tuple-element.82.nbr_ref, s32[64,96]{1,0:T(8,128)S(1)} %get-tuple-element.83.valid_ref, f32[64,384]{1,0:T(8,128)S(1)} %get-tuple-element.84.bias_ref, bf16[512,512]{1,0:T(8,128)(2,1)} %wk_hbm.1, ...), custom_call_target="tpu_custom_call" | custom-call | flops 1073741824 | bytes 8388608 | tf_op jit(solution)/shard_map/slots/pallas_call | solution.py:48
  22.6 4.9 %middle.1 = (bf16[1024,512]{1,0:T(8,128)(2,1)S(1)}, bf16[768,1024]{1,0:T(8,128)(2,1)S(1)}, bf16[64,512]{1,0:T(8,128)(2,1)S(1)}, bf16[64,512]{1,0:T(8,128)(2,1)S(1)}, bf16[768,512]{1,0:T(8,128)(2,1)S(1)}) custom-call(s32[1]{0:T(128)} %bitcast.core_ref, bf16[256,512]{1,0:T(8,128)(2,1)S(1)} %collective-permute-done.near, ...), custom_call_target="tpu_custom_call" | custom-call | flops 3221225472 | bytes 8388608 | tf_op jit(solution)/shard_map/middle/pallas_call | solution.py:48
  28.4 1.7 %back.1 = (bf16[3,64,512]{2,1,0:T(8,128)(2,1)S(1)}, bf16[3,64,512]{2,1,0:T(8,128)(2,1)S(1)}, bf16[3,64,512]{2,1,0:T(8,128)(2,1)}, bf16[3,64,512]{2,1,0:T(8,128)(2,1)S(1)}) custom-call(bf16[768,1024]{1,0:T(8,128)(2,1)S(1)} %get-tuple-element.88.part_ref, bf16[512,1024]{1,0:T(8,128)(2,1)S(1)} %get-tuple-element.86.wkv_ref), custom_call_target="tpu_custom_call" | custom-call | flops 1073741824 | bytes 3145728 | tf_op jit(solution)/shard_map/back/pallas_call | solution.py:48
  31.4 9.1 %all-to-all-start = ((bf16[16,64,512]{2,1,0:T(8,128)(2,1)}), bf16[16,64,512]{2,1,0:T(8,128)(2,1)S(1)}, u32[]{:S(2)}, u32[]{:S(2)}) async-start(bf16[16,64,512]{2,1,0:T(8,128)(2,1)} %bitcast.4), calls=%async_computation | async-start | bytes 2097152 | tf_op jit(solution)/shard_map/all_to_all | solution.py:452
  40.5 1.3 %collective-permute-start.10 = (bf16[3,64,512]{2,1,0:T(8,128)(2,1)}, bf16[3,64,512]{2,1,0:T(8,128)(2,1)S(1)}, u32[]{:S(2)}, u32[]{:S(2)}) collective-permute-start(bf16[3,64,512]{2,1,0:T(8,128)(2,1)} %get-tuple-element.94), channel_id=1, source_target_pairs={{0,2},{1,3},{2,0},{3,1},{4,6},{5,7},{6,4},{7,5},{8,10},{9,11},{10,... | collective-permute-start | bytes 589832 | tf_op jit(solution)/shard_map/ppermute | solution.py:365
  42.9 1.6 %collective-permute-start.9 = (bf16[3,64,512]{2,1,0:T(8,128)(2,1)S(1)}, bf16[3,64,512]{2,1,0:T(8,128)(2,1)S(1)}, u32[]{:S(2)}, u32[]{:S(2)}) collective-permute-start(bf16[3,64,512]{2,1,0:T(8,128)(2,1)S(1)} %get-tuple-element.93), channel_id=1, source_target_pairs={{0,3},{1,0},{2,1},{3,2},{4,7},{5,4},{6,5},{7,6},{8,11},{9,8},{10,9... | collective-permute-start | bytes 589832 | tf_op jit(solution)/shard_map/ppermute | solution.py:365
  45.5 2.7 %collective-permute-done.10.p2.s2 = bf16[3,64,512]{2,1,0:T(8,128)(2,1)S(1)} collective-permute-done((bf16[3,64,512]{2,1,0:T(8,128)(2,1)}, bf16[3,64,512]{2,1,0:T(8,128)(2,1)S(1)}, u32[]{:S(2)}, u32[]{:S(2)}) %collective-permute-start.10) | collective-permute-done | bytes 196640 | tf_op jit(solution)/shard_map/ppermute | solution.py:365
  48.2 5.0 %collective-permute-done.11.p3.s3 = bf16[3,64,512]{2,1,0:T(8,128)(2,1)S(1)} collective-permute-done((bf16[3,64,512]{2,1,0:T(8,128)(2,1)S(1)}, bf16[3,64,512]{2,1,0:T(8,128)(2,1)S(1)}, u32[]{:S(2)}, u32[]{:S(2)}) %collective-permute-start.11) | collective-permute-done | bytes 196640 | tf_op jit(solution)/shard_map/ppermute | solution.py:365
  53.3 3.0 %all-to-all-done.parts_ref = bf16[16,64,512]{2,1,0:T(8,128)(2,1)S(1)} async-done(((bf16[16,64,512]{2,1,0:T(8,128)(2,1)}), bf16[16,64,512]{2,1,0:T(8,128)(2,1)S(1)}, u32[]{:S(2)}, u32[]{:S(2)}) %all-to-all-start) | async-done | bytes 1048608 | tf_op jit(solution)/shard_map/all_to_all | solution.py:452
  57.0 2.7 %collective-permute-start.13 = (bf16[64,512]{1,0:T(8,128)(2,1)S(1)}, bf16[64,512]{1,0:T(8,128)(2,1)S(1)}, u32[]{:S(2)}, u32[]{:S(2)}) collective-permute-start(bf16[64,512]{1,0:T(8,128)(2,1)S(1)} %plane.1.p0), channel_id=1, source_target_pairs={{0,2},{1,3},{2,0},{3,1},{4,6},{5,7},{6,4},{7,5},{8,10},{9,11},{10,... | collective-permute-start | bytes 196616 | tf_op jit(solution)/shard_map/ppermute | solution.py:365
  63.9 4.8 %all-to-all-start.1 = ((bf16[16,64,512]{2,1,0:T(8,128)(2,1)}), bf16[16,64,512]{2,1,0:T(8,128)(2,1)S(1)}, u32[]{:S(2)}, u32[]{:S(2)}) async-start(bf16[16,64,512]{2,1,0:T(8,128)(2,1)} %spread.1), calls=%async_computation.1 | async-start | bytes 2097152 | tf_op jit(solution)/shard_map/all_to_all | solution.py:473
  68.7 3.6 %collective-permute-start.16 = (bf16[256,512]{1,0:T(8,128)(2,1)S(1)}, bf16[256,512]{1,0:T(8,128)(2,1)S(1)}, u32[]{:S(2)}, u32[]{:S(2)}) collective-permute-start(bf16[256,512]{1,0:T(8,128)(2,1)S(1)} %get-tuple-element.110), channel_id=1, source_target_pairs={{0,4},{4,0},{1,5},{5,1},{2,6},{6,2},{3,7},{7,3},{8,12},{12,8},{9,1... | collective-permute-start | bytes 786440 | tf_op jit(solution)/shard_map/ppermute | solution.py:365
  72.3 3.3 %collective-permute-start.15 = (bf16[256,512]{1,0:T(8,128)(2,1)S(1)}, bf16[256,512]{1,0:T(8,128)(2,1)S(1)}, u32[]{:S(2)}, u32[]{:S(2)}) collective-permute-start(bf16[256,512]{1,0:T(8,128)(2,1)S(1)} %get-tuple-element.109), channel_id=1, source_target_pairs={{4,8},{12,16},{20,24},{28,32},{36,40},{44,48},{52,56},{60,64},{68,... | collective-permute-start | bytes 786440 | tf_op jit(solution)/shard_map/ppermute | solution.py:371
  75.7 3.1 %grid_near.1.prior_hbm = bf16[2048,512]{1,0:T(8,128)(2,1)} custom-call(s32[1]{0:T(128)} %bitcast.1.sub_ref, s32[1]{0:T(128)} %bitcast.core_ref, bf16[256,512]{1,0:T(8,128)(2,1)S(1)} %collective-permute-done.16.near, bf16[3,64,512]{2,1,0:T(8,128)(2,1)S(1)} %get-tuple-element.105.p0.s0, bf16[3,64,512]{2,1,0:T(8,128)(2,1)S(1)} %collective-permute-done.9.p1.s1, ...), custom_call_target="tpu_custom_call" | custom-call | flops 536870912 | bytes 3145728 | tf_op jit(solution)/shard_map/grid_near/pallas_call | solution.py:48
  78.8 8.3 %collective-permute-done.15.far = bf16[256,512]{1,0:T(8,128)(2,1)S(1)} collective-permute-done((bf16[256,512]{1,0:T(8,128)(2,1)S(1)}, bf16[256,512]{1,0:T(8,128)(2,1)S(1)}, u32[]{:S(2)}, u32[]{:S(2)}) %collective-permute-start.15) | collective-permute-done | bytes 262176 | tf_op jit(solution)/shard_map/ppermute | solution.py:371
  87.0 1.8 %collective-permute-start.17 = (bf16[1024,512]{1,0:T(8,128)(2,1)S(1)}, bf16[1024,512]{1,0:T(8,128)(2,1)S(1)}, u32[]{:S(2)}, u32[]{:S(2)}) collective-permute-start(bf16[1024,512]{1,0:T(8,128)(2,1)S(1)} %bitcast.6), channel_id=1, source_target_pairs={{0,4},{4,0},{1,5},{5,1},{2,6},{6,2},{3,7},{7,3},{8,12},{12,8},{9,1... | collective-permute-start | bytes 3145736 | tf_op jit(solution)/shard_map/ppermute | solution.py:365
  88.8 3.2 %grid_far.1 = (bf16[2048,512]{1,0:T(8,128)(2,1)}, f32[4,512,512]{2,1,0:T(8,128)}) custom-call(s32[1]{0:T(128)} %bitcast.1.sub_ref, s32[1]{0:T(128)} %bitcast.core_ref, bf16[256,512]{1,0:T(8,128)(2,1)S(1)} %collective-permute-done.15.far, bf16[3,64,512]{2,1,0:T(8,128)(2,1)S(1)} %get-tuple-element.105.p0.s0, ...), custom_call_target="tpu_custom_call", output_to_operand_aliasing={{0}: (11, {})} | custom-call | flops 536870912 | bytes 5242880 | tf_op jit(solution)/shard_map/grid_far/pallas_call | solution.py:48
  92.0 1.4 %widen.1 = f32[4,512,512]{2,1,0:T(8,128)} custom-call(s32[1]{0:T(128)} %bitcast.core_ref, bf16[1024,512]{1,0:T(8,128)(2,1)S(1)} %collective-permute-done.17.half_ref, f32[4,512,512]{2,1,0:T(8,128)} %get-tuple-element.117.prior_hbm), custom_call_target="tpu_custom_call", output_to_operand_aliasing={{}: (2, {})} | custom-call | flops 1048576 | bytes 3145728 | tf_op jit(solution)/shard_map/widen/pallas_call | solution.py:48
  (32 shorter events, 13.1 us)
Async XLA Ops:
  4.2 4.7 %collective-permute-start = (bf16[256,512]{1,0:T(8,128)(2,1)S(1)}, bf16[256,512]{1,0:T(8,128)(2,1)S(1)}, u32[]{:S(2)}, u32[]{:S(2)}) collective-permute-start(bf16[256,512]{1,0:T(8,128)(2,1)S(1)} %get-tuple-element.61), channel_id=1, source_target_pairs={{0,4},{4,0},{1,5},{5,1},{2,6},{6,2},{3,7},{7,3},{8,12},{12,8},{9,1... | collective-permute-start | bytes 786440 | tf_op jit(solution)/shard_map/ppermute | solution.py:365
  5.7 9.4 %collective-permute-start.1 = (bf16[256,512]{1,0:T(8,128)(2,1)S(1)}, bf16[256,512]{1,0:T(8,128)(2,1)S(1)}, u32[]{:S(2)}, u32[]{:S(2)}) collective-permute-start(bf16[256,512]{1,0:T(8,128)(2,1)S(1)} %get-tuple-element.62), channel_id=1, source_target_pairs={{4,8},{12,16},{20,24},{28,32},{36,40},{44,48},{52,56},{60,64},{68,... | collective-permute-start | bytes 786440 | tf_op jit(solution)/shard_map/ppermute | solution.py:371
  8.9 6.2 %collective-permute-start.2 = (bf16[128,512]{1,0:T(8,128)(2,1)S(1)}, bf16[128,512]{1,0:T(8,128)(2,1)S(1)}, u32[]{:S(2)}, u32[]{:S(2)}) collective-permute-start(bf16[128,512]{1,0:T(8,128)(2,1)S(1)} %get-tuple-element.64), channel_id=1, source_target_pairs={{0,1},{1,2},{2,3},{3,0},{4,5},{5,6},{6,7},{7,4},{8,9},{9,10},{10,1... | collective-permute-start | bytes 393224 | tf_op jit(solution)/shard_map/ppermute | solution.py:365
  10.6 10.3 %collective-permute-start.3 = (bf16[128,512]{1,0:T(8,128)(2,1)S(1)}, bf16[128,512]{1,0:T(8,128)(2,1)S(1)}, u32[]{:S(2)}, u32[]{:S(2)}) collective-permute-start(bf16[128,512]{1,0:T(8,128)(2,1)S(1)} %get-tuple-element.73), channel_id=1, source_target_pairs={{0,2},{1,3},{2,0},{3,1},{4,6},{5,7},{6,4},{7,5},{8,10},{9,11},{10,... | collective-permute-start | bytes 393224 | tf_op jit(solution)/shard_map/ppermute | solution.py:365
  13.9 7.0 %collective-permute-start.4 = (bf16[128,512]{1,0:T(8,128)(2,1)S(1)}, bf16[128,512]{1,0:T(8,128)(2,1)S(1)}, u32[]{:S(2)}, u32[]{:S(2)}) collective-permute-start(bf16[128,512]{1,0:T(8,128)(2,1)S(1)} %get-tuple-element.74), channel_id=1, source_target_pairs={{0,3},{1,0},{2,1},{3,2},{4,7},{5,4},{6,5},{7,6},{8,11},{9,8},{10,9... | collective-permute-start | bytes 393224 | tf_op jit(solution)/shard_map/ppermute | solution.py:365
  15.1 6.5 %collective-permute-start.5 = (bf16[64,512]{1,0:T(8,128)(2,1)S(1)}, bf16[64,512]{1,0:T(8,128)(2,1)S(1)}, u32[]{:S(2)}, u32[]{:S(2)}) collective-permute-start(bf16[64,512]{1,0:T(8,128)(2,1)S(1)} %get-tuple-element.75), channel_id=1, source_target_pairs={{0,1},{1,2},{2,3},{3,0},{4,5},{5,6},{6,7},{7,4},{8,9},{9,10},{10,1... | collective-permute-start | bytes 196616 | tf_op jit(solution)/shard_map/ppermute | solution.py:365
  15.9 6.2 %collective-permute-start.6 = (bf16[64,512]{1,0:T(8,128)(2,1)S(1)}, bf16[64,512]{1,0:T(8,128)(2,1)S(1)}, u32[]{:S(2)}, u32[]{:S(2)}) collective-permute-start(bf16[64,512]{1,0:T(8,128)(2,1)S(1)} %get-tuple-element.76), channel_id=1, source_target_pairs={{0,2},{1,3},{2,0},{3,1},{4,6},{5,7},{6,4},{7,5},{8,10},{9,11},{10,... | collective-permute-start | bytes 196616 | tf_op jit(solution)/shard_map/ppermute | solution.py:365
  19.5 3.1 %collective-permute-start.7 = (bf16[64,512]{1,0:T(8,128)(2,1)S(1)}, bf16[64,512]{1,0:T(8,128)(2,1)S(1)}, u32[]{:S(2)}, u32[]{:S(2)}) collective-permute-start(bf16[64,512]{1,0:T(8,128)(2,1)S(1)} %get-tuple-element.77), channel_id=1, source_target_pairs={{0,3},{1,0},{2,1},{3,2},{4,7},{5,4},{6,5},{7,6},{8,11},{9,8},{10,9... | collective-permute-start | bytes 196616 | tf_op jit(solution)/shard_map/ppermute | solution.py:365
  27.6 2.7 %collective-permute-start.8 = (bf16[1024,512]{1,0:T(8,128)(2,1)S(1)}, bf16[1024,512]{1,0:T(8,128)(2,1)S(1)}, u32[]{:S(2)}, u32[]{:S(2)}) collective-permute-start(bf16[1024,512]{1,0:T(8,128)(2,1)S(1)} %get-tuple-element.87), channel_id=1, source_target_pairs={{0,4},{4,0},{1,5},{5,1},{2,6},{6,2},{3,7},{7,3},{8,12},{12,8},{9,1... | collective-permute-start | bytes 3145736 | tf_op jit(solution)/shard_map/ppermute | solution.py:365
  31.4 24.9 %all-to-all-start = ((bf16[16,64,512]{2,1,0:T(8,128)(2,1)}), bf16[16,64,512]{2,1,0:T(8,128)(2,1)S(1)}, u32[]{:S(2)}, u32[]{:S(2)}) async-start(bf16[16,64,512]{2,1,0:T(8,128)(2,1)} %bitcast.4), calls=%async_computation | async-start | bytes 2097152 | tf_op jit(solution)/shard_map/all_to_all | solution.py:452
  40.5 7.8 %collective-permute-start.10 = (bf16[3,64,512]{2,1,0:T(8,128)(2,1)}, bf16[3,64,512]{2,1,0:T(8,128)(2,1)S(1)}, u32[]{:S(2)}, u32[]{:S(2)}) collective-permute-start(bf16[3,64,512]{2,1,0:T(8,128)(2,1)} %get-tuple-element.94), channel_id=1, source_target_pairs={{0,2},{1,3},{2,0},{3,1},{4,6},{5,7},{6,4},{7,5},{8,10},{9,11},{10,... | collective-permute-start | bytes 589832 | tf_op jit(solution)/shard_map/ppermute | solution.py:365
  41.8 11.5 %collective-permute-start.11 = (bf16[3,64,512]{2,1,0:T(8,128)(2,1)S(1)}, bf16[3,64,512]{2,1,0:T(8,128)(2,1)S(1)}, u32[]{:S(2)}, u32[]{:S(2)}) collective-permute-start(bf16[3,64,512]{2,1,0:T(8,128)(2,1)S(1)} %get-tuple-element.95), channel_id=1, source_target_pairs={{0,1},{1,2},{2,3},{3,0},{4,5},{5,6},{6,7},{7,4},{8,9},{9,10},{10,1... | collective-permute-start | bytes 589832 | tf_op jit(solution)/shard_map/ppermute | solution.py:365
  42.9 10.4 %collective-permute-start.9 = (bf16[3,64,512]{2,1,0:T(8,128)(2,1)S(1)}, bf16[3,64,512]{2,1,0:T(8,128)(2,1)S(1)}, u32[]{:S(2)}, u32[]{:S(2)}) collective-permute-start(bf16[3,64,512]{2,1,0:T(8,128)(2,1)S(1)} %get-tuple-element.93), channel_id=1, source_target_pairs={{0,3},{1,0},{2,1},{3,2},{4,7},{5,4},{6,5},{7,6},{8,11},{9,8},{10,9... | collective-permute-start | bytes 589832 | tf_op jit(solution)/shard_map/ppermute | solution.py:365
  56.4 4.6 %collective-permute-start.12 = (bf16[64,512]{1,0:T(8,128)(2,1)S(1)}, bf16[64,512]{1,0:T(8,128)(2,1)S(1)}, u32[]{:S(2)}, u32[]{:S(2)}) collective-permute-start(bf16[64,512]{1,0:T(8,128)(2,1)S(1)} %plane.1.p0), channel_id=1, source_target_pairs={{0,1},{1,2},{2,3},{3,0},{4,5},{5,6},{6,7},{7,4},{8,9},{9,10},{10,1... | collective-permute-start | bytes 196616 | tf_op jit(solution)/shard_map/ppermute | solution.py:365
  57.0 5.0 %collective-permute-start.13 = (bf16[64,512]{1,0:T(8,128)(2,1)S(1)}, bf16[64,512]{1,0:T(8,128)(2,1)S(1)}, u32[]{:S(2)}, u32[]{:S(2)}) collective-permute-start(bf16[64,512]{1,0:T(8,128)(2,1)S(1)} %plane.1.p0), channel_id=1, source_target_pairs={{0,2},{1,3},{2,0},{3,1},{4,6},{5,7},{6,4},{7,5},{8,10},{9,11},{10,... | collective-permute-start | bytes 196616 | tf_op jit(solution)/shard_map/ppermute | solution.py:365
  59.6 3.1 %collective-permute-start.14 = (bf16[64,512]{1,0:T(8,128)(2,1)S(1)}, bf16[64,512]{1,0:T(8,128)(2,1)S(1)}, u32[]{:S(2)}, u32[]{:S(2)}) collective-permute-start(bf16[64,512]{1,0:T(8,128)(2,1)S(1)} %plane.1.p0), channel_id=1, source_target_pairs={{0,3},{1,0},{2,1},{3,2},{4,7},{5,4},{6,5},{7,6},{8,11},{9,8},{10,9... | collective-permute-start | bytes 196616 | tf_op jit(solution)/shard_map/ppermute | solution.py:365
  63.9 23.1 %all-to-all-start.1 = ((bf16[16,64,512]{2,1,0:T(8,128)(2,1)}), bf16[16,64,512]{2,1,0:T(8,128)(2,1)S(1)}, u32[]{:S(2)}, u32[]{:S(2)}) async-start(bf16[16,64,512]{2,1,0:T(8,128)(2,1)} %spread.1), calls=%async_computation.1 | async-start | bytes 2097152 | tf_op jit(solution)/shard_map/all_to_all | solution.py:473
  68.7 6.9 %collective-permute-start.16 = (bf16[256,512]{1,0:T(8,128)(2,1)S(1)}, bf16[256,512]{1,0:T(8,128)(2,1)S(1)}, u32[]{:S(2)}, u32[]{:S(2)}) collective-permute-start(bf16[256,512]{1,0:T(8,128)(2,1)S(1)} %get-tuple-element.110), channel_id=1, source_target_pairs={{0,4},{4,0},{1,5},{5,1},{2,6},{6,2},{3,7},{7,3},{8,12},{12,8},{9,1... | collective-permute-start | bytes 786440 | tf_op jit(solution)/shard_map/ppermute | solution.py:365
  72.3 14.7 %collective-permute-start.15 = (bf16[256,512]{1,0:T(8,128)(2,1)S(1)}, bf16[256,512]{1,0:T(8,128)(2,1)S(1)}, u32[]{:S(2)}, u32[]{:S(2)}) collective-permute-start(bf16[256,512]{1,0:T(8,128)(2,1)S(1)} %get-tuple-element.109), channel_id=1, source_target_pairs={{4,8},{12,16},{20,24},{28,32},{36,40},{44,48},{52,56},{60,64},{68,... | collective-permute-start | bytes 786440 | tf_op jit(solution)/shard_map/ppermute | solution.py:371
  87.0 5.0 %collective-permute-start.17 = (bf16[1024,512]{1,0:T(8,128)(2,1)S(1)}, bf16[1024,512]{1,0:T(8,128)(2,1)S(1)}, u32[]{:S(2)}, u32[]{:S(2)}) collective-permute-start(bf16[1024,512]{1,0:T(8,128)(2,1)S(1)} %bitcast.6), channel_id=1, source_target_pairs={{0,4},{4,0},{1,5},{5,1},{2,6},{6,2},{3,7},{7,3},{8,12},{12,8},{9,1... | collective-permute-start | bytes 3145736 | tf_op jit(solution)/shard_map/ppermute | solution.py:365

commit v15 on v14

--- a/solution.py
+++ b/solution.py
@@ -70,19 +70,20 @@
     return [pltpu.VMEM(a.shape, a.dtype) for a in args] + [pltpu.SemaphoreType.DMA((len(args),))]
 
 
-def assemble(rows, near_first, near, far, own, *pieces):
+def early_body(core_ref, near, own, m1, m2, m3, wkv_ref, rows, keys, vals):
     block = near.shape[0]
     cap = block // 4
-    near_at = pl.multiple_of((1 - near_first) * (2 * block), block)
-    far_at = pl.multiple_of(near_first * (2 * block), block)
+    width = rows.shape[1]
+    near_at = pl.multiple_of(core_ref[0] * (2 * block), block)
     rows[block : block + cap] = own[0:cap]
     rows[pl.ds(near_at, cap), :] = near[0:cap]
-    rows[pl.ds(far_at, cap), :] = far[0:cap]
-    for k in range(1, 4):
-        mixed, last = pieces[k - 1], pieces[len(pieces) - 4 + k]
+    for k, mixed in enumerate((m1, m2, m3), 1):
         rows[block + k * cap : block + (k + 1) * cap] = mixed[0:cap]
         rows[pl.ds(near_at + k * cap, cap), :] = mixed[cap : 2 * cap]
-        rows[pl.ds(far_at + k * cap, cap), :] = last[last.shape[0] - cap :]
+    for first in (block, near_at):
+        at = pl.ds(first, block)
+        keys[at, :] = nn(rows[at, :], wkv_ref[:, :width]).astype(BF16)
+        vals[at, :] = nn(rows[at, :], wkv_ref[:, width:]).astype(BF16)
 
 
 def gather_body(sub_ref, core_ref, rows_hbm, gain_hbm, x_hbm, *refs):
@@ -172,14 +173,20 @@
         copy.wait()
 
 
-def middle_body(core_ref, near, far, own, m1, m2, m3, f1, f2, f3, q_ref, ag_ref, mn_ref, og_ref,
-                bias_ref, wkv_ref, send_ref, part_ref, att_ref, qg_ref, rows, keys, vals):
+def middle_body(core_ref, far, f1, f2, f3, q_ref, ag_ref, mn_ref, og_ref, bias_ref, wkv_ref,
+                rows_in, keys_in, vals_in, send_ref, part_ref, att_ref, qg_ref, rows, keys, vals):
     width = q_ref.shape[1]
     heads = bias_ref.shape[0]
     core = core_ref[0]
-    assemble(rows, 1 - core, near, far, own, m1, m2, m3, f1, f2, f3)
-    keys[...] = nn(rows[...], wkv_ref[:, :width]).astype(BF16)
-    vals[...] = nn(rows[...], wkv_ref[:, width:]).astype(BF16)
+    block = far.shape[0]
+    cap = block // 4
+    far_at = pl.multiple_of((1 - core) * (2 * block), block)
+    rows[pl.ds(far_at, cap), :] = far[0:cap]
+    for k, piece in enumerate((f1, f2, f3), 1):
+        rows[pl.ds(far_at + k * cap, cap), :] = piece[...]
+    at = pl.ds(far_at, block)
+    keys[at, :] = nn(rows[at, :], wkv_ref[:, :width]).astype(BF16)
+    vals[at, :] = nn(rows[at, :], wkv_ref[:, width:]).astype(BF16)
     for h in range(heads):
         at = slice(h * 128, (h + 1) * 128)
         q, ag = q_ref[:, at], ag_ref[:, at]
@@ -415,7 +422,6 @@
     far, mixed[0], queries = lax.optimization_barrier((far, mixed[0], queries))
     outer = call(split_body, [one] * 3, [VM], (far,), 0, 1 << 19, "split")
     outer = [shifted(f, "z", k) for k, f in enumerate(outer, 1)]
-    received = near, far, own, *mixed, *outer
     sub2, far = lax.optimization_barrier((sub1, far))
     dense, weights_near = call(
         slots_body, [sds((heads, nodes, slots), F32), sds((width, 2 * width))],
@@ -424,13 +430,17 @@
         [pltpu.VMEM((nodes * 8, 128), F32), pltpu.VMEM((heads, nodes, 128), F32),
          pltpu.SemaphoreType.DMA((2,))],
     )
-    send, part_grads, attended, query_grad, rows = call(
+    table = sds((slots, width))
+    rows, keys, vals = call(
+        early_body, [table] * 3, [SM] + [VM] * 6, (core1, near, own, *mixed, weights_near),
+        1 << 29, 3 << 20, "early",
+    )
+    send, part_grads, attended, query_grad, rows, *_ = call(
         middle_body,
-        [sds((2 * width, width)), sds((slots, 2 * width))] + [sds((nodes, width))] * 2
-        + [sds((slots, width))],
-        [SM] + [VM] * 15,
-        (core1, *received, queries, att_grad, mesh_normed, og_near, dense, weights_near),
-        3 << 30, 8 << 20, "middle", [pltpu.VMEM((slots, width), BF16)] * 2,
+        [sds((2 * width, width)), sds((slots, 2 * width))] + [sds((nodes, width))] * 2 + [table] * 3,
+        [SM] + [VM] * 13,
+        (core1, far, *outer, queries, att_grad, mesh_normed, og_near, dense, weights_near, rows, keys, vals),
+        3 << 30, 8 << 20, "middle", (), None, {11: 4, 12: 5, 13: 6},
     )
 
     other = shifted(send, "gc", 1)

time: 94 us -> 93.3 us (level)
    pallas_call x16 -> x17, Pallas kernels: 23.8 us -> 24 us  [call(): pl.pallas_call(body, out_shape=outs, in_specs=in_specs, out_specs=out_spe...]
  transfers between devices with their start and end apart: 20 -> 20, of which waited for: 11 -> 10; matrix products, arithmetic and copies ran while one was open for 0% -> 0% of each run, Pallas kernels for 12% -> 13%
where the time goes in v15:
time: 93.3 us; the launch traced here: 92.9 us
  starting transfers between devices  44.9 us (48%)
  Pallas kernels  24 us (26%)
  waiting for transfers between devices  23 us (25%)
  between operations  1.01 us (1%)
    ppermute x16, starting transfers between devices, shifted(): return lax.ppermute(block, axis, [(i, (i + k) % n) for i in range(n)])  24.5 us
    pallas_call x17, Pallas kernels, call(): pl.pallas_call(body, out_shape=outs, in_specs=in_specs, out_specs=out_spe...  24 us
    ppermute x16, waiting for transfers between devices, shifted(): return lax.ppermute(block, axis, [(i, (i + k) % n) for i in range(n)])  11.7 us
    all_to_all x1, starting transfers between devices, shards(): lax.all_to_all(own.reshape(plane, share, width), PLANE, 0, 0, tiled=True)  9.07 us
    ppermute x2, waiting for transfers between devices, swapped_far(): return lax.ppermute(block, SLAB, pairs + [(j, i) for i, j in pairs])  8.26 us
    ppermute x2, starting transfers between devices, swapped_far(): return lax.ppermute(block, SLAB, pairs + [(j, i) for i, j in pairs])  6.53 us
    all_to_all x1, starting transfers between devices, shards(): lax.all_to_all(spread, PLANE, 0, 0, tiled=True).reshape(2 * width, width)  4.81 us
    all_to_all x1, waiting for transfers between devices, shards(): lax.all_to_all(own.reshape(plane, share, width), PLANE, 0, 0, tiled=True)  2.99 us
  transfers between devices with their start and end apart: 20, of which 10 were waited for; matrix products, arithmetic and copies ran while one was open for 0% of the time, Pallas kernels for 13%

profile of v15, /device:TPU:1, one launch (start us, length us, event | category | flops | bytes accessed | tf_op | source)
XLA Modules:
  0.0 92.9 jit_solution(6335668570605583526)
XLA Ops:
  0.6 3.5 %gather_rows.1 = (bf16[256,512]{1,0:T(8,128)(2,1)S(1)}, bf16[256,512]{1,0:T(8,128)(2,1)S(1)}, bf16[256,512]{1,0:T(8,128)(2,1)S(1)}, s32[1,3,4,64]{3,2,1,0:T(4,12...) custom-call(s32[1]{0:T(128)} %bitcast.1.sub_ref, ...), custom_call_target="tpu_custom_call" | custom-call | flops 1073741824 | bytes 5242880 | tf_op jit(solution)/shard_map/gather_rows/pallas_call | solution.py:48
  4.2 1.5 %collective-permute-start.1 = (bf16[256,512]{1,0:T(8,128)(2,1)S(1)}, bf16[256,512]{1,0:T(8,128)(2,1)S(1)}, u32[]{:S(2)}, u32[]{:S(2)}) collective-permute-start(bf16[256,512]{1,0:T(8,128)(2,1)S(1)} %get-tuple-element.67), channel_id=1, source_target_pairs={{0,4},{4,0},{1,5},{5,1},{2,6},{6,2},{3,7},{7,3},{8,12},{12,8},{9,1... | collective-permute-start | bytes 786440 | tf_op jit(solution)/shard_map/ppermute | solution.py:372
  5.7 3.2 %collective-permute-start = (bf16[256,512]{1,0:T(8,128)(2,1)S(1)}, bf16[256,512]{1,0:T(8,128)(2,1)S(1)}, u32[]{:S(2)}, u32[]{:S(2)}) collective-permute-start(bf16[256,512]{1,0:T(8,128)(2,1)S(1)} %get-tuple-element.65), channel_id=1, source_target_pairs={{4,8},{12,16},{20,24},{28,32},{36,40},{44,48},{52,56},{60,64},{68,... | collective-permute-start | bytes 786440 | tf_op jit(solution)/shard_map/ppermute | solution.py:378
  8.9 1.7 %collective-permute-start.2 = (bf16[128,512]{1,0:T(8,128)(2,1)S(1)}, bf16[128,512]{1,0:T(8,128)(2,1)S(1)}, u32[]{:S(2)}, u32[]{:S(2)}) collective-permute-start(bf16[128,512]{1,0:T(8,128)(2,1)S(1)} %get-tuple-element.68), channel_id=1, source_target_pairs={{0,1},{1,2},{2,3},{3,0},{4,5},{5,6},{6,7},{7,4},{8,9},{9,10},{10,1... | collective-permute-start | bytes 393224 | tf_op jit(solution)/shard_map/ppermute | solution.py:372
  10.6 3.3 %collective-permute-start.6 = (bf16[128,512]{1,0:T(8,128)(2,1)S(1)}, bf16[128,512]{1,0:T(8,128)(2,1)S(1)}, u32[]{:S(2)}, u32[]{:S(2)}) collective-permute-start(bf16[128,512]{1,0:T(8,128)(2,1)S(1)} %get-tuple-element.90), channel_id=1, source_target_pairs={{0,2},{1,3},{2,0},{3,1},{4,6},{5,7},{6,4},{7,5},{8,10},{9,11},{10,... | collective-permute-start | bytes 393224 | tf_op jit(solution)/shard_map/ppermute | solution.py:372
  15.9 3.6 %collective-permute-start.4 = (bf16[64,512]{1,0:T(8,128)(2,1)S(1)}, bf16[64,512]{1,0:T(8,128)(2,1)S(1)}, u32[]{:S(2)}, u32[]{:S(2)}) collective-permute-start(bf16[64,512]{1,0:T(8,128)(2,1)S(1)} %get-tuple-element.78), channel_id=1, source_target_pairs={{0,2},{1,3},{2,0},{3,1},{4,6},{5,7},{6,4},{7,5},{8,10},{9,11},{10,... | collective-permute-start | bytes 196616 | tf_op jit(solution)/shard_map/ppermute | solution.py:372
  19.5 1.4 %slots.1 = (f32[4,64,768]{2,1,0:T(8,128)S(1)}, bf16[512,1024]{1,0:T(8,128)(2,1)S(1)}) custom-call(s32[1]{0:T(128)} %bitcast.1.sub_ref, s32[64,96]{1,0:T(8,128)S(1)} %get-tuple-element.84.nbr_ref, s32[64,96]{1,0:T(8,128)S(1)} %get-tuple-element.85.valid_ref, f32[64,384]{1,0:T(8,128)S(1)} %get-tuple-element.86.bias_ref, bf16[512,512]{1,0:T(8,128)(2,1)} %wk_hbm.1, ...), custom_call_target="tpu_custom_call" | custom-call | flops 1073741824 | bytes 8388608 | tf_op jit(solution)/shard_map/slots/pallas_call | solution.py:48
  22.6 4.4 %middle.1 = (bf16[1024,512]{1,0:T(8,128)(2,1)S(1)}, bf16[768,1024]{1,0:T(8,128)(2,1)S(1)}, bf16[64,512]{1,0:T(8,128)(2,1)S(1)}, bf16[64,512]{1,0:T(8,128)(2,1)S(...) custom-call(s32[1]{0:T(128)} %bitcast.core_ref, ...), custom_call_target="tpu_custom_call", output_to_operand_aliasing={{4}: (11, {}), {5}: (12, {}), {6}: (13, {})} | custom-call | flops 3221225472 | bytes 8388608 | tf_op jit(solution)/shard_map/middle/pallas_call | solution.py:48
  27.9 1.7 %back.1 = (bf16[3,64,512]{2,1,0:T(8,128)(2,1)S(1)}, bf16[3,64,512]{2,1,0:T(8,128)(2,1)S(1)}, bf16[3,64,512]{2,1,0:T(8,128)(2,1)}, bf16[3,64,512]{2,1,0:T(8,128)(2,1)S(1)}) custom-call(bf16[768,1024]{1,0:T(8,128)(2,1)S(1)} %get-tuple-element.96.part_ref, bf16[512,1024]{1,0:T(8,128)(2,1)S(1)} %get-tuple-element.88.wkv_ref), custom_call_target="tpu_custom_call" | custom-call | flops 1073741824 | bytes 3145728 | tf_op jit(solution)/shard_map/back/pallas_call | solution.py:48
  30.8 9.1 %all-to-all-start = ((bf16[16,64,512]{2,1,0:T(8,128)(2,1)}), bf16[16,64,512]{2,1,0:T(8,128)(2,1)S(1)}, u32[]{:S(2)}, u32[]{:S(2)}) async-start(bf16[16,64,512]{2,1,0:T(8,128)(2,1)} %bitcast.4), calls=%async_computation | async-start | bytes 2097152 | tf_op jit(solution)/shard_map/all_to_all | solution.py:462
  39.9 1.3 %collective-permute-start.10 = (bf16[3,64,512]{2,1,0:T(8,128)(2,1)}, bf16[3,64,512]{2,1,0:T(8,128)(2,1)S(1)}, u32[]{:S(2)}, u32[]{:S(2)}) collective-permute-start(bf16[3,64,512]{2,1,0:T(8,128)(2,1)} %get-tuple-element.102), channel_id=1, source_target_pairs={{0,2},{1,3},{2,0},{3,1},{4,6},{5,7},{6,4},{7,5},{8,10},{9,11},{10,... | collective-permute-start | bytes 589832 | tf_op jit(solution)/shard_map/ppermute | solution.py:372
  42.3 1.6 %collective-permute-start.9 = (bf16[3,64,512]{2,1,0:T(8,128)(2,1)S(1)}, bf16[3,64,512]{2,1,0:T(8,128)(2,1)S(1)}, u32[]{:S(2)}, u32[]{:S(2)}) collective-permute-start(bf16[3,64,512]{2,1,0:T(8,128)(2,1)S(1)} %get-tuple-element.101), channel_id=1, source_target_pairs={{0,3},{1,0},{2,1},{3,2},{4,7},{5,4},{6,5},{7,6},{8,11},{9,8},{10,9... | collective-permute-start | bytes 589832 | tf_op jit(solution)/shard_map/ppermute | solution.py:372
  45.0 2.7 %collective-permute-done.10.p2.s2 = bf16[3,64,512]{2,1,0:T(8,128)(2,1)S(1)} collective-permute-done((bf16[3,64,512]{2,1,0:T(8,128)(2,1)}, bf16[3,64,512]{2,1,0:T(8,128)(2,1)S(1)}, u32[]{:S(2)}, u32[]{:S(2)}) %collective-permute-start.10) | collective-permute-done | bytes 196640 | tf_op jit(solution)/shard_map/ppermute | solution.py:372
  47.7 5.0 %collective-permute-done.11.p3.s3 = bf16[3,64,512]{2,1,0:T(8,128)(2,1)S(1)} collective-permute-done((bf16[3,64,512]{2,1,0:T(8,128)(2,1)S(1)}, bf16[3,64,512]{2,1,0:T(8,128)(2,1)S(1)}, u32[]{:S(2)}, u32[]{:S(2)}) %collective-permute-start.11) | collective-permute-done | bytes 196640 | tf_op jit(solution)/shard_map/ppermute | solution.py:372
  52.7 3.0 %all-to-all-done.parts_ref = bf16[16,64,512]{2,1,0:T(8,128)(2,1)S(1)} async-done(((bf16[16,64,512]{2,1,0:T(8,128)(2,1)}), bf16[16,64,512]{2,1,0:T(8,128)(2,1)S(1)}, u32[]{:S(2)}, u32[]{:S(2)}) %all-to-all-start) | async-done | bytes 1048608 | tf_op jit(solution)/shard_map/all_to_all | solution.py:462
  56.2 2.7 %collective-permute-start.13 = (bf16[64,512]{1,0:T(8,128)(2,1)S(1)}, bf16[64,512]{1,0:T(8,128)(2,1)S(1)}, u32[]{:S(2)}, u32[]{:S(2)}) collective-permute-start(bf16[64,512]{1,0:T(8,128)(2,1)S(1)} %plane.1.p0), channel_id=1, source_target_pairs={{0,2},{1,3},{2,0},{3,1},{4,6},{5,7},{6,4},{7,5},{8,10},{9,11},{10,... | collective-permute-start | bytes 196616 | tf_op jit(solution)/shard_map/ppermute | solution.py:372
  63.2 4.8 %all-to-all-start.1 = ((bf16[16,64,512]{2,1,0:T(8,128)(2,1)}), bf16[16,64,512]{2,1,0:T(8,128)(2,1)S(1)}, u32[]{:S(2)}, u32[]{:S(2)}) async-start(bf16[16,64,512]{2,1,0:T(8,128)(2,1)} %spread.1), calls=%async_computation.1 | async-start | bytes 2097152 | tf_op jit(solution)/shard_map/all_to_all | solution.py:483
  68.0 3.6 %collective-permute-start.16 = (bf16[256,512]{1,0:T(8,128)(2,1)S(1)}, bf16[256,512]{1,0:T(8,128)(2,1)S(1)}, u32[]{:S(2)}, u32[]{:S(2)}) collective-permute-start(bf16[256,512]{1,0:T(8,128)(2,1)S(1)} %get-tuple-element.118), channel_id=1, source_target_pairs={{0,4},{4,0},{1,5},{5,1},{2,6},{6,2},{3,7},{7,3},{8,12},{12,8},{9,1... | collective-permute-start | bytes 786440 | tf_op jit(solution)/shard_map/ppermute | solution.py:372
  71.6 3.3 %collective-permute-start.15 = (bf16[256,512]{1,0:T(8,128)(2,1)S(1)}, bf16[256,512]{1,0:T(8,128)(2,1)S(1)}, u32[]{:S(2)}, u32[]{:S(2)}) collective-permute-start(bf16[256,512]{1,0:T(8,128)(2,1)S(1)} %get-tuple-element.117), channel_id=1, source_target_pairs={{4,8},{12,16},{20,24},{28,32},{36,40},{44,48},{52,56},{60,64},{68,... | collective-permute-start | bytes 786440 | tf_op jit(solution)/shard_map/ppermute | solution.py:378
  74.9 3.1 %grid_near.1.prior_hbm = bf16[2048,512]{1,0:T(8,128)(2,1)} custom-call(s32[1]{0:T(128)} %bitcast.1.sub_ref, s32[1]{0:T(128)} %bitcast.core_ref, bf16[256,512]{1,0:T(8,128)(2,1)S(1)} %collective-permute-done.16.near, bf16[3,64,512]{2,1,0:T(8,128)(2,1)S(1)} %get-tuple-element.113.p0.s0, bf16[3,64,512]{2,1,0:T(8,128)(2,1)S(1)} %collective-permute-done.9.p1.s1, ...), custom_call_target="tpu_custom_call" | custom-call | flops 536870912 | bytes 3145728 | tf_op jit(solution)/shard_map/grid_near/pallas_call | solution.py:48
  78.0 8.3 %collective-permute-done.15.far = bf16[256,512]{1,0:T(8,128)(2,1)S(1)} collective-permute-done((bf16[256,512]{1,0:T(8,128)(2,1)S(1)}, bf16[256,512]{1,0:T(8,128)(2,1)S(1)}, u32[]{:S(2)}, u32[]{:S(2)}) %collective-permute-start.15) | collective-permute-done | bytes 262176 | tf_op jit(solution)/shard_map/ppermute | solution.py:378
  86.3 1.8 %collective-permute-start.17 = (bf16[1024,512]{1,0:T(8,128)(2,1)S(1)}, bf16[1024,512]{1,0:T(8,128)(2,1)S(1)}, u32[]{:S(2)}, u32[]{:S(2)}) collective-permute-start(bf16[1024,512]{1,0:T(8,128)(2,1)S(1)} %bitcast.6), channel_id=1, source_target_pairs={{0,4},{4,0},{1,5},{5,1},{2,6},{6,2},{3,7},{7,3},{8,12},{12,8},{9,1... | collective-permute-start | bytes 3145736 | tf_op jit(solution)/shard_map/ppermute | solution.py:372
  88.1 3.2 %grid_far.1 = (bf16[2048,512]{1,0:T(8,128)(2,1)}, f32[4,512,512]{2,1,0:T(8,128)}) custom-call(s32[1]{0:T(128)} %bitcast.1.sub_ref, s32[1]{0:T(128)} %bitcast.core_ref, bf16[256,512]{1,0:T(8,128)(2,1)S(1)} %collective-permute-done.15.far, bf16[3,64,512]{2,1,0:T(8,128)(2,1)S(1)} %get-tuple-element.113.p0.s0, ...), custom_call_target="tpu_custom_call", output_to_operand_aliasing={{0}: (11, {})} | custom-call | flops 536870912 | bytes 5242880 | tf_op jit(solution)/shard_map/grid_far/pallas_call | solution.py:48
  91.3 1.4 %widen.1 = f32[4,512,512]{2,1,0:T(8,128)} custom-call(s32[1]{0:T(128)} %bitcast.core_ref, bf16[1024,512]{1,0:T(8,128)(2,1)S(1)} %collective-permute-done.17.half_ref, f32[4,512,512]{2,1,0:T(8,128)} %get-tuple-element.125.prior_hbm), custom_call_target="tpu_custom_call", output_to_operand_aliasing={{}: (2, {})} | custom-call | flops 1048576 | bytes 3145728 | tf_op jit(solution)/shard_map/widen/pallas_call | solution.py:48
  (33 shorter events, 12.8 us)
Async XLA Ops:
  4.2 4.7 %collective-permute-start.1 = (bf16[256,512]{1,0:T(8,128)(2,1)S(1)}, bf16[256,512]{1,0:T(8,128)(2,1)S(1)}, u32[]{:S(2)}, u32[]{:S(2)}) collective-permute-start(bf16[256,512]{1,0:T(8,128)(2,1)S(1)} %get-tuple-element.67), channel_id=1, source_target_pairs={{0,4},{4,0},{1,5},{5,1},{2,6},{6,2},{3,7},{7,3},{8,12},{12,8},{9,1... | collective-permute-start | bytes 786440 | tf_op jit(solution)/shard_map/ppermute | solution.py:372
  5.7 9.4 %collective-permute-start = (bf16[256,512]{1,0:T(8,128)(2,1)S(1)}, bf16[256,512]{1,0:T(8,128)(2,1)S(1)}, u32[]{:S(2)}, u32[]{:S(2)}) collective-permute-start(bf16[256,512]{1,0:T(8,128)(2,1)S(1)} %get-tuple-element.65), channel_id=1, source_target_pairs={{4,8},{12,16},{20,24},{28,32},{36,40},{44,48},{52,56},{60,64},{68,... | collective-permute-start | bytes 786440 | tf_op jit(solution)/shard_map/ppermute | solution.py:378
  8.9 6.2 %collective-permute-start.2 = (bf16[128,512]{1,0:T(8,128)(2,1)S(1)}, bf16[128,512]{1,0:T(8,128)(2,1)S(1)}, u32[]{:S(2)}, u32[]{:S(2)}) collective-permute-start(bf16[128,512]{1,0:T(8,128)(2,1)S(1)} %get-tuple-element.68), channel_id=1, source_target_pairs={{0,1},{1,2},{2,3},{3,0},{4,5},{5,6},{6,7},{7,4},{8,9},{9,10},{10,1... | collective-permute-start | bytes 393224 | tf_op jit(solution)/shard_map/ppermute | solution.py:372
  10.6 10.3 %collective-permute-start.6 = (bf16[128,512]{1,0:T(8,128)(2,1)S(1)}, bf16[128,512]{1,0:T(8,128)(2,1)S(1)}, u32[]{:S(2)}, u32[]{:S(2)}) collective-permute-start(bf16[128,512]{1,0:T(8,128)(2,1)S(1)} %get-tuple-element.90), channel_id=1, source_target_pairs={{0,2},{1,3},{2,0},{3,1},{4,6},{5,7},{6,4},{7,5},{8,10},{9,11},{10,... | collective-permute-start | bytes 393224 | tf_op jit(solution)/shard_map/ppermute | solution.py:372
  13.9 7.0 %collective-permute-start.7 = (bf16[128,512]{1,0:T(8,128)(2,1)S(1)}, bf16[128,512]{1,0:T(8,128)(2,1)S(1)}, u32[]{:S(2)}, u32[]{:S(2)}) collective-permute-start(bf16[128,512]{1,0:T(8,128)(2,1)S(1)} %get-tuple-element.91), channel_id=1, source_target_pairs={{0,3},{1,0},{2,1},{3,2},{4,7},{5,4},{6,5},{7,6},{8,11},{9,8},{10,9... | collective-permute-start | bytes 393224 | tf_op jit(solution)/shard_map/ppermute | solution.py:372
  15.1 6.6 %collective-permute-start.3 = (bf16[64,512]{1,0:T(8,128)(2,1)S(1)}, bf16[64,512]{1,0:T(8,128)(2,1)S(1)}, u32[]{:S(2)}, u32[]{:S(2)}) collective-permute-start(bf16[64,512]{1,0:T(8,128)(2,1)S(1)} %get-tuple-element.77), channel_id=1, source_target_pairs={{0,1},{1,2},{2,3},{3,0},{4,5},{5,6},{6,7},{7,4},{8,9},{9,10},{10,1... | collective-permute-start | bytes 196616 | tf_op jit(solution)/shard_map/ppermute | solution.py:372
  15.9 6.2 %collective-permute-start.4 = (bf16[64,512]{1,0:T(8,128)(2,1)S(1)}, bf16[64,512]{1,0:T(8,128)(2,1)S(1)}, u32[]{:S(2)}, u32[]{:S(2)}) collective-permute-start(bf16[64,512]{1,0:T(8,128)(2,1)S(1)} %get-tuple-element.78), channel_id=1, source_target_pairs={{0,2},{1,3},{2,0},{3,1},{4,6},{5,7},{6,4},{7,5},{8,10},{9,11},{10,... | collective-permute-start | bytes 196616 | tf_op jit(solution)/shard_map/ppermute | solution.py:372
  19.5 3.1 %collective-permute-start.5 = (bf16[64,512]{1,0:T(8,128)(2,1)S(1)}, bf16[64,512]{1,0:T(8,128)(2,1)S(1)}, u32[]{:S(2)}, u32[]{:S(2)}) collective-permute-start(bf16[64,512]{1,0:T(8,128)(2,1)S(1)} %get-tuple-element.79), channel_id=1, source_target_pairs={{0,3},{1,0},{2,1},{3,2},{4,7},{5,4},{6,5},{7,6},{8,11},{9,8},{10,9... | collective-permute-start | bytes 196616 | tf_op jit(solution)/shard_map/ppermute | solution.py:372
  27.0 2.7 %collective-permute-start.8 = (bf16[1024,512]{1,0:T(8,128)(2,1)S(1)}, bf16[1024,512]{1,0:T(8,128)(2,1)S(1)}, u32[]{:S(2)}, u32[]{:S(2)}) collective-permute-start(bf16[1024,512]{1,0:T(8,128)(2,1)S(1)} %get-tuple-element.95), channel_id=1, source_target_pairs={{0,4},{4,0},{1,5},{5,1},{2,6},{6,2},{3,7},{7,3},{8,12},{12,8},{9,1... | collective-permute-start | bytes 3145736 | tf_op jit(solution)/shard_map/ppermute | solution.py:372
  30.8 24.9 %all-to-all-start = ((bf16[16,64,512]{2,1,0:T(8,128)(2,1)}), bf16[16,64,512]{2,1,0:T(8,128)(2,1)S(1)}, u32[]{:S(2)}, u32[]{:S(2)}) async-start(bf16[16,64,512]{2,1,0:T(8,128)(2,1)} %bitcast.4), calls=%async_computation | async-start | bytes 2097152 | tf_op jit(solution)/shard_map/all_to_all | solution.py:462
  39.9 7.8 %collective-permute-start.10 = (bf16[3,64,512]{2,1,0:T(8,128)(2,1)}, bf16[3,64,512]{2,1,0:T(8,128)(2,1)S(1)}, u32[]{:S(2)}, u32[]{:S(2)}) collective-permute-start(bf16[3,64,512]{2,1,0:T(8,128)(2,1)} %get-tuple-element.102), channel_id=1, source_target_pairs={{0,2},{1,3},{2,0},{3,1},{4,6},{5,7},{6,4},{7,5},{8,10},{9,11},{10,... | collective-permute-start | bytes 589832 | tf_op jit(solution)/shard_map/ppermute | solution.py:372
  41.2 11.5 %collective-permute-start.11 = (bf16[3,64,512]{2,1,0:T(8,128)(2,1)S(1)}, bf16[3,64,512]{2,1,0:T(8,128)(2,1)S(1)}, u32[]{:S(2)}, u32[]{:S(2)}) collective-permute-start(bf16[3,64,512]{2,1,0:T(8,128)(2,1)S(1)} %get-tuple-element.103), channel_id=1, source_target_pairs={{0,1},{1,2},{2,3},{3,0},{4,5},{5,6},{6,7},{7,4},{8,9},{9,10},{10,1... | collective-permute-start | bytes 589832 | tf_op jit(solution)/shard_map/ppermute | solution.py:372
  42.3 10.4 %collective-permute-start.9 = (bf16[3,64,512]{2,1,0:T(8,128)(2,1)S(1)}, bf16[3,64,512]{2,1,0:T(8,128)(2,1)S(1)}, u32[]{:S(2)}, u32[]{:S(2)}) collective-permute-start(bf16[3,64,512]{2,1,0:T(8,128)(2,1)S(1)} %get-tuple-element.101), channel_id=1, source_target_pairs={{0,3},{1,0},{2,1},{3,2},{4,7},{5,4},{6,5},{7,6},{8,11},{9,8},{10,9... | collective-permute-start | bytes 589832 | tf_op jit(solution)/shard_map/ppermute | solution.py:372
  55.9 4.4 %collective-permute-start.12 = (bf16[64,512]{1,0:T(8,128)(2,1)S(1)}, bf16[64,512]{1,0:T(8,128)(2,1)S(1)}, u32[]{:S(2)}, u32[]{:S(2)}) collective-permute-start(bf16[64,512]{1,0:T(8,128)(2,1)S(1)} %plane.1.p0), channel_id=1, source_target_pairs={{0,1},{1,2},{2,3},{3,0},{4,5},{5,6},{6,7},{7,4},{8,9},{9,10},{10,1... | collective-permute-start | bytes 196616 | tf_op jit(solution)/shard_map/ppermute | solution.py:372
  56.2 5.0 %collective-permute-start.13 = (bf16[64,512]{1,0:T(8,128)(2,1)S(1)}, bf16[64,512]{1,0:T(8,128)(2,1)S(1)}, u32[]{:S(2)}, u32[]{:S(2)}) collective-permute-start(bf16[64,512]{1,0:T(8,128)(2,1)S(1)} %plane.1.p0), channel_id=1, source_target_pairs={{0,2},{1,3},{2,0},{3,1},{4,6},{5,7},{6,4},{7,5},{8,10},{9,11},{10,... | collective-permute-start | bytes 196616 | tf_op jit(solution)/shard_map/ppermute | solution.py:372
  58.9 3.1 %collective-permute-start.14 = (bf16[64,512]{1,0:T(8,128)(2,1)S(1)}, bf16[64,512]{1,0:T(8,128)(2,1)S(1)}, u32[]{:S(2)}, u32[]{:S(2)}) collective-permute-start(bf16[64,512]{1,0:T(8,128)(2,1)S(1)} %plane.1.p0), channel_id=1, source_target_pairs={{0,3},{1,0},{2,1},{3,2},{4,7},{5,4},{6,5},{7,6},{8,11},{9,8},{10,9... | collective-permute-start | bytes 196616 | tf_op jit(solution)/shard_map/ppermute | solution.py:372
  63.2 23.1 %all-to-all-start.1 = ((bf16[16,64,512]{2,1,0:T(8,128)(2,1)}), bf16[16,64,512]{2,1,0:T(8,128)(2,1)S(1)}, u32[]{:S(2)}, u32[]{:S(2)}) async-start(bf16[16,64,512]{2,1,0:T(8,128)(2,1)} %spread.1), calls=%async_computation.1 | async-start | bytes 2097152 | tf_op jit(solution)/shard_map/all_to_all | solution.py:483
  68.0 6.9 %collective-permute-start.16 = (bf16[256,512]{1,0:T(8,128)(2,1)S(1)}, bf16[256,512]{1,0:T(8,128)(2,1)S(1)}, u32[]{:S(2)}, u32[]{:S(2)}) collective-permute-start(bf16[256,512]{1,0:T(8,128)(2,1)S(1)} %get-tuple-element.118), channel_id=1, source_target_pairs={{0,4},{4,0},{1,5},{5,1},{2,6},{6,2},{3,7},{7,3},{8,12},{12,8},{9,1... | collective-permute-start | bytes 786440 | tf_op jit(solution)/shard_map/ppermute | solution.py:372
  71.6 14.7 %collective-permute-start.15 = (bf16[256,512]{1,0:T(8,128)(2,1)S(1)}, bf16[256,512]{1,0:T(8,128)(2,1)S(1)}, u32[]{:S(2)}, u32[]{:S(2)}) collective-permute-start(bf16[256,512]{1,0:T(8,128)(2,1)S(1)} %get-tuple-element.117), channel_id=1, source_target_pairs={{4,8},{12,16},{20,24},{28,32},{36,40},{44,48},{52,56},{60,64},{68,... | collective-permute-start | bytes 786440 | tf_op jit(solution)/shard_map/ppermute | solution.py:378
  86.3 5.0 %collective-permute-start.17 = (bf16[1024,512]{1,0:T(8,128)(2,1)S(1)}, bf16[1024,512]{1,0:T(8,128)(2,1)S(1)}, u32[]{:S(2)}, u32[]{:S(2)}) collective-permute-start(bf16[1024,512]{1,0:T(8,128)(2,1)S(1)} %bitcast.6), channel_id=1, source_target_pairs={{0,4},{4,0},{1,5},{5,1},{2,6},{6,2},{3,7},{7,3},{8,12},{12,8},{9,1... | collective-permute-start | bytes 3145736 | tf_op jit(solution)/shard_map/ppermute | solution.py:372

commit v16 on v15

--- a/solution.py
+++ b/solution.py
@@ -70,7 +70,8 @@
     return [pltpu.VMEM(a.shape, a.dtype) for a in args] + [pltpu.SemaphoreType.DMA((len(args),))]
 
 
-def early_body(core_ref, near, own, m1, m2, m3, wkv_ref, rows, keys, vals):
+def early_body(core_ref, near, own, m1, m2, m3, wkv_ref, q_ref, ag_ref, bias_ref, rows, keys, vals,
+               scores_ref, pg_ref):
     block = near.shape[0]
     cap = block // 4
     width = rows.shape[1]
@@ -81,9 +82,19 @@
         rows[block + k * cap : block + (k + 1) * cap] = mixed[0:cap]
         rows[pl.ds(near_at + k * cap, cap), :] = mixed[cap : 2 * cap]
     for first in (block, near_at):
-        at = pl.ds(first, block)
-        keys[at, :] = nn(rows[at, :], wkv_ref[:, :width]).astype(BF16)
-        vals[at, :] = nn(rows[at, :], wkv_ref[:, width:]).astype(BF16)
+        columns(pl.ds(first, block), wkv_ref, q_ref, ag_ref, bias_ref, rows, keys, vals, scores_ref, pg_ref)
+
+
+def columns(at, wkv_ref, q_ref, ag_ref, bias_ref, rows, keys, vals, scores_ref, pg_ref):
+    width = rows.shape[1]
+    keys_at = nn(rows[at, :], wkv_ref[:, :width]).astype(BF16)
+    vals_at = nn(rows[at, :], wkv_ref[:, width:]).astype(BF16)
+    keys[at, :] = keys_at
+    vals[at, :] = vals_at
+    for h in range(bias_ref.shape[0]):
+        head = slice(h * 128, (h + 1) * 128)
+        scores_ref[h, :, at] = nt(q_ref[:, head], keys_at[:, head]) + bias_ref[h, :, at]
+        pg_ref[h, :, at] = nt(ag_ref[:, head], vals_at[:, head])
 
 
 def gather_body(sub_ref, core_ref, rows_hbm, gain_hbm, x_hbm, *refs):
@@ -174,7 +185,8 @@
 
 
 def middle_body(core_ref, far, f1, f2, f3, q_ref, ag_ref, mn_ref, og_ref, bias_ref, wkv_ref,
-                rows_in, keys_in, vals_in, send_ref, part_ref, att_ref, qg_ref, rows, keys, vals):
+                rows_in, keys_in, vals_in, scores_in, pg_in,
+                send_ref, part_ref, att_ref, qg_ref, rows, keys, vals, scores_ref, pg_ref):
     width = q_ref.shape[1]
     heads = bias_ref.shape[0]
     core = core_ref[0]
@@ -184,20 +196,20 @@
     rows[pl.ds(far_at, cap), :] = far[0:cap]
     for k, piece in enumerate((f1, f2, f3), 1):
         rows[pl.ds(far_at + k * cap, cap), :] = piece[...]
-    at = pl.ds(far_at, block)
-    keys[at, :] = nn(rows[at, :], wkv_ref[:, :width]).astype(BF16)
-    vals[at, :] = nn(rows[at, :], wkv_ref[:, width:]).astype(BF16)
+    columns(
+        pl.ds(far_at, block), wkv_ref, q_ref, ag_ref, bias_ref, rows, keys, vals, scores_ref, pg_ref
+    )
     for h in range(heads):
         at = slice(h * 128, (h + 1) * 128)
         q, ag = q_ref[:, at], ag_ref[:, at]
         kh, vh = keys[:, at], vals[:, at]
-        scores = nt(q, kh) + bias_ref[h]
+        scores = scores_ref[h]
         peak = jnp.max(scores, axis=1, keepdims=True)
         terms = jnp.exp(scores - peak)
         probs = terms * (1.0 / jnp.sum(terms, axis=1, keepdims=True))
         probs_b = probs.astype(BF16)
         att_ref[:, at] = nn(probs_b, vh).astype(BF16)
-        pg = nt(ag, vh)
+        pg = pg_ref[h]
         sg = (probs * (pg - jnp.sum(probs * pg, axis=1, keepdims=True))).astype(BF16)
         qg_ref[:, at] = (nn(sg, kh) * (128 ** -0.5)).astype(BF16)
         part_ref[:, at] = tn(sg, q).astype(BF16)
@@ -431,16 +443,20 @@
          pltpu.SemaphoreType.DMA((2,))],
     )
     table = sds((slots, width))
-    rows, keys, vals = call(
-        early_body, [table] * 3, [SM] + [VM] * 6, (core1, near, own, *mixed, weights_near),
+    map_of = sds((heads, nodes, slots), F32)
+    rows, keys, vals, scores, prob_grads = call(
+        early_body, [table] * 3 + [map_of] * 2, [SM] + [VM] * 9,
+        (core1, near, own, *mixed, weights_near, queries, att_grad, dense),
         1 << 29, 3 << 20, "early",
     )
     send, part_grads, attended, query_grad, rows, *_ = call(
         middle_body,
-        [sds((2 * width, width)), sds((slots, 2 * width))] + [sds((nodes, width))] * 2 + [table] * 3,
-        [SM] + [VM] * 13,
-        (core1, far, *outer, queries, att_grad, mesh_normed, og_near, dense, weights_near, rows, keys, vals),
-        3 << 30, 8 << 20, "middle", (), None, {11: 4, 12: 5, 13: 6},
+        [sds((2 * width, width)), sds((slots, 2 * width))] + [sds((nodes, width))] * 2 + [table] * 3
+        + [map_of] * 2,
+        [SM] + [VM] * 15,
+        (core1, far, *outer, queries, att_grad, mesh_normed, og_near, dense, weights_near, rows, keys, vals,
+         scores, prob_grads),
+        3 << 30, 8 << 20, "middle", (), None, {11: 4, 12: 5, 13: 6, 14: 7, 15: 8},
     )
 
     other = shifted(send, "gc", 1)

time: 93.3 us -> 92.5 us (level)
  waiting for transfers between devices: 23 us -> 24.4 us
  Pallas kernels: 24 us -> 22.8 us
  starting transfers between devices: 44.9 us -> 43.9 us
    ppermute x16, waiting for transfers between devices: 11.7 us -> 13.1 us  [shifted(): return lax.ppermute(block, axis, [(i, (i + k) % n) for i in range(n)])]
    pallas_call x17, Pallas kernels: 24 us -> 22.8 us  [call(): pl.pallas_call(body, out_shape=outs, in_specs=in_specs, out_specs=out_spe...]
  transfers between devices with their start and end apart: 20 -> 20, of which waited for: 10 -> 9; matrix products, arithmetic and copies ran while one was open for 0% -> 0% of each run, Pallas kernels for 13% -> 14%
where the time goes in v16:
time: 92.5 us; the launch traced here: 92.1 us
  starting transfers between devices  43.9 us (47%)
  waiting for transfers between devices  24.4 us (26%)
  Pallas kernels  22.8 us (25%)
  between operations  1.01 us (1%)
    ppermute x16, starting transfers between devices, shifted(): return lax.ppermute(block, axis, [(i, (i + k) % n) for i in range(n)])  23.8 us
    pallas_call x17, Pallas kernels, call(): pl.pallas_call(body, out_shape=outs, in_specs=in_specs, out_specs=out_spe...  22.8 us
    ppermute x16, waiting for transfers between devices, shifted(): return lax.ppermute(block, axis, [(i, (i + k) % n) for i in range(n)])  13.1 us
    all_to_all x1, starting transfers between devices, shards(): lax.all_to_all(own.reshape(plane, share, width), PLANE, 0, 0, tiled=True)  9.07 us
    ppermute x2, waiting for transfers between devices, swapped_far(): return lax.ppermute(block, SLAB, pairs + [(j, i) for i, j in pairs])  8.25 us
    ppermute x2, starting transfers between devices, swapped_far(): return lax.ppermute(block, SLAB, pairs + [(j, i) for i, j in pairs])  6.53 us
    all_to_all x1, starting transfers between devices, shards(): lax.all_to_all(spread, PLANE, 0, 0, tiled=True).reshape(2 * width, width)  4.51 us
    all_to_all x1, waiting for transfers between devices, shards(): lax.all_to_all(own.reshape(plane, share, width), PLANE, 0, 0, tiled=True)  2.99 us
  transfers between devices with their start and end apart: 20, of which 9 were waited for; matrix products, arithmetic and copies ran while one was open for 0% of the time, Pallas kernels for 14%

profile of v16, /device:TPU:1, one launch (start us, length us, event | category | flops | bytes accessed | tf_op | source)
XLA Modules:
  0.0 92.1 jit_solution(14237737467097647474)
XLA Ops:
  0.6 3.5 %gather_rows.1 = (bf16[256,512]{1,0:T(8,128)(2,1)S(1)}, bf16[256,512]{1,0:T(8,128)(2,1)S(1)}, bf16[256,512]{1,0:T(8,128)(2,1)S(1)}, s32[1,3,4,64]{3,2,1,0:T(4,12...) custom-call(s32[1]{0:T(128)} %bitcast.1.sub_ref, ...), custom_call_target="tpu_custom_call" | custom-call | flops 1073741824 | bytes 5242880 | tf_op jit(solution)/shard_map/gather_rows/pallas_call | solution.py:48
  4.2 1.5 %collective-permute-start.1 = (bf16[256,512]{1,0:T(8,128)(2,1)S(1)}, bf16[256,512]{1,0:T(8,128)(2,1)S(1)}, u32[]{:S(2)}, u32[]{:S(2)}) collective-permute-start(bf16[256,512]{1,0:T(8,128)(2,1)S(1)} %get-tuple-element.69), channel_id=1, source_target_pairs={{0,4},{4,0},{1,5},{5,1},{2,6},{6,2},{3,7},{7,3},{8,12},{12,8},{9,1... | collective-permute-start | bytes 786440 | tf_op jit(solution)/shard_map/ppermute | solution.py:384
  5.7 3.2 %collective-permute-start = (bf16[256,512]{1,0:T(8,128)(2,1)S(1)}, bf16[256,512]{1,0:T(8,128)(2,1)S(1)}, u32[]{:S(2)}, u32[]{:S(2)}) collective-permute-start(bf16[256,512]{1,0:T(8,128)(2,1)S(1)} %get-tuple-element.67), channel_id=1, source_target_pairs={{4,8},{12,16},{20,24},{28,32},{36,40},{44,48},{52,56},{60,64},{68,... | collective-permute-start | bytes 786440 | tf_op jit(solution)/shard_map/ppermute | solution.py:390
  8.9 1.7 %collective-permute-start.2 = (bf16[128,512]{1,0:T(8,128)(2,1)S(1)}, bf16[128,512]{1,0:T(8,128)(2,1)S(1)}, u32[]{:S(2)}, u32[]{:S(2)}) collective-permute-start(bf16[128,512]{1,0:T(8,128)(2,1)S(1)} %get-tuple-element.70), channel_id=1, source_target_pairs={{0,1},{1,2},{2,3},{3,0},{4,5},{5,6},{6,7},{7,4},{8,9},{9,10},{10,1... | collective-permute-start | bytes 393224 | tf_op jit(solution)/shard_map/ppermute | solution.py:384
  10.6 3.3 %collective-permute-start.6 = (bf16[128,512]{1,0:T(8,128)(2,1)S(1)}, bf16[128,512]{1,0:T(8,128)(2,1)S(1)}, u32[]{:S(2)}, u32[]{:S(2)}) collective-permute-start(bf16[128,512]{1,0:T(8,128)(2,1)S(1)} %get-tuple-element.92), channel_id=1, source_target_pairs={{0,2},{1,3},{2,0},{3,1},{4,6},{5,7},{6,4},{7,5},{8,10},{9,11},{10,... | collective-permute-start | bytes 393224 | tf_op jit(solution)/shard_map/ppermute | solution.py:384
  15.9 3.6 %collective-permute-start.4 = (bf16[64,512]{1,0:T(8,128)(2,1)S(1)}, bf16[64,512]{1,0:T(8,128)(2,1)S(1)}, u32[]{:S(2)}, u32[]{:S(2)}) collective-permute-start(bf16[64,512]{1,0:T(8,128)(2,1)S(1)} %get-tuple-element.80), channel_id=1, source_target_pairs={{0,2},{1,3},{2,0},{3,1},{4,6},{5,7},{6,4},{7,5},{8,10},{9,11},{10,... | collective-permute-start | bytes 196616 | tf_op jit(solution)/shard_map/ppermute | solution.py:384
  19.5 1.4 %slots.1 = (f32[4,64,768]{2,1,0:T(8,128)S(1)}, bf16[512,1024]{1,0:T(8,128)(2,1)S(1)}) custom-call(s32[1]{0:T(128)} %bitcast.1.sub_ref, s32[64,96]{1,0:T(8,128)S(1)} %get-tuple-element.86.nbr_ref, s32[64,96]{1,0:T(8,128)S(1)} %get-tuple-element.87.valid_ref, f32[64,384]{1,0:T(8,128)S(1)} %get-tuple-element.88.bias_ref, bf16[512,512]{1,0:T(8,128)(2,1)} %wk_hbm.1, ...), custom_call_target="tpu_custom_call" | custom-call | flops 1073741824 | bytes 8388608 | tf_op jit(solution)/shard_map/slots/pallas_call | solution.py:48
  22.6 2.7 %middle.1 = (bf16[1024,512]{1,0:T(8,128)(2,1)S(1)}, bf16[768,1024]{1,0:T(8,128)(2,1)S(1)}, bf16[64,512]{1,0:T(8,128)(2,1)S(1)}, bf16[64,512]{1,0:T(8,128)(2,1)S(...) custom-call(s32[1]{0:T(128)} %bitcast.core_ref, ...), custom_call_target="tpu_custom_call", output_to_operand_aliasing={{4}: (11, {}), {5}: (12, {}), {6}: (13, {}), {7}: (14, {}),... | custom-call | flops 3221225472 | bytes 8388608 | tf_op jit(solution)/shard_map/middle/pallas_call | solution.py:48
  26.2 1.7 %back.1 = (bf16[3,64,512]{2,1,0:T(8,128)(2,1)S(1)}, bf16[3,64,512]{2,1,0:T(8,128)(2,1)S(1)}, bf16[3,64,512]{2,1,0:T(8,128)(2,1)}, bf16[3,64,512]{2,1,0:T(8,128)(2,1)S(1)}) custom-call(bf16[768,1024]{1,0:T(8,128)(2,1)S(1)} %get-tuple-element.100.part_ref, bf16[512,1024]{1,0:T(8,128)(2,1)S(1)} %get-tuple-element.90.wkv_ref), custom_call_target="tpu_custom_call" | custom-call | flops 1073741824 | bytes 3145728 | tf_op jit(solution)/shard_map/back/pallas_call | solution.py:48
  29.1 9.1 %all-to-all-start = ((bf16[16,64,512]{2,1,0:T(8,128)(2,1)}), bf16[16,64,512]{2,1,0:T(8,128)(2,1)S(1)}, u32[]{:S(2)}, u32[]{:S(2)}) async-start(bf16[16,64,512]{2,1,0:T(8,128)(2,1)} %bitcast.4), calls=%async_computation | async-start | bytes 2097152 | tf_op jit(solution)/shard_map/all_to_all | solution.py:478
  40.6 1.6 %collective-permute-start.9 = (bf16[3,64,512]{2,1,0:T(8,128)(2,1)S(1)}, bf16[3,64,512]{2,1,0:T(8,128)(2,1)S(1)}, u32[]{:S(2)}, u32[]{:S(2)}) collective-permute-start(bf16[3,64,512]{2,1,0:T(8,128)(2,1)S(1)} %get-tuple-element.105), channel_id=1, source_target_pairs={{0,3},{1,0},{2,1},{3,2},{4,7},{5,4},{6,5},{7,6},{8,11},{9,8},{10,9... | collective-permute-start | bytes 589832 | tf_op jit(solution)/shard_map/ppermute | solution.py:384
  43.3 2.7 %collective-permute-done.10.p2.s2 = bf16[3,64,512]{2,1,0:T(8,128)(2,1)S(1)} collective-permute-done((bf16[3,64,512]{2,1,0:T(8,128)(2,1)}, bf16[3,64,512]{2,1,0:T(8,128)(2,1)S(1)}, u32[]{:S(2)}, u32[]{:S(2)}) %collective-permute-start.10) | collective-permute-done | bytes 196640 | tf_op jit(solution)/shard_map/ppermute | solution.py:384
  46.0 5.1 %collective-permute-done.11.p3.s3 = bf16[3,64,512]{2,1,0:T(8,128)(2,1)S(1)} collective-permute-done((bf16[3,64,512]{2,1,0:T(8,128)(2,1)S(1)}, bf16[3,64,512]{2,1,0:T(8,128)(2,1)S(1)}, u32[]{:S(2)}, u32[]{:S(2)}) %collective-permute-start.11) | collective-permute-done | bytes 196640 | tf_op jit(solution)/shard_map/ppermute | solution.py:384
  51.0 3.0 %all-to-all-done.parts_ref = bf16[16,64,512]{2,1,0:T(8,128)(2,1)S(1)} async-done(((bf16[16,64,512]{2,1,0:T(8,128)(2,1)}), bf16[16,64,512]{2,1,0:T(8,128)(2,1)S(1)}, u32[]{:S(2)}, u32[]{:S(2)}) %all-to-all-start) | async-done | bytes 1048608 | tf_op jit(solution)/shard_map/all_to_all | solution.py:478
  54.2 2.0 %collective-permute-start.14 = (bf16[64,512]{1,0:T(8,128)(2,1)S(1)}, bf16[64,512]{1,0:T(8,128)(2,1)S(1)}, u32[]{:S(2)}, u32[]{:S(2)}) collective-permute-start(bf16[64,512]{1,0:T(8,128)(2,1)S(1)} %plane.1.p0), channel_id=1, source_target_pairs={{0,3},{1,0},{2,1},{3,2},{4,7},{5,4},{6,5},{7,6},{8,11},{9,8},{10,9... | collective-permute-start | bytes 196616 | tf_op jit(solution)/shard_map/ppermute | solution.py:384
  58.1 2.8 %collective-permute-done.13.p2 = bf16[64,512]{1,0:T(8,128)(2,1)S(1)} collective-permute-done((bf16[64,512]{1,0:T(8,128)(2,1)S(1)}, bf16[64,512]{1,0:T(8,128)(2,1)S(1)}, u32[]{:S(2)}, u32[]{:S(2)}) %collective-permute-start.13) | collective-permute-done | bytes 65568 | tf_op jit(solution)/shard_map/ppermute | solution.py:384
  62.7 4.5 %all-to-all-start.1 = ((bf16[16,64,512]{2,1,0:T(8,128)(2,1)}), bf16[16,64,512]{2,1,0:T(8,128)(2,1)S(1)}, u32[]{:S(2)}, u32[]{:S(2)}) async-start(bf16[16,64,512]{2,1,0:T(8,128)(2,1)} %spread.1), calls=%async_computation.1 | async-start | bytes 2097152 | tf_op jit(solution)/shard_map/all_to_all | solution.py:499
  67.2 3.6 %collective-permute-start.16 = (bf16[256,512]{1,0:T(8,128)(2,1)S(1)}, bf16[256,512]{1,0:T(8,128)(2,1)S(1)}, u32[]{:S(2)}, u32[]{:S(2)}) collective-permute-start(bf16[256,512]{1,0:T(8,128)(2,1)S(1)} %get-tuple-element.122), channel_id=1, source_target_pairs={{0,4},{4,0},{1,5},{5,1},{2,6},{6,2},{3,7},{7,3},{8,12},{12,8},{9,1... | collective-permute-start | bytes 786440 | tf_op jit(solution)/shard_map/ppermute | solution.py:384
  70.8 3.3 %collective-permute-start.15 = (bf16[256,512]{1,0:T(8,128)(2,1)S(1)}, bf16[256,512]{1,0:T(8,128)(2,1)S(1)}, u32[]{:S(2)}, u32[]{:S(2)}) collective-permute-start(bf16[256,512]{1,0:T(8,128)(2,1)S(1)} %get-tuple-element.121), channel_id=1, source_target_pairs={{4,8},{12,16},{20,24},{28,32},{36,40},{44,48},{52,56},{60,64},{68,... | collective-permute-start | bytes 786440 | tf_op jit(solution)/shard_map/ppermute | solution.py:390
  74.2 3.1 %grid_near.1.prior_hbm = bf16[2048,512]{1,0:T(8,128)(2,1)} custom-call(s32[1]{0:T(128)} %bitcast.1.sub_ref, s32[1]{0:T(128)} %bitcast.core_ref, bf16[256,512]{1,0:T(8,128)(2,1)S(1)} %collective-permute-done.16.near, bf16[3,64,512]{2,1,0:T(8,128)(2,1)S(1)} %get-tuple-element.117.p0.s0, bf16[3,64,512]{2,1,0:T(8,128)(2,1)S(1)} %collective-permute-done.9.p1.s1, ...), custom_call_target="tpu_custom_call" | custom-call | flops 536870912 | bytes 3145728 | tf_op jit(solution)/shard_map/grid_near/pallas_call | solution.py:48
  77.2 8.2 %collective-permute-done.15.far = bf16[256,512]{1,0:T(8,128)(2,1)S(1)} collective-permute-done((bf16[256,512]{1,0:T(8,128)(2,1)S(1)}, bf16[256,512]{1,0:T(8,128)(2,1)S(1)}, u32[]{:S(2)}, u32[]{:S(2)}) %collective-permute-start.15) | collective-permute-done | bytes 262176 | tf_op jit(solution)/shard_map/ppermute | solution.py:390
  85.5 1.8 %collective-permute-start.17 = (bf16[1024,512]{1,0:T(8,128)(2,1)S(1)}, bf16[1024,512]{1,0:T(8,128)(2,1)S(1)}, u32[]{:S(2)}, u32[]{:S(2)}) collective-permute-start(bf16[1024,512]{1,0:T(8,128)(2,1)S(1)} %bitcast.6), channel_id=1, source_target_pairs={{0,4},{4,0},{1,5},{5,1},{2,6},{6,2},{3,7},{7,3},{8,12},{12,8},{9,1... | collective-permute-start | bytes 3145736 | tf_op jit(solution)/shard_map/ppermute | solution.py:384
  87.3 3.2 %grid_far.1 = (bf16[2048,512]{1,0:T(8,128)(2,1)}, f32[4,512,512]{2,1,0:T(8,128)}) custom-call(s32[1]{0:T(128)} %bitcast.1.sub_ref, s32[1]{0:T(128)} %bitcast.core_ref, bf16[256,512]{1,0:T(8,128)(2,1)S(1)} %collective-permute-done.15.far, bf16[3,64,512]{2,1,0:T(8,128)(2,1)S(1)} %get-tuple-element.117.p0.s0, ...), custom_call_target="tpu_custom_call", output_to_operand_aliasing={{0}: (11, {})} | custom-call | flops 536870912 | bytes 5242880 | tf_op jit(solution)/shard_map/grid_far/pallas_call | solution.py:48
  90.5 1.4 %widen.1 = f32[4,512,512]{2,1,0:T(8,128)} custom-call(s32[1]{0:T(128)} %bitcast.core_ref, bf16[1024,512]{1,0:T(8,128)(2,1)S(1)} %collective-permute-done.17.half_ref, f32[4,512,512]{2,1,0:T(8,128)} %get-tuple-element.129.prior_hbm), custom_call_target="tpu_custom_call", output_to_operand_aliasing={{}: (2, {})} | custom-call | flops 1048576 | bytes 3145728 | tf_op jit(solution)/shard_map/widen/pallas_call | solution.py:48
  (33 shorter events, 13.2 us)
Async XLA Ops:
  4.2 4.7 %collective-permute-start.1 = (bf16[256,512]{1,0:T(8,128)(2,1)S(1)}, bf16[256,512]{1,0:T(8,128)(2,1)S(1)}, u32[]{:S(2)}, u32[]{:S(2)}) collective-permute-start(bf16[256,512]{1,0:T(8,128)(2,1)S(1)} %get-tuple-element.69), channel_id=1, source_target_pairs={{0,4},{4,0},{1,5},{5,1},{2,6},{6,2},{3,7},{7,3},{8,12},{12,8},{9,1... | collective-permute-start | bytes 786440 | tf_op jit(solution)/shard_map/ppermute | solution.py:384
  5.7 9.4 %collective-permute-start = (bf16[256,512]{1,0:T(8,128)(2,1)S(1)}, bf16[256,512]{1,0:T(8,128)(2,1)S(1)}, u32[]{:S(2)}, u32[]{:S(2)}) collective-permute-start(bf16[256,512]{1,0:T(8,128)(2,1)S(1)} %get-tuple-element.67), channel_id=1, source_target_pairs={{4,8},{12,16},{20,24},{28,32},{36,40},{44,48},{52,56},{60,64},{68,... | collective-permute-start | bytes 786440 | tf_op jit(solution)/shard_map/ppermute | solution.py:390
  8.9 6.2 %collective-permute-start.2 = (bf16[128,512]{1,0:T(8,128)(2,1)S(1)}, bf16[128,512]{1,0:T(8,128)(2,1)S(1)}, u32[]{:S(2)}, u32[]{:S(2)}) collective-permute-start(bf16[128,512]{1,0:T(8,128)(2,1)S(1)} %get-tuple-element.70), channel_id=1, source_target_pairs={{0,1},{1,2},{2,3},{3,0},{4,5},{5,6},{6,7},{7,4},{8,9},{9,10},{10,1... | collective-permute-start | bytes 393224 | tf_op jit(solution)/shard_map/ppermute | solution.py:384
  10.6 10.3 %collective-permute-start.6 = (bf16[128,512]{1,0:T(8,128)(2,1)S(1)}, bf16[128,512]{1,0:T(8,128)(2,1)S(1)}, u32[]{:S(2)}, u32[]{:S(2)}) collective-permute-start(bf16[128,512]{1,0:T(8,128)(2,1)S(1)} %get-tuple-element.92), channel_id=1, source_target_pairs={{0,2},{1,3},{2,0},{3,1},{4,6},{5,7},{6,4},{7,5},{8,10},{9,11},{10,... | collective-permute-start | bytes 393224 | tf_op jit(solution)/shard_map/ppermute | solution.py:384
  13.9 7.0 %collective-permute-start.7 = (bf16[128,512]{1,0:T(8,128)(2,1)S(1)}, bf16[128,512]{1,0:T(8,128)(2,1)S(1)}, u32[]{:S(2)}, u32[]{:S(2)}) collective-permute-start(bf16[128,512]{1,0:T(8,128)(2,1)S(1)} %get-tuple-element.93), channel_id=1, source_target_pairs={{0,3},{1,0},{2,1},{3,2},{4,7},{5,4},{6,5},{7,6},{8,11},{9,8},{10,9... | collective-permute-start | bytes 393224 | tf_op jit(solution)/shard_map/ppermute | solution.py:384
  15.1 7.0 %collective-permute-start.3 = (bf16[64,512]{1,0:T(8,128)(2,1)S(1)}, bf16[64,512]{1,0:T(8,128)(2,1)S(1)}, u32[]{:S(2)}, u32[]{:S(2)}) collective-permute-start(bf16[64,512]{1,0:T(8,128)(2,1)S(1)} %get-tuple-element.79), channel_id=1, source_target_pairs={{0,1},{1,2},{2,3},{3,0},{4,5},{5,6},{6,7},{7,4},{8,9},{9,10},{10,1... | collective-permute-start | bytes 196616 | tf_op jit(solution)/shard_map/ppermute | solution.py:384
  15.9 6.2 %collective-permute-start.4 = (bf16[64,512]{1,0:T(8,128)(2,1)S(1)}, bf16[64,512]{1,0:T(8,128)(2,1)S(1)}, u32[]{:S(2)}, u32[]{:S(2)}) collective-permute-start(bf16[64,512]{1,0:T(8,128)(2,1)S(1)} %get-tuple-element.80), channel_id=1, source_target_pairs={{0,2},{1,3},{2,0},{3,1},{4,6},{5,7},{6,4},{7,5},{8,10},{9,11},{10,... | collective-permute-start | bytes 196616 | tf_op jit(solution)/shard_map/ppermute | solution.py:384
  19.5 3.1 %collective-permute-start.5 = (bf16[64,512]{1,0:T(8,128)(2,1)S(1)}, bf16[64,512]{1,0:T(8,128)(2,1)S(1)}, u32[]{:S(2)}, u32[]{:S(2)}) collective-permute-start(bf16[64,512]{1,0:T(8,128)(2,1)S(1)} %get-tuple-element.81), channel_id=1, source_target_pairs={{0,3},{1,0},{2,1},{3,2},{4,7},{5,4},{6,5},{7,6},{8,11},{9,8},{10,9... | collective-permute-start | bytes 196616 | tf_op jit(solution)/shard_map/ppermute | solution.py:384
  25.3 2.7 %collective-permute-start.8 = (bf16[1024,512]{1,0:T(8,128)(2,1)S(1)}, bf16[1024,512]{1,0:T(8,128)(2,1)S(1)}, u32[]{:S(2)}, u32[]{:S(2)}) collective-permute-start(bf16[1024,512]{1,0:T(8,128)(2,1)S(1)} %get-tuple-element.99), channel_id=1, source_target_pairs={{0,4},{4,0},{1,5},{5,1},{2,6},{6,2},{3,7},{7,3},{8,12},{12,8},{9,1... | collective-permute-start | bytes 3145736 | tf_op jit(solution)/shard_map/ppermute | solution.py:384
  29.1 24.9 %all-to-all-start = ((bf16[16,64,512]{2,1,0:T(8,128)(2,1)}), bf16[16,64,512]{2,1,0:T(8,128)(2,1)S(1)}, u32[]{:S(2)}, u32[]{:S(2)}) async-start(bf16[16,64,512]{2,1,0:T(8,128)(2,1)} %bitcast.4), calls=%async_computation | async-start | bytes 2097152 | tf_op jit(solution)/shard_map/all_to_all | solution.py:478
  38.2 7.8 %collective-permute-start.10 = (bf16[3,64,512]{2,1,0:T(8,128)(2,1)}, bf16[3,64,512]{2,1,0:T(8,128)(2,1)S(1)}, u32[]{:S(2)}, u32[]{:S(2)}) collective-permute-start(bf16[3,64,512]{2,1,0:T(8,128)(2,1)} %get-tuple-element.106), channel_id=1, source_target_pairs={{0,2},{1,3},{2,0},{3,1},{4,6},{5,7},{6,4},{7,5},{8,10},{9,11},{10,... | collective-permute-start | bytes 589832 | tf_op jit(solution)/shard_map/ppermute | solution.py:384
  39.5 11.5 %collective-permute-start.11 = (bf16[3,64,512]{2,1,0:T(8,128)(2,1)S(1)}, bf16[3,64,512]{2,1,0:T(8,128)(2,1)S(1)}, u32[]{:S(2)}, u32[]{:S(2)}) collective-permute-start(bf16[3,64,512]{2,1,0:T(8,128)(2,1)S(1)} %get-tuple-element.107), channel_id=1, source_target_pairs={{0,1},{1,2},{2,3},{3,0},{4,5},{5,6},{6,7},{7,4},{8,9},{9,10},{10,1... | collective-permute-start | bytes 589832 | tf_op jit(solution)/shard_map/ppermute | solution.py:384
  40.6 10.4 %collective-permute-start.9 = (bf16[3,64,512]{2,1,0:T(8,128)(2,1)S(1)}, bf16[3,64,512]{2,1,0:T(8,128)(2,1)S(1)}, u32[]{:S(2)}, u32[]{:S(2)}) collective-permute-start(bf16[3,64,512]{2,1,0:T(8,128)(2,1)S(1)} %get-tuple-element.105), channel_id=1, source_target_pairs={{0,3},{1,0},{2,1},{3,2},{4,7},{5,4},{6,5},{7,6},{8,11},{9,8},{10,9... | collective-permute-start | bytes 589832 | tf_op jit(solution)/shard_map/ppermute | solution.py:384
  54.2 3.9 %collective-permute-start.14 = (bf16[64,512]{1,0:T(8,128)(2,1)S(1)}, bf16[64,512]{1,0:T(8,128)(2,1)S(1)}, u32[]{:S(2)}, u32[]{:S(2)}) collective-permute-start(bf16[64,512]{1,0:T(8,128)(2,1)S(1)} %plane.1.p0), channel_id=1, source_target_pairs={{0,3},{1,0},{2,1},{3,2},{4,7},{5,4},{6,5},{7,6},{8,11},{9,8},{10,9... | collective-permute-start | bytes 196616 | tf_op jit(solution)/shard_map/ppermute | solution.py:384
  56.2 4.7 %collective-permute-start.13 = (bf16[64,512]{1,0:T(8,128)(2,1)S(1)}, bf16[64,512]{1,0:T(8,128)(2,1)S(1)}, u32[]{:S(2)}, u32[]{:S(2)}) collective-permute-start(bf16[64,512]{1,0:T(8,128)(2,1)S(1)} %plane.1.p0), channel_id=1, source_target_pairs={{0,2},{1,3},{2,0},{3,1},{4,6},{5,7},{6,4},{7,5},{8,10},{9,11},{10,... | collective-permute-start | bytes 196616 | tf_op jit(solution)/shard_map/ppermute | solution.py:384
  56.5 5.0 %collective-permute-start.12 = (bf16[64,512]{1,0:T(8,128)(2,1)S(1)}, bf16[64,512]{1,0:T(8,128)(2,1)S(1)}, u32[]{:S(2)}, u32[]{:S(2)}) collective-permute-start(bf16[64,512]{1,0:T(8,128)(2,1)S(1)} %plane.1.p0), channel_id=1, source_target_pairs={{0,1},{1,2},{2,3},{3,0},{4,5},{5,6},{6,7},{7,4},{8,9},{9,10},{10,1... | collective-permute-start | bytes 196616 | tf_op jit(solution)/shard_map/ppermute | solution.py:384
  62.7 22.8 %all-to-all-start.1 = ((bf16[16,64,512]{2,1,0:T(8,128)(2,1)}), bf16[16,64,512]{2,1,0:T(8,128)(2,1)S(1)}, u32[]{:S(2)}, u32[]{:S(2)}) async-start(bf16[16,64,512]{2,1,0:T(8,128)(2,1)} %spread.1), calls=%async_computation.1 | async-start | bytes 2097152 | tf_op jit(solution)/shard_map/all_to_all | solution.py:499
  67.2 6.9 %collective-permute-start.16 = (bf16[256,512]{1,0:T(8,128)(2,1)S(1)}, bf16[256,512]{1,0:T(8,128)(2,1)S(1)}, u32[]{:S(2)}, u32[]{:S(2)}) collective-permute-start(bf16[256,512]{1,0:T(8,128)(2,1)S(1)} %get-tuple-element.122), channel_id=1, source_target_pairs={{0,4},{4,0},{1,5},{5,1},{2,6},{6,2},{3,7},{7,3},{8,12},{12,8},{9,1... | collective-permute-start | bytes 786440 | tf_op jit(solution)/shard_map/ppermute | solution.py:384
  70.8 14.7 %collective-permute-start.15 = (bf16[256,512]{1,0:T(8,128)(2,1)S(1)}, bf16[256,512]{1,0:T(8,128)(2,1)S(1)}, u32[]{:S(2)}, u32[]{:S(2)}) collective-permute-start(bf16[256,512]{1,0:T(8,128)(2,1)S(1)} %get-tuple-element.121), channel_id=1, source_target_pairs={{4,8},{12,16},{20,24},{28,32},{36,40},{44,48},{52,56},{60,64},{68,... | collective-permute-start | bytes 786440 | tf_op jit(solution)/shard_map/ppermute | solution.py:390
  85.5 5.0 %collective-permute-start.17 = (bf16[1024,512]{1,0:T(8,128)(2,1)S(1)}, bf16[1024,512]{1,0:T(8,128)(2,1)S(1)}, u32[]{:S(2)}, u32[]{:S(2)}) collective-permute-start(bf16[1024,512]{1,0:T(8,128)(2,1)S(1)} %bitcast.6), channel_id=1, source_target_pairs={{0,4},{4,0},{1,5},{5,1},{2,6},{6,2},{3,7},{7,3},{8,12},{12,8},{9,1... | collective-permute-start | bytes 3145736 | tf_op jit(solution)/shard_map/ppermute | solution.py:384
